TPU v7x, 32 devices: a whole 2x2x4 slice. The times are simulated.
32 devices in a mesh: panel: 2 (over x), lat: 4 (over z), lon: 4 (over y, core).
Axes of the slice: x: 2, y: 2, z: 4, core: 2. Of those that a mesh axis runs over, the one named last changes fastest.
Arguments:
- state: float32 [2, 64, 64, 8, 128], P('panel', 'lat', 'lon'), may hold values from -6 to 6
- rim_base: int32 [2, 512, 2], P('panel', ('lat', 'lon')), may hold values from 1 to 61, as said below
- rim_weight: float32 [2, 512, 16], P('panel', ('lat', 'lon')), may hold values from -0.1 to 0.2
- rim_angle: float32 [2, 512], P('panel', ('lat', 'lon')), may hold values from -3 to 3
- rim_target: int32 [2, 512, 2], P('panel'), may hold values from -2 to 65, as said below
Outputs:
- change: float32 [2, 64, 64, 8, 128], P('panel', 'lat', 'lon')
Inputs may be any that keep to these rules, and one draw needn't show every extreme that they name: `rim_base`: entry e of panel p names a base cell (row, column) of panel p whose 4 x 4 donor stencil, rows and columns from base - 1 to base + 2, lies inside the panel; the base cell lies in block e // 32 of 16 x 16 cells, blocks numbered row by row with 4 blocks to a row. `rim_target`: the rim of panel q is a loop of 512 positions: rows -2 and -1 at columns 0 to 64 - 1 (column by column, row -2 first), then columns 64 and 65 at rows 0 to 64 - 1 (row by row), then rows 64 and 65 at columns 63 down to 0, then columns -2 and -1 at rows 63 down to 0. Entry e, with b = e // 32 and i = e % 32, fills loop position (i * 16 + b + o_q) mod 512, for one offset o_q per panel.
All inputs are finite; a program needn't handle non-finite values.
Results may differ from a plain program's by a relative error of at most 0.00015.
Values sent between devices are 32-bit elements; how exact they have to be, the bound alone decides.
No kernel may reach another device: no remote copies, remote signals or barrier semaphores. Data moves between devices by JAX's collectives and lax.ppermute only.
A program may use at most 64 MiB of HBM per device.

v0:
```python
import math

import jax
import jax.numpy as jnp
from jax import lax
from jax.sharding import PartitionSpec as P

ETA_COEF = 0.2
NU_COEF = 0.2
KAPPA_COEF = 0.3
SOUND_SQ = 1.0
ARCHIMEDES_LIFT = 0.5
TIME_STEP = 0.2


def extended(x, sides, width):
    for axis, dim in sides:
        count, length = (lax.axis_size(axis), x.shape[dim])
        up = [(i, (i + 1) % count) for i in range(count - 1)]
        down = [(j, i) for i, j in up]
        last = lax.slice_in_dim(x, length - width, length, axis=dim)
        leading = lax.slice_in_dim(x, 0, width, axis=dim)
        before = lax.ppermute(last, axis, up)
        after = lax.ppermute(leading, axis, down)
        x = jnp.concatenate([before, x, after], axis=dim)
    return x


def from_partner(block, axis, distance):
    count = lax.axis_size(axis)
    route = []
    for low in range(count):
        high = low | 1 << distance
        if high != low and high < count:
            route += [(low, high), (high, low)]
    return lax.ppermute(block, axis, route)


def grid_geometry(levels, theta_count, phi_count):
    radius_scale = 2.0 * theta_count / math.pi
    radial_step = 0.65 * radius_scale / levels
    radius = (
        0.35 * radius_scale
        + (jnp.arange(levels, dtype=jnp.int32).astype(jnp.float32) + 0.5) * radial_step
    )
    return (radius, radial_step, math.pi / (2 * theta_count), 1.5 * math.pi / phi_count)


def theta_sine(first_row, count, theta_count):
    row_index = first_row + jnp.arange(count, dtype=jnp.int32)
    colatitude = math.pi / 4 + (row_index.astype(jnp.float32) + 0.5) * (math.pi / (2 * theta_count))
    return jnp.sin(colatitude)


def inner_volumes(quantity):
    return quantity[1:-1, 1:-1]


def diff_theta(quantity, spacing):
    return (quantity[2:, 1:-1] - quantity[:-2, 1:-1]) * (0.5 / spacing)


def diff_phi(quantity, spacing):
    return (quantity[1:-1, 2:] - quantity[1:-1, :-2]) * (0.5 / spacing)


def diff_radius(quantity, spacing):
    zero_layer = jnp.zeros(quantity.shape[:-1] + (1,), quantity.dtype)
    upper_part = jnp.concatenate([quantity[..., 1:], zero_layer], axis=-1)
    lower_part = jnp.concatenate([zero_layer, quantity[..., :-1]], axis=-1)
    return (upper_part - lower_part) * (0.5 / spacing)


def curl_of(directional_components, colatitude_factor_list, spherical_layout):
    radius, radial_step, polar_step, azimuth_step = spherical_layout
    radial_part, polar_part, azimuth_part = directional_components
    polar_factor_halfway = colatitude_factor_list[1:-1]
    out_radial = (
        diff_theta(colatitude_factor_list * azimuth_part, polar_step)
        - diff_phi(polar_part, azimuth_step)
    ) / (radius * polar_factor_halfway)
    out_polar = (
        diff_phi(radial_part, azimuth_step) / polar_factor_halfway
        - diff_radius(inner_volumes(radius * azimuth_part), radial_step)
    ) / radius
    out_azimuth = (
        diff_radius(inner_volumes(radius * polar_part), radial_step)
        - diff_theta(radial_part, polar_step)
    ) / radius
    return (out_radial, out_polar, out_azimuth)


def slope_quantity(quantity, colatitude_factor_list, spherical_layout):
    radius, radial_step, polar_step, azimuth_step = spherical_layout
    polar_factor_halfway = colatitude_factor_list[1:-1]
    return (
        diff_radius(inner_volumes(quantity), radial_step),
        diff_theta(quantity, polar_step) / radius,
        diff_phi(quantity, azimuth_step) / (radius * polar_factor_halfway),
    )


def outflow_density(directional_components, colatitude_factor_list, spherical_layout):
    radius, radial_step, polar_step, azimuth_step = spherical_layout
    radial_part, polar_part, azimuth_part = directional_components
    polar_factor_halfway = colatitude_factor_list[1:-1]
    radial_term = diff_radius(inner_volumes(radius * radius * radial_part), radial_step) / (
        radius * radius
    )
    return radial_term + (
        diff_theta(colatitude_factor_list * polar_part, polar_step)
        + diff_phi(azimuth_part, azimuth_step)
    ) / (radius * polar_factor_halfway)


def cross_product(left, right):
    return (
        left[1] * right[2] - left[2] * right[1],
        left[2] * right[0] - left[0] * right[2],
        left[0] * right[1] - left[1] * right[0],
    )


def dot_product(left, right):
    return left[0] * right[0] + left[1] * right[1] + left[2] * right[2]


def tendency(padded, colatitude_factor_list, spherical_layout):
    directional_components = [padded[:, :, number, :] for number in range(8)]
    velocity = tuple(directional_components[0:3])
    magnetic = tuple(directional_components[3:6])
    warmth_state = directional_components[6]
    pressure = directional_components[7]
    polar_factor_halfway = colatitude_factor_list[1:-1]
    current = curl_of(magnetic, colatitude_factor_list, spherical_layout)
    vorticity = curl_of(velocity, colatitude_factor_list, spherical_layout)
    warmth_slope = slope_quantity(warmth_state, colatitude_factor_list, spherical_layout)
    velocity_mid = tuple((inner_volumes(part) for part in velocity))
    magnetic_mid = tuple((inner_volumes(part) for part in magnetic))
    induced = cross_product(velocity_mid, magnetic_mid)
    electric = tuple((induced[number] - ETA_COEF * current[number] for number in range(3)))
    magnetic_rate = curl_of(electric, polar_factor_halfway, spherical_layout)
    vorticity_curl = curl_of(vorticity, polar_factor_halfway, spherical_layout)
    thermal_flux = outflow_density(warmth_slope, polar_factor_halfway, spherical_layout)
    total_head = inner_volumes(pressure) + 0.5 * dot_product(velocity_mid, velocity_mid)
    head_grad = slope_quantity(total_head, polar_factor_halfway, spherical_layout)
    pressure_rate = -SOUND_SQ * outflow_density(
        velocity_mid, polar_factor_halfway, spherical_layout
    )
    velocity_in = tuple((inner_volumes(part) for part in velocity_mid))
    magnetic_in = tuple((inner_volumes(part) for part in magnetic_mid))
    current_in = tuple((inner_volumes(part) for part in current))
    vorticity_in = tuple((inner_volumes(part) for part in vorticity))
    slope_heat_entering = tuple((inner_volumes(part) for part in warmth_slope))
    warmth_entering = inner_volumes(inner_volumes(warmth_state))
    lorentz = cross_product(current_in, magnetic_in)
    advect = cross_product(velocity_in, vorticity_in)
    flow_acceleration = [
        advect[number] + lorentz[number] - head_grad[number] - NU_COEF * vorticity_curl[number]
        for number in range(3)
    ]
    flow_acceleration[0] = flow_acceleration[0] + ARCHIMEDES_LIFT * warmth_entering
    temp_rate = KAPPA_COEF * thermal_flux - dot_product(velocity_in, slope_heat_entering)
    return jnp.stack(flow_acceleration + list(magnetic_rate) + [temp_rate, pressure_rate], axis=2)


def interpolate(donors, weights, turning):
    mixed = jnp.einsum("ek,ekfr->efr", weights, donors, precision=lax.Precision.HIGHEST)
    cosine = jnp.cos(turning)[:, None]
    sine_turn = jnp.sin(turning)[:, None]
    return jnp.stack(
        [
            mixed[:, 0],
            cosine * mixed[:, 1] - sine_turn * mixed[:, 2],
            sine_turn * mixed[:, 1] + cosine * mixed[:, 2],
            mixed[:, 3],
            cosine * mixed[:, 4] - sine_turn * mixed[:, 5],
            sine_turn * mixed[:, 4] + cosine * mixed[:, 5],
            mixed[:, 6],
            mixed[:, 7],
        ],
        axis=1,
    )


def neighbour_block(position, owner, block_len, block_total, inside_band):
    rest = position - owner * block_len
    step_dir = jnp.where(rest < 2, -1, jnp.where(rest >= block_len - 2, 1, 0))
    beside = owner + step_dir
    usable = inside_band & (step_dir != 0) & (beside >= 0) & (beside < block_total)
    return (beside, usable)


def per_device(state, rim_base, rim_weight, rim_angle, rim_target):
    own_block = state[0]
    block_rows = own_block.shape[0]
    block_cols = own_block.shape[1]
    field_count = own_block.shape[2]
    level_count = own_block.shape[3]
    lat_count = lax.axis_size("lat")
    lon_count = lax.axis_size("lon")
    theta_count = block_rows * lat_count
    phi_count = block_cols * lon_count
    first_row = lax.axis_index("lat") * block_rows
    first_col = lax.axis_index("lon") * block_cols
    padded_cols = block_cols + 4
    padded_cells = (block_rows + 4) * padded_cols
    spherical_layout = grid_geometry(level_count, theta_count, phi_count)
    colatitude_factor_list = theta_sine(first_row - 2, block_rows + 4, theta_count)[:, None, None]
    base_cell = rim_base[0]
    entry_count = base_cell.shape[0]
    base_flat = (base_cell[:, 0] - first_row + 2) * padded_cols + (base_cell[:, 1] - first_col + 2)
    steps_row = jnp.arange(4, dtype=jnp.int32)
    offsets = ((steps_row[:, None] - 1) * padded_cols + steps_row[None, :] - 1).reshape(1, 16)
    donor_index = base_flat[:, None] + offsets
    weights = rim_weight[0]
    turning = rim_angle[0]
    block_total = lat_count * lon_count
    slot_count = 2 * ((2 * (max(block_rows, block_cols) + 4) + block_total - 1) // block_total)
    bucket_total = block_total * slot_count
    my_block = lax.axis_index("lat") * lon_count + lax.axis_index("lon")
    entry_target = lax.dynamic_slice_in_dim(rim_target[0], my_block * entry_count, entry_count, 0)
    target_row = entry_target[:, 0]
    target_col = entry_target[:, 1]
    row_inside = (target_row >= 0) & (target_row < theta_count)
    col_inside = (target_col >= 0) & (target_col < phi_count)
    owner_row = jnp.clip(target_row, 0, theta_count - 1) // block_rows
    owner_col = jnp.clip(target_col, 0, phi_count - 1) // block_cols
    next_row, row_usable = neighbour_block(target_row, owner_row, block_rows, lat_count, row_inside)
    next_col, col_usable = neighbour_block(target_col, owner_col, block_cols, lon_count, col_inside)
    first_dest = owner_row * lon_count + owner_col
    second_dest = jnp.where(
        row_usable,
        next_row * lon_count + owner_col,
        jnp.where(col_usable, owner_row * lon_count + next_col, -1),
    )
    dest_all = jnp.concatenate([first_dest, second_dest])
    order_ids = jnp.arange(2 * entry_count, dtype=jnp.int32)
    earlier = (dest_all[:, None] == dest_all[None, :]) & (order_ids[None, :] < order_ids[:, None])
    rank = jnp.sum(earlier.astype(jnp.int32), axis=1)
    slot_ids = jnp.where(dest_all >= 0, dest_all * slot_count + rank, bucket_total)
    source_ids = jnp.concatenate(
        [jnp.arange(entry_count, dtype=jnp.int32), jnp.arange(entry_count, dtype=jnp.int32)]
    )
    send_coords = (
        jnp.full((bucket_total, 2), -1000, jnp.int32)
        .at[slot_ids]
        .set(entry_target[source_ids], mode="drop")
    )
    got_coords = lax.all_to_all(
        send_coords, ("lat", "lon"), split_axis=0, concat_axis=0, tiled=True
    )
    local_row = got_coords[:, 0] - first_row + 2
    local_col = got_coords[:, 1] - first_col + 2
    inside = (
        (local_row >= 0)
        & (local_row < block_rows + 4)
        & (local_col >= 0)
        & (local_col < padded_cols)
    )
    routed_flat = jnp.where(inside, local_row * padded_cols + local_col, padded_cells)

    def evaluate(current_fields):
        padded = extended(current_fields, (("lat", 0), ("lon", 1)), 2)
        flat_cells = padded.reshape(padded_cells, field_count, level_count)
        values = interpolate(flat_cells[donor_index], weights, turning)
        partner = from_partner(values, "panel", 0)
        send_values = (
            jnp.zeros((bucket_total, field_count, level_count), jnp.float32)
            .at[slot_ids]
            .set(partner[source_ids], mode="drop")
        )
        got_values = lax.all_to_all(
            send_values, ("lat", "lon"), split_axis=0, concat_axis=0, tiled=True
        )
        flat_cells = flat_cells.at[routed_flat].set(got_values, mode="drop")
        framed = flat_cells.reshape(block_rows + 4, padded_cols, field_count, level_count)
        return tendency(framed, colatitude_factor_list, spherical_layout)

    first_rate = evaluate(own_block)
    second_rate = evaluate(own_block + TIME_STEP * first_rate)
    return (0.5 * TIME_STEP * (first_rate + second_rate))[None]


def solution(mesh):
    return jax.shard_map(
        per_device,
        mesh=mesh,
        in_specs=(
            P("panel", "lat", "lon", None, None),
            P("panel", ("lat", "lon"), None),
            P("panel", ("lat", "lon"), None),
            P("panel", ("lat", "lon")),
            P("panel", None, None),
        ),
        out_specs=P("panel", "lat", "lon", None, None),
        check_vma=False,
    )
```

profile of v0, /device:TPU:0, one launch (start us, length us, event | category | flops | bytes accessed | tf_op | source)
XLA Modules:
  0.0 142.3 jit_solution(7656148086394840452)
XLA Ops:
  2.4 5.6 %collective-permute-start = (f32[2,16,8,128]{3,2,1,0:T(8,128)S(1)}, f32[2,16,8,128]{3,2,1,0:T(8,128)S(1)}, u32[]{:S(2)}, u32[]{:S(2)}) collective-permute-start(f32[2,16,8,128]{3,2,1,0:T(8,128)S(1)} %get-tuple-element.77), channel_id=1, source_target_pairs={{0,4},{4,8},{8,12},{1,5},{5,9},{9,13},{2,6},{6,10},{10,14},{3,7},{... | collective-permute-start | bytes 393224 | tf_op jit(solution)/shard_map/ppermute | solution.py:23
  10.4 5.4 %all-to-all-start = ((s32[16,6,2]{1,2,0:T(2,128)}), s32[16,6,2]{1,2,0:T(2,128)S(1)}, u32[]{:S(2)}, u32[]{:S(2)}) async-start(s32[16,6,2]{1,2,0:T(2,128)} %copy.102), calls=%async_computation | async-start | bytes 32768 | tf_op jit(solution)/shard_map/all_to_all | solution.py:250
  18.5 1.3 collective-permute-start.3
  19.8 3.0 %collective-permute-start.2 = (f32[20,2,8,128]{3,2,1,0:T(8,128)S(1)}, f32[20,2,8,128]{3,2,1,0:T(8,128)S(1)}, u32[]{:S(2)}, u32[]{:S(2)}) collective-permute-start(f32[20,2,8,128]{3,2,1,0:T(8,128)S(1)} %get-tuple-element.73), channel_id=1, source_target_pairs={{0,1},{1,2},{2,3},{4,5},{5,6},{6,7},{8,9},{9,10},{10,11},{12,13},{... | collective-permute-start | bytes 491528 | tf_op jit(solution)/shard_map/ppermute | solution.py:23
  24.0 2.7 %gather_fusion = f32[512,8,128]{2,1,0:T(8,128)} fusion(f32[400,8,128]{2,1,0:T(8,128)S(1)} %bitcast.206, s32[1024]{0:T(1024)S(1)} %pad_clamp_fusion), kind=kCustom, calls=%fused_computation.1 | custom fusion | bytes 4196352 | tf_op jit(solution)/shard_map/gather | solution.py:266
  26.7 3.0 %fusion.2 = f32[32,1,8,128]{3,1,2,0:T(1,128)S(1)} fusion(f32[32,16,1,1]{1,2,3,0:T(1,128)S(1)} %copy.131, f32[32,16,8,128]{3,2,1,0:T(8,128)} %bitcast.232), kind=kOutput, calls=%fused_computation.12 | convolution fusion | flops 6291456 | bytes 2230272 | tf_op jit(solution)/shard_map/ek,ekfr->efr/dot_general | solution.py:168
  30.0 1.6 %collective-permute-start.4 = (f32[32,8,128]{2,0,1:T(8,128)S(1)}, f32[32,8,128]{2,0,1:T(8,128)S(1)}, u32[]{:S(2)}, u32[]{:S(2)}) collective-permute-start(f32[32,8,128]{2,0,1:T(8,128)S(1)} %constant_dynamic-update-slice_fusion), channel_id=1, source_target_pairs={{0,16},{16,0},{1,17},{17,1},{2,18},{18,2},{3,19},{19,3},{4,20},{20... | collective-permute-start | bytes 393224 | tf_op jit(solution)/shard_map/ppermute | solution.py:36
  31.8 3.3 %collective-permute-done.4 = f32[32,8,128]{2,0,1:T(8,128)S(1)} collective-permute-done((f32[32,8,128]{2,0,1:T(8,128)S(1)}, f32[32,8,128]{2,0,1:T(8,128)S(1)}, u32[]{:S(2)}, u32[]{:S(2)}) %collective-permute-start.4) | collective-permute-done | bytes 131104 | tf_op jit(solution)/shard_map/ppermute | solution.py:36
  36.6 7.2 %scatter_fusion = f32[96,8,128]{2,1,0:T(8,128)} fusion(f32[96,8,128]{2,1,0:T(8,128)} %broadcast.566.clone, s32[64]{0:T(128)S(1)} %fusion.180, f32[64,8,128]{2,1,0:T(8,128)S(1)} %gather_fusion.1), kind=kCustom, calls=%fused_computation.6 | custom fusion | bytes 786688 | tf_op jit(solution)/shard_map/scatter | solution.py:271
  43.7 9.5 %all-to-all-start.1 = ((f32[96,8,128]{2,1,0:T(8,128)}), f32[96,8,128]{2,1,0:T(8,128)S(1)}, u32[]{:S(2)}, u32[]{:S(2)}) async-start(f32[96,8,128]{2,1,0:T(8,128)} %scatter_fusion), calls=%async_computation.1 | async-start | bytes 786432 | tf_op jit(solution)/shard_map/all_to_all | solution.py:273
  53.5 11.9 %all-to-all-done.1 = f32[96,8,128]{2,1,0:T(8,128)S(1)} async-done(((f32[96,8,128]{2,1,0:T(8,128)}), f32[96,8,128]{2,1,0:T(8,128)S(1)}, u32[]{:S(2)}, u32[]{:S(2)}) %all-to-all-start.1) | async-done | bytes 393248 | tf_op jit(solution)/shard_map/all_to_all | solution.py:273
  65.4 3.4 %scatter_fusion.1 = f32[400,8,128]{2,1,0:T(8,128)S(1)} fusion(f32[400,8,128]{2,1,0:T(8,128)S(1)} %bitcast.207, s32[96]{0:T(128)S(1)} %fusion.179, f32[96,8,128]{2,1,0:T(8,128)S(1)} %all-to-all-done.1), kind=kCustom, calls=%fused_computation.7 | custom fusion | bytes 1180032 | tf_op jit(solution)/shard_map/scatter | solution.py:276
  79.4 2.9 %stack.106 = f32[16,16,8,128]{3,2,1,0:T(8,128)S(1)} concatenate(f32[16,16,1,128]{3,2,1,0:T(1,128)} %bitcast.262, f32[16,16,1,128]{3,2,1,0:T(1,128)} %bitcast.269, f32[16,16,1,128]{3,2,1,0:T(1,128)} %bitcast.263, f32[16,16,1,128]{3,2,1,0:T(1,128)} %bitcast.264, f32[16,16,1,128]{3,2,1,0:T(1,128)} %bitcast.266, f32[16,16,1,128]{3,2,1,0:T(1,128)} %bitcast.267, ...), dimensions={2} | concatenate | bytes 2097152 | tf_op jit(solution)/shard_map/stack | solution.py:164
  82.6 1.3 collective-permute-start.6
  83.9 4.6 %collective-permute-start.5 = (f32[2,16,8,128]{3,2,1,0:T(8,128)S(1)}, f32[2,16,8,128]{3,2,1,0:T(8,128)S(1)}, u32[]{:S(2)}, u32[]{:S(2)}) collective-permute-start(f32[2,16,8,128]{3,2,1,0:T(8,128)S(1)} %get-tuple-element.75), channel_id=1, source_target_pairs={{0,4},{4,8},{8,12},{1,5},{5,9},{9,13},{2,6},{6,10},{10,14},{3,7},{... | collective-permute-start | bytes 393224 | tf_op jit(solution)/shard_map/ppermute | solution.py:23
  88.4 1.6 %collective-permute-done.6 = f32[2,16,8,128]{3,2,1,0:T(8,128)S(1)} collective-permute-done((f32[2,16,8,128]{3,2,1,0:T(8,128)S(1)}, f32[2,16,8,128]{3,2,1,0:T(8,128)S(1)}, u32[]{:S(2)}, u32[]{:S(2)}) %collective-permute-start.6) | collective-permute-done | bytes 131104 | tf_op jit(solution)/shard_map/ppermute | solution.py:24
  92.6 3.2 %collective-permute-start.7 = (f32[20,2,8,128]{3,2,1,0:T(8,128)S(1)}, f32[20,2,8,128]{3,2,1,0:T(8,128)S(1)}, u32[]{:S(2)}, u32[]{:S(2)}) collective-permute-start(f32[20,2,8,128]{3,2,1,0:T(8,128)S(1)} %get-tuple-element.71), channel_id=1, source_target_pairs={{0,1},{1,2},{2,3},{4,5},{5,6},{6,7},{8,9},{9,10},{10,11},{12,13},{... | collective-permute-start | bytes 491528 | tf_op jit(solution)/shard_map/ppermute | solution.py:23
  96.8 2.7 %gather_fusion.2 = f32[512,8,128]{2,1,0:T(8,128)} fusion(f32[400,8,128]{2,1,0:T(8,128)S(1)} %bitcast.209, s32[1024]{0:T(1024)S(1)} %pad_clamp_fusion), kind=kCustom, calls=%fused_computation.3 | custom fusion | bytes 4196352 | tf_op jit(solution)/shard_map/gather | solution.py:266
  99.5 3.0 %fusion = f32[32,1,8,128]{3,1,2,0:T(1,128)S(1)} fusion(f32[32,16,1,1]{1,2,3,0:T(1,128)S(1)} %copy.131, f32[32,16,8,128]{3,2,1,0:T(8,128)} %bitcast.231), kind=kOutput, calls=%fused_computation.10 | convolution fusion | flops 6291456 | bytes 2230272 | tf_op jit(solution)/shard_map/ek,ekfr->efr/dot_general | solution.py:168
  103.7 4.9 %collective-permute-done.9 = f32[32,8,128]{2,0,1:T(8,128)S(1)} collective-permute-done((f32[32,8,128]{2,0,1:T(8,128)S(1)}, f32[32,8,128]{2,0,1:T(8,128)S(1)}, u32[]{:S(2)}, u32[]{:S(2)}) %collective-permute-start.9) | collective-permute-done | bytes 131104 | tf_op jit(solution)/shard_map/ppermute | solution.py:36
  109.3 2.5 %scatter_fusion.2 = f32[96,8,128]{2,1,0:T(8,128)S(1)} fusion(f32[96,8,128]{2,1,0:T(8,128)S(1)} %broadcast.566, s32[64]{0:T(128)S(1)} %fusion.180, f32[64,8,128]{2,1,0:T(8,128)S(1)} %gather_fusion.3), kind=kCustom, calls=%fused_computation.8 | custom fusion | bytes 786688 | tf_op jit(solution)/shard_map/scatter | solution.py:271
  111.8 19.8 %all_to_all.22 = f32[96,8,128]{2,1,0:T(8,128)S(1)} all-to-all(f32[96,8,128]{2,1,0:T(8,128)S(1)} %scatter_fusion.2), channel_id=1, replica_groups=mesh['panel'=2,'lat'=4,'lon'=4] {'lat','lon'}, dimensions={0} | all-to-all | bytes 786432 | tf_op jit(solution)/shard_map/all_to_all | solution.py:273
  131.5 3.4 %scatter_fusion.3 = f32[400,8,128]{2,1,0:T(8,128)S(1)} fusion(f32[400,8,128]{2,1,0:T(8,128)S(1)} %bitcast.210, s32[96]{0:T(128)S(1)} %fusion.179, f32[96,8,128]{2,1,0:T(8,128)S(1)} %all_to_all.22), kind=kCustom, calls=%fused_computation.9 | custom fusion | bytes 1180032 | tf_op jit(solution)/shard_map/scatter | solution.py:276
  140.8 1.6 %copy.129 = f32[1,16,16,8,128]{4,3,2,1,0:T(8,128)} copy(f32[1,16,16,8,128]{4,2,1,3,0:T(8,128)S(1)} %add_multiply_fusion) | data formatting | bytes 2097152 | tf_op jit(solution)/shard_map/mul | solution.py:282
  (155 shorter events, 32.4 us)
Async XLA Ops:
  0.0 8.0 %copy-start = (s32[1,512,2]{1,2,0:T(2,128)S(1)}, s32[1,512,2]{1,2,0:T(2,128)}, u32[]{:S(2)}) copy-start(s32[1,512,2]{1,2,0:T(2,128)} %param.9) | copy-start | bytes 12292
  0.0 23.9 %copy-start.1 = (f32[1,16,16,8,128]{4,3,2,1,0:T(8,128)S(1)}, f32[1,16,16,8,128]{4,3,2,1,0:T(8,128)}, u32[]{:S(2)}) copy-start(f32[1,16,16,8,128]{4,3,2,1,0:T(8,128)} %param.5) | copy-start | bytes 3145732
  0.0 22.9 %copy-start.2 = (f32[1,32,16]{1,2,0:T(8,128)S(1)}, f32[1,32,16]{1,2,0:T(8,128)}, u32[]{:S(2)}) copy-start(f32[1,32,16]{1,2,0:T(8,128)} %param.7) | copy-start | bytes 6148
  1.1 16.4 %collective-permute-start.1 = (f32[2,16,8,128]{3,2,1,0:T(8,128)S(1)}, f32[2,16,8,128]{3,2,1,0:T(8,128)S(1)}, u32[]{:S(2)}, u32[]{:S(2)}) collective-permute-start(f32[2,16,8,128]{3,2,1,0:T(8,128)S(1)} %get-tuple-element.78), channel_id=1, source_target_pairs={{4,0},{8,4},{12,8},{5,1},{9,5},{13,9},{6,2},{10,6},{14,10},{7,3},{... | collective-permute-start | bytes 393224 | tf_op jit(solution)/shard_map/ppermute | solution.py:24
  2.4 15.1 %collective-permute-start = (f32[2,16,8,128]{3,2,1,0:T(8,128)S(1)}, f32[2,16,8,128]{3,2,1,0:T(8,128)S(1)}, u32[]{:S(2)}, u32[]{:S(2)}) collective-permute-start(f32[2,16,8,128]{3,2,1,0:T(8,128)S(1)} %get-tuple-element.77), channel_id=1, source_target_pairs={{0,4},{4,8},{8,12},{1,5},{5,9},{9,13},{2,6},{6,10},{10,14},{3,7},{... | collective-permute-start | bytes 393224 | tf_op jit(solution)/shard_map/ppermute | solution.py:23
  10.4 33.3 %all-to-all-start = ((s32[16,6,2]{1,2,0:T(2,128)}), s32[16,6,2]{1,2,0:T(2,128)S(1)}, u32[]{:S(2)}, u32[]{:S(2)}) async-start(s32[16,6,2]{1,2,0:T(2,128)} %copy.102), calls=%async_computation | async-start | bytes 32768 | tf_op jit(solution)/shard_map/all_to_all | solution.py:250
  18.5 4.5 %collective-permute-start.3 = (f32[20,2,8,128]{3,2,1,0:T(8,128)S(1)}, f32[20,2,8,128]{3,2,1,0:T(8,128)S(1)}, u32[]{:S(2)}, u32[]{:S(2)}) collective-permute-start(f32[20,2,8,128]{3,2,1,0:T(8,128)S(1)} %get-tuple-element.74), channel_id=1, source_target_pairs={{1,0},{2,1},{3,2},{5,4},{6,5},{7,6},{9,8},{10,9},{11,10},{13,12},{... | collective-permute-start | bytes 491528 | tf_op jit(solution)/shard_map/ppermute | solution.py:24
  19.8 4.0 %collective-permute-start.2 = (f32[20,2,8,128]{3,2,1,0:T(8,128)S(1)}, f32[20,2,8,128]{3,2,1,0:T(8,128)S(1)}, u32[]{:S(2)}, u32[]{:S(2)}) collective-permute-start(f32[20,2,8,128]{3,2,1,0:T(8,128)S(1)} %get-tuple-element.73), channel_id=1, source_target_pairs={{0,1},{1,2},{2,3},{4,5},{5,6},{6,7},{8,9},{9,10},{10,11},{12,13},{... | collective-permute-start | bytes 491528 | tf_op jit(solution)/shard_map/ppermute | solution.py:23
  30.0 5.0 %collective-permute-start.4 = (f32[32,8,128]{2,0,1:T(8,128)S(1)}, f32[32,8,128]{2,0,1:T(8,128)S(1)}, u32[]{:S(2)}, u32[]{:S(2)}) collective-permute-start(f32[32,8,128]{2,0,1:T(8,128)S(1)} %constant_dynamic-update-slice_fusion), channel_id=1, source_target_pairs={{0,16},{16,0},{1,17},{17,1},{2,18},{18,2},{3,19},{19,3},{4,20},{20... | collective-permute-start | bytes 393224 | tf_op jit(solution)/shard_map/ppermute | solution.py:36
  31.6 38.3 %copy-start.5 = (f32[20]{0:T(128)}, f32[20]{0:T(128)S(1)}, u32[]{:S(2)}) copy-start(f32[20]{0:T(128)S(1)} %add_sine_fusion) | copy-start | bytes 244
  43.7 21.6 %all-to-all-start.1 = ((f32[96,8,128]{2,1,0:T(8,128)}), f32[96,8,128]{2,1,0:T(8,128)S(1)}, u32[]{:S(2)}, u32[]{:S(2)}) async-start(f32[96,8,128]{2,1,0:T(8,128)} %scatter_fusion), calls=%async_computation.1 | async-start | bytes 786432 | tf_op jit(solution)/shard_map/all_to_all | solution.py:273
  53.2 19.3 %copy-start.3 = (f32[128]{0:T(128)}, f32[128]{0:T(128)S(1)}, u32[]{:S(2)}) copy-start(f32[128]{0:T(128)S(1)} %broadcast_multiply_fusion.28) | copy-start | bytes 1540
  82.6 7.5 %collective-permute-start.6 = (f32[2,16,8,128]{3,2,1,0:T(8,128)S(1)}, f32[2,16,8,128]{3,2,1,0:T(8,128)S(1)}, u32[]{:S(2)}, u32[]{:S(2)}) collective-permute-start(f32[2,16,8,128]{3,2,1,0:T(8,128)S(1)} %get-tuple-element.76), channel_id=1, source_target_pairs={{4,0},{8,4},{12,8},{5,1},{9,5},{13,9},{6,2},{10,6},{14,10},{7,3},{... | collective-permute-start | bytes 393224 | tf_op jit(solution)/shard_map/ppermute | solution.py:24
  83.9 7.4 %collective-permute-start.5 = (f32[2,16,8,128]{3,2,1,0:T(8,128)S(1)}, f32[2,16,8,128]{3,2,1,0:T(8,128)S(1)}, u32[]{:S(2)}, u32[]{:S(2)}) collective-permute-start(f32[2,16,8,128]{3,2,1,0:T(8,128)S(1)} %get-tuple-element.75), channel_id=1, source_target_pairs={{0,4},{4,8},{8,12},{1,5},{5,9},{9,13},{2,6},{6,10},{10,14},{3,7},{... | collective-permute-start | bytes 393224 | tf_op jit(solution)/shard_map/ppermute | solution.py:23
  91.3 4.5 %collective-permute-start.8 = (f32[20,2,8,128]{3,2,1,0:T(8,128)S(1)}, f32[20,2,8,128]{3,2,1,0:T(8,128)S(1)}, u32[]{:S(2)}, u32[]{:S(2)}) collective-permute-start(f32[20,2,8,128]{3,2,1,0:T(8,128)S(1)} %get-tuple-element.72), channel_id=1, source_target_pairs={{1,0},{2,1},{3,2},{5,4},{6,5},{7,6},{9,8},{10,9},{11,10},{13,12},{... | collective-permute-start | bytes 491528 | tf_op jit(solution)/shard_map/ppermute | solution.py:24
  92.6 4.0 %collective-permute-start.7 = (f32[20,2,8,128]{3,2,1,0:T(8,128)S(1)}, f32[20,2,8,128]{3,2,1,0:T(8,128)S(1)}, u32[]{:S(2)}, u32[]{:S(2)}) collective-permute-start(f32[20,2,8,128]{3,2,1,0:T(8,128)S(1)} %get-tuple-element.71), channel_id=1, source_target_pairs={{0,1},{1,2},{2,3},{4,5},{5,6},{6,7},{8,9},{9,10},{10,11},{12,13},{... | collective-permute-start | bytes 491528 | tf_op jit(solution)/shard_map/ppermute | solution.py:23
  102.8 5.7 %collective-permute-start.9 = (f32[32,8,128]{2,0,1:T(8,128)S(1)}, f32[32,8,128]{2,0,1:T(8,128)S(1)}, u32[]{:S(2)}, u32[]{:S(2)}) collective-permute-start(f32[32,8,128]{2,0,1:T(8,128)S(1)} %constant_dynamic-update-slice_fusion.7), channel_id=1, source_target_pairs={{0,16},{16,0},{1,17},{17,1},{2,18},{18,2},{3,19},{19,3},{4,20},{20... | collective-permute-start | bytes 393224 | tf_op jit(solution)/shard_map/ppermute | solution.py:36
  135.0 1.2 copy-start.6
  138.3 0.6 copy-start.4
where the time goes:
time: 143 us; the launch traced here: 142 us
  starting transfers between devices  38.8 us (27%)
  local copies, waits for them, and re-layouts  38 us (27%)
  waiting for transfers between devices  24.5 us (17%)
  blocking collectives  19.8 us (14%)
  other arithmetic  14.6 us (10%)
  matrix products  5.91 us (4%)
    all_to_all x1, blocking collectives, evaluate(): lax.all_to_all(send_values, ('lat', 'lon'), split_axis=0, concat_axis=0,...  19.8 us
    ppermute x4, starting transfers between devices, extended(): before = lax.ppermute(last, axis, up)  16.4 us
    all_to_all x1, waiting for transfers between devices, evaluate(): lax.all_to_all(send_values, ('lat', 'lon'), split_axis=0, concat_axis=0,...  11.9 us
    scatter x2, local copies, waits for them, and re-layouts, evaluate(): send_values = jnp.zeros((bucket_total, field_count, level_count), jnp.flo...  9.65 us
    all_to_all x1, starting transfers between devices, evaluate(): lax.all_to_all(send_values, ('lat', 'lon'), split_axis=0, concat_axis=0,...  9.47 us
    ppermute x2, waiting for transfers between devices, from_partner(): return lax.ppermute(block, axis, route)  8.15 us
    unnamed x22, other arithmetic  7.61 us
    scatter x2, local copies, waits for them, and re-layouts, evaluate(): flat_cells = flat_cells.at[routed_flat].set(got_values, mode='drop')  6.85 us
  transfers between devices with their start and end apart: 12, of which 7 were waited for; matrix products, arithmetic and copies ran while one was open for 14% of the time, Pallas kernels for 0%

commit v1 on v0

v1 whole, which is shorter than its diff:
```python
import math

import jax
import jax.numpy as jnp
import numpy as np
from jax import lax
from jax.experimental import pallas as pl
from jax.experimental.pallas import tpu as pltpu
from jax.sharding import PartitionSpec as P

ETA_COEF = 0.2
NU_COEF = 0.2
KAPPA_COEF = 0.3
SOUND_SQ = 1.0
ARCHIMEDES_LIFT = 0.5
TIME_STEP = 0.2

HALO = 4
PAD = 8
TILE = 8


def is_power_of_two(count):
    return count & (count - 1) == 0


def to_device(index, step, count):
    return index ^ step if is_power_of_two(count) else (index + step) % count


def from_device(index, step, count):
    return index ^ step if is_power_of_two(count) else (index + count - step) % count


def even_pairs(count):
    return [(i, i ^ 1) for i in range(count) if i ^ 1 < count]


def odd_pairs(count):
    route = []
    for low in range(1, count - 1, 2):
        route += [(low, low + 1), (low + 1, low)]
    return route


def lon_route(step, count):
    return [(i, to_device(i, step, count)) for i in range(count)]


def lat_route(step, count):
    return [
        (side * count + i, (1 - side) * count + to_device(i, step, count))
        for side in range(2)
        for i in range(count)
    ]


class Loop:
    def __init__(self, rows, cols, lat_count, lon_count):
        self.rows, self.cols = rows, cols
        self.lat_count, self.lon_count = lat_count, lon_count
        self.nth, self.nph = rows * lat_count, cols * lon_count
        self.total = 4 * (self.nth + self.nph)
        self.blocks = lat_count * lon_count
        longest = max(
            2 * (rows + cols + 2 * HALO), 2 * (rows + 2 * HALO), 2 * (cols + 2 * HALO)
        )
        self.slots = -(-longest // self.blocks)

    def position(self, row, col):
        nth, nph = self.nth, self.nph
        top = 2 * col + row + 2
        right = 2 * nph + 2 * row + col - nph
        bottom = 2 * nph + 2 * nth + 2 * (nph - 1 - col) + row - nth
        left = 4 * nph + 2 * nth + 2 * (nth - 1 - row) + col + 2
        return jnp.where(
            row < 0, top, jnp.where(row >= nth, bottom, jnp.where(col >= nph, right, left))
        )

    def cell(self, place):
        nth, nph = self.nth, self.nph
        right = place - 2 * nph
        bottom = right - 2 * nth
        left = bottom - 2 * nph
        on_top, on_right, on_bottom = right < 0, bottom < 0, left < 0
        row = jnp.where(
            on_top,
            place % 2 - 2,
            jnp.where(
                on_right, right // 2, jnp.where(on_bottom, nth + bottom % 2, nth - 1 - left // 2)
            ),
        )
        col = jnp.where(
            on_top,
            place // 2,
            jnp.where(
                on_right, nph + right % 2, jnp.where(on_bottom, nph - 1 - bottom // 2, left % 2 - 2)
            ),
        )
        return row, col

    def stretch(self, lat, lon):
        nth, nph = self.nth, self.nph
        row_low = jnp.maximum(lat * self.rows - HALO, 0)
        row_high = jnp.minimum(lat * self.rows + self.rows + HALO, nth)
        col_low = jnp.maximum(lon * self.cols - HALO, 0)
        col_high = jnp.minimum(lon * self.cols + self.cols + HALO, nph)
        top, bottom = lat == 0, lat == self.lat_count - 1
        left, right = lon == 0, lon == self.lon_count - 1
        left_start = 4 * nph + 2 * nth + 2 * (nth - row_high)
        bottom_start = 2 * nph + 2 * nth + 2 * (nph - col_high)
        start = jnp.where(
            top & left,
            left_start,
            jnp.where(
                top,
                2 * col_low,
                jnp.where(
                    right, 2 * nph + 2 * row_low, jnp.where(bottom, bottom_start, left_start)
                ),
            ),
        )
        span = jnp.where(top | bottom, 2 * (col_high - col_low), 0) + jnp.where(
            left | right, 2 * (row_high - row_low), 0
        )
        return start, span

    def first_entry(self, start, donor, offset):
        lead = 2 * self.total
        return (start - donor - offset + lead + self.blocks - 1) // self.blocks - (
            lead // self.blocks
        )


def whole(count):
    return [pl.BlockSpec(memory_space=pltpu.VMEM)] * count


def scalars(count):
    return [pl.BlockSpec(memory_space=pltpu.SMEM)] * count


def tiles(index, count):
    if isinstance(index, int):
        return pl.ds(index * TILE, count * TILE)
    return pl.ds(pl.multiple_of(index * TILE, TILE), count * TILE)


def strip_kernel(rows, cols, flag_ref, state_ref, even_ref, odd_ref, send_even_ref, send_odd_ref):
    lat_even = flag_ref[0] == 0
    lon_even = flag_ref[1] == 0

    def copy_rows(first, count, source):
        for out_ref, last in ((send_even_ref, lon_even), (send_odd_ref, jnp.logical_not(lon_even))):
            low = jnp.where(last, cols - HALO, 0)
            for row in range(count):
                out_ref[tiles((first + row) * HALO, HALO), :] = source[
                    tiles(row * cols + low, HALO), :
                ]

    copy_rows(HALO, rows, state_ref)

    @pl.when(lat_even)
    def _():
        copy_rows(0, HALO, odd_ref)
        copy_rows(HALO + rows, HALO, even_ref)

    @pl.when(jnp.logical_not(lat_even))
    def _():
        copy_rows(0, HALO, even_ref)
        copy_rows(HALO + rows, HALO, odd_ref)


def mix_and_pack(entries, wide, table, float_ref, int_ref, frame_ref, value_ref, send_refs, picks):
    field = lax.broadcasted_iota(jnp.int32, (TILE, 128), 0)
    takes_next = (field == 1) | (field == 4)
    turned = takes_next | (field == 2) | (field == 5)

    def one_entry(entry, carry):
        base = int_ref[table["base"] + entry]
        total = None
        for a in range(4):
            for b in range(4):
                weight = float_ref[table["weight"] + entry * 16 + 4 * a + b]
                part = weight * frame_ref[tiles(base + a * wide + b, 1), :]
                total = part if total is None else total + part
        cosine = float_ref[table["cosine"] + entry]
        sine = float_ref[table["sine"] + entry]
        other = jnp.where(
            takes_next, pltpu.roll(total, TILE - 1, 0), pltpu.roll(total, 1, 0)
        )
        mixed = cosine * total + jnp.where(takes_next, -sine, sine) * other
        value_ref[tiles(entry, 1), :] = jnp.where(turned, mixed, total)
        return carry

    lax.fori_loop(0, entries, one_entry, 0, unroll=4)
    for step, send_ref in enumerate(send_refs):
        for place in range(picks):
            entry = int_ref[table["send"] + step * picks + place]
            send_ref[tiles(place, 1), :] = value_ref[tiles(entry, 1), :]


def frame_kernel(
    rows, cols, entries, table, picks, steps,
    flag_ref, int_ref, float_ref, state_ref, lat_even_ref, lat_odd_ref, lon_even_ref, lon_odd_ref,
    frame_ref, *rest,
):
    send_refs, value_ref = rest[:steps], rest[steps]
    wide = cols + 2 * HALO
    lat_even = flag_ref[0] == 0
    lon_even = flag_ref[1] == 0

    def copy_rows(first, count, source, left, width):
        for row in range(count):
            frame_ref[tiles((first + row) * wide + left, width), :] = source[
                tiles(row * width, width), :
            ]

    copy_rows(HALO, rows, state_ref, HALO, cols)

    @pl.when(lat_even)
    def _():
        copy_rows(0, HALO, lat_odd_ref, HALO, cols)
        copy_rows(HALO + rows, HALO, lat_even_ref, HALO, cols)

    @pl.when(jnp.logical_not(lat_even))
    def _():
        copy_rows(0, HALO, lat_even_ref, HALO, cols)
        copy_rows(HALO + rows, HALO, lat_odd_ref, HALO, cols)

    @pl.when(lon_even)
    def _():
        copy_rows(0, rows + 2 * HALO, lon_odd_ref, 0, HALO)
        copy_rows(0, rows + 2 * HALO, lon_even_ref, HALO + cols, HALO)

    @pl.when(jnp.logical_not(lon_even))
    def _():
        copy_rows(0, rows + 2 * HALO, lon_even_ref, 0, HALO)
        copy_rows(0, rows + 2 * HALO, lon_odd_ref, HALO + cols, HALO)

    mix_and_pack(
        entries, wide, table, float_ref, int_ref, frame_ref, value_ref, send_refs, picks
    )


def swap_kernel(lat_count, lon_count, slots, *refs):
    got_refs, out_refs = refs[:lon_count], refs[lon_count:]
    for lat_step in range(lat_count):
        for lon_step in range(lon_count):
            out_refs[lat_step][tiles(lon_step * slots, slots), :] = got_refs[lon_step][
                tiles(lat_step * slots, slots), :
            ]


def section(
    rows, cols, table, arrivals, lat_count, radial_ref, int_ref, float_ref, frame_ref, got_refs,
    plane_ref, work_ref, rate_rows, rate_chunks, emit,
):
    tall, wide = rows + 2 * HALO, cols + 2 * HALO
    pitch = wide + 2 * PAD

    def spread_row(row, carry):
        for chunk in range(0, wide, 8):
            for f in range(TILE):
                start = (row * wide + chunk) * TILE + f
                plane_ref[pl.ds((f * tall + row) * pitch + PAD + chunk, 8), :] = frame_ref[
                    pl.ds(start, 8, stride=TILE), :
                ]
        return carry

    first_row, last_row = rate_rows
    lax.fori_loop(first_row - 2, last_row + 2, spread_row, 0)
    for lat_step in range(lat_count):
        for place in range(arrivals):
            spot = int_ref[table["receive"] + lat_step * arrivals + place]
            plane_ref[pl.ds(spot, TILE, stride=tall * pitch), :] = got_refs[lat_step][
                tiles(place, 1), :
            ]

    levels = radial_ref.shape[-1]
    inverse_radius, ru, rl, du, dl, qu, ql = [radial_ref[n] for n in range(7)]

    def up(x):
        return pltpu.roll(x, levels - 1, 1)

    def down(x):
        return pltpu.roll(x, 1, 1)

    half_theta = table["half_theta"]

    def row_factors(row):
        return (
            float_ref[table["theta_up"] + row],
            float_ref[table["theta_down"] + row],
            float_ref[table["phi"] + row],
        )

    def reader(ref, row, col):
        def at(number, row_step=0, col_step=0):
            return ref[
                pl.ds((number * tall + row + row_step) * pitch + PAD + col + col_step, 8), :
            ]

        return at

    def curl(at, first, factors, with_phi, with_theta):
        tu, td, ph = factors
        a, b, c = first, first + 1, first + 2
        mid_b, mid_c = at(b), at(c)
        radial = inverse_radius * (
            (tu * at(c, 1) - td * at(c, -1)) - ph * (at(b, 0, 1) - at(b, 0, -1))
        )
        polar = with_phi * (at(a, 0, 1) - at(a, 0, -1)) - (ru * up(mid_c) - rl * down(mid_c))
        azimuth = (ru * up(mid_b) - rl * down(mid_b)) - with_theta * (at(a, 1) - at(a, -1))
        return radial, polar, azimuth

    def slope(at, number, with_phi, with_theta):
        mid = at(number)
        return (
            du * up(mid) - dl * down(mid),
            with_theta * (at(number, 1) - at(number, -1)),
            with_phi * (at(number, 0, 1) - at(number, 0, -1)),
        )

    def outflow(at, first, factors):
        tu, td, ph = factors
        mid = at(first)
        return (qu * up(mid) - ql * down(mid)) + inverse_radius * (
            (tu * at(first + 1, 1) - td * at(first + 1, -1))
            + ph * (at(first + 2, 0, 1) - at(first + 2, 0, -1))
        )

    def cross(x, y):
        return (
            x[1] * y[2] - x[2] * y[1],
            x[2] * y[0] - x[0] * y[2],
            x[0] * y[1] - x[1] * y[0],
        )

    def dot(x, y):
        return x[0] * y[0] + x[1] * y[1] + x[2] * y[2]

    with_theta = inverse_radius * half_theta

    def first_pass(row, carry):
        factors = row_factors(row)
        with_phi = inverse_radius * factors[2]
        for chunk in range(0, wide, 8):
            at = reader(plane_ref, row, chunk)

            def put(number, value):
                work_ref[pl.ds((number * tall + row) * pitch + PAD + chunk, 8), :] = value

            flow = [at(n) for n in range(3)]
            field = [at(n) for n in range(3, 6)]
            current = curl(at, 3, factors, with_phi, with_theta)
            spin = curl(at, 0, factors, with_phi, with_theta)
            induced = cross(flow, field)
            warm = slope(at, 6, with_phi, with_theta)
            for n in range(3):
                put(n, current[n])
                put(3 + n, spin[n])
                put(6 + n, induced[n] - ETA_COEF * current[n])
                put(9 + n, warm[n])
            put(12, at(7) + 0.5 * dot(flow, flow))
        return carry

    lax.fori_loop(first_row - 1, last_row + 1, first_pass, 0)

    def second_pass(row, carry):
        factors = row_factors(row)
        with_phi = inverse_radius * factors[2]
        for chunk in rate_chunks:
            at = reader(plane_ref, row, chunk)
            work = reader(work_ref, row, chunk)
            flow = [at(n) for n in range(3)]
            field = [at(n) for n in range(3, 6)]
            current = [work(n) for n in range(3)]
            spin = [work(3 + n) for n in range(3)]
            warm = [work(9 + n) for n in range(3)]
            field_rate = curl(work, 6, factors, with_phi, with_theta)
            spin_curl = curl(work, 3, factors, with_phi, with_theta)
            head = slope(work, 12, with_phi, with_theta)
            lorentz = cross(current, field)
            advect = cross(flow, spin)
            speed = [
                advect[n] + lorentz[n] - head[n] - NU_COEF * spin_curl[n] for n in range(3)
            ]
            speed[0] = speed[0] + ARCHIMEDES_LIFT * at(6)
            heat = KAPPA_COEF * outflow(work, 9, factors) - dot(flow, warm)
            squeeze = -SOUND_SQ * outflow(at, 0, factors)
            emit(row, chunk, at, speed + list(field_rate) + [heat, squeeze])
        return carry

    lax.fori_loop(first_row, last_row, second_pass, 0)


def first_section_kernel(
    rows, cols, entries, table, picks, steps, arrivals, lat_count, nth, nph,
    int_ref, float_ref, radial_ref, frame_in_ref, *rest,
):
    got_refs, rest = rest[:lat_count], rest[lat_count:]
    frame_ref, rate_ref, rest = rest[0], rest[1], rest[2:]
    send_refs, (value_ref, plane_ref, work_ref) = rest[:steps], rest[steps:]
    tall, wide = rows + 2 * HALO, cols + 2 * HALO
    first_row = int_ref[table["corner"]]
    first_col = int_ref[table["corner"] + 1]

    def emit(row, chunk, at, rate):
        in_row = (row + first_row >= 0) & (row + first_row < nth)
        col = lax.broadcasted_iota(jnp.int32, (8, 128), 0) + (chunk + first_col)
        inside = (col >= jnp.where(in_row, 0, nph)) & (col < nph)
        for f in range(TILE):
            rate_ref[f, row, pl.ds(chunk, 8), :] = rate[f]
            start = (row * wide + chunk) * TILE + f
            frame_ref[pl.ds(start, 8, stride=TILE), :] = jnp.where(
                inside, at(f) + TIME_STEP * rate[f], 0.0
            )

    section(
        rows, cols, table, arrivals, lat_count, radial_ref, int_ref, float_ref, frame_in_ref,
        got_refs, plane_ref, work_ref, (2, tall - 2), range(0, wide, 8), emit,
    )
    mix_and_pack(
        entries, wide, table, float_ref, int_ref, frame_ref, value_ref, send_refs, picks
    )


def second_section_kernel(
    rows, cols, table, arrivals, lat_count,
    int_ref, float_ref, radial_ref, frame_in_ref, rate_ref, *rest,
):
    got_refs, rest = rest[:lat_count], rest[lat_count:]
    change_ref, plane_ref, work_ref = rest

    def emit(row, chunk, at, rate):
        for f in range(TILE):
            start = ((row - HALO) * cols + chunk - HALO) * TILE + f
            change_ref[pl.ds(start, 8, stride=TILE), :] = (0.5 * TIME_STEP) * (
                rate_ref[f, row, pl.ds(chunk, 8), :] + rate[f]
            )

    section(
        rows, cols, table, arrivals, lat_count, radial_ref, int_ref, float_ref, frame_in_ref,
        got_refs, plane_ref, work_ref, (HALO, HALO + rows), range(HALO, HALO + cols, 8), emit,
    )


def radial_factors(levels, theta_count):
    scale = 2.0 * theta_count / math.pi
    step = 0.65 * scale / levels
    radius = 0.35 * scale + (np.arange(levels) + 0.5) * step
    half = 0.5 / step
    above = np.append(radius[1:], 0.0)
    below = np.append(0.0, radius[:-1])
    ones_above = np.append(np.ones(levels - 1), 0.0)
    ones_below = np.append(0.0, np.ones(levels - 1))
    rows = np.stack(
        [
            1.0 / radius,
            half * above / radius,
            half * below / radius,
            half * ones_above,
            half * ones_below,
            half * above**2 / radius**2,
            half * below**2 / radius**2,
        ]
    )
    return np.repeat(rows[:, None, :], 8, axis=1).astype(np.float32)


def per_device(state, rim_base, rim_weight, rim_angle, rim_target):
    _, rows, cols, fields, levels = state.shape
    lat_count, lon_count = lax.axis_size("lat"), lax.axis_size("lon")
    loop = Loop(rows, cols, lat_count, lon_count)
    nth, nph, slots = loop.nth, loop.nph, loop.slots
    entries = rim_base.shape[1]
    tall, wide = rows + 2 * HALO, cols + 2 * HALO
    pitch = wide + 2 * PAD
    lat, lon = lax.axis_index("lat"), lax.axis_index("lon")
    first_row, first_col = lat * rows - HALO, lon * cols - HALO
    block = state[0].reshape(rows * cols * fields, levels)
    f32 = jnp.float32

    def tile_array(count):
        return jax.ShapeDtypeStruct((count * TILE, levels), f32)

    mine = loop.position(rim_target[0, 0:1, 0], rim_target[0, 0:1, 1]) % loop.total
    other = lax.ppermute(mine, "panel", [(0, 1), (1, 0)])

    flags = jnp.stack([lat % 2, lon % 2]).astype(jnp.int32)
    cells = state[0]
    last_first = lat % 2 == 0
    head, tail = cells[:HALO], cells[rows - HALO :]
    send_even = jnp.where(last_first, tail, head).reshape(HALO * cols * fields, levels)
    send_odd = jnp.where(last_first, head, tail).reshape(HALO * cols * fields, levels)
    lat_even = lax.ppermute(send_even, "lat", even_pairs(lat_count))
    lat_odd = lax.ppermute(send_odd, "lat", odd_pairs(lat_count))

    strip_even, strip_odd = pl.pallas_call(
        lambda *refs: strip_kernel(rows, cols, *refs),
        out_shape=[tile_array(tall * HALO)] * 2,
        in_specs=scalars(1) + whole(3),
        out_specs=whole(2),
        name="strips",
    )(flags, block, lat_even, lat_odd)
    lon_even = lax.ppermute(strip_even, "lon", even_pairs(lon_count))
    lon_odd = lax.ppermute(strip_odd, "lon", odd_pairs(lon_count))

    base_cell = rim_base[0]
    base = (base_cell[:, 0] - first_row - 1) * wide + (base_cell[:, 1] - first_col - 1)
    lat_step = jnp.arange(lat_count, dtype=jnp.int32)
    lon_step = jnp.arange(lon_count, dtype=jnp.int32)
    slot = jnp.arange(slots, dtype=jnp.int32)
    start, _ = loop.stretch(
        to_device(lat, lat_step, lat_count)[None, :], to_device(lon, lon_step, lon_count)[:, None]
    )
    lead = loop.first_entry(start, lat * lon_count + lon, other)
    send = (lead[:, :, None] + slot) % entries
    donor = (
        from_device(lat, lat_step, lat_count)[:, None] * lon_count
        + from_device(lon, lon_step, lon_count)[None, :]
    )
    start, span = loop.stretch(lat, lon)
    lead = loop.first_entry(start, donor, mine)
    place = (lead[:, :, None] + slot) * loop.blocks + donor[:, :, None] + mine
    row, col = loop.cell(place % loop.total)
    receive = jnp.where(
        place < start + span, (row - first_row) * pitch + PAD + (col - first_col), 0
    )
    ints = jnp.concatenate(
        [
            base.reshape(-1),
            send.reshape(-1),
            receive.reshape(-1),
            first_row[None],
            first_col[None],
        ]
    ).astype(jnp.int32)
    picks = lat_count * slots
    arrivals = lon_count * slots

    polar_step, azimuth_step = math.pi / (2 * nth), 1.5 * math.pi / nph
    row_ids = first_row - 1 + jnp.arange(tall + 2, dtype=jnp.int32)
    sines = jnp.sin(math.pi / 4 + (row_ids.astype(f32) + 0.5) * (math.pi / (2 * nth)))
    middle = sines[1:-1]
    floats = jnp.concatenate(
        [
            sines[2:] / middle * (0.5 / polar_step),
            sines[:-2] / middle * (0.5 / polar_step),
            (0.5 / azimuth_step) / middle,
            jnp.cos(rim_angle[0]),
            jnp.sin(rim_angle[0]),
            rim_weight[0].reshape(-1),
        ]
    )
    table = {
        "base": 0,
        "send": entries,
        "receive": entries + lon_count * picks,
        "corner": entries + lon_count * picks + lat_count * arrivals,
        "theta_up": 0,
        "theta_down": tall,
        "phi": 2 * tall,
        "cosine": 3 * tall,
        "sine": 3 * tall + entries,
        "weight": 3 * tall + 2 * entries,
        "half_theta": 0.5 / polar_step,
    }
    radial = jnp.asarray(radial_factors(levels, nth))

    frame, *packed = pl.pallas_call(
        lambda *refs: frame_kernel(rows, cols, entries, table, picks, lon_count, *refs),
        out_shape=[tile_array(tall * wide)] + [tile_array(picks)] * lon_count,
        in_specs=scalars(3) + whole(5),
        out_specs=whole(1 + lon_count),
        scratch_shapes=[pltpu.VMEM((entries * TILE, levels), f32)],
        name="frame",
    )(flags, ints, floats, block, lat_even, lat_odd, lon_even, lon_odd)

    def exchange(packed):
        got = [packed[0]] + [
            lax.ppermute(packed[step], "lon", lon_route(step, lon_count))
            for step in range(1, lon_count)
        ]
        turned = pl.pallas_call(
            lambda *refs: swap_kernel(lat_count, lon_count, slots, *refs),
            out_shape=[tile_array(arrivals)] * lat_count,
            in_specs=whole(lon_count),
            out_specs=whole(lat_count),
            name="swap",
        )(*got)
        return [
            lax.ppermute(turned[step], ("panel", "lat"), lat_route(step, lat_count))
            for step in range(lat_count)
        ]

    got = exchange(packed)
    planes = [
        pltpu.VMEM((fields * tall * (wide + 2 * PAD), levels), f32),
        pltpu.VMEM((13 * tall * (wide + 2 * PAD), levels), f32),
    ]
    frame, rate, *packed = pl.pallas_call(
        lambda *refs: first_section_kernel(
            rows, cols, entries, table, picks, lon_count, arrivals, lat_count, nth, nph, *refs
        ),
        out_shape=[tile_array(tall * wide), jax.ShapeDtypeStruct((fields, tall, wide, levels), f32)]
        + [tile_array(picks)] * lon_count,
        in_specs=scalars(2) + whole(2 + lat_count),
        out_specs=whole(2 + lon_count),
        scratch_shapes=[pltpu.VMEM((entries * TILE, levels), f32)] + planes,
        name="first_section",
    )(ints, floats, radial, frame, *got)

    got = exchange(packed)
    change = pl.pallas_call(
        lambda *refs: second_section_kernel(rows, cols, table, arrivals, lat_count, *refs),
        out_shape=tile_array(rows * cols),
        in_specs=scalars(2) + whole(3 + lat_count),
        out_specs=whole(1)[0],
        scratch_shapes=planes,
        name="second_section",
    )(ints, floats, radial, frame, rate, *got)
    return change.reshape(1, rows, cols, fields, levels)


def solution(mesh):
    return jax.shard_map(
        per_device,
        mesh=mesh,
        in_specs=(
            P("panel", "lat", "lon", None, None),
            P("panel", ("lat", "lon"), None),
            P("panel", ("lat", "lon"), None),
            P("panel", ("lat", "lon")),
            P("panel", None, None),
        ),
        out_specs=P("panel", "lat", "lon", None, None),
        check_vma=False,
    )
```

time: 143 us -> 104 us (0.73)
  local copies, waits for them, and re-layouts: 38 us -> 9.25 us
  Pallas kernels: 0 us -> 27 us
  blocking collectives: 19.8 us -> 0 us
  other arithmetic: 14.6 us -> 3.58 us
  between operations: 0.77 us -> 7.35 us
  matrix products: 5.91 us -> 0 us
  starting transfers between devices: 38.8 us -> 33 us
    pallas_call x0 -> x6, Pallas kernels: none -> 27 us  [the longest x1 9.83 us: per_device(): pl.pallas_call(lambda *refs: first_section_kernel(rows, cols, entries, ta...]
    all_to_all x1 -> x0, blocking collectives: 19.8 us -> none  [evaluate(): lax.all_to_all(send_values, ('lat', 'lon'), split_axis=0, concat_axis=0,...]
    scatter x6 -> x0, local copies, waits for them, and re-layouts: 17.5 us -> none  [the longest x2 9.65 us: evaluate(): send_values = jnp.zeros((bucket_total, field_count, level_count), jnp.flo...]
    all_to_all x2 -> x0, starting transfers between devices: 14.8 us -> none  [the longest x1 9.47 us: evaluate(): lax.all_to_all(send_values, ('lat', 'lon'), split_axis=0, concat_axis=0,...]
    all_to_all x2 -> x0, waiting for transfers between devices: 11.9 us -> none  [the longest x1 11.9 us: evaluate(): lax.all_to_all(send_values, ('lat', 'lon'), split_axis=0, concat_axis=0,...]
    ppermute x10 -> x19, waiting for transfers between devices: 12.6 us -> 23.6 us  [the longest x8 13.9 us: exchange(): lax.ppermute(turned[step], ('panel', 'lat'), lat_route(step, lat_count))]
    ppermute x10 -> x19, starting transfers between devices: 24 us -> 33 us  [the longest x8 15.3 us: exchange(): lax.ppermute(turned[step], ('panel', 'lat'), lat_route(step, lat_count))]
    unnamed x22 -> x0, other arithmetic: 7.61 us -> none
  transfers between devices with their start and end apart: 12 -> 19, of which waited for: 7 -> 8; matrix products, arithmetic and copies ran while one was open for 14% -> 6% of each run, Pallas kernels for 0% -> 0%
where the time goes in v1:
time: 104 us
  starting transfers between devices  33 us (32%)
  Pallas kernels  27 us (26%)
  waiting for transfers between devices  23.6 us (23%)
  local copies, waits for them, and re-layouts  9.25 us (9%)
  between operations  7.35 us (7%)
  other arithmetic  3.58 us (3%)
    ppermute x8, starting transfers between devices, exchange(): lax.ppermute(turned[step], ('panel', 'lat'), lat_route(step, lat_count))  15.3 us
    ppermute x8, waiting for transfers between devices, exchange(): lax.ppermute(turned[step], ('panel', 'lat'), lat_route(step, lat_count))  13.9 us
    ppermute x6, starting transfers between devices, exchange(): lax.ppermute(packed[step], 'lon', lon_route(step, lon_count))  10.4 us
    pallas_call x1, Pallas kernels, per_device(): pl.pallas_call(lambda *refs: first_section_kernel(rows, cols, entries, ta...  9.83 us
    ppermute x6, waiting for transfers between devices, exchange(): lax.ppermute(packed[step], 'lon', lon_route(step, lon_count))  9.19 us
    pallas_call x1, Pallas kernels, per_device(): pl.pallas_call(lambda *refs: second_section_kernel(rows, cols, table, arr...  7.57 us
    unnamed x37, local copies, waits for them, and re-layouts  5.66 us
    ppermute x1, starting transfers between devices, per_device(): other = lax.ppermute(mine, 'panel', [(0, 1), (1, 0)])  4.33 us
  transfers between devices with their start and end apart: 19, of which 8 were waited for; matrix products, arithmetic and copies ran while one was open for 6% of the time, Pallas kernels for 0%

profile of v1, /device:TPU:0, one launch (start us, length us, event | category | flops | bytes accessed | tf_op | source)
XLA Modules:
  0.0 103.7 jit_solution(9591497570831830168)
XLA Ops:
  0.0 1.3 %fusion.24 = (s32[1,1,1]{1,2,0:T(1,128)}, s32[1,1,1]{1,2,0:T(1,128)}) fusion(s32[1,512,2]{1,2,0:T(2,128)} %param.10), kind=kLoop, calls=%fused_computation.84 | loop fusion | bytes 16 | tf_op jit(solution)/shard_map/slice | solution.py:488
  8.4 4.3 %collective-permute-start = (s32[1]{0:T(128)}, s32[1]{0:T(128)}, u32[]{:S(2)}, u32[]{:S(2)}) collective-permute-start(s32[1]{0:T(128)} %select_n.202), channel_id=1, source_target_pairs={{0,16},{16,0},{1,17},{17,1},{2,18},{18,2},{3,19},{19,3},{4,20},{20... | collective-permute-start | bytes 20 | tf_op jit(solution)/shard_map/ppermute | solution.py:489
  12.7 1.1 %slice_select_fusion = (f32[1,4,16,8,128]{4,3,2,1,0:T(8,128)S(1)}, f32[1,4,16,8,128]{4,3,2,1,0:T(8,128)S(1)}) fusion(f32[1,16,16,8,128]{4,3,2,1,0:T(8,128)} %param.6, pred[]{:T(512)S(6)} %eq.68), kind=kLoop, calls=%fused_computation | loop fusion | flops 131072 | bytes 1048577 | tf_op jit(solution)/shard_map/jit(_where)/select_n | solution.py:496
  13.8 1.6 %collective-permute-start.1 = (f32[512,128]{1,0:T(8,128)S(1)}, f32[512,128]{1,0:T(8,128)S(1)}, u32[]{:S(2)}, u32[]{:S(2)}) collective-permute-start(f32[512,128]{1,0:T(8,128)S(1)} %bitcast.22), channel_id=1, source_target_pairs={{0,4},{4,0},{8,12},{12,8},{1,5},{5,1},{9,13},{13,9},{2,6},{6,2},{1... | collective-permute-start | bytes 786440 | tf_op jit(solution)/shard_map/ppermute | solution.py:497
  21.8 2.3 %strips.1 = (f32[768,128]{1,0:T(8,128)}, f32[768,128]{1,0:T(8,128)}) custom-call(s32[2]{0:T(128)} %pad_add_fusion.refs_0_, f32[2048,128]{1,0:T(8,128)} %bitcast.19, f32[512,128]{1,0:T(8,128)} %copy-done, f32[512,128]{1,0:T(8,128)} %copy-done.1), custom_call_target="tpu_custom_call" | custom-call | tf_op jit(solution)/shard_map/strips/pallas_call | solution.py:500
  27.5 3.8 %frame.1 = (f32[4608,128]{1,0:T(8,128)}, f32[160,128]{1,0:T(8,128)}, f32[160,128]{1,0:T(8,128)}, f32[160,128]{1,0:T(8,128)}, f32[160,128]{1,0:T(8,128)}) custom-call(s32[2]{0:T(128)} %pad_add_fusion.refs_0_, s32[194]{0:T(256)} %concatenate.6.refs_1_.refs_0_, f32[648]{0:T(1024)} %concatenate.7.refs_2_.refs_1_, f32[2048,128]{1,0:T(8,128)} %bitcast.20, ...), custom_call_target="tpu_custom_call" | custom-call | tf_op jit(solution)/shard_map/frame/pallas_call | solution.py:572
  31.4 7.1 %collective-permute-start.5 = (f32[160,128]{1,0:T(8,128)}, f32[160,128]{1,0:T(8,128)S(1)}, u32[]{:S(2)}, u32[]{:S(2)}) collective-permute-start(f32[160,128]{1,0:T(8,128)} %get-tuple-element.30), channel_id=1, source_target_pairs={{0,1},{1,0},{2,3},{3,2},{4,5},{5,4},{6,7},{7,6},{8,9},{9,8},{10,11... | collective-permute-start | bytes 245768 | tf_op jit(solution)/shard_map/ppermute | solution.py:583
  38.5 1.1 %collective-permute-start.6 = (f32[160,128]{1,0:T(8,128)}, f32[160,128]{1,0:T(8,128)S(1)}, u32[]{:S(2)}, u32[]{:S(2)}) collective-permute-start(f32[160,128]{1,0:T(8,128)} %get-tuple-element.31), channel_id=1, source_target_pairs={{0,2},{1,3},{2,0},{3,1},{4,6},{5,7},{6,4},{7,5},{8,10},{9,11},{10,... | collective-permute-start | bytes 245768 | tf_op jit(solution)/shard_map/ppermute | solution.py:583
  39.9 3.6 %collective-permute-done.6.refs_2_ = f32[160,128]{1,0:T(8,128)S(1)} collective-permute-done((f32[160,128]{1,0:T(8,128)}, f32[160,128]{1,0:T(8,128)S(1)}, u32[]{:S(2)}, u32[]{:S(2)}) %collective-permute-start.6) | collective-permute-done | bytes 81952 | tf_op jit(solution)/shard_map/ppermute | solution.py:583
  45.1 1.7 %swap.2 = (f32[160,128]{1,0:T(8,128)}, f32[160,128]{1,0:T(8,128)}, f32[160,128]{1,0:T(8,128)}, f32[160,128]{1,0:T(8,128)}) custom-call(f32[160,128]{1,0:T(8,128)} %get-tuple-element.29.refs_0_, f32[160,128]{1,0:T(8,128)} %copy-done.8, f32[160,128]{1,0:T(8,128)} %copy-done.10, f32[160,128]{1,0:T(8,128)} %copy-done.12), custom_call_target="tpu_custom_call" | custom-call | tf_op jit(solution)/shard_map/swap/pallas_call | solution.py:586
  47.4 5.4 %collective-permute-start.9 = (f32[160,128]{1,0:T(8,128)}, f32[160,128]{1,0:T(8,128)S(1)}, u32[]{:S(2)}, u32[]{:S(2)}) collective-permute-start(f32[160,128]{1,0:T(8,128)} %get-tuple-element.34), channel_id=1, source_target_pairs={{0,20},{4,16},{8,28},{12,24},{16,4},{20,0},{24,12},{28,8},{1,21},{... | collective-permute-start | bytes 245768 | tf_op jit(solution)/shard_map/ppermute | solution.py:594
  52.8 1.2 %collective-permute-start.10 = (f32[160,128]{1,0:T(8,128)}, f32[160,128]{1,0:T(8,128)S(1)}, u32[]{:S(2)}, u32[]{:S(2)}) collective-permute-start(f32[160,128]{1,0:T(8,128)} %get-tuple-element.35), channel_id=1, source_target_pairs={{0,24},{4,28},{8,16},{12,20},{16,8},{20,12},{24,0},{28,4},{1,25},{... | collective-permute-start | bytes 245768 | tf_op jit(solution)/shard_map/ppermute | solution.py:594
  54.0 1.4 %collective-permute-start.11 = (f32[160,128]{1,0:T(8,128)}, f32[160,128]{1,0:T(8,128)S(1)}, u32[]{:S(2)}, u32[]{:S(2)}) collective-permute-start(f32[160,128]{1,0:T(8,128)} %get-tuple-element.36), channel_id=1, source_target_pairs={{0,28},{4,24},{8,20},{12,16},{16,12},{20,8},{24,4},{28,0},{1,29},{... | collective-permute-start | bytes 245768 | tf_op jit(solution)/shard_map/ppermute | solution.py:594
  55.9 7.1 %collective-permute-done.10.refs_6_ = f32[160,128]{1,0:T(8,128)S(1)} collective-permute-done((f32[160,128]{1,0:T(8,128)}, f32[160,128]{1,0:T(8,128)S(1)}, u32[]{:S(2)}, u32[]{:S(2)}) %collective-permute-start.10) | collective-permute-done | bytes 81952 | tf_op jit(solution)/shard_map/ppermute | solution.py:594
  63.6 9.8 %first_section.1 = (f32[4608,128]{1,0:T(8,128)}, f32[8,24,24,128]{3,2,1,0:T(8,128)}, f32[160,128]{1,0:T(8,128)}, f32[160,128]{1,0:T(8,128)}, f32[160,128]{1,0:T(8,128)}, /*index=5*/f32[160,128]{1,0:T(8,128)}) custom-call(s32[194]{0:T(256)} %concatenate.6.refs_1_.refs_0_, f32[648]{0:T(1024)} %concatenate.7.refs_2_.refs_1_, ...), custom_call_target="tpu_custom_call" | custom-call | tf_op jit(solution)/shard_map/first_section/pallas_call | solution.py:603
  73.5 1.5 %collective-permute-start.13 = (f32[160,128]{1,0:T(8,128)}, f32[160,128]{1,0:T(8,128)S(1)}, u32[]{:S(2)}, u32[]{:S(2)}) collective-permute-start(f32[160,128]{1,0:T(8,128)} %get-tuple-element.41), channel_id=1, source_target_pairs={{0,2},{1,3},{2,0},{3,1},{4,6},{5,7},{6,4},{7,5},{8,10},{9,11},{10,... | collective-permute-start | bytes 245768 | tf_op jit(solution)/shard_map/ppermute | solution.py:583
  75.3 3.6 %collective-permute-done.13.refs_2_ = f32[160,128]{1,0:T(8,128)S(1)} collective-permute-done((f32[160,128]{1,0:T(8,128)}, f32[160,128]{1,0:T(8,128)S(1)}, u32[]{:S(2)}, u32[]{:S(2)}) %collective-permute-start.13) | collective-permute-done | bytes 81952 | tf_op jit(solution)/shard_map/ppermute | solution.py:583
  78.9 1.0 collective-permute-done.14.refs_3_
  80.5 1.7 %swap.3 = (f32[160,128]{1,0:T(8,128)}, f32[160,128]{1,0:T(8,128)}, f32[160,128]{1,0:T(8,128)}, f32[160,128]{1,0:T(8,128)}) custom-call(f32[160,128]{1,0:T(8,128)} %get-tuple-element.39.refs_0_, f32[160,128]{1,0:T(8,128)} %copy-done.9, f32[160,128]{1,0:T(8,128)} %copy-done.11, f32[160,128]{1,0:T(8,128)} %copy-done.13), custom_call_target="tpu_custom_call" | custom-call | tf_op jit(solution)/shard_map/swap/pallas_call | solution.py:586
  82.7 2.9 %collective-permute-start.16 = (f32[160,128]{1,0:T(8,128)}, f32[160,128]{1,0:T(8,128)S(1)}, u32[]{:S(2)}, u32[]{:S(2)}) collective-permute-start(f32[160,128]{1,0:T(8,128)} %get-tuple-element.44), channel_id=1, source_target_pairs={{0,20},{4,16},{8,28},{12,24},{16,4},{20,0},{24,12},{28,8},{1,21},{... | collective-permute-start | bytes 245768 | tf_op jit(solution)/shard_map/ppermute | solution.py:594
  85.5 1.3 %collective-permute-start.17 = (f32[160,128]{1,0:T(8,128)}, f32[160,128]{1,0:T(8,128)S(1)}, u32[]{:S(2)}, u32[]{:S(2)}) collective-permute-start(f32[160,128]{1,0:T(8,128)} %get-tuple-element.45), channel_id=1, source_target_pairs={{0,24},{4,28},{8,16},{12,20},{16,8},{20,12},{24,0},{28,4},{1,25},{... | collective-permute-start | bytes 245768 | tf_op jit(solution)/shard_map/ppermute | solution.py:594
  86.8 2.2 %collective-permute-start.18 = (f32[160,128]{1,0:T(8,128)}, f32[160,128]{1,0:T(8,128)S(1)}, u32[]{:S(2)}, u32[]{:S(2)}) collective-permute-start(f32[160,128]{1,0:T(8,128)} %get-tuple-element.46), channel_id=1, source_target_pairs={{0,28},{4,24},{8,20},{12,16},{16,12},{20,8},{24,4},{28,0},{1,29},{... | collective-permute-start | bytes 245768 | tf_op jit(solution)/shard_map/ppermute | solution.py:594
  89.0 6.5 %collective-permute-done.17.refs_7_ = f32[160,128]{1,0:T(8,128)S(1)} collective-permute-done((f32[160,128]{1,0:T(8,128)}, f32[160,128]{1,0:T(8,128)S(1)}, u32[]{:S(2)}, u32[]{:S(2)}) %collective-permute-start.17) | collective-permute-done | bytes 81952 | tf_op jit(solution)/shard_map/ppermute | solution.py:594
  96.2 7.6 %second_section.1 = f32[2048,128]{1,0:T(8,128)} custom-call(s32[194]{0:T(256)} %concatenate.6.refs_1_.refs_0_, f32[648]{0:T(1024)} %concatenate.7.refs_2_.refs_1_, f32[7,8,128]{2,1,0:T(8,128)} %constant.249.clone.refs_2_, f32[4608,128]{1,0:T(8,128)} %get-tuple-element.37.refs_3_, f32[8,24,24,128]{3,2,1,0:T(8,128)} %get-tuple-element.38.refs_4_, ...), custom_call_target="tpu_custom_call" | custom-call | tf_op jit(solution)/shard_map/second_section/pallas_call | solution.py:616
  (80 shorter events, 15.3 us)
Async XLA Ops:
  8.4 11.9 %collective-permute-start = (s32[1]{0:T(128)}, s32[1]{0:T(128)}, u32[]{:S(2)}, u32[]{:S(2)}) collective-permute-start(s32[1]{0:T(128)} %select_n.202), channel_id=1, source_target_pairs={{0,16},{16,0},{1,17},{17,1},{2,18},{18,2},{3,19},{19,3},{4,20},{20... | collective-permute-start | bytes 20 | tf_op jit(solution)/shard_map/ppermute | solution.py:489
  13.8 7.3 %collective-permute-start.1 = (f32[512,128]{1,0:T(8,128)S(1)}, f32[512,128]{1,0:T(8,128)S(1)}, u32[]{:S(2)}, u32[]{:S(2)}) collective-permute-start(f32[512,128]{1,0:T(8,128)S(1)} %bitcast.22), channel_id=1, source_target_pairs={{0,4},{4,0},{8,12},{12,8},{1,5},{5,1},{9,13},{13,9},{2,6},{6,2},{1... | collective-permute-start | bytes 786440 | tf_op jit(solution)/shard_map/ppermute | solution.py:497
  15.4 5.6 %collective-permute-start.2 = (f32[512,128]{1,0:T(8,128)S(1)}, f32[512,128]{1,0:T(8,128)S(1)}, u32[]{:S(2)}, u32[]{:S(2)}) collective-permute-start(f32[512,128]{1,0:T(8,128)S(1)} %bitcast.21), channel_id=1, source_target_pairs={{4,8},{8,4},{5,9},{9,5},{6,10},{10,6},{7,11},{11,7},{20,24},{24,20... | collective-permute-start | bytes 786440 | tf_op jit(solution)/shard_map/ppermute | solution.py:498
  24.1 1.9 %collective-permute-start.3 = (f32[768,128]{1,0:T(8,128)}, f32[768,128]{1,0:T(8,128)S(1)}, u32[]{:S(2)}, u32[]{:S(2)}) collective-permute-start(f32[768,128]{1,0:T(8,128)} %get-tuple-element.26), channel_id=1, source_target_pairs={{0,1},{1,0},{2,3},{3,2},{4,5},{5,4},{6,7},{7,6},{8,9},{9,8},{10,11... | collective-permute-start | bytes 1179656 | tf_op jit(solution)/shard_map/ppermute | solution.py:507
  24.1 1.9 %collective-permute-start.4 = (f32[768,128]{1,0:T(8,128)}, f32[768,128]{1,0:T(8,128)S(1)}, u32[]{:S(2)}, u32[]{:S(2)}) collective-permute-start(f32[768,128]{1,0:T(8,128)} %get-tuple-element.27), channel_id=1, source_target_pairs={{1,2},{2,1},{5,6},{6,5},{9,10},{10,9},{13,14},{14,13},{17,18},{18,... | collective-permute-start | bytes 1179656 | tf_op jit(solution)/shard_map/ppermute | solution.py:508
  31.4 8.5 %collective-permute-start.5 = (f32[160,128]{1,0:T(8,128)}, f32[160,128]{1,0:T(8,128)S(1)}, u32[]{:S(2)}, u32[]{:S(2)}) collective-permute-start(f32[160,128]{1,0:T(8,128)} %get-tuple-element.30), channel_id=1, source_target_pairs={{0,1},{1,0},{2,3},{3,2},{4,5},{5,4},{6,7},{7,6},{8,9},{9,8},{10,11... | collective-permute-start | bytes 245768 | tf_op jit(solution)/shard_map/ppermute | solution.py:583
  38.5 5.0 %collective-permute-start.6 = (f32[160,128]{1,0:T(8,128)}, f32[160,128]{1,0:T(8,128)S(1)}, u32[]{:S(2)}, u32[]{:S(2)}) collective-permute-start(f32[160,128]{1,0:T(8,128)} %get-tuple-element.31), channel_id=1, source_target_pairs={{0,2},{1,3},{2,0},{3,1},{4,6},{5,7},{6,4},{7,5},{8,10},{9,11},{10,... | collective-permute-start | bytes 245768 | tf_op jit(solution)/shard_map/ppermute | solution.py:583
  39.5 5.0 %collective-permute-start.7 = (f32[160,128]{1,0:T(8,128)}, f32[160,128]{1,0:T(8,128)S(1)}, u32[]{:S(2)}, u32[]{:S(2)}) collective-permute-start(f32[160,128]{1,0:T(8,128)} %get-tuple-element.32), channel_id=1, source_target_pairs={{0,3},{1,2},{2,1},{3,0},{4,7},{5,6},{6,5},{7,4},{8,11},{9,10},{10,... | collective-permute-start | bytes 245768 | tf_op jit(solution)/shard_map/ppermute | solution.py:583
  39.9 4.6 %copy-start.8 = (f32[160,128]{1,0:T(8,128)}, f32[160,128]{1,0:T(8,128)S(1)}, u32[]{:S(2)}) copy-start(f32[160,128]{1,0:T(8,128)S(1)} %collective-permute-done.5.refs_1_) | copy-start | bytes 245764
  46.9 8.6 %collective-permute-start.8 = (f32[160,128]{1,0:T(8,128)}, f32[160,128]{1,0:T(8,128)S(1)}, u32[]{:S(2)}, u32[]{:S(2)}) collective-permute-start(f32[160,128]{1,0:T(8,128)} %get-tuple-element.33), channel_id=1, source_target_pairs={{0,16},{4,20},{8,24},{12,28},{16,0},{20,4},{24,8},{28,12},{1,17},{... | collective-permute-start | bytes 245768 | tf_op jit(solution)/shard_map/ppermute | solution.py:594
  47.4 8.4 %collective-permute-start.9 = (f32[160,128]{1,0:T(8,128)}, f32[160,128]{1,0:T(8,128)S(1)}, u32[]{:S(2)}, u32[]{:S(2)}) collective-permute-start(f32[160,128]{1,0:T(8,128)} %get-tuple-element.34), channel_id=1, source_target_pairs={{0,20},{4,16},{8,28},{12,24},{16,4},{20,0},{24,12},{28,8},{1,21},{... | collective-permute-start | bytes 245768 | tf_op jit(solution)/shard_map/ppermute | solution.py:594
  52.8 10.1 %collective-permute-start.10 = (f32[160,128]{1,0:T(8,128)}, f32[160,128]{1,0:T(8,128)S(1)}, u32[]{:S(2)}, u32[]{:S(2)}) collective-permute-start(f32[160,128]{1,0:T(8,128)} %get-tuple-element.35), channel_id=1, source_target_pairs={{0,24},{4,28},{8,16},{12,20},{16,8},{20,12},{24,0},{28,4},{1,25},{... | collective-permute-start | bytes 245768 | tf_op jit(solution)/shard_map/ppermute | solution.py:594
  54.0 8.9 %collective-permute-start.11 = (f32[160,128]{1,0:T(8,128)}, f32[160,128]{1,0:T(8,128)S(1)}, u32[]{:S(2)}, u32[]{:S(2)}) collective-permute-start(f32[160,128]{1,0:T(8,128)} %get-tuple-element.36), channel_id=1, source_target_pairs={{0,28},{4,24},{8,20},{12,16},{16,12},{20,8},{24,4},{28,0},{1,29},{... | collective-permute-start | bytes 245768 | tf_op jit(solution)/shard_map/ppermute | solution.py:594
  55.5 7.5 %copy-start.4 = (f32[160,128]{1,0:T(8,128)}, f32[160,128]{1,0:T(8,128)S(1)}, u32[]{:S(2)}) copy-start(f32[160,128]{1,0:T(8,128)S(1)} %collective-permute-done.8.refs_4_) | copy-start | bytes 245764
  55.8 7.1 %copy-start.5 = (f32[160,128]{1,0:T(8,128)}, f32[160,128]{1,0:T(8,128)S(1)}, u32[]{:S(2)}) copy-start(f32[160,128]{1,0:T(8,128)S(1)} %collective-permute-done.9.refs_5_) | copy-start | bytes 245764
  73.4 1.9 %collective-permute-start.12 = (f32[160,128]{1,0:T(8,128)}, f32[160,128]{1,0:T(8,128)S(1)}, u32[]{:S(2)}, u32[]{:S(2)}) collective-permute-start(f32[160,128]{1,0:T(8,128)} %get-tuple-element.40), channel_id=1, source_target_pairs={{0,1},{1,0},{2,3},{3,2},{4,5},{5,4},{6,7},{7,6},{8,9},{9,8},{10,11... | collective-permute-start | bytes 245768 | tf_op jit(solution)/shard_map/ppermute | solution.py:583
  73.5 5.4 %collective-permute-start.13 = (f32[160,128]{1,0:T(8,128)}, f32[160,128]{1,0:T(8,128)S(1)}, u32[]{:S(2)}, u32[]{:S(2)}) collective-permute-start(f32[160,128]{1,0:T(8,128)} %get-tuple-element.41), channel_id=1, source_target_pairs={{0,2},{1,3},{2,0},{3,1},{4,6},{5,7},{6,4},{7,5},{8,10},{9,11},{10,... | collective-permute-start | bytes 245768 | tf_op jit(solution)/shard_map/ppermute | solution.py:583
  74.9 5.0 %collective-permute-start.14 = (f32[160,128]{1,0:T(8,128)}, f32[160,128]{1,0:T(8,128)S(1)}, u32[]{:S(2)}, u32[]{:S(2)}) collective-permute-start(f32[160,128]{1,0:T(8,128)} %get-tuple-element.42), channel_id=1, source_target_pairs={{0,3},{1,2},{2,1},{3,0},{4,7},{5,6},{6,5},{7,4},{8,11},{9,10},{10,... | collective-permute-start | bytes 245768 | tf_op jit(solution)/shard_map/ppermute | solution.py:583
  82.3 6.8 %collective-permute-start.15 = (f32[160,128]{1,0:T(8,128)}, f32[160,128]{1,0:T(8,128)S(1)}, u32[]{:S(2)}, u32[]{:S(2)}) collective-permute-start(f32[160,128]{1,0:T(8,128)} %get-tuple-element.43), channel_id=1, source_target_pairs={{0,16},{4,20},{8,24},{12,28},{16,0},{20,4},{24,8},{28,12},{1,17},{... | collective-permute-start | bytes 245768 | tf_op jit(solution)/shard_map/ppermute | solution.py:594
  82.7 6.3 %collective-permute-start.16 = (f32[160,128]{1,0:T(8,128)}, f32[160,128]{1,0:T(8,128)S(1)}, u32[]{:S(2)}, u32[]{:S(2)}) collective-permute-start(f32[160,128]{1,0:T(8,128)} %get-tuple-element.44), channel_id=1, source_target_pairs={{0,20},{4,16},{8,28},{12,24},{16,4},{20,0},{24,12},{28,8},{1,21},{... | collective-permute-start | bytes 245768 | tf_op jit(solution)/shard_map/ppermute | solution.py:594
  85.5 10.0 %collective-permute-start.17 = (f32[160,128]{1,0:T(8,128)}, f32[160,128]{1,0:T(8,128)S(1)}, u32[]{:S(2)}, u32[]{:S(2)}) collective-permute-start(f32[160,128]{1,0:T(8,128)} %get-tuple-element.45), channel_id=1, source_target_pairs={{0,24},{4,28},{8,16},{12,20},{16,8},{20,12},{24,0},{28,4},{1,25},{... | collective-permute-start | bytes 245768 | tf_op jit(solution)/shard_map/ppermute | solution.py:594
  86.8 8.7 %collective-permute-start.18 = (f32[160,128]{1,0:T(8,128)}, f32[160,128]{1,0:T(8,128)S(1)}, u32[]{:S(2)}, u32[]{:S(2)}) collective-permute-start(f32[160,128]{1,0:T(8,128)} %get-tuple-element.46), channel_id=1, source_target_pairs={{0,28},{4,24},{8,20},{12,16},{16,12},{20,8},{24,4},{28,0},{1,29},{... | collective-permute-start | bytes 245768 | tf_op jit(solution)/shard_map/ppermute | solution.py:594
  89.0 6.5 %copy-start.14 = (f32[160,128]{1,0:T(8,128)}, f32[160,128]{1,0:T(8,128)S(1)}, u32[]{:S(2)}) copy-start(f32[160,128]{1,0:T(8,128)S(1)} %collective-permute-done.15.refs_5_) | copy-start | bytes 245764
  89.0 6.5 %copy-start.15 = (f32[160,128]{1,0:T(8,128)}, f32[160,128]{1,0:T(8,128)S(1)}, u32[]{:S(2)}) copy-start(f32[160,128]{1,0:T(8,128)S(1)} %collective-permute-done.16.refs_6_) | copy-start | bytes 245764
  (13 other events, 13.5 us)

commit v2 on v1

--- a/solution.py
+++ b/solution.py
@@ -138,6 +138,10 @@
 
 def scalars(count):
     return [pl.BlockSpec(memory_space=pltpu.SMEM)] * count
+
+
+def grant(mebibytes):
+    return pltpu.CompilerParams(vmem_limit_bytes=mebibytes << 20)
 
 
 def tiles(index, count):
@@ -485,8 +489,10 @@
     def tile_array(count):
         return jax.ShapeDtypeStruct((count * TILE, levels), f32)
 
-    mine = loop.position(rim_target[0, 0:1, 0], rim_target[0, 0:1, 1]) % loop.total
-    other = lax.ppermute(mine, "panel", [(0, 1), (1, 0)])
+    first_cell = rim_target[0, 0]
+    other_cell = lax.ppermute(first_cell, "panel", [(0, 1), (1, 0)])
+    mine = loop.position(first_cell[0], first_cell[1])
+    other = loop.position(other_cell[0], other_cell[1])
 
     flags = jnp.stack([lat % 2, lon % 2]).astype(jnp.int32)
     cells = state[0]
@@ -502,6 +508,7 @@
         out_shape=[tile_array(tall * HALO)] * 2,
         in_specs=scalars(1) + whole(3),
         out_specs=whole(2),
+        compiler_params=grant(4),
         name="strips",
     )(flags, block, lat_even, lat_odd)
     lon_even = lax.ppermute(strip_even, "lon", even_pairs(lon_count))
@@ -575,6 +582,7 @@
         in_specs=scalars(3) + whole(5),
         out_specs=whole(1 + lon_count),
         scratch_shapes=[pltpu.VMEM((entries * TILE, levels), f32)],
+        compiler_params=grant(8),
         name="frame",
     )(flags, ints, floats, block, lat_even, lat_odd, lon_even, lon_odd)
 
@@ -588,7 +596,8 @@
             out_shape=[tile_array(arrivals)] * lat_count,
             in_specs=whole(lon_count),
             out_specs=whole(lat_count),
-            name="swap",
+            compiler_params=grant(4),
+        name="swap",
         )(*got)
         return [
             lax.ppermute(turned[step], ("panel", "lat"), lat_route(step, lat_count))
@@ -609,6 +618,7 @@
         in_specs=scalars(2) + whole(2 + lat_count),
         out_specs=whole(2 + lon_count),
         scratch_shapes=[pltpu.VMEM((entries * TILE, levels), f32)] + planes,
+        compiler_params=grant(24),
         name="first_section",
     )(ints, floats, radial, frame, *got)
 
@@ -619,6 +629,7 @@
         in_specs=scalars(2) + whole(3 + lat_count),
         out_specs=whole(1)[0],
         scratch_shapes=planes,
+        compiler_params=grant(24),
         name="second_section",
     )(ints, floats, radial, frame, rate, *got)
     return change.reshape(1, rows, cols, fields, levels)

time: 104 us -> 92.6 us (0.89)
  Pallas kernels: 27 us -> 14.1 us
  between operations: 7.35 us -> 14.6 us
  local copies, waits for them, and re-layouts: 9.25 us -> 6.01 us
  other arithmetic: 3.58 us -> 2.43 us
  waiting for transfers between devices: 23.6 us -> 22.5 us
    unnamed x37 -> x7, local copies, waits for them, and re-layouts: 5.66 us -> 2 us
    pallas_call x2, Pallas kernels: 3.47 us -> 0.04 us  [exchange(): pl.pallas_call(lambda *refs: swap_kernel(lat_count, lon_count, slots, *re...]
    pallas_call x1, Pallas kernels: 9.83 us -> 6.48 us  [per_device(): pl.pallas_call(lambda *refs: first_section_kernel(rows, cols, entries, ta...]
    pallas_call x1, Pallas kernels: 3.81 us -> 1.3 us  [per_device(): pl.pallas_call(lambda *refs: frame_kernel(rows, cols, entries, table, pic...]
    pallas_call x1, Pallas kernels: 7.57 us -> 5.71 us  [per_device(): pl.pallas_call(lambda *refs: second_section_kernel(rows, cols, table, arr...]
    pallas_call x1, Pallas kernels: 2.29 us -> 0.6 us  [per_device(): pl.pallas_call(lambda *refs: strip_kernel(rows, cols, *refs), out_shape=[...]
    slice x1 -> x3, local copies, waits for them, and re-layouts: 1.29 us -> 2.87 us  [the longest x1 1.34 us: per_device(): mine = loop.position(first_cell[0], first_cell[1])]
    ppermute x1, starting transfers between devices: 4.33 us -> 3.02 us  [per_device(): other_cell = lax.ppermute(first_cell, 'panel', [(0, 1), (1, 0)])]
  transfers between devices with their start and end apart: 19 -> 19, of which waited for: 8 -> 8; matrix products, arithmetic and copies ran while one was open for 6% -> 7% of each run, Pallas kernels for 0% -> 0%
where the time goes in v2:
time: 92.6 us; the launch traced here: 92 us
  starting transfers between devices  32.4 us (35%)
  waiting for transfers between devices  22.5 us (24%)
  between operations  14.6 us (16%)
  Pallas kernels  14.1 us (15%)
  local copies, waits for them, and re-layouts  6.01 us (6%)
  other arithmetic  2.43 us (3%)
    ppermute x8, starting transfers between devices, exchange(): lax.ppermute(turned[step], ('panel', 'lat'), lat_route(step, lat_count))  15.1 us
    ppermute x8, waiting for transfers between devices, exchange(): lax.ppermute(turned[step], ('panel', 'lat'), lat_route(step, lat_count))  12.9 us
    ppermute x6, starting transfers between devices, exchange(): lax.ppermute(packed[step], 'lon', lon_route(step, lon_count))  11.3 us
    ppermute x6, waiting for transfers between devices, exchange(): lax.ppermute(packed[step], 'lon', lon_route(step, lon_count))  8.82 us
    pallas_call x1, Pallas kernels, per_device(): pl.pallas_call(lambda *refs: first_section_kernel(rows, cols, entries, ta...  6.48 us
    pallas_call x1, Pallas kernels, per_device(): pl.pallas_call(lambda *refs: second_section_kernel(rows, cols, table, arr...  5.71 us
    ppermute x1, starting transfers between devices, per_device(): other_cell = lax.ppermute(first_cell, 'panel', [(0, 1), (1, 0)])  3.02 us
    unnamed x7, local copies, waits for them, and re-layouts  2 us
  transfers between devices with their start and end apart: 19, of which 8 were waited for; matrix products, arithmetic and copies ran while one was open for 7% of the time, Pallas kernels for 0%

profile of v2, /device:TPU:0, one launch (start us, length us, event | category | flops | bytes accessed | tf_op | source)
XLA Modules:
  0.0 92.0 jit_solution(9814237075318366487)
XLA Ops:
  0.0 0.9 slice_reduce_fusion
  0.9 3.0 %collective-permute-start = (s32[2]{0:T(128)S(1)}, s32[2]{0:T(128)S(1)}, u32[]{:S(2)}, u32[]{:S(2)}) collective-permute-start(s32[2]{0:T(128)S(1)} %slice_reduce_fusion), channel_id=1, source_target_pairs={{0,16},{16,0},{1,17},{17,1},{2,18},{18,2},{3,19},{19,3},{4,20},{20... | collective-permute-start | bytes 32 | tf_op jit(solution)/shard_map/ppermute | solution.py:493
  3.9 1.1 %slice_select_fusion = (f32[1,4,16,8,128]{4,3,2,1,0:T(8,128)S(1)}, f32[1,4,16,8,128]{4,3,2,1,0:T(8,128)S(1)}) fusion(f32[1,16,16,8,128]{4,3,2,1,0:T(8,128)} %param.6, pred[]{:T(512)S(6)} %eq.66), kind=kLoop, calls=%fused_computation | loop fusion | flops 131072 | bytes 1048577 | tf_op jit(solution)/shard_map/jit(_where)/select_n | solution.py:502
  5.0 1.6 %collective-permute-start.1 = (f32[512,128]{1,0:T(8,128)S(1)}, f32[512,128]{1,0:T(8,128)S(1)}, u32[]{:S(2)}, u32[]{:S(2)}) collective-permute-start(f32[512,128]{1,0:T(8,128)S(1)} %bitcast.22), channel_id=1, source_target_pairs={{0,4},{4,0},{8,12},{12,8},{1,5},{5,1},{9,13},{13,9},{2,6},{6,2},{1... | collective-permute-start | bytes 786440 | tf_op jit(solution)/shard_map/ppermute | solution.py:503
  7.3 1.3 %fusion.24 = (s32[1,1,1]{1,2,0:T(1,128)}, s32[1,1,1]{1,2,0:T(1,128)}) fusion(s32[1,512,2]{1,2,0:T(2,128)} %param.10), kind=kLoop, calls=%fused_computation.85 | loop fusion | bytes 16 | tf_op jit(solution)/shard_map/slice | solution.py:494
  17.5 0.8 copy.7
  26.8 1.2 %copy-done = f32[1,16,16,8,128]{4,3,2,1,0:T(8,128)S(1)} copy-done((f32[1,16,16,8,128]{4,3,2,1,0:T(8,128)S(1)}, f32[1,16,16,8,128]{4,3,2,1,0:T(8,128)}, u32[]{:S(2)}) %copy-start) | copy-done | bytes 1048600
  30.4 1.3 %frame.1 = (f32[4608,128]{1,0:T(8,128)S(1)}, f32[160,128]{1,0:T(8,128)S(1)}, f32[160,128]{1,0:T(8,128)S(1)}, f32[160,128]{1,0:T(8,128)S(1)}, f32[160,128]{1,0:T(8,128)S(1)}) custom-call(s32[2]{0:T(128)S(1)} %pad_add_fusion.refs_0_, s32[194]{0:T(256)S(1)} %concatenate.6.refs_1_.refs_0_, f32[648]{0:T(1024)S(1)} %concatenate.7.refs_2_.refs_1_, ...), custom_call_target="tpu_custom_call" | custom-call | tf_op jit(solution)/shard_map/frame/pallas_call | solution.py:579
  31.7 7.9 %collective-permute-start.5 = (f32[160,128]{1,0:T(8,128)S(1)}, f32[160,128]{1,0:T(8,128)S(1)}, u32[]{:S(2)}, u32[]{:S(2)}) collective-permute-start(f32[160,128]{1,0:T(8,128)S(1)} %get-tuple-element.30), channel_id=1, source_target_pairs={{0,1},{1,0},{2,3},{3,2},{4,5},{5,4},{6,7},{7,6},{8,9},{9,8},{10,11... | collective-permute-start | bytes 245768 | tf_op jit(solution)/shard_map/ppermute | solution.py:591
  39.7 1.1 %collective-permute-start.6 = (f32[160,128]{1,0:T(8,128)S(1)}, f32[160,128]{1,0:T(8,128)S(1)}, u32[]{:S(2)}, u32[]{:S(2)}) collective-permute-start(f32[160,128]{1,0:T(8,128)S(1)} %get-tuple-element.31), channel_id=1, source_target_pairs={{0,2},{1,3},{2,0},{3,1},{4,6},{5,7},{6,4},{7,5},{8,10},{9,11},{10,... | collective-permute-start | bytes 245768 | tf_op jit(solution)/shard_map/ppermute | solution.py:591
  41.1 3.3 %collective-permute-done.6.refs_2_ = f32[160,128]{1,0:T(8,128)S(1)} collective-permute-done((f32[160,128]{1,0:T(8,128)S(1)}, f32[160,128]{1,0:T(8,128)S(1)}, u32[]{:S(2)}, u32[]{:S(2)}) %collective-permute-start.6) | collective-permute-done | bytes 81952 | tf_op jit(solution)/shard_map/ppermute | solution.py:591
  44.4 1.1 %collective-permute-done.7.refs_3_ = f32[160,128]{1,0:T(8,128)S(1)} collective-permute-done((f32[160,128]{1,0:T(8,128)S(1)}, f32[160,128]{1,0:T(8,128)S(1)}, u32[]{:S(2)}, u32[]{:S(2)}) %collective-permute-start.7) | collective-permute-done | bytes 81952 | tf_op jit(solution)/shard_map/ppermute | solution.py:591
  46.1 5.3 %collective-permute-start.9 = (f32[160,128]{1,0:T(8,128)S(1)}, f32[160,128]{1,0:T(8,128)S(1)}, u32[]{:S(2)}, u32[]{:S(2)}) collective-permute-start(f32[160,128]{1,0:T(8,128)S(1)} %get-tuple-element.34), channel_id=1, source_target_pairs={{0,20},{4,16},{8,28},{12,24},{16,4},{20,0},{24,12},{28,8},{1,21},{... | collective-permute-start | bytes 245768 | tf_op jit(solution)/shard_map/ppermute | solution.py:603
  51.4 2.3 %collective-permute-start.11 = (f32[160,128]{1,0:T(8,128)S(1)}, f32[160,128]{1,0:T(8,128)S(1)}, u32[]{:S(2)}, u32[]{:S(2)}) collective-permute-start(f32[160,128]{1,0:T(8,128)S(1)} %get-tuple-element.36), channel_id=1, source_target_pairs={{0,28},{4,24},{8,20},{12,16},{16,12},{20,8},{24,4},{28,0},{1,29},{... | collective-permute-start | bytes 245768 | tf_op jit(solution)/shard_map/ppermute | solution.py:603
  54.3 5.8 %collective-permute-done.10.refs_6_ = f32[160,128]{1,0:T(8,128)S(1)} collective-permute-done((f32[160,128]{1,0:T(8,128)S(1)}, f32[160,128]{1,0:T(8,128)S(1)}, u32[]{:S(2)}, u32[]{:S(2)}) %collective-permute-start.10) | collective-permute-done | bytes 81952 | tf_op jit(solution)/shard_map/ppermute | solution.py:603
  60.1 6.5 %first_section.1 = (f32[4608,128]{1,0:T(8,128)S(1)}, f32[8,24,24,128]{3,2,1,0:T(8,128)S(1)}, f32[160,128]{1,0:T(8,128)S(1)}, f32[160,128]{1,0:T(8,128)S(1)}, f32...) custom-call(s32[194]{0:T(256)S(1)} %concatenate.6.refs_1_.refs_0_, f32[648]{0:T(1024)S(1)} %concatenate.7.refs_2_.refs_1_, ...), custom_call_target="tpu_custom_call" | custom-call | tf_op jit(solution)/shard_map/first_section/pallas_call | solution.py:612
  66.7 1.5 %collective-permute-start.13 = (f32[160,128]{1,0:T(8,128)S(1)}, f32[160,128]{1,0:T(8,128)S(1)}, u32[]{:S(2)}, u32[]{:S(2)}) collective-permute-start(f32[160,128]{1,0:T(8,128)S(1)} %get-tuple-element.41), channel_id=1, source_target_pairs={{0,2},{1,3},{2,0},{3,1},{4,6},{5,7},{6,4},{7,5},{8,10},{9,11},{10,... | collective-permute-start | bytes 245768 | tf_op jit(solution)/shard_map/ppermute | solution.py:591
  68.5 3.4 %collective-permute-done.13.refs_2_ = f32[160,128]{1,0:T(8,128)S(1)} collective-permute-done((f32[160,128]{1,0:T(8,128)S(1)}, f32[160,128]{1,0:T(8,128)S(1)}, u32[]{:S(2)}, u32[]{:S(2)}) %collective-permute-start.13) | collective-permute-done | bytes 81952 | tf_op jit(solution)/shard_map/ppermute | solution.py:591
  71.9 1.0 %collective-permute-done.14.refs_3_ = f32[160,128]{1,0:T(8,128)S(1)} collective-permute-done((f32[160,128]{1,0:T(8,128)S(1)}, f32[160,128]{1,0:T(8,128)S(1)}, u32[]{:S(2)}, u32[]{:S(2)}) %collective-permute-start.14) | collective-permute-done | bytes 81952 | tf_op jit(solution)/shard_map/ppermute | solution.py:591
  72.9 1.4 %collective-permute-start.15 = (f32[160,128]{1,0:T(8,128)S(1)}, f32[160,128]{1,0:T(8,128)S(1)}, u32[]{:S(2)}, u32[]{:S(2)}) collective-permute-start(f32[160,128]{1,0:T(8,128)S(1)} %get-tuple-element.43), channel_id=1, source_target_pairs={{0,16},{4,20},{8,24},{12,28},{16,0},{20,4},{24,8},{28,12},{1,17},{... | collective-permute-start | bytes 245768 | tf_op jit(solution)/shard_map/ppermute | solution.py:603
  74.3 2.3 %collective-permute-start.16 = (f32[160,128]{1,0:T(8,128)S(1)}, f32[160,128]{1,0:T(8,128)S(1)}, u32[]{:S(2)}, u32[]{:S(2)}) collective-permute-start(f32[160,128]{1,0:T(8,128)S(1)} %get-tuple-element.44), channel_id=1, source_target_pairs={{0,20},{4,16},{8,28},{12,24},{16,4},{20,0},{24,12},{28,8},{1,21},{... | collective-permute-start | bytes 245768 | tf_op jit(solution)/shard_map/ppermute | solution.py:603
  77.0 2.8 %collective-permute-start.18 = (f32[160,128]{1,0:T(8,128)S(1)}, f32[160,128]{1,0:T(8,128)S(1)}, u32[]{:S(2)}, u32[]{:S(2)}) collective-permute-start(f32[160,128]{1,0:T(8,128)S(1)} %get-tuple-element.46), channel_id=1, source_target_pairs={{0,28},{4,24},{8,20},{12,16},{16,12},{20,8},{24,4},{28,0},{1,29},{... | collective-permute-start | bytes 245768 | tf_op jit(solution)/shard_map/ppermute | solution.py:603
  79.8 6.6 %collective-permute-done.17.refs_7_ = f32[160,128]{1,0:T(8,128)S(1)} collective-permute-done((f32[160,128]{1,0:T(8,128)S(1)}, f32[160,128]{1,0:T(8,128)S(1)}, u32[]{:S(2)}, u32[]{:S(2)}) %collective-permute-start.17) | collective-permute-done | bytes 81952 | tf_op jit(solution)/shard_map/ppermute | solution.py:603
  86.3 5.7 %second_section.1 = f32[2048,128]{1,0:T(8,128)} custom-call(s32[194]{0:T(256)S(1)} %concatenate.6.refs_1_.refs_0_, f32[648]{0:T(1024)S(1)} %concatenate.7.refs_2_.refs_1_, f32[7,8,128]{2,1,0:T(8,128)S(1)} %copy-done.2, f32[4608,128]{1,0:T(8,128)S(1)} %get-tuple-element.37.refs_3_, f32[8,24,24,128]{3,2,1,0:T(8,128)S(1)} %get-tuple-element.38.refs_4_, ...), custom_call_target="tpu_custom_call" | custom-call | tf_op jit(solution)/shard_map/second_section/pallas_call | solution.py:626
  (52 shorter events, 8.2 us)
Async XLA Ops:
  0.0 30.4 %copy-start.1 = (f32[1,16,16,8,128]{4,3,2,1,0:T(8,128)S(1)}, f32[1,16,16,8,128]{4,3,2,1,0:T(8,128)}, u32[]{:S(2)}) copy-start(f32[1,16,16,8,128]{4,3,2,1,0:T(8,128)} %param.6) | copy-start | bytes 3145732
  0.9 17.7 %collective-permute-start = (s32[2]{0:T(128)S(1)}, s32[2]{0:T(128)S(1)}, u32[]{:S(2)}, u32[]{:S(2)}) collective-permute-start(s32[2]{0:T(128)S(1)} %slice_reduce_fusion), channel_id=1, source_target_pairs={{0,16},{16,0},{1,17},{17,1},{2,18},{18,2},{3,19},{19,3},{4,20},{20... | collective-permute-start | bytes 32 | tf_op jit(solution)/shard_map/ppermute | solution.py:493
  5.0 55.1 %copy-start.2 = (f32[7,8,128]{2,1,0:T(8,128)S(1)}, f32[7,8,128]{2,1,0:T(8,128)}, u32[]{:S(2)}) copy-start(f32[7,8,128]{2,1,0:T(8,128)} %constant.223.clone.refs_2_) | copy-start | bytes 86020
  5.0 21.8 %collective-permute-start.1 = (f32[512,128]{1,0:T(8,128)S(1)}, f32[512,128]{1,0:T(8,128)S(1)}, u32[]{:S(2)}, u32[]{:S(2)}) collective-permute-start(f32[512,128]{1,0:T(8,128)S(1)} %bitcast.22), channel_id=1, source_target_pairs={{0,4},{4,0},{8,12},{12,8},{1,5},{5,1},{9,13},{13,9},{2,6},{6,2},{1... | collective-permute-start | bytes 786440 | tf_op jit(solution)/shard_map/ppermute | solution.py:503
  6.6 20.1 %collective-permute-start.2 = (f32[512,128]{1,0:T(8,128)S(1)}, f32[512,128]{1,0:T(8,128)S(1)}, u32[]{:S(2)}, u32[]{:S(2)}) collective-permute-start(f32[512,128]{1,0:T(8,128)S(1)} %bitcast.21), channel_id=1, source_target_pairs={{4,8},{8,4},{5,9},{9,5},{6,10},{10,6},{7,11},{11,7},{20,24},{24,20... | collective-permute-start | bytes 786440 | tf_op jit(solution)/shard_map/ppermute | solution.py:504
  26.8 1.2 %copy-start = (f32[1,16,16,8,128]{4,3,2,1,0:T(8,128)S(1)}, f32[1,16,16,8,128]{4,3,2,1,0:T(8,128)}, u32[]{:S(2)}) copy-start(f32[1,16,16,8,128]{4,3,2,1,0:T(8,128)} %param.6) | copy-start | bytes 3145732
  28.6 1.8 %collective-permute-start.3 = (f32[768,128]{1,0:T(8,128)S(1)}, f32[768,128]{1,0:T(8,128)S(1)}, u32[]{:S(2)}, u32[]{:S(2)}) collective-permute-start(f32[768,128]{1,0:T(8,128)S(1)} %get-tuple-element.26), channel_id=1, source_target_pairs={{0,1},{1,0},{2,3},{3,2},{4,5},{5,4},{6,7},{7,6},{8,9},{9,8},{10,11... | collective-permute-start | bytes 1179656 | tf_op jit(solution)/shard_map/ppermute | solution.py:514
  28.7 1.7 %collective-permute-start.4 = (f32[768,128]{1,0:T(8,128)S(1)}, f32[768,128]{1,0:T(8,128)S(1)}, u32[]{:S(2)}, u32[]{:S(2)}) collective-permute-start(f32[768,128]{1,0:T(8,128)S(1)} %get-tuple-element.27), channel_id=1, source_target_pairs={{1,2},{2,1},{5,6},{6,5},{9,10},{10,9},{13,14},{14,13},{17,18},{18,... | collective-permute-start | bytes 1179656 | tf_op jit(solution)/shard_map/ppermute | solution.py:515
  31.7 9.4 %collective-permute-start.5 = (f32[160,128]{1,0:T(8,128)S(1)}, f32[160,128]{1,0:T(8,128)S(1)}, u32[]{:S(2)}, u32[]{:S(2)}) collective-permute-start(f32[160,128]{1,0:T(8,128)S(1)} %get-tuple-element.30), channel_id=1, source_target_pairs={{0,1},{1,0},{2,3},{3,2},{4,5},{5,4},{6,7},{7,6},{8,9},{9,8},{10,11... | collective-permute-start | bytes 245768 | tf_op jit(solution)/shard_map/ppermute | solution.py:591
  39.7 4.8 %collective-permute-start.6 = (f32[160,128]{1,0:T(8,128)S(1)}, f32[160,128]{1,0:T(8,128)S(1)}, u32[]{:S(2)}, u32[]{:S(2)}) collective-permute-start(f32[160,128]{1,0:T(8,128)S(1)} %get-tuple-element.31), channel_id=1, source_target_pairs={{0,2},{1,3},{2,0},{3,1},{4,6},{5,7},{6,4},{7,5},{8,10},{9,11},{10,... | collective-permute-start | bytes 245768 | tf_op jit(solution)/shard_map/ppermute | solution.py:591
  40.8 4.7 %collective-permute-start.7 = (f32[160,128]{1,0:T(8,128)S(1)}, f32[160,128]{1,0:T(8,128)S(1)}, u32[]{:S(2)}, u32[]{:S(2)}) collective-permute-start(f32[160,128]{1,0:T(8,128)S(1)} %get-tuple-element.32), channel_id=1, source_target_pairs={{0,3},{1,2},{2,1},{3,0},{4,7},{5,6},{6,5},{7,4},{8,11},{9,10},{10,... | collective-permute-start | bytes 245768 | tf_op jit(solution)/shard_map/ppermute | solution.py:591
  45.5 8.2 %collective-permute-start.8 = (f32[160,128]{1,0:T(8,128)S(1)}, f32[160,128]{1,0:T(8,128)S(1)}, u32[]{:S(2)}, u32[]{:S(2)}) collective-permute-start(f32[160,128]{1,0:T(8,128)S(1)} %get-tuple-element.33), channel_id=1, source_target_pairs={{0,16},{4,20},{8,24},{12,28},{16,0},{20,4},{24,8},{28,12},{1,17},{... | collective-permute-start | bytes 245768 | tf_op jit(solution)/shard_map/ppermute | solution.py:603
  46.1 8.1 %collective-permute-start.9 = (f32[160,128]{1,0:T(8,128)S(1)}, f32[160,128]{1,0:T(8,128)S(1)}, u32[]{:S(2)}, u32[]{:S(2)}) collective-permute-start(f32[160,128]{1,0:T(8,128)S(1)} %get-tuple-element.34), channel_id=1, source_target_pairs={{0,20},{4,16},{8,28},{12,24},{16,4},{20,0},{24,12},{28,8},{1,21},{... | collective-permute-start | bytes 245768 | tf_op jit(solution)/shard_map/ppermute | solution.py:603
  51.4 8.7 %collective-permute-start.10 = (f32[160,128]{1,0:T(8,128)S(1)}, f32[160,128]{1,0:T(8,128)S(1)}, u32[]{:S(2)}, u32[]{:S(2)}) collective-permute-start(f32[160,128]{1,0:T(8,128)S(1)} %get-tuple-element.35), channel_id=1, source_target_pairs={{0,24},{4,28},{8,16},{12,20},{16,8},{20,12},{24,0},{28,4},{1,25},{... | collective-permute-start | bytes 245768 | tf_op jit(solution)/shard_map/ppermute | solution.py:603
  51.4 8.7 %collective-permute-start.11 = (f32[160,128]{1,0:T(8,128)S(1)}, f32[160,128]{1,0:T(8,128)S(1)}, u32[]{:S(2)}, u32[]{:S(2)}) collective-permute-start(f32[160,128]{1,0:T(8,128)S(1)} %get-tuple-element.36), channel_id=1, source_target_pairs={{0,28},{4,24},{8,20},{12,16},{16,12},{20,8},{24,4},{28,0},{1,29},{... | collective-permute-start | bytes 245768 | tf_op jit(solution)/shard_map/ppermute | solution.py:603
  66.6 1.9 %collective-permute-start.12 = (f32[160,128]{1,0:T(8,128)S(1)}, f32[160,128]{1,0:T(8,128)S(1)}, u32[]{:S(2)}, u32[]{:S(2)}) collective-permute-start(f32[160,128]{1,0:T(8,128)S(1)} %get-tuple-element.40), channel_id=1, source_target_pairs={{0,1},{1,0},{2,3},{3,2},{4,5},{5,4},{6,7},{7,6},{8,9},{9,8},{10,11... | collective-permute-start | bytes 245768 | tf_op jit(solution)/shard_map/ppermute | solution.py:591
  66.7 5.2 %collective-permute-start.13 = (f32[160,128]{1,0:T(8,128)S(1)}, f32[160,128]{1,0:T(8,128)S(1)}, u32[]{:S(2)}, u32[]{:S(2)}) collective-permute-start(f32[160,128]{1,0:T(8,128)S(1)} %get-tuple-element.41), channel_id=1, source_target_pairs={{0,2},{1,3},{2,0},{3,1},{4,6},{5,7},{6,4},{7,5},{8,10},{9,11},{10,... | collective-permute-start | bytes 245768 | tf_op jit(solution)/shard_map/ppermute | solution.py:591
  68.2 4.7 %collective-permute-start.14 = (f32[160,128]{1,0:T(8,128)S(1)}, f32[160,128]{1,0:T(8,128)S(1)}, u32[]{:S(2)}, u32[]{:S(2)}) collective-permute-start(f32[160,128]{1,0:T(8,128)S(1)} %get-tuple-element.42), channel_id=1, source_target_pairs={{0,3},{1,2},{2,1},{3,0},{4,7},{5,6},{6,5},{7,4},{8,11},{9,10},{10,... | collective-permute-start | bytes 245768 | tf_op jit(solution)/shard_map/ppermute | solution.py:591
  72.9 6.8 %collective-permute-start.15 = (f32[160,128]{1,0:T(8,128)S(1)}, f32[160,128]{1,0:T(8,128)S(1)}, u32[]{:S(2)}, u32[]{:S(2)}) collective-permute-start(f32[160,128]{1,0:T(8,128)S(1)} %get-tuple-element.43), channel_id=1, source_target_pairs={{0,16},{4,20},{8,24},{12,28},{16,0},{20,4},{24,8},{28,12},{1,17},{... | collective-permute-start | bytes 245768 | tf_op jit(solution)/shard_map/ppermute | solution.py:603
  74.3 5.4 %collective-permute-start.16 = (f32[160,128]{1,0:T(8,128)S(1)}, f32[160,128]{1,0:T(8,128)S(1)}, u32[]{:S(2)}, u32[]{:S(2)}) collective-permute-start(f32[160,128]{1,0:T(8,128)S(1)} %get-tuple-element.44), channel_id=1, source_target_pairs={{0,20},{4,16},{8,28},{12,24},{16,4},{20,0},{24,12},{28,8},{1,21},{... | collective-permute-start | bytes 245768 | tf_op jit(solution)/shard_map/ppermute | solution.py:603
  76.7 9.7 %collective-permute-start.17 = (f32[160,128]{1,0:T(8,128)S(1)}, f32[160,128]{1,0:T(8,128)S(1)}, u32[]{:S(2)}, u32[]{:S(2)}) collective-permute-start(f32[160,128]{1,0:T(8,128)S(1)} %get-tuple-element.45), channel_id=1, source_target_pairs={{0,24},{4,28},{8,16},{12,20},{16,8},{20,12},{24,0},{28,4},{1,25},{... | collective-permute-start | bytes 245768 | tf_op jit(solution)/shard_map/ppermute | solution.py:603
  77.0 9.4 %collective-permute-start.18 = (f32[160,128]{1,0:T(8,128)S(1)}, f32[160,128]{1,0:T(8,128)S(1)}, u32[]{:S(2)}, u32[]{:S(2)}) collective-permute-start(f32[160,128]{1,0:T(8,128)S(1)} %get-tuple-element.46), channel_id=1, source_target_pairs={{0,28},{4,24},{8,20},{12,16},{16,12},{20,8},{24,4},{28,0},{1,29},{... | collective-permute-start | bytes 245768 | tf_op jit(solution)/shard_map/ppermute | solution.py:603

commit v3 on v2

v3 whole, which is shorter than its diff:
```python
import math

import jax
import jax.numpy as jnp
import numpy as np
from jax import lax
from jax.experimental import pallas as pl
from jax.experimental.pallas import tpu as pltpu
from jax.sharding import PartitionSpec as P

ETA_COEF = 0.2
NU_COEF = 0.2
KAPPA_COEF = 0.3
SOUND_SQ = 1.0
ARCHIMEDES_LIFT = 0.5
TIME_STEP = 0.2

HALO = 4
PAD = 8
TILE = 8


def is_power_of_two(count):
    return count & (count - 1) == 0


def to_device(index, step, count):
    return index ^ step if is_power_of_two(count) else (index + step) % count


def from_device(index, step, count):
    return index ^ step if is_power_of_two(count) else (index + count - step) % count


def even_pairs(count):
    return [(i, i ^ 1) for i in range(count) if i ^ 1 < count]


def odd_pairs(count):
    route = []
    for low in range(1, count - 1, 2):
        route += [(low, low + 1), (low + 1, low)]
    return route


def lon_route(step, count):
    return [(i, to_device(i, step, count)) for i in range(count)]


def lat_route(step, lat_count, lon_count):
    route = []
    for side in range(2):
        for lat in range(lat_count):
            for lon in range(lon_count):
                target = to_device(lat, step, lat_count)
                if 0 < target < lat_count - 1 and 0 < lon < lon_count - 1:
                    continue
                here = (side * lat_count + lat) * lon_count + lon
                there = ((1 - side) * lat_count + target) * lon_count + lon
                route.append((here, there))
    return route


class Loop:
    def __init__(self, rows, cols, lat_count, lon_count, entries):
        self.rows, self.cols = rows, cols
        self.lat_count, self.lon_count = lat_count, lon_count
        self.nth, self.nph = rows * lat_count, cols * lon_count
        self.total = 4 * (self.nth + self.nph)
        self.blocks = lat_count * lon_count
        self.entries = entries
        one_row = 2 * (cols + 2 * HALO)
        one_col = 2 * (rows + 2 * HALO)
        corner = 2 * (rows + cols + 2 * HALO)
        self.slots = -(-max(corner, one_row, one_col) // self.blocks)
        self.half = -(-one_row // self.blocks)
        side = 4 * (cols + HALO) + 2 * self.nth
        self.column_slots = max(-(-side // self.blocks), 2 * self.half)

    def position(self, row, col):
        nth, nph = self.nth, self.nph
        top = 2 * col + row + 2
        right = 2 * nph + 2 * row + col - nph
        bottom = 2 * nph + 2 * nth + 2 * (nph - 1 - col) + row - nth
        left = 4 * nph + 2 * nth + 2 * (nth - 1 - row) + col + 2
        return jnp.where(
            row < 0, top, jnp.where(row >= nth, bottom, jnp.where(col >= nph, right, left))
        )

    def cell(self, place):
        nth, nph = self.nth, self.nph
        right = place - 2 * nph
        bottom = right - 2 * nth
        left = bottom - 2 * nph
        on_top, on_right, on_bottom = right < 0, bottom < 0, left < 0
        row = jnp.where(
            on_top,
            (place & 1) - 2,
            jnp.where(
                on_right,
                right >> 1,
                jnp.where(on_bottom, nth + (bottom & 1), nth - 1 - (left >> 1)),
            ),
        )
        col = jnp.where(
            on_top,
            place >> 1,
            jnp.where(
                on_right,
                nph + (right & 1),
                jnp.where(on_bottom, nph - 1 - (bottom >> 1), (left & 1) - 2),
            ),
        )
        return row, col

    def top_start(self, lon):
        return 2 * jnp.maximum(lon * self.cols - HALO, 0)

    def bottom_start(self, lon):
        high = jnp.minimum(lon * self.cols + self.cols + HALO, self.nph)
        return 2 * self.nph + 2 * self.nth + 2 * (self.nph - high)

    def stretch(self, lat, lon):
        nth, nph = self.nth, self.nph
        row_low = jnp.maximum(lat * self.rows - HALO, 0)
        row_high = jnp.minimum(lat * self.rows + self.rows + HALO, nth)
        col_low = jnp.maximum(lon * self.cols - HALO, 0)
        col_high = jnp.minimum(lon * self.cols + self.cols + HALO, nph)
        top, bottom = lat == 0, lat == self.lat_count - 1
        left, right = lon == 0, lon == self.lon_count - 1
        left_start = 4 * nph + 2 * nth + 2 * (nth - row_high)
        start = jnp.where(
            top & left,
            left_start,
            jnp.where(
                top,
                self.top_start(lon),
                jnp.where(
                    right,
                    2 * nph + 2 * row_low,
                    jnp.where(bottom, self.bottom_start(lon), left_start),
                ),
            ),
        )
        span = jnp.where(top | bottom, 2 * (col_high - col_low), 0) + jnp.where(
            left | right, 2 * (row_high - row_low), 0
        )
        return start, span

    def first_entry(self, start, donor, offset):
        lead = -(-2 * self.total // self.blocks)
        raised = start - donor - offset + lead * self.blocks + self.blocks - 1
        if is_power_of_two(self.blocks):
            return (raised >> (self.blocks.bit_length() - 1)) - lead
        return lax.div(raised, jnp.full_like(raised, self.blocks)) - lead

    def wrap(self, entry):
        for bound in (8, 4, 2, 1):
            entry = jnp.where(entry < 0, entry + self.entries * bound, entry)
        for bound in (8, 4, 2, 1):
            over = entry - self.entries * bound
            entry = jnp.where(over >= 0, over, entry)
        return entry

    def column_entry(self, lon, donor, offset, slot):
        side = (lon == 0) | (lon == self.lon_count - 1)
        top = self.first_entry(self.top_start(lon), donor, offset)
        bottom = self.first_entry(self.bottom_start(lon), donor, offset)
        lower = (lon == 0) | jnp.logical_not(side) & (slot >= self.half)
        skipped = jnp.where(jnp.logical_not(side) & (slot >= self.half), self.half, 0)
        return jnp.where(lower, bottom, top) + slot - skipped

    def column_slot(self, lat, lon, donor, offset):
        side = (lon == 0) | (lon == self.lon_count - 1)
        start, _ = self.stretch(lat, lon)
        ahead = self.first_entry(start, donor, offset) - self.first_entry(
            jnp.where(lon == 0, self.bottom_start(lon), self.top_start(lon)), donor, offset
        )
        middle = jnp.where(lat == self.lat_count - 1, self.half, 0)
        return jnp.where(side, jnp.maximum(ahead, 0), middle)


def padded_rows(count):
    return -(-count // 1024) * 8


def table_ids(outer, inner, slots):
    rows = padded_rows(outer * inner * slots)
    flat = np.minimum(np.arange(rows * 128), outer * inner * slots - 1)
    return np.stack(
        [flat // (inner * slots), flat // slots % inner, flat % slots]
    ).reshape(3, rows, 128).astype(np.int32)


def whole(count):
    return [pl.BlockSpec(memory_space=pltpu.VMEM)] * count


def scalars(count):
    return [pl.BlockSpec(memory_space=pltpu.SMEM)] * count


def lookup(table_ref, index):
    return table_ref[index // 128, index % 128]


def grant(mebibytes):
    return pltpu.CompilerParams(vmem_limit_bytes=mebibytes << 20)


def tiles(index, count):
    if isinstance(index, int):
        return pl.ds(index * TILE, count * TILE)
    return pl.ds(pl.multiple_of(index * TILE, TILE), count * TILE)


def table_kernel(
    loop, pitch, cell_ref, other_ref, send_id_ref, swap_id_ref, got_id_ref,
    send_ref, swap_ref, receive_ref,
):
    lat, lon = lax.axis_index("lat"), lax.axis_index("lon")
    lat_count, lon_count = loop.lat_count, loop.lon_count
    mine = loop.position(cell_ref[0], cell_ref[1])
    other = loop.position(other_ref[0], other_ref[1])

    step, _, slot = [send_id_ref[n] for n in range(3)]
    entry = loop.column_entry(
        to_device(lon, step, lon_count), lat * lon_count + lon, other, slot
    )
    send_ref[...] = loop.wrap(entry)

    lat_step, lon_step, slot = [swap_id_ref[n] for n in range(3)]
    donor = lat * lon_count + from_device(lon, lon_step, lon_count)
    here = jnp.full_like(slot, lon)
    ahead = loop.column_slot(to_device(lat, lat_step, lat_count), here, donor, other)
    swap_ref[...] = jnp.minimum(ahead + slot, loop.column_slots - 1)

    lat_step, lon_step, slot = [got_id_ref[n] for n in range(3)]
    donor = from_device(lat, lat_step, lat_count) * lon_count + from_device(
        lon, lon_step, lon_count
    )
    start, span = loop.stretch(jnp.full_like(slot, lat), jnp.full_like(slot, lon))
    entry = loop.first_entry(start, donor, mine) + slot
    place = entry * loop.blocks + donor + mine
    wrapped = jnp.where(place >= loop.total, place - loop.total, place)
    row, col = loop.cell(wrapped)
    spot = (row - lat * loop.rows + HALO) * pitch + PAD + (col - lon * loop.cols + HALO)
    receive_ref[...] = jnp.where(place < start + span, spot, 0)


def strip_kernel(rows, cols, state_ref, even_ref, odd_ref, send_even_ref, send_odd_ref):
    lat_even = lax.rem(lax.axis_index("lat"), 2) == 0
    lon_even = lax.rem(lax.axis_index("lon"), 2) == 0

    def copy_rows(first, count, source):
        for out_ref, last in ((send_even_ref, lon_even), (send_odd_ref, jnp.logical_not(lon_even))):
            low = jnp.where(last, cols - HALO, 0)
            for row in range(count):
                out_ref[tiles((first + row) * HALO, HALO), :] = source[
                    tiles(row * cols + low, HALO), :
                ]

    copy_rows(HALO, rows, state_ref)

    @pl.when(lat_even)
    def _():
        copy_rows(0, HALO, odd_ref)
        copy_rows(HALO + rows, HALO, even_ref)

    @pl.when(jnp.logical_not(lat_even))
    def _():
        copy_rows(0, HALO, even_ref)
        copy_rows(HALO + rows, HALO, odd_ref)


def mix_and_pack(loop, wide, rim, frame_ref, value_ref, send_refs):
    send_table_ref, base_ref, weight_ref, cosine_ref, sine_ref = rim
    field = lax.broadcasted_iota(jnp.int32, (TILE, 128), 0)
    takes_next = (field == 1) | (field == 4)
    turned = takes_next | (field == 2) | (field == 5)
    first_row = lax.axis_index("lat") * loop.rows - HALO + 1
    first_col = lax.axis_index("lon") * loop.cols - HALO + 1

    def one_entry(entry, carry):
        base = (base_ref[entry, 0] - first_row) * wide + (base_ref[entry, 1] - first_col)
        total = None
        for a in range(4):
            for b in range(4):
                weight = weight_ref[entry, 4 * a + b]
                part = weight * frame_ref[tiles(base + a * wide + b, 1), :]
                total = part if total is None else total + part
        cosine, sine = cosine_ref[entry], sine_ref[entry]
        other = jnp.where(
            takes_next, pltpu.roll(total, TILE - 1, 0), pltpu.roll(total, 1, 0)
        )
        mixed = cosine * total + jnp.where(takes_next, -sine, sine) * other
        value_ref[tiles(entry, 1), :] = jnp.where(turned, mixed, total)
        return carry

    lax.fori_loop(0, loop.entries, one_entry, 0, unroll=4)
    for step, send_ref in enumerate(send_refs):
        for slot in range(loop.column_slots):
            entry = lookup(send_table_ref, step * loop.column_slots + slot)
            send_ref[tiles(slot, 1), :] = value_ref[tiles(entry, 1), :]


def frame_kernel(loop, *refs):
    rim, refs = refs[:5], refs[5:]
    state_ref, lat_even_ref, lat_odd_ref, lon_even_ref, lon_odd_ref, frame_ref = refs[:6]
    send_refs, value_ref = refs[6:-1], refs[-1]
    rows, cols = loop.rows, loop.cols
    wide = cols + 2 * HALO
    lat_even = lax.rem(lax.axis_index("lat"), 2) == 0
    lon_even = lax.rem(lax.axis_index("lon"), 2) == 0

    def copy_rows(first, count, source, left, width):
        for row in range(count):
            frame_ref[tiles((first + row) * wide + left, width), :] = source[
                tiles(row * width, width), :
            ]

    copy_rows(HALO, rows, state_ref, HALO, cols)

    @pl.when(lat_even)
    def _():
        copy_rows(0, HALO, lat_odd_ref, HALO, cols)
        copy_rows(HALO + rows, HALO, lat_even_ref, HALO, cols)

    @pl.when(jnp.logical_not(lat_even))
    def _():
        copy_rows(0, HALO, lat_even_ref, HALO, cols)
        copy_rows(HALO + rows, HALO, lat_odd_ref, HALO, cols)

    @pl.when(lon_even)
    def _():
        copy_rows(0, rows + 2 * HALO, lon_odd_ref, 0, HALO)
        copy_rows(0, rows + 2 * HALO, lon_even_ref, HALO + cols, HALO)

    @pl.when(jnp.logical_not(lon_even))
    def _():
        copy_rows(0, rows + 2 * HALO, lon_even_ref, 0, HALO)
        copy_rows(0, rows + 2 * HALO, lon_odd_ref, HALO + cols, HALO)

    mix_and_pack(loop, wide, rim, frame_ref, value_ref, send_refs)


def swap_kernel(loop, table_ref, *refs):
    got_refs, out_refs = refs[: loop.lon_count], refs[loop.lon_count :]
    for lat_step in range(loop.lat_count):
        for lon_step in range(loop.lon_count):
            for slot in range(loop.slots):
                place = lon_step * loop.slots + slot
                source = lookup(table_ref, lat_step * loop.lon_count * loop.slots + place)
                out_refs[lat_step][tiles(place, 1), :] = got_refs[lon_step][tiles(source, 1), :]


def section(
    loop, receive_ref, factor_ref, radial_ref, frame_ref, got_refs, plane_ref, work_ref,
    rate_rows, rate_chunks, emit,
):
    tall, wide = loop.rows + 2 * HALO, loop.cols + 2 * HALO
    pitch = wide + 2 * PAD
    arrivals = loop.lon_count * loop.slots

    def spread_row(row, carry):
        for chunk in range(0, wide, 8):
            for f in range(TILE):
                start = (row * wide + chunk) * TILE + f
                plane_ref[pl.ds((f * tall + row) * pitch + PAD + chunk, 8), :] = frame_ref[
                    pl.ds(start, 8, stride=TILE), :
                ]
        return carry

    first_row, last_row = rate_rows
    lax.fori_loop(first_row - 2, last_row + 2, spread_row, 0)
    for lat_step in range(loop.lat_count):
        for place in range(arrivals):
            spot = lookup(receive_ref, lat_step * arrivals + place)
            plane_ref[pl.ds(spot, TILE, stride=tall * pitch), :] = got_refs[lat_step][
                tiles(place, 1), :
            ]

    levels = radial_ref.shape[-1]
    inverse_radius, ru, rl, du, dl, qu, ql = [radial_ref[n] for n in range(7)]

    def up(x):
        return pltpu.roll(x, levels - 1, 1)

    def down(x):
        return pltpu.roll(x, 1, 1)

    half_theta = loop.nth / math.pi
    lat = lax.axis_index("lat")

    def row_factors(row):
        return [factor_ref[(lat * 3 + n) * tall + row] for n in range(3)]

    def reader(ref, row, col):
        def at(number, row_step=0, col_step=0):
            return ref[
                pl.ds((number * tall + row + row_step) * pitch + PAD + col + col_step, 8), :
            ]

        return at

    def curl(at, first, factors, with_phi, with_theta):
        tu, td, ph = factors
        a, b, c = first, first + 1, first + 2
        mid_b, mid_c = at(b), at(c)
        radial = inverse_radius * (
            (tu * at(c, 1) - td * at(c, -1)) - ph * (at(b, 0, 1) - at(b, 0, -1))
        )
        polar = with_phi * (at(a, 0, 1) - at(a, 0, -1)) - (ru * up(mid_c) - rl * down(mid_c))
        azimuth = (ru * up(mid_b) - rl * down(mid_b)) - with_theta * (at(a, 1) - at(a, -1))
        return radial, polar, azimuth

    def slope(at, number, with_phi, with_theta):
        mid = at(number)
        return (
            du * up(mid) - dl * down(mid),
            with_theta * (at(number, 1) - at(number, -1)),
            with_phi * (at(number, 0, 1) - at(number, 0, -1)),
        )

    def outflow(at, first, factors):
        tu, td, ph = factors
        mid = at(first)
        return (qu * up(mid) - ql * down(mid)) + inverse_radius * (
            (tu * at(first + 1, 1) - td * at(first + 1, -1))
            + ph * (at(first + 2, 0, 1) - at(first + 2, 0, -1))
        )

    def cross(x, y):
        return (
            x[1] * y[2] - x[2] * y[1],
            x[2] * y[0] - x[0] * y[2],
            x[0] * y[1] - x[1] * y[0],
        )

    def dot(x, y):
        return x[0] * y[0] + x[1] * y[1] + x[2] * y[2]

    with_theta = inverse_radius * half_theta

    def first_pass(row, carry):
        factors = row_factors(row)
        with_phi = inverse_radius * factors[2]
        for chunk in range(0, wide, 8):
            at = reader(plane_ref, row, chunk)

            def put(number, value):
                work_ref[pl.ds((number * tall + row) * pitch + PAD + chunk, 8), :] = value

            flow = [at(n) for n in range(3)]
            field = [at(n) for n in range(3, 6)]
            current = curl(at, 3, factors, with_phi, with_theta)
            spin = curl(at, 0, factors, with_phi, with_theta)
            induced = cross(flow, field)
            warm = slope(at, 6, with_phi, with_theta)
            for n in range(3):
                put(n, current[n])
                put(3 + n, spin[n])
                put(6 + n, induced[n] - ETA_COEF * current[n])
                put(9 + n, warm[n])
            put(12, at(7) + 0.5 * dot(flow, flow))
        return carry

    lax.fori_loop(first_row - 1, last_row + 1, first_pass, 0)

    def second_pass(row, carry):
        factors = row_factors(row)
        with_phi = inverse_radius * factors[2]
        for chunk in rate_chunks:
            at = reader(plane_ref, row, chunk)
            work = reader(work_ref, row, chunk)
            flow = [at(n) for n in range(3)]
            field = [at(n) for n in range(3, 6)]
            current = [work(n) for n in range(3)]
            spin = [work(3 + n) for n in range(3)]
            warm = [work(9 + n) for n in range(3)]
            field_rate = curl(work, 6, factors, with_phi, with_theta)
            spin_curl = curl(work, 3, factors, with_phi, with_theta)
            head = slope(work, 12, with_phi, with_theta)
            lorentz = cross(current, field)
            advect = cross(flow, spin)
            speed = [
                advect[n] + lorentz[n] - head[n] - NU_COEF * spin_curl[n] for n in range(3)
            ]
            speed[0] = speed[0] + ARCHIMEDES_LIFT * at(6)
            heat = KAPPA_COEF * outflow(work, 9, factors) - dot(flow, warm)
            squeeze = -SOUND_SQ * outflow(at, 0, factors)
            emit(row, chunk, at, speed + list(field_rate) + [heat, squeeze])
        return carry

    lax.fori_loop(first_row, last_row, second_pass, 0)


def first_section_kernel(loop, *refs):
    rim, refs = refs[:5], refs[5:]
    receive_ref, factor_ref, radial_ref, frame_in_ref = refs[:4]
    got_refs, refs = refs[4 : 4 + loop.lat_count], refs[4 + loop.lat_count :]
    frame_ref, rate_ref = refs[:2]
    send_refs, (value_ref, plane_ref, work_ref) = refs[2:-3], refs[-3:]
    tall, wide = loop.rows + 2 * HALO, loop.cols + 2 * HALO
    first_row = lax.axis_index("lat") * loop.rows - HALO
    first_col = lax.axis_index("lon") * loop.cols - HALO

    def emit(row, chunk, at, rate):
        in_row = (row + first_row >= 0) & (row + first_row < loop.nth)
        col = lax.broadcasted_iota(jnp.int32, (8, 128), 0) + (chunk + first_col)
        inside = (col >= jnp.where(in_row, 0, loop.nph)) & (col < loop.nph)
        for f in range(TILE):
            rate_ref[f, row, pl.ds(chunk, 8), :] = rate[f]
            start = (row * wide + chunk) * TILE + f
            frame_ref[pl.ds(start, 8, stride=TILE), :] = jnp.where(
                inside, at(f) + TIME_STEP * rate[f], 0.0
            )

    section(
        loop, receive_ref, factor_ref, radial_ref, frame_in_ref, got_refs, plane_ref, work_ref,
        (2, tall - 2), range(0, wide, 8), emit,
    )
    mix_and_pack(loop, wide, rim, frame_ref, value_ref, send_refs)


def second_section_kernel(loop, receive_ref, factor_ref, radial_ref, frame_ref, rate_ref, *refs):
    got_refs, (change_ref, plane_ref, work_ref) = refs[: loop.lat_count], refs[loop.lat_count :]
    rows, cols = loop.rows, loop.cols

    def emit(row, chunk, at, rate):
        for f in range(TILE):
            start = ((row - HALO) * cols + chunk - HALO) * TILE + f
            change_ref[pl.ds(start, 8, stride=TILE), :] = (0.5 * TIME_STEP) * (
                rate_ref[f, row, pl.ds(chunk, 8), :] + rate[f]
            )

    section(
        loop, receive_ref, factor_ref, radial_ref, frame_ref, got_refs, plane_ref, work_ref,
        (HALO, HALO + rows), range(HALO, HALO + cols, 8), emit,
    )


def radial_factors(levels, theta_count):
    scale = 2.0 * theta_count / math.pi
    step = 0.65 * scale / levels
    radius = 0.35 * scale + (np.arange(levels) + 0.5) * step
    half = 0.5 / step
    above = np.append(radius[1:], 0.0)
    below = np.append(0.0, radius[:-1])
    ones_above = np.append(np.ones(levels - 1), 0.0)
    ones_below = np.append(0.0, np.ones(levels - 1))
    rows = np.stack(
        [
            1.0 / radius,
            half * above / radius,
            half * below / radius,
            half * ones_above,
            half * ones_below,
            half * above**2 / radius**2,
            half * below**2 / radius**2,
        ]
    )
    return np.repeat(rows[:, None, :], 8, axis=1).astype(np.float32)


def row_factors(rows, lat_count, nth, nph):
    polar_step, azimuth_step = math.pi / (2 * nth), 1.5 * math.pi / nph
    tall = rows + 2 * HALO
    parts = []
    for lat in range(lat_count):
        row = lat * rows - HALO - 1 + np.arange(tall + 2)
        sines = np.sin(math.pi / 4 + (row + 0.5) * polar_step)
        middle = sines[1:-1]
        parts += [
            sines[2:] / middle * (0.5 / polar_step),
            sines[:-2] / middle * (0.5 / polar_step),
            (0.5 / azimuth_step) / middle,
        ]
    return np.concatenate(parts).astype(np.float32)


def per_device(state, rim_base, rim_weight, rim_angle, rim_target):
    _, rows, cols, fields, levels = state.shape
    lat_count, lon_count = lax.axis_size("lat"), lax.axis_size("lon")
    entries = rim_base.shape[1]
    loop = Loop(rows, cols, lat_count, lon_count, entries)
    tall, wide = rows + 2 * HALO, cols + 2 * HALO
    pitch = wide + 2 * PAD
    block = state[0].reshape(rows * cols * fields, levels)
    f32 = jnp.float32

    def tile_array(count):
        return jax.ShapeDtypeStruct((count * TILE, levels), f32)

    first_cell = rim_target[0, 0]
    other_cell = lax.ppermute(first_cell, "panel", [(0, 1), (1, 0)])

    cells = state[0]
    last_first = lax.axis_index("lat") % 2 == 0
    head, tail = cells[:HALO], cells[rows - HALO :]
    send_even = jnp.where(last_first, tail, head).reshape(HALO * cols * fields, levels)
    send_odd = jnp.where(last_first, head, tail).reshape(HALO * cols * fields, levels)
    lat_even = lax.ppermute(send_even, "lat", even_pairs(lat_count))
    lat_odd = lax.ppermute(send_odd, "lat", odd_pairs(lat_count))

    send_ids = table_ids(1, lon_count, loop.column_slots)[[1, 0, 2]]
    got_ids = table_ids(lat_count, lon_count, loop.slots)
    send_table, swap_table, receive_table = pl.pallas_call(
        lambda *refs: table_kernel(loop, pitch, *refs),
        out_shape=[
            jax.ShapeDtypeStruct(ids.shape[1:], jnp.int32) for ids in (send_ids, got_ids, got_ids)
        ],
        in_specs=scalars(2) + whole(3),
        out_specs=whole(3),
        compiler_params=grant(4),
        name="tables",
    )(first_cell, other_cell, jnp.asarray(send_ids), jnp.asarray(got_ids), jnp.asarray(got_ids))
    angle = rim_angle[0]
    rim = (send_table, rim_base[0], rim_weight[0], jnp.cos(angle), jnp.sin(angle))
    factors = jnp.asarray(row_factors(rows, lat_count, loop.nth, loop.nph))
    radial = jnp.asarray(radial_factors(levels, loop.nth))

    strip_even, strip_odd = pl.pallas_call(
        lambda *refs: strip_kernel(rows, cols, *refs),
        out_shape=[tile_array(tall * HALO)] * 2,
        in_specs=whole(3),
        out_specs=whole(2),
        compiler_params=grant(4),
        name="strips",
    )(block, lat_even, lat_odd)
    lon_even = lax.ppermute(strip_even, "lon", even_pairs(lon_count))
    lon_odd = lax.ppermute(strip_odd, "lon", odd_pairs(lon_count))

    packed_shapes = [tile_array(loop.column_slots)] * lon_count
    frame, *packed = pl.pallas_call(
        lambda *refs: frame_kernel(loop, *refs),
        out_shape=[tile_array(tall * wide)] + packed_shapes,
        in_specs=scalars(5) + whole(5),
        out_specs=whole(1 + lon_count),
        scratch_shapes=[pltpu.VMEM((entries * TILE, levels), f32)],
        compiler_params=grant(8),
        name="frame",
    )(*rim, block, lat_even, lat_odd, lon_even, lon_odd)

    def exchange(packed):
        got = [packed[0]] + [
            lax.ppermute(packed[step], "lon", lon_route(step, lon_count))
            for step in range(1, lon_count)
        ]
        turned = pl.pallas_call(
            lambda *refs: swap_kernel(loop, *refs),
            out_shape=[tile_array(lon_count * loop.slots)] * lat_count,
            in_specs=scalars(1) + whole(lon_count),
            out_specs=whole(lat_count),
            compiler_params=grant(4),
            name="swap",
        )(swap_table, *got)
        return [
            lax.ppermute(
                turned[step], ("panel", "lat", "lon"), lat_route(step, lat_count, lon_count)
            )
            for step in range(lat_count)
        ]

    got = exchange(packed)
    planes = [
        pltpu.VMEM((fields * tall * pitch, levels), f32),
        pltpu.VMEM((13 * tall * pitch, levels), f32),
    ]
    frame, rate, *packed = pl.pallas_call(
        lambda *refs: first_section_kernel(loop, *refs),
        out_shape=[tile_array(tall * wide), jax.ShapeDtypeStruct((fields, tall, wide, levels), f32)]
        + packed_shapes,
        in_specs=scalars(7) + whole(2 + lat_count),
        out_specs=whole(2 + lon_count),
        scratch_shapes=[pltpu.VMEM((entries * TILE, levels), f32)] + planes,
        compiler_params=grant(24),
        name="first_section",
    )(*rim, receive_table, factors, radial, frame, *got)

    got = exchange(packed)
    change = pl.pallas_call(
        lambda *refs: second_section_kernel(loop, *refs),
        out_shape=tile_array(rows * cols),
        in_specs=scalars(2) + whole(3 + lat_count),
        out_specs=whole(1)[0],
        scratch_shapes=planes,
        compiler_params=grant(24),
        name="second_section",
    )(receive_table, factors, radial, frame, rate, *got)
    return change.reshape(1, rows, cols, fields, levels)


def solution(mesh):
    return jax.shard_map(
        per_device,
        mesh=mesh,
        in_specs=(
            P("panel", "lat", "lon", None, None),
            P("panel", ("lat", "lon"), None),
            P("panel", ("lat", "lon"), None),
            P("panel", ("lat", "lon")),
            P("panel", None, None),
        ),
        out_specs=P("panel", "lat", "lon", None, None),
        check_vma=False,
    )
```

time: 92.6 us -> 89.7 us (0.969)
  between operations: 14.6 us -> 0.25 us
  starting transfers between devices: 32.4 us -> 44.5 us
  Pallas kernels: 14.1 us -> 16.7 us
  local copies, waits for them, and re-layouts: 6.01 us -> 3.65 us
  other arithmetic: 2.43 us -> 1.16 us
    ppermute x8, starting transfers between devices: 15.1 us -> 31.7 us  [exchange(): lax.ppermute(turned[step], ('panel', 'lat', 'lon'), lat_route(step, lat_c...]
    ppermute x1, waiting for transfers between devices: 0.01 us -> 5.63 us  [per_device(): lat_even = lax.ppermute(send_even, 'lat', even_pairs(lat_count))]
    ppermute x6, starting transfers between devices: 11.3 us -> 6.53 us  [exchange(): lax.ppermute(packed[step], 'lon', lon_route(step, lon_count))]
    ppermute x8, waiting for transfers between devices: 12.9 us -> 9.58 us  [exchange(): lax.ppermute(turned[step], ('panel', 'lat', 'lon'), lat_route(step, lat_c...]
    pallas_call x5 -> x6, Pallas kernels: 13.5 us -> 16.7 us  [the longest x1 7.15 us: per_device(): pl.pallas_call(lambda *refs: first_section_kernel(loop, *refs), out_shape...]
    ppermute x6, waiting for transfers between devices: 8.82 us -> 6.62 us  [exchange(): lax.ppermute(packed[step], 'lon', lon_route(step, lon_count))]
    slice x2 -> x0, local copies, waits for them, and re-layouts: 1.99 us -> none  [the longest x1 1.34 us: per_device(): mine = loop.position(first_cell[0], first_cell[1])]
    ppermute x1, starting transfers between devices: 1.64 us -> 3.14 us  [per_device(): lat_even = lax.ppermute(send_even, 'lat', even_pairs(lat_count))]
  transfers between devices with their start and end apart: 19 -> 19, of which waited for: 8 -> 10; matrix products, arithmetic and copies ran while one was open for 7% -> 2% of each run, Pallas kernels for 0% -> 1%
where the time goes in v3:
time: 89.7 us; the launch traced here: 89.1 us
  starting transfers between devices  44.5 us (50%)
  waiting for transfers between devices  22.9 us (26%)
  Pallas kernels  16.7 us (19%)
  local copies, waits for them, and re-layouts  3.65 us (4%)
  other arithmetic  1.16 us (1%)
    ppermute x8, starting transfers between devices, exchange(): lax.ppermute(turned[step], ('panel', 'lat', 'lon'), lat_route(step, lat_c...  31.7 us
    ppermute x8, waiting for transfers between devices, exchange(): lax.ppermute(turned[step], ('panel', 'lat', 'lon'), lat_route(step, lat_c...  9.58 us
    pallas_call x1, Pallas kernels, per_device(): pl.pallas_call(lambda *refs: first_section_kernel(loop, *refs), out_shape...  7.15 us
    ppermute x6, waiting for transfers between devices, exchange(): lax.ppermute(packed[step], 'lon', lon_route(step, lon_count))  6.62 us
    ppermute x6, starting transfers between devices, exchange(): lax.ppermute(packed[step], 'lon', lon_route(step, lon_count))  6.53 us
    pallas_call x1, Pallas kernels, per_device(): pl.pallas_call(lambda *refs: second_section_kernel(loop, *refs), out_shap...  5.73 us
    ppermute x1, waiting for transfers between devices, per_device(): lat_even = lax.ppermute(send_even, 'lat', even_pairs(lat_count))  5.63 us
    ppermute x1, starting transfers between devices, per_device(): lat_even = lax.ppermute(send_even, 'lat', even_pairs(lat_count))  3.14 us
  transfers between devices with their start and end apart: 19, of which 10 were waited for; matrix products, arithmetic and copies ran while one was open for 2% of the time, Pallas kernels for 1%

profile of v3, /device:TPU:0, one launch (start us, length us, event | category | flops | bytes accessed | tf_op | source)
XLA Modules:
  0.0 89.1 jit_solution(18065162841975233970)
XLA Ops:
  1.2 3.1 %collective-permute-start.1 = (f32[512,128]{1,0:T(8,128)S(1)}, f32[512,128]{1,0:T(8,128)S(1)}, u32[]{:S(2)}, u32[]{:S(2)}) collective-permute-start(f32[512,128]{1,0:T(8,128)S(1)} %bitcast.15), channel_id=1, source_target_pairs={{0,4},{4,0},{8,12},{12,8},{1,5},{5,1},{9,13},{13,9},{2,6},{6,2},{1... | collective-permute-start | bytes 786440 | tf_op jit(solution)/shard_map/ppermute | solution.py:603
  5.0 5.6 %collective-permute-done.1.refs_1_.refs_6_ = f32[512,128]{1,0:T(8,128)S(1)} collective-permute-done((f32[512,128]{1,0:T(8,128)S(1)}, f32[512,128]{1,0:T(8,128)S(1)}, u32[]{:S(2)}, u32[]{:S(2)}) %collective-permute-start.1) | collective-permute-done | bytes 262176 | tf_op jit(solution)/shard_map/ppermute | solution.py:603
  10.6 1.2 %copy-done = f32[1,16,16,8,128]{4,3,2,1,0:T(8,128)S(1)} copy-done((f32[1,16,16,8,128]{4,3,2,1,0:T(8,128)S(1)}, f32[1,16,16,8,128]{4,3,2,1,0:T(8,128)}, u32[]{:S(2)}) %copy-start) | copy-done | bytes 1048600
  13.5 1.7 %collective-permute-start = (s32[2]{0:T(128)S(1)}, s32[2]{0:T(128)S(1)}, u32[]{:S(2)}, u32[]{:S(2)}) collective-permute-start(s32[2]{0:T(128)S(1)} %slice_reduce_fusion.refs_0_), channel_id=1, source_target_pairs={{0,16},{16,0},{1,17},{17,1},{2,18},{18,2},{3,19},{19,3},{4,20},{20... | collective-permute-start | bytes 32 | tf_op jit(solution)/shard_map/ppermute | solution.py:596
  18.5 1.9 %frame.1 = (f32[4608,128]{1,0:T(8,128)S(1)}, f32[104,128]{1,0:T(8,128)S(1)}, f32[104,128]{1,0:T(8,128)S(1)}, f32[104,128]{1,0:T(8,128)S(1)}, f32[104,128]{1,0:T(8,128)S(1)}) custom-call(s32[8,128]{1,0:T(8,128)S(1)} %get-tuple-element.30.refs_0_, s32[32,2]{1,0:T(8,128)S(1)} %copy.12.refs_1_, f32[32,16]{1,0:T(8,128)S(1)} %bitcast.12, ...), custom_call_target="tpu_custom_call" | custom-call | tf_op jit(solution)/shard_map/frame/pallas_call | solution.py:635
  20.3 3.2 %collective-permute-start.5 = (f32[104,128]{1,0:T(8,128)S(1)}, f32[104,128]{1,0:T(8,128)S(1)}, u32[]{:S(2)}, u32[]{:S(2)}) collective-permute-start(f32[104,128]{1,0:T(8,128)S(1)} %get-tuple-element.36), channel_id=1, source_target_pairs={{0,1},{1,0},{2,3},{3,2},{4,5},{5,4},{6,7},{7,6},{8,9},{9,8},{10,11... | collective-permute-start | bytes 159752 | tf_op jit(solution)/shard_map/ppermute | solution.py:647
  23.5 1.3 %collective-permute-start.6 = (f32[104,128]{1,0:T(8,128)S(1)}, f32[104,128]{1,0:T(8,128)S(1)}, u32[]{:S(2)}, u32[]{:S(2)}) collective-permute-start(f32[104,128]{1,0:T(8,128)S(1)} %get-tuple-element.37), channel_id=1, source_target_pairs={{0,2},{1,3},{2,0},{3,1},{4,6},{5,7},{6,4},{7,5},{8,10},{9,11},{10,... | collective-permute-start | bytes 159752 | tf_op jit(solution)/shard_map/ppermute | solution.py:647
  25.0 2.7 %collective-permute-done.6.refs_3_ = f32[104,128]{1,0:T(8,128)S(1)} collective-permute-done((f32[104,128]{1,0:T(8,128)S(1)}, f32[104,128]{1,0:T(8,128)S(1)}, u32[]{:S(2)}, u32[]{:S(2)}) %collective-permute-start.6) | collective-permute-done | bytes 53280 | tf_op jit(solution)/shard_map/ppermute | solution.py:647
  29.3 3.5 %collective-permute-start.8 = (f32[160,128]{1,0:T(8,128)S(1)}, f32[160,128]{1,0:T(8,128)S(1)}, u32[]{:S(2)}, u32[]{:S(2)}) collective-permute-start(f32[160,128]{1,0:T(8,128)S(1)} %get-tuple-element.39), channel_id=1, source_target_pairs={{0,16},{1,17},{2,18},{3,19},{4,20},{7,23},{8,24},{11,27},{12,28},{... | collective-permute-start | bytes 245768 | tf_op jit(solution)/shard_map/ppermute | solution.py:659
  32.7 6.5 %collective-permute-start.9 = (f32[160,128]{1,0:T(8,128)S(1)}, f32[160,128]{1,0:T(8,128)S(1)}, u32[]{:S(2)}, u32[]{:S(2)}) collective-permute-start(f32[160,128]{1,0:T(8,128)S(1)} %get-tuple-element.40), channel_id=1, source_target_pairs={{0,20},{3,23},{4,16},{5,17},{6,18},{7,19},{8,28},{9,29},{10,30},{1... | collective-permute-start | bytes 245768 | tf_op jit(solution)/shard_map/ppermute | solution.py:659
  39.2 3.1 %collective-permute-start.10 = (f32[160,128]{1,0:T(8,128)S(1)}, f32[160,128]{1,0:T(8,128)S(1)}, u32[]{:S(2)}, u32[]{:S(2)}) collective-permute-start(f32[160,128]{1,0:T(8,128)S(1)} %get-tuple-element.41), channel_id=1, source_target_pairs={{0,24},{3,27},{4,28},{5,29},{6,30},{7,31},{8,16},{9,17},{10,18},{1... | collective-permute-start | bytes 245768 | tf_op jit(solution)/shard_map/ppermute | solution.py:659
  42.3 4.3 %collective-permute-start.11 = (f32[160,128]{1,0:T(8,128)S(1)}, f32[160,128]{1,0:T(8,128)S(1)}, u32[]{:S(2)}, u32[]{:S(2)}) collective-permute-start(f32[160,128]{1,0:T(8,128)S(1)} %get-tuple-element.42), channel_id=1, source_target_pairs={{0,28},{1,29},{2,30},{3,31},{4,24},{7,27},{8,20},{11,23},{12,16},{... | collective-permute-start | bytes 245768 | tf_op jit(solution)/shard_map/ppermute | solution.py:659
  46.7 1.3 %collective-permute-done.10.refs_11_ = f32[160,128]{1,0:T(8,128)S(1)} collective-permute-done((f32[160,128]{1,0:T(8,128)S(1)}, f32[160,128]{1,0:T(8,128)S(1)}, u32[]{:S(2)}, u32[]{:S(2)}) %collective-permute-start.10) | collective-permute-done | bytes 81952 | tf_op jit(solution)/shard_map/ppermute | solution.py:659
  48.0 3.4 %collective-permute-done.11.refs_12_ = f32[160,128]{1,0:T(8,128)S(1)} collective-permute-done((f32[160,128]{1,0:T(8,128)S(1)}, f32[160,128]{1,0:T(8,128)S(1)}, u32[]{:S(2)}, u32[]{:S(2)}) %collective-permute-start.11) | collective-permute-done | bytes 81952 | tf_op jit(solution)/shard_map/ppermute | solution.py:659
  51.4 7.1 %first_section.1 = (f32[4608,128]{1,0:T(8,128)S(1)}, f32[8,24,24,128]{3,2,1,0:T(8,128)S(1)}, f32[104,128]{1,0:T(8,128)S(1)}, f32[104,128]{1,0:T(8,128)S(1)}, f32...) custom-call(s32[8,128]{1,0:T(8,128)S(1)} %get-tuple-element.30.refs_0_, s32[32,2]{1,0:T(8,128)S(1)} %copy.12.refs_1_, ...), custom_call_target="tpu_custom_call" | custom-call | tf_op jit(solution)/shard_map/first_section/pallas_call | solution.py:670
  58.7 1.8 %collective-permute-start.14 = (f32[104,128]{1,0:T(8,128)S(1)}, f32[104,128]{1,0:T(8,128)S(1)}, u32[]{:S(2)}, u32[]{:S(2)}) collective-permute-start(f32[104,128]{1,0:T(8,128)S(1)} %get-tuple-element.48), channel_id=1, source_target_pairs={{0,3},{1,2},{2,1},{3,0},{4,7},{5,6},{6,5},{7,4},{8,11},{9,10},{10,... | collective-permute-start | bytes 159752 | tf_op jit(solution)/shard_map/ppermute | solution.py:647
  60.5 2.9 %collective-permute-done.13.refs_3_ = f32[104,128]{1,0:T(8,128)S(1)} collective-permute-done((f32[104,128]{1,0:T(8,128)S(1)}, f32[104,128]{1,0:T(8,128)S(1)}, u32[]{:S(2)}, u32[]{:S(2)}) %collective-permute-start.13) | collective-permute-done | bytes 53280 | tf_op jit(solution)/shard_map/ppermute | solution.py:647
  64.1 3.5 %collective-permute-start.15 = (f32[160,128]{1,0:T(8,128)S(1)}, f32[160,128]{1,0:T(8,128)S(1)}, u32[]{:S(2)}, u32[]{:S(2)}) collective-permute-start(f32[160,128]{1,0:T(8,128)S(1)} %get-tuple-element.49), channel_id=1, source_target_pairs={{0,16},{1,17},{2,18},{3,19},{4,20},{7,23},{8,24},{11,27},{12,28},{... | collective-permute-start | bytes 245768 | tf_op jit(solution)/shard_map/ppermute | solution.py:659
  67.6 3.3 %collective-permute-start.16 = (f32[160,128]{1,0:T(8,128)S(1)}, f32[160,128]{1,0:T(8,128)S(1)}, u32[]{:S(2)}, u32[]{:S(2)}) collective-permute-start(f32[160,128]{1,0:T(8,128)S(1)} %get-tuple-element.50), channel_id=1, source_target_pairs={{0,20},{3,23},{4,16},{5,17},{6,18},{7,19},{8,28},{9,29},{10,30},{1... | collective-permute-start | bytes 245768 | tf_op jit(solution)/shard_map/ppermute | solution.py:659
  70.9 3.5 %collective-permute-start.17 = (f32[160,128]{1,0:T(8,128)S(1)}, f32[160,128]{1,0:T(8,128)S(1)}, u32[]{:S(2)}, u32[]{:S(2)}) collective-permute-start(f32[160,128]{1,0:T(8,128)S(1)} %get-tuple-element.51), channel_id=1, source_target_pairs={{0,24},{3,27},{4,28},{5,29},{6,30},{7,31},{8,16},{9,17},{10,18},{1... | collective-permute-start | bytes 245768 | tf_op jit(solution)/shard_map/ppermute | solution.py:659
  74.4 4.2 %collective-permute-start.18 = (f32[160,128]{1,0:T(8,128)S(1)}, f32[160,128]{1,0:T(8,128)S(1)}, u32[]{:S(2)}, u32[]{:S(2)}) collective-permute-start(f32[160,128]{1,0:T(8,128)S(1)} %get-tuple-element.52), channel_id=1, source_target_pairs={{0,28},{1,29},{2,30},{3,31},{4,24},{7,27},{8,20},{11,23},{12,16},{... | collective-permute-start | bytes 245768 | tf_op jit(solution)/shard_map/ppermute | solution.py:659
  78.6 1.5 %collective-permute-done.17.refs_7_ = f32[160,128]{1,0:T(8,128)S(1)} collective-permute-done((f32[160,128]{1,0:T(8,128)S(1)}, f32[160,128]{1,0:T(8,128)S(1)}, u32[]{:S(2)}, u32[]{:S(2)}) %collective-permute-start.17) | collective-permute-done | bytes 81952 | tf_op jit(solution)/shard_map/ppermute | solution.py:659
  80.1 3.3 %collective-permute-done.18.refs_8_ = f32[160,128]{1,0:T(8,128)S(1)} collective-permute-done((f32[160,128]{1,0:T(8,128)S(1)}, f32[160,128]{1,0:T(8,128)S(1)}, u32[]{:S(2)}, u32[]{:S(2)}) %collective-permute-start.18) | collective-permute-done | bytes 81952 | tf_op jit(solution)/shard_map/ppermute | solution.py:659
  83.4 5.7 %second_section.1 = f32[2048,128]{1,0:T(8,128)} custom-call(s32[8,128]{1,0:T(8,128)S(1)} %get-tuple-element.29.refs_5_.refs_0_, f32[288]{0:T(512)S(1)} %copy-done.5, f32[7,8,128]{2,1,0:T(8,128)S(1)} %copy-done.2, f32[4608,128]{1,0:T(8,128)S(1)} %get-tuple-element.43.refs_3_, f32[8,24,24,128]{3,2,1,0:T(8,128)S(1)} %get-tuple-element.44.refs_4_, ...), custom_call_target="tpu_custom_call" | custom-call | tf_op jit(solution)/shard_map/second_section/pallas_call | solution.py:682
  (42 shorter events, 9.3 us)
Async XLA Ops:
  0.0 17.1 %copy-start.3 = (s32[3,8,128]{2,1,0:T(8,128)S(1)}, s32[3,8,128]{2,1,0:T(8,128)}, u32[]{:S(2)}) copy-start(s32[3,8,128]{2,1,0:T(8,128)} %constant.28.clone.refs_3_.refs_4_) | copy-start | bytes 36868
  0.0 18.5 %copy-start.1 = (f32[1,16,16,8,128]{4,3,2,1,0:T(8,128)S(1)}, f32[1,16,16,8,128]{4,3,2,1,0:T(8,128)}, u32[]{:S(2)}) copy-start(f32[1,16,16,8,128]{4,3,2,1,0:T(8,128)} %param.9) | copy-start | bytes 3145732
  0.0 16.1 %copy-start.7 = (f32[1,32]{1,0:T(1,128)S(1)}, f32[1,32]{1,0:T(1,128)}, u32[]{:S(2)}) copy-start(f32[1,32]{1,0:T(1,128)} %param.12) | copy-start | bytes 388
  0.0 51.4 %copy-start.2 = (f32[7,8,128]{2,1,0:T(8,128)S(1)}, f32[7,8,128]{2,1,0:T(8,128)}, u32[]{:S(2)}) copy-start(f32[7,8,128]{2,1,0:T(8,128)} %constant.30.clone.refs_7_.refs_2_) | copy-start | bytes 86020
  1.2 50.2 %copy-start.5 = (f32[288]{0:T(512)S(1)}, f32[288]{0:T(512)}, u32[]{:S(2)}) copy-start(f32[288]{0:T(512)} %constant.29.clone.refs_6_.refs_1_) | copy-start | bytes 3460
  1.2 9.4 %collective-permute-start.1 = (f32[512,128]{1,0:T(8,128)S(1)}, f32[512,128]{1,0:T(8,128)S(1)}, u32[]{:S(2)}, u32[]{:S(2)}) collective-permute-start(f32[512,128]{1,0:T(8,128)S(1)} %bitcast.15), channel_id=1, source_target_pairs={{0,4},{4,0},{8,12},{12,8},{1,5},{5,1},{9,13},{13,9},{2,6},{6,2},{1... | collective-permute-start | bytes 786440 | tf_op jit(solution)/shard_map/ppermute | solution.py:603
  4.3 6.3 %collective-permute-start.2 = (f32[512,128]{1,0:T(8,128)S(1)}, f32[512,128]{1,0:T(8,128)S(1)}, u32[]{:S(2)}, u32[]{:S(2)}) collective-permute-start(f32[512,128]{1,0:T(8,128)S(1)} %bitcast.14), channel_id=1, source_target_pairs={{4,8},{8,4},{5,9},{9,5},{6,10},{10,6},{7,11},{11,7},{20,24},{24,20... | collective-permute-start | bytes 786440 | tf_op jit(solution)/shard_map/ppermute | solution.py:604
  11.9 6.5 %collective-permute-start.3 = (f32[768,128]{1,0:T(8,128)S(1)}, f32[768,128]{1,0:T(8,128)S(1)}, u32[]{:S(2)}, u32[]{:S(2)}) collective-permute-start(f32[768,128]{1,0:T(8,128)S(1)} %get-tuple-element.31), channel_id=1, source_target_pairs={{0,1},{1,0},{2,3},{3,2},{4,5},{5,4},{6,7},{7,6},{8,9},{9,8},{10,11... | collective-permute-start | bytes 1179656 | tf_op jit(solution)/shard_map/ppermute | solution.py:631
  12.0 6.4 %collective-permute-start.4 = (f32[768,128]{1,0:T(8,128)S(1)}, f32[768,128]{1,0:T(8,128)S(1)}, u32[]{:S(2)}, u32[]{:S(2)}) collective-permute-start(f32[768,128]{1,0:T(8,128)S(1)} %get-tuple-element.32), channel_id=1, source_target_pairs={{1,2},{2,1},{5,6},{6,5},{9,10},{10,9},{13,14},{14,13},{17,18},{18,... | collective-permute-start | bytes 1179656 | tf_op jit(solution)/shard_map/ppermute | solution.py:632
  13.5 3.6 %collective-permute-start = (s32[2]{0:T(128)S(1)}, s32[2]{0:T(128)S(1)}, u32[]{:S(2)}, u32[]{:S(2)}) collective-permute-start(s32[2]{0:T(128)S(1)} %slice_reduce_fusion.refs_0_), channel_id=1, source_target_pairs={{0,16},{16,0},{1,17},{17,1},{2,18},{18,2},{3,19},{19,3},{4,20},{20... | collective-permute-start | bytes 32 | tf_op jit(solution)/shard_map/ppermute | solution.py:596
  20.3 4.6 %collective-permute-start.5 = (f32[104,128]{1,0:T(8,128)S(1)}, f32[104,128]{1,0:T(8,128)S(1)}, u32[]{:S(2)}, u32[]{:S(2)}) collective-permute-start(f32[104,128]{1,0:T(8,128)S(1)} %get-tuple-element.36), channel_id=1, source_target_pairs={{0,1},{1,0},{2,3},{3,2},{4,5},{5,4},{6,7},{7,6},{8,9},{9,8},{10,11... | collective-permute-start | bytes 159752 | tf_op jit(solution)/shard_map/ppermute | solution.py:647
  23.5 4.1 %collective-permute-start.6 = (f32[104,128]{1,0:T(8,128)S(1)}, f32[104,128]{1,0:T(8,128)S(1)}, u32[]{:S(2)}, u32[]{:S(2)}) collective-permute-start(f32[104,128]{1,0:T(8,128)S(1)} %get-tuple-element.37), channel_id=1, source_target_pairs={{0,2},{1,3},{2,0},{3,1},{4,6},{5,7},{6,4},{7,5},{8,10},{9,11},{10,... | collective-permute-start | bytes 159752 | tf_op jit(solution)/shard_map/ppermute | solution.py:647
  24.8 3.8 %collective-permute-start.7 = (f32[104,128]{1,0:T(8,128)S(1)}, f32[104,128]{1,0:T(8,128)S(1)}, u32[]{:S(2)}, u32[]{:S(2)}) collective-permute-start(f32[104,128]{1,0:T(8,128)S(1)} %get-tuple-element.38), channel_id=1, source_target_pairs={{0,3},{1,2},{2,1},{3,0},{4,7},{5,6},{6,5},{7,4},{8,11},{9,10},{10,... | collective-permute-start | bytes 159752 | tf_op jit(solution)/shard_map/ppermute | solution.py:647
  29.3 17.4 %collective-permute-start.8 = (f32[160,128]{1,0:T(8,128)S(1)}, f32[160,128]{1,0:T(8,128)S(1)}, u32[]{:S(2)}, u32[]{:S(2)}) collective-permute-start(f32[160,128]{1,0:T(8,128)S(1)} %get-tuple-element.39), channel_id=1, source_target_pairs={{0,16},{1,17},{2,18},{3,19},{4,20},{7,23},{8,24},{11,27},{12,28},{... | collective-permute-start | bytes 245768 | tf_op jit(solution)/shard_map/ppermute | solution.py:659
  32.7 13.9 %collective-permute-start.9 = (f32[160,128]{1,0:T(8,128)S(1)}, f32[160,128]{1,0:T(8,128)S(1)}, u32[]{:S(2)}, u32[]{:S(2)}) collective-permute-start(f32[160,128]{1,0:T(8,128)S(1)} %get-tuple-element.40), channel_id=1, source_target_pairs={{0,20},{3,23},{4,16},{5,17},{6,18},{7,19},{8,28},{9,29},{10,30},{1... | collective-permute-start | bytes 245768 | tf_op jit(solution)/shard_map/ppermute | solution.py:659
  39.2 8.8 %collective-permute-start.10 = (f32[160,128]{1,0:T(8,128)S(1)}, f32[160,128]{1,0:T(8,128)S(1)}, u32[]{:S(2)}, u32[]{:S(2)}) collective-permute-start(f32[160,128]{1,0:T(8,128)S(1)} %get-tuple-element.41), channel_id=1, source_target_pairs={{0,24},{3,27},{4,28},{5,29},{6,30},{7,31},{8,16},{9,17},{10,18},{1... | collective-permute-start | bytes 245768 | tf_op jit(solution)/shard_map/ppermute | solution.py:659
  42.3 9.1 %collective-permute-start.11 = (f32[160,128]{1,0:T(8,128)S(1)}, f32[160,128]{1,0:T(8,128)S(1)}, u32[]{:S(2)}, u32[]{:S(2)}) collective-permute-start(f32[160,128]{1,0:T(8,128)S(1)} %get-tuple-element.42), channel_id=1, source_target_pairs={{0,28},{1,29},{2,30},{3,31},{4,24},{7,27},{8,20},{11,23},{12,16},{... | collective-permute-start | bytes 245768 | tf_op jit(solution)/shard_map/ppermute | solution.py:659
  58.5 1.9 %collective-permute-start.12 = (f32[104,128]{1,0:T(8,128)S(1)}, f32[104,128]{1,0:T(8,128)S(1)}, u32[]{:S(2)}, u32[]{:S(2)}) collective-permute-start(f32[104,128]{1,0:T(8,128)S(1)} %get-tuple-element.46), channel_id=1, source_target_pairs={{0,1},{1,0},{2,3},{3,2},{4,5},{5,4},{6,7},{7,6},{8,9},{9,8},{10,11... | collective-permute-start | bytes 159752 | tf_op jit(solution)/shard_map/ppermute | solution.py:647
  58.6 4.8 %collective-permute-start.13 = (f32[104,128]{1,0:T(8,128)S(1)}, f32[104,128]{1,0:T(8,128)S(1)}, u32[]{:S(2)}, u32[]{:S(2)}) collective-permute-start(f32[104,128]{1,0:T(8,128)S(1)} %get-tuple-element.47), channel_id=1, source_target_pairs={{0,2},{1,3},{2,0},{3,1},{4,6},{5,7},{6,4},{7,5},{8,10},{9,11},{10,... | collective-permute-start | bytes 159752 | tf_op jit(solution)/shard_map/ppermute | solution.py:647
  58.7 4.8 %collective-permute-start.14 = (f32[104,128]{1,0:T(8,128)S(1)}, f32[104,128]{1,0:T(8,128)S(1)}, u32[]{:S(2)}, u32[]{:S(2)}) collective-permute-start(f32[104,128]{1,0:T(8,128)S(1)} %get-tuple-element.48), channel_id=1, source_target_pairs={{0,3},{1,2},{2,1},{3,0},{4,7},{5,6},{6,5},{7,4},{8,11},{9,10},{10,... | collective-permute-start | bytes 159752 | tf_op jit(solution)/shard_map/ppermute | solution.py:647
  64.1 14.4 %collective-permute-start.15 = (f32[160,128]{1,0:T(8,128)S(1)}, f32[160,128]{1,0:T(8,128)S(1)}, u32[]{:S(2)}, u32[]{:S(2)}) collective-permute-start(f32[160,128]{1,0:T(8,128)S(1)} %get-tuple-element.49), channel_id=1, source_target_pairs={{0,16},{1,17},{2,18},{3,19},{4,20},{7,23},{8,24},{11,27},{12,28},{... | collective-permute-start | bytes 245768 | tf_op jit(solution)/shard_map/ppermute | solution.py:659
  67.6 10.9 %collective-permute-start.16 = (f32[160,128]{1,0:T(8,128)S(1)}, f32[160,128]{1,0:T(8,128)S(1)}, u32[]{:S(2)}, u32[]{:S(2)}) collective-permute-start(f32[160,128]{1,0:T(8,128)S(1)} %get-tuple-element.50), channel_id=1, source_target_pairs={{0,20},{3,23},{4,16},{5,17},{6,18},{7,19},{8,28},{9,29},{10,30},{1... | collective-permute-start | bytes 245768 | tf_op jit(solution)/shard_map/ppermute | solution.py:659
  70.9 9.2 %collective-permute-start.17 = (f32[160,128]{1,0:T(8,128)S(1)}, f32[160,128]{1,0:T(8,128)S(1)}, u32[]{:S(2)}, u32[]{:S(2)}) collective-permute-start(f32[160,128]{1,0:T(8,128)S(1)} %get-tuple-element.51), channel_id=1, source_target_pairs={{0,24},{3,27},{4,28},{5,29},{6,30},{7,31},{8,16},{9,17},{10,18},{1... | collective-permute-start | bytes 245768 | tf_op jit(solution)/shard_map/ppermute | solution.py:659
  74.4 9.0 %collective-permute-start.18 = (f32[160,128]{1,0:T(8,128)S(1)}, f32[160,128]{1,0:T(8,128)S(1)}, u32[]{:S(2)}, u32[]{:S(2)}) collective-permute-start(f32[160,128]{1,0:T(8,128)S(1)} %get-tuple-element.52), channel_id=1, source_target_pairs={{0,28},{1,29},{2,30},{3,31},{4,24},{7,27},{8,20},{11,23},{12,16},{... | collective-permute-start | bytes 245768 | tf_op jit(solution)/shard_map/ppermute | solution.py:659
  (3 other events, 17.1 us)

commit v4 on v3

--- a/solution.py
+++ b/solution.py
@@ -47,18 +47,12 @@
     return [(i, to_device(i, step, count)) for i in range(count)]
 
 
-def lat_route(step, lat_count, lon_count):
-    route = []
-    for side in range(2):
-        for lat in range(lat_count):
-            for lon in range(lon_count):
-                target = to_device(lat, step, lat_count)
-                if 0 < target < lat_count - 1 and 0 < lon < lon_count - 1:
-                    continue
-                here = (side * lat_count + lat) * lon_count + lon
-                there = ((1 - side) * lat_count + target) * lon_count + lon
-                route.append((here, there))
-    return route
+def lat_route(step, count):
+    return [
+        (side * count + i, (1 - side) * count + to_device(i, step, count))
+        for side in range(2)
+        for i in range(count)
+    ]
 
 
 class Loop:
@@ -248,29 +242,31 @@
     receive_ref[...] = jnp.where(place < start + span, spot, 0)
 
 
-def strip_kernel(rows, cols, state_ref, even_ref, odd_ref, send_even_ref, send_odd_ref):
+def strip_kernel(rows, cols, own_even_ref, own_odd_ref, even_ref, odd_ref, *send_refs):
     lat_even = lax.rem(lax.axis_index("lat"), 2) == 0
     lon_even = lax.rem(lax.axis_index("lon"), 2) == 0
-
-    def copy_rows(first, count, source):
-        for out_ref, last in ((send_even_ref, lon_even), (send_odd_ref, jnp.logical_not(lon_even))):
-            low = jnp.where(last, cols - HALO, 0)
-            for row in range(count):
-                out_ref[tiles((first + row) * HALO, HALO), :] = source[
+    high = cols - HALO
+    lows = (jnp.where(lon_even, high, 0), jnp.where(lon_even, 0, high))
+
+    def copy_halo(first, source):
+        for send_ref, low in zip(send_refs, lows):
+            for row in range(HALO):
+                send_ref[tiles((first + row) * HALO, HALO), :] = source[
                     tiles(row * cols + low, HALO), :
                 ]
 
-    copy_rows(HALO, rows, state_ref)
+    for send_ref, own_ref in zip(send_refs, (own_even_ref, own_odd_ref)):
+        send_ref[tiles(HALO * HALO, rows * HALO), :] = own_ref[...]
 
     @pl.when(lat_even)
     def _():
-        copy_rows(0, HALO, odd_ref)
-        copy_rows(HALO + rows, HALO, even_ref)
+        copy_halo(0, odd_ref)
+        copy_halo(HALO + rows, even_ref)
 
     @pl.when(jnp.logical_not(lat_even))
     def _():
-        copy_rows(0, HALO, even_ref)
-        copy_rows(HALO + rows, HALO, odd_ref)
+        copy_halo(0, even_ref)
+        copy_halo(HALO + rows, odd_ref)
 
 
 def mix_and_pack(loop, wide, rim, frame_ref, value_ref, send_refs):
@@ -620,14 +616,18 @@
     factors = jnp.asarray(row_factors(rows, lat_count, loop.nth, loop.nph))
     radial = jnp.asarray(radial_factors(levels, loop.nth))
 
+    east_first = lax.axis_index("lon") % 2 == 0
+    head, tail = cells[:, :HALO], cells[:, cols - HALO :]
+    own_even = jnp.where(east_first, tail, head).reshape(rows * HALO * fields, levels)
+    own_odd = jnp.where(east_first, head, tail).reshape(rows * HALO * fields, levels)
     strip_even, strip_odd = pl.pallas_call(
         lambda *refs: strip_kernel(rows, cols, *refs),
         out_shape=[tile_array(tall * HALO)] * 2,
-        in_specs=whole(3),
+        in_specs=whole(4),
         out_specs=whole(2),
         compiler_params=grant(4),
         name="strips",
-    )(block, lat_even, lat_odd)
+    )(own_even, own_odd, lat_even, lat_odd)
     lon_even = lax.ppermute(strip_even, "lon", even_pairs(lon_count))
     lon_odd = lax.ppermute(strip_odd, "lon", odd_pairs(lon_count))
 
@@ -656,9 +656,7 @@
             name="swap",
         )(swap_table, *got)
         return [
-            lax.ppermute(
-                turned[step], ("panel", "lat", "lon"), lat_route(step, lat_count, lon_count)
-            )
+            lax.ppermute(turned[step], ("panel", "lat"), lat_route(step, lat_count))
             for step in range(lat_count)
         ]
 

time: 89.7 us -> 76.3 us (0.85)
  starting transfers between devices: 44.5 us -> 30.1 us
  waiting for transfers between devices: 22.9 us -> 25.9 us
  local copies, waits for them, and re-layouts: 3.65 us -> 1.03 us
  other arithmetic: 1.16 us -> 2.23 us
    ppermute x8, starting transfers between devices: 31.7 us -> 16.6 us  [exchange(): lax.ppermute(turned[step], ('panel', 'lat'), lat_route(step, lat_count))]
    ppermute x8, waiting for transfers between devices: 9.58 us -> 12.8 us  [exchange(): lax.ppermute(turned[step], ('panel', 'lat'), lat_route(step, lat_count))]
    unnamed x17, local copies, waits for them, and re-layouts: 2.73 us -> 0.11 us
    ppermute x1, waiting for transfers between devices: 5.63 us -> 4.51 us  [per_device(): lat_even = lax.ppermute(send_even, 'lat', even_pairs(lat_count))]
    select_n x0 -> x1, other arithmetic: none -> 1.08 us  [per_device(): jnp.where(east_first, head, tail).reshape(rows * HALO * fields, levels)]
  transfers between devices with their start and end apart: 19 -> 19, of which waited for: 10 -> 9; matrix products, arithmetic and copies ran while one was open for 2% -> 3% of each run, Pallas kernels for 1% -> 1%
where the time goes in v4:
time: 76.3 us; the launch traced here: 76.2 us
  starting transfers between devices  30.1 us (39%)
  waiting for transfers between devices  25.9 us (34%)
  Pallas kernels  16.7 us (22%)
  other arithmetic  2.23 us (3%)
  local copies, waits for them, and re-layouts  1.03 us (1%)
    ppermute x8, starting transfers between devices, exchange(): lax.ppermute(turned[step], ('panel', 'lat'), lat_route(step, lat_count))  16.6 us
    ppermute x8, waiting for transfers between devices, exchange(): lax.ppermute(turned[step], ('panel', 'lat'), lat_route(step, lat_count))  12.8 us
    ppermute x6, starting transfers between devices, exchange(): lax.ppermute(packed[step], 'lon', lon_route(step, lon_count))  7.24 us
    pallas_call x1, Pallas kernels, per_device(): pl.pallas_call(lambda *refs: first_section_kernel(loop, *refs), out_shape...  7.16 us
    ppermute x6, waiting for transfers between devices, exchange(): lax.ppermute(packed[step], 'lon', lon_route(step, lon_count))  6.85 us
    pallas_call x1, Pallas kernels, per_device(): pl.pallas_call(lambda *refs: second_section_kernel(loop, *refs), out_shap...  5.74 us
    ppermute x1, waiting for transfers between devices, per_device(): lat_even = lax.ppermute(send_even, 'lat', even_pairs(lat_count))  4.51 us
    ppermute x1, starting transfers between devices, per_device(): lat_even = lax.ppermute(send_even, 'lat', even_pairs(lat_count))  3.13 us
  transfers between devices with their start and end apart: 19, of which 9 were waited for; matrix products, arithmetic and copies ran while one was open for 3% of the time, Pallas kernels for 1%

profile of v4, /device:TPU:0, one launch (start us, length us, event | category | flops | bytes accessed | tf_op | source)
XLA Modules:
  0.0 76.2 jit_solution(4596323060028811789)
XLA Ops:
  0.0 1.2 %slice_select_fusion.2 = (f32[1,4,16,8,128]{4,3,2,1,0:T(8,128)S(1)}, f32[1,4,16,8,128]{4,3,2,1,0:T(8,128)S(1)}) fusion(f32[1,16,16,8,128]{4,3,2,1,0:T(8,128)} %param.9, pred[]{:T(512)S(6)} %eq.9), kind=kLoop, calls=%fused_computation.2 | loop fusion | flops 131072 | bytes 1048577 | tf_op jit(solution)/shard_map/jit(_where)/select_n | solution.py:598
  1.2 3.1 %collective-permute-start.1 = (f32[512,128]{1,0:T(8,128)S(1)}, f32[512,128]{1,0:T(8,128)S(1)}, u32[]{:S(2)}, u32[]{:S(2)}) collective-permute-start(f32[512,128]{1,0:T(8,128)S(1)} %bitcast.20), channel_id=1, source_target_pairs={{0,4},{4,0},{8,12},{12,8},{1,5},{5,1},{9,13},{13,9},{2,6},{6,2},{1... | collective-permute-start | bytes 786440 | tf_op jit(solution)/shard_map/ppermute | solution.py:599
  5.0 1.1 %slice_select_fusion = (f32[16,4,8,128]{3,2,1,0:T(8,128)S(1)}, f32[16,4,8,128]{3,2,1,0:T(8,128)S(1)}) fusion(f32[16,16,8,128]{3,2,1,0:T(8,128)} %bitcast.13, pred[]{:T(512)S(6)} %eq.10), kind=kLoop, calls=%fused_computation | loop fusion | flops 131072 | bytes 1048577 | tf_op jit(solution)/shard_map/jit(_where)/select_n | solution.py:622
  6.1 4.5 %collective-permute-done.1.refs_2_.refs_6_ = f32[512,128]{1,0:T(8,128)S(1)} collective-permute-done((f32[512,128]{1,0:T(8,128)S(1)}, f32[512,128]{1,0:T(8,128)S(1)}, u32[]{:S(2)}, u32[]{:S(2)}) %collective-permute-start.1) | collective-permute-done | bytes 262176 | tf_op jit(solution)/shard_map/ppermute | solution.py:599
  12.3 1.7 %collective-permute-start = (s32[2]{0:T(128)S(1)}, s32[2]{0:T(128)S(1)}, u32[]{:S(2)}, u32[]{:S(2)}) collective-permute-start(s32[2]{0:T(128)S(1)} %slice_reduce_fusion.refs_0_), channel_id=1, source_target_pairs={{0,16},{16,0},{1,17},{17,1},{2,18},{18,2},{3,19},{19,3},{4,20},{20... | collective-permute-start | bytes 32 | tf_op jit(solution)/shard_map/ppermute | solution.py:592
  14.2 1.7 %collective-permute-done.refs_1_ = s32[2]{0:T(128)S(1)} collective-permute-done((s32[2]{0:T(128)S(1)}, s32[2]{0:T(128)S(1)}, u32[]{:S(2)}, u32[]{:S(2)}) %collective-permute-start) | collective-permute-done | bytes 40 | tf_op jit(solution)/shard_map/ppermute | solution.py:592
  16.5 1.9 %frame.1 = (f32[4608,128]{1,0:T(8,128)S(1)}, f32[104,128]{1,0:T(8,128)S(1)}, f32[104,128]{1,0:T(8,128)S(1)}, f32[104,128]{1,0:T(8,128)S(1)}, f32[104,128]{1,0:T(8,128)S(1)}) custom-call(s32[8,128]{1,0:T(8,128)S(1)} %get-tuple-element.30.refs_0_, s32[32,2]{1,0:T(8,128)S(1)} %copy.12.refs_1_, f32[32,16]{1,0:T(8,128)S(1)} %bitcast.17, ...), custom_call_target="tpu_custom_call" | custom-call | tf_op jit(solution)/shard_map/frame/pallas_call | solution.py:635
  18.4 3.9 %collective-permute-start.5 = (f32[104,128]{1,0:T(8,128)S(1)}, f32[104,128]{1,0:T(8,128)S(1)}, u32[]{:S(2)}, u32[]{:S(2)}) collective-permute-start(f32[104,128]{1,0:T(8,128)S(1)} %get-tuple-element.36), channel_id=1, source_target_pairs={{0,1},{1,0},{2,3},{3,2},{4,5},{5,4},{6,7},{7,6},{8,9},{9,8},{10,11... | collective-permute-start | bytes 159752 | tf_op jit(solution)/shard_map/ppermute | solution.py:647
  22.3 1.3 %collective-permute-start.6 = (f32[104,128]{1,0:T(8,128)S(1)}, f32[104,128]{1,0:T(8,128)S(1)}, u32[]{:S(2)}, u32[]{:S(2)}) collective-permute-start(f32[104,128]{1,0:T(8,128)S(1)} %get-tuple-element.37), channel_id=1, source_target_pairs={{0,2},{1,3},{2,0},{3,1},{4,6},{5,7},{6,4},{7,5},{8,10},{9,11},{10,... | collective-permute-start | bytes 159752 | tf_op jit(solution)/shard_map/ppermute | solution.py:647
  23.7 2.7 %collective-permute-done.6.refs_3_ = f32[104,128]{1,0:T(8,128)S(1)} collective-permute-done((f32[104,128]{1,0:T(8,128)S(1)}, f32[104,128]{1,0:T(8,128)S(1)}, u32[]{:S(2)}, u32[]{:S(2)}) %collective-permute-start.6) | collective-permute-done | bytes 53280 | tf_op jit(solution)/shard_map/ppermute | solution.py:647
  28.0 1.6 %collective-permute-start.8 = (f32[160,128]{1,0:T(8,128)S(1)}, f32[160,128]{1,0:T(8,128)S(1)}, u32[]{:S(2)}, u32[]{:S(2)}) collective-permute-start(f32[160,128]{1,0:T(8,128)S(1)} %get-tuple-element.39), channel_id=1, source_target_pairs={{0,16},{4,20},{8,24},{12,28},{16,0},{20,4},{24,8},{28,12},{1,17},{... | collective-permute-start | bytes 245768 | tf_op jit(solution)/shard_map/ppermute | solution.py:659
  29.7 4.6 %collective-permute-start.9 = (f32[160,128]{1,0:T(8,128)S(1)}, f32[160,128]{1,0:T(8,128)S(1)}, u32[]{:S(2)}, u32[]{:S(2)}) collective-permute-start(f32[160,128]{1,0:T(8,128)S(1)} %get-tuple-element.40), channel_id=1, source_target_pairs={{0,20},{4,16},{8,28},{12,24},{16,4},{20,0},{24,12},{28,8},{1,21},{... | collective-permute-start | bytes 245768 | tf_op jit(solution)/shard_map/ppermute | solution.py:659
  34.2 1.2 %collective-permute-start.10 = (f32[160,128]{1,0:T(8,128)S(1)}, f32[160,128]{1,0:T(8,128)S(1)}, u32[]{:S(2)}, u32[]{:S(2)}) collective-permute-start(f32[160,128]{1,0:T(8,128)S(1)} %get-tuple-element.41), channel_id=1, source_target_pairs={{0,24},{4,28},{8,16},{12,20},{16,8},{20,12},{24,0},{28,4},{1,25},{... | collective-permute-start | bytes 245768 | tf_op jit(solution)/shard_map/ppermute | solution.py:659
  35.4 2.4 %collective-permute-start.11 = (f32[160,128]{1,0:T(8,128)S(1)}, f32[160,128]{1,0:T(8,128)S(1)}, u32[]{:S(2)}, u32[]{:S(2)}) collective-permute-start(f32[160,128]{1,0:T(8,128)S(1)} %get-tuple-element.42), channel_id=1, source_target_pairs={{0,28},{4,24},{8,20},{12,16},{16,12},{20,8},{24,4},{28,0},{1,29},{... | collective-permute-start | bytes 245768 | tf_op jit(solution)/shard_map/ppermute | solution.py:659
  37.8 6.2 %collective-permute-done.10.refs_11_ = f32[160,128]{1,0:T(8,128)S(1)} collective-permute-done((f32[160,128]{1,0:T(8,128)S(1)}, f32[160,128]{1,0:T(8,128)S(1)}, u32[]{:S(2)}, u32[]{:S(2)}) %collective-permute-start.10) | collective-permute-done | bytes 81952 | tf_op jit(solution)/shard_map/ppermute | solution.py:659
  44.0 7.2 %first_section.1 = (f32[4608,128]{1,0:T(8,128)S(1)}, f32[8,24,24,128]{3,2,1,0:T(8,128)S(1)}, f32[104,128]{1,0:T(8,128)S(1)}, f32[104,128]{1,0:T(8,128)S(1)}, f32...) custom-call(s32[8,128]{1,0:T(8,128)S(1)} %get-tuple-element.30.refs_0_, s32[32,2]{1,0:T(8,128)S(1)} %copy.12.refs_1_, ...), custom_call_target="tpu_custom_call" | custom-call | tf_op jit(solution)/shard_map/first_section/pallas_call | solution.py:668
  51.2 1.2 %collective-permute-start.13 = (f32[104,128]{1,0:T(8,128)S(1)}, f32[104,128]{1,0:T(8,128)S(1)}, u32[]{:S(2)}, u32[]{:S(2)}) collective-permute-start(f32[104,128]{1,0:T(8,128)S(1)} %get-tuple-element.47), channel_id=1, source_target_pairs={{0,2},{1,3},{2,0},{3,1},{4,6},{5,7},{6,4},{7,5},{8,10},{9,11},{10,... | collective-permute-start | bytes 159752 | tf_op jit(solution)/shard_map/ppermute | solution.py:647
  53.1 2.4 %collective-permute-done.13.refs_3_ = f32[104,128]{1,0:T(8,128)S(1)} collective-permute-done((f32[104,128]{1,0:T(8,128)S(1)}, f32[104,128]{1,0:T(8,128)S(1)}, u32[]{:S(2)}, u32[]{:S(2)}) %collective-permute-start.13) | collective-permute-done | bytes 53280 | tf_op jit(solution)/shard_map/ppermute | solution.py:647
  57.0 1.6 %collective-permute-start.15 = (f32[160,128]{1,0:T(8,128)S(1)}, f32[160,128]{1,0:T(8,128)S(1)}, u32[]{:S(2)}, u32[]{:S(2)}) collective-permute-start(f32[160,128]{1,0:T(8,128)S(1)} %get-tuple-element.49), channel_id=1, source_target_pairs={{0,16},{4,20},{8,24},{12,28},{16,0},{20,4},{24,8},{28,12},{1,17},{... | collective-permute-start | bytes 245768 | tf_op jit(solution)/shard_map/ppermute | solution.py:659
  58.5 2.0 %collective-permute-start.16 = (f32[160,128]{1,0:T(8,128)S(1)}, f32[160,128]{1,0:T(8,128)S(1)}, u32[]{:S(2)}, u32[]{:S(2)}) collective-permute-start(f32[160,128]{1,0:T(8,128)S(1)} %get-tuple-element.50), channel_id=1, source_target_pairs={{0,20},{4,16},{8,28},{12,24},{16,4},{20,0},{24,12},{28,8},{1,21},{... | collective-permute-start | bytes 245768 | tf_op jit(solution)/shard_map/ppermute | solution.py:659
  60.5 1.3 %collective-permute-start.17 = (f32[160,128]{1,0:T(8,128)S(1)}, f32[160,128]{1,0:T(8,128)S(1)}, u32[]{:S(2)}, u32[]{:S(2)}) collective-permute-start(f32[160,128]{1,0:T(8,128)S(1)} %get-tuple-element.51), channel_id=1, source_target_pairs={{0,24},{4,28},{8,16},{12,20},{16,8},{20,12},{24,0},{28,4},{1,25},{... | collective-permute-start | bytes 245768 | tf_op jit(solution)/shard_map/ppermute | solution.py:659
  61.8 2.0 %collective-permute-start.18 = (f32[160,128]{1,0:T(8,128)S(1)}, f32[160,128]{1,0:T(8,128)S(1)}, u32[]{:S(2)}, u32[]{:S(2)}) collective-permute-start(f32[160,128]{1,0:T(8,128)S(1)} %get-tuple-element.52), channel_id=1, source_target_pairs={{0,28},{4,24},{8,20},{12,16},{16,12},{20,8},{24,4},{28,0},{1,29},{... | collective-permute-start | bytes 245768 | tf_op jit(solution)/shard_map/ppermute | solution.py:659
  63.9 6.5 %collective-permute-done.17.refs_7_ = f32[160,128]{1,0:T(8,128)S(1)} collective-permute-done((f32[160,128]{1,0:T(8,128)S(1)}, f32[160,128]{1,0:T(8,128)S(1)}, u32[]{:S(2)}, u32[]{:S(2)}) %collective-permute-start.17) | collective-permute-done | bytes 81952 | tf_op jit(solution)/shard_map/ppermute | solution.py:659
  70.4 5.7 %second_section.1 = f32[2048,128]{1,0:T(8,128)} custom-call(s32[8,128]{1,0:T(8,128)S(1)} %get-tuple-element.29.refs_5_.refs_0_, f32[288]{0:T(512)S(1)} %copy-done.4, f32[7,8,128]{2,1,0:T(8,128)S(1)} %copy-done.1, f32[4608,128]{1,0:T(8,128)S(1)} %get-tuple-element.43.refs_3_, f32[8,24,24,128]{3,2,1,0:T(8,128)S(1)} %get-tuple-element.44.refs_4_, ...), custom_call_target="tpu_custom_call" | custom-call | tf_op jit(solution)/shard_map/second_section/pallas_call | solution.py:680
  (43 shorter events, 7.1 us)
Async XLA Ops:
  0.0 15.9 %copy-start.2 = (s32[3,8,128]{2,1,0:T(8,128)S(1)}, s32[3,8,128]{2,1,0:T(8,128)}, u32[]{:S(2)}) copy-start(s32[3,8,128]{2,1,0:T(8,128)} %constant.34.clone.refs_3_.refs_4_) | copy-start | bytes 36868
  0.0 15.9 %copy-start.3 = (s32[3,8,128]{2,1,0:T(8,128)S(1)}, s32[3,8,128]{2,1,0:T(8,128)}, u32[]{:S(2)}) copy-start(s32[3,8,128]{2,1,0:T(8,128)} %constant.33.clone.refs_2_) | copy-start | bytes 36868
  0.0 16.5 %copy-start = (f32[1,16,16,8,128]{4,3,2,1,0:T(8,128)S(1)}, f32[1,16,16,8,128]{4,3,2,1,0:T(8,128)}, u32[]{:S(2)}) copy-start(f32[1,16,16,8,128]{4,3,2,1,0:T(8,128)} %param.9) | copy-start | bytes 3145732
  1.2 9.4 %collective-permute-start.1 = (f32[512,128]{1,0:T(8,128)S(1)}, f32[512,128]{1,0:T(8,128)S(1)}, u32[]{:S(2)}, u32[]{:S(2)}) collective-permute-start(f32[512,128]{1,0:T(8,128)S(1)} %bitcast.20), channel_id=1, source_target_pairs={{0,4},{4,0},{8,12},{12,8},{1,5},{5,1},{9,13},{13,9},{2,6},{6,2},{1... | collective-permute-start | bytes 786440 | tf_op jit(solution)/shard_map/ppermute | solution.py:599
  4.3 6.3 %collective-permute-start.2 = (f32[512,128]{1,0:T(8,128)S(1)}, f32[512,128]{1,0:T(8,128)S(1)}, u32[]{:S(2)}, u32[]{:S(2)}) collective-permute-start(f32[512,128]{1,0:T(8,128)S(1)} %bitcast.19), channel_id=1, source_target_pairs={{4,8},{8,4},{5,9},{9,5},{6,10},{10,6},{7,11},{11,7},{20,24},{24,20... | collective-permute-start | bytes 786440 | tf_op jit(solution)/shard_map/ppermute | solution.py:600
  5.0 39.0 %copy-start.1 = (f32[7,8,128]{2,1,0:T(8,128)S(1)}, f32[7,8,128]{2,1,0:T(8,128)}, u32[]{:S(2)}) copy-start(f32[7,8,128]{2,1,0:T(8,128)} %constant.36.clone.refs_7_.refs_2_) | copy-start | bytes 86020
  5.0 39.0 %copy-start.4 = (f32[288]{0:T(512)S(1)}, f32[288]{0:T(512)}, u32[]{:S(2)}) copy-start(f32[288]{0:T(512)} %constant.35.clone.refs_6_.refs_1_) | copy-start | bytes 3460
  10.7 5.8 %collective-permute-start.3 = (f32[768,128]{1,0:T(8,128)S(1)}, f32[768,128]{1,0:T(8,128)S(1)}, u32[]{:S(2)}, u32[]{:S(2)}) collective-permute-start(f32[768,128]{1,0:T(8,128)S(1)} %get-tuple-element.31), channel_id=1, source_target_pairs={{0,1},{1,0},{2,3},{3,2},{4,5},{5,4},{6,7},{7,6},{8,9},{9,8},{10,11... | collective-permute-start | bytes 1179656 | tf_op jit(solution)/shard_map/ppermute | solution.py:631
  10.8 5.7 %collective-permute-start.4 = (f32[768,128]{1,0:T(8,128)S(1)}, f32[768,128]{1,0:T(8,128)S(1)}, u32[]{:S(2)}, u32[]{:S(2)}) collective-permute-start(f32[768,128]{1,0:T(8,128)S(1)} %get-tuple-element.32), channel_id=1, source_target_pairs={{1,2},{2,1},{5,6},{6,5},{9,10},{10,9},{13,14},{14,13},{17,18},{18,... | collective-permute-start | bytes 1179656 | tf_op jit(solution)/shard_map/ppermute | solution.py:632
  12.3 3.6 %collective-permute-start = (s32[2]{0:T(128)S(1)}, s32[2]{0:T(128)S(1)}, u32[]{:S(2)}, u32[]{:S(2)}) collective-permute-start(s32[2]{0:T(128)S(1)} %slice_reduce_fusion.refs_0_), channel_id=1, source_target_pairs={{0,16},{16,0},{1,17},{17,1},{2,18},{18,2},{3,19},{19,3},{4,20},{20... | collective-permute-start | bytes 32 | tf_op jit(solution)/shard_map/ppermute | solution.py:592
  18.4 5.3 %collective-permute-start.5 = (f32[104,128]{1,0:T(8,128)S(1)}, f32[104,128]{1,0:T(8,128)S(1)}, u32[]{:S(2)}, u32[]{:S(2)}) collective-permute-start(f32[104,128]{1,0:T(8,128)S(1)} %get-tuple-element.36), channel_id=1, source_target_pairs={{0,1},{1,0},{2,3},{3,2},{4,5},{5,4},{6,7},{7,6},{8,9},{9,8},{10,11... | collective-permute-start | bytes 159752 | tf_op jit(solution)/shard_map/ppermute | solution.py:647
  22.3 4.1 %collective-permute-start.6 = (f32[104,128]{1,0:T(8,128)S(1)}, f32[104,128]{1,0:T(8,128)S(1)}, u32[]{:S(2)}, u32[]{:S(2)}) collective-permute-start(f32[104,128]{1,0:T(8,128)S(1)} %get-tuple-element.37), channel_id=1, source_target_pairs={{0,2},{1,3},{2,0},{3,1},{4,6},{5,7},{6,4},{7,5},{8,10},{9,11},{10,... | collective-permute-start | bytes 159752 | tf_op jit(solution)/shard_map/ppermute | solution.py:647
  23.6 3.8 %collective-permute-start.7 = (f32[104,128]{1,0:T(8,128)S(1)}, f32[104,128]{1,0:T(8,128)S(1)}, u32[]{:S(2)}, u32[]{:S(2)}) collective-permute-start(f32[104,128]{1,0:T(8,128)S(1)} %get-tuple-element.38), channel_id=1, source_target_pairs={{0,3},{1,2},{2,1},{3,0},{4,7},{5,6},{6,5},{7,4},{8,11},{9,10},{10,... | collective-permute-start | bytes 159752 | tf_op jit(solution)/shard_map/ppermute | solution.py:647
  28.0 9.8 %collective-permute-start.8 = (f32[160,128]{1,0:T(8,128)S(1)}, f32[160,128]{1,0:T(8,128)S(1)}, u32[]{:S(2)}, u32[]{:S(2)}) collective-permute-start(f32[160,128]{1,0:T(8,128)S(1)} %get-tuple-element.39), channel_id=1, source_target_pairs={{0,16},{4,20},{8,24},{12,28},{16,0},{20,4},{24,8},{28,12},{1,17},{... | collective-permute-start | bytes 245768 | tf_op jit(solution)/shard_map/ppermute | solution.py:659
  29.7 8.1 %collective-permute-start.9 = (f32[160,128]{1,0:T(8,128)S(1)}, f32[160,128]{1,0:T(8,128)S(1)}, u32[]{:S(2)}, u32[]{:S(2)}) collective-permute-start(f32[160,128]{1,0:T(8,128)S(1)} %get-tuple-element.40), channel_id=1, source_target_pairs={{0,20},{4,16},{8,28},{12,24},{16,4},{20,0},{24,12},{28,8},{1,21},{... | collective-permute-start | bytes 245768 | tf_op jit(solution)/shard_map/ppermute | solution.py:659
  34.2 9.8 %collective-permute-start.10 = (f32[160,128]{1,0:T(8,128)S(1)}, f32[160,128]{1,0:T(8,128)S(1)}, u32[]{:S(2)}, u32[]{:S(2)}) collective-permute-start(f32[160,128]{1,0:T(8,128)S(1)} %get-tuple-element.41), channel_id=1, source_target_pairs={{0,24},{4,28},{8,16},{12,20},{16,8},{20,12},{24,0},{28,4},{1,25},{... | collective-permute-start | bytes 245768 | tf_op jit(solution)/shard_map/ppermute | solution.py:659
  35.4 8.6 %collective-permute-start.11 = (f32[160,128]{1,0:T(8,128)S(1)}, f32[160,128]{1,0:T(8,128)S(1)}, u32[]{:S(2)}, u32[]{:S(2)}) collective-permute-start(f32[160,128]{1,0:T(8,128)S(1)} %get-tuple-element.42), channel_id=1, source_target_pairs={{0,28},{4,24},{8,20},{12,16},{16,12},{20,8},{24,4},{28,0},{1,29},{... | collective-permute-start | bytes 245768 | tf_op jit(solution)/shard_map/ppermute | solution.py:659
  51.2 1.9 %collective-permute-start.12 = (f32[104,128]{1,0:T(8,128)S(1)}, f32[104,128]{1,0:T(8,128)S(1)}, u32[]{:S(2)}, u32[]{:S(2)}) collective-permute-start(f32[104,128]{1,0:T(8,128)S(1)} %get-tuple-element.46), channel_id=1, source_target_pairs={{0,1},{1,0},{2,3},{3,2},{4,5},{5,4},{6,7},{7,6},{8,9},{9,8},{10,11... | collective-permute-start | bytes 159752 | tf_op jit(solution)/shard_map/ppermute | solution.py:647
  51.2 4.2 %collective-permute-start.13 = (f32[104,128]{1,0:T(8,128)S(1)}, f32[104,128]{1,0:T(8,128)S(1)}, u32[]{:S(2)}, u32[]{:S(2)}) collective-permute-start(f32[104,128]{1,0:T(8,128)S(1)} %get-tuple-element.47), channel_id=1, source_target_pairs={{0,2},{1,3},{2,0},{3,1},{4,6},{5,7},{6,4},{7,5},{8,10},{9,11},{10,... | collective-permute-start | bytes 159752 | tf_op jit(solution)/shard_map/ppermute | solution.py:647
  52.5 3.8 %collective-permute-start.14 = (f32[104,128]{1,0:T(8,128)S(1)}, f32[104,128]{1,0:T(8,128)S(1)}, u32[]{:S(2)}, u32[]{:S(2)}) collective-permute-start(f32[104,128]{1,0:T(8,128)S(1)} %get-tuple-element.48), channel_id=1, source_target_pairs={{0,3},{1,2},{2,1},{3,0},{4,7},{5,6},{6,5},{7,4},{8,11},{9,10},{10,... | collective-permute-start | bytes 159752 | tf_op jit(solution)/shard_map/ppermute | solution.py:647
  57.0 6.8 %collective-permute-start.15 = (f32[160,128]{1,0:T(8,128)S(1)}, f32[160,128]{1,0:T(8,128)S(1)}, u32[]{:S(2)}, u32[]{:S(2)}) collective-permute-start(f32[160,128]{1,0:T(8,128)S(1)} %get-tuple-element.49), channel_id=1, source_target_pairs={{0,16},{4,20},{8,24},{12,28},{16,0},{20,4},{24,8},{28,12},{1,17},{... | collective-permute-start | bytes 245768 | tf_op jit(solution)/shard_map/ppermute | solution.py:659
  58.5 5.3 %collective-permute-start.16 = (f32[160,128]{1,0:T(8,128)S(1)}, f32[160,128]{1,0:T(8,128)S(1)}, u32[]{:S(2)}, u32[]{:S(2)}) collective-permute-start(f32[160,128]{1,0:T(8,128)S(1)} %get-tuple-element.50), channel_id=1, source_target_pairs={{0,20},{4,16},{8,28},{12,24},{16,4},{20,0},{24,12},{28,8},{1,21},{... | collective-permute-start | bytes 245768 | tf_op jit(solution)/shard_map/ppermute | solution.py:659
  60.5 9.9 %collective-permute-start.17 = (f32[160,128]{1,0:T(8,128)S(1)}, f32[160,128]{1,0:T(8,128)S(1)}, u32[]{:S(2)}, u32[]{:S(2)}) collective-permute-start(f32[160,128]{1,0:T(8,128)S(1)} %get-tuple-element.51), channel_id=1, source_target_pairs={{0,24},{4,28},{8,16},{12,20},{16,8},{20,12},{24,0},{28,4},{1,25},{... | collective-permute-start | bytes 245768 | tf_op jit(solution)/shard_map/ppermute | solution.py:659
  61.8 8.6 %collective-permute-start.18 = (f32[160,128]{1,0:T(8,128)S(1)}, f32[160,128]{1,0:T(8,128)S(1)}, u32[]{:S(2)}, u32[]{:S(2)}) collective-permute-start(f32[160,128]{1,0:T(8,128)S(1)} %get-tuple-element.52), channel_id=1, source_target_pairs={{0,28},{4,24},{8,20},{12,16},{16,12},{20,8},{24,4},{28,0},{1,29},{... | collective-permute-start | bytes 245768 | tf_op jit(solution)/shard_map/ppermute | solution.py:659
  (3 other events, 42.2 us)

commit v5 on v4

--- a/solution.py
+++ b/solution.py
@@ -350,158 +350,204 @@
                 out_refs[lat_step][tiles(place, 1), :] = got_refs[lon_step][tiles(source, 1), :]
 
 
-def section(
-    loop, receive_ref, factor_ref, radial_ref, frame_ref, got_refs, plane_ref, work_ref,
-    rate_rows, rate_chunks, emit,
-):
-    tall, wide = loop.rows + 2 * HALO, loop.cols + 2 * HALO
-    pitch = wide + 2 * PAD
-    arrivals = loop.lon_count * loop.slots
-
-    def spread_row(row, carry):
-        for chunk in range(0, wide, 8):
-            for f in range(TILE):
-                start = (row * wide + chunk) * TILE + f
-                plane_ref[pl.ds((f * tall + row) * pitch + PAD + chunk, 8), :] = frame_ref[
-                    pl.ds(start, 8, stride=TILE), :
-                ]
-        return carry
-
-    first_row, last_row = rate_rows
-    lax.fori_loop(first_row - 2, last_row + 2, spread_row, 0)
-    for lat_step in range(loop.lat_count):
-        for place in range(arrivals):
-            spot = lookup(receive_ref, lat_step * arrivals + place)
-            plane_ref[pl.ds(spot, TILE, stride=tall * pitch), :] = got_refs[lat_step][
-                tiles(place, 1), :
-            ]
-
-    levels = radial_ref.shape[-1]
-    inverse_radius, ru, rl, du, dl, qu, ql = [radial_ref[n] for n in range(7)]
-
-    def up(x):
-        return pltpu.roll(x, levels - 1, 1)
-
-    def down(x):
+class Section:
+    def __init__(self, loop, factor_ref, radial_ref, plane_ref, work_ref):
+        self.loop = loop
+        self.tall, self.wide = loop.rows + 2 * HALO, loop.cols + 2 * HALO
+        self.pitch = self.wide + 2 * PAD
+        self.factor_ref, self.radial_ref = factor_ref, radial_ref
+        self.plane_ref, self.work_ref = plane_ref, work_ref
+        lat, lon = lax.axis_index("lat"), lax.axis_index("lon")
+        self.lat = lat
+        self.at_top, self.at_left = lat == 0, lon == 0
+        self.on_row_edge = self.at_top | (lat == loop.lat_count - 1)
+        self.on_col_edge = self.at_left | (lon == loop.lon_count - 1)
+
+    def spread(self, frame_ref, rows):
+        def one_row(row, carry):
+            for chunk in range(0, self.wide, 8):
+                for f in range(TILE):
+                    start = (row * self.wide + chunk) * TILE + f
+                    self.plane_ref[self.at(f, row, chunk), :] = frame_ref[
+                        pl.ds(start, 8, stride=TILE), :
+                    ]
+            return carry
+
+        lax.fori_loop(*rows, one_row, 0)
+
+    def scatter(self, receive_ref, got_refs):
+        arrivals = self.loop.lon_count * self.loop.slots
+        for lat_step in range(self.loop.lat_count):
+            for place in range(arrivals):
+                spot = lookup(receive_ref, lat_step * arrivals + place)
+                self.plane_ref[pl.ds(spot, TILE, stride=self.tall * self.pitch), :] = got_refs[
+                    lat_step
+                ][tiles(place, 1), :]
+
+    def at(self, number, row, col):
+        return pl.ds((number * self.tall + row) * self.pitch + PAD + col, 8)
+
+    def reader(self, ref, row, col):
+        def read(number, row_step=0, col_step=0):
+            return ref[self.at(number, row + row_step, col + col_step), :]
+
+        return read
+
+    def prepare(self, row):
+        factors = [self.factor_ref[(self.lat * 3 + n) * self.tall + row] for n in range(3)]
+        inverse_radius = self.radial_ref[0]
+        with_theta = inverse_radius * (self.loop.nth / math.pi)
+        return factors, inverse_radius * factors[2], with_theta
+
+    def up(self, x):
+        return pltpu.roll(x, x.shape[-1] - 1, 1)
+
+    def down(self, x):
         return pltpu.roll(x, 1, 1)
 
-    half_theta = loop.nth / math.pi
-    lat = lax.axis_index("lat")
-
-    def row_factors(row):
-        return [factor_ref[(lat * 3 + n) * tall + row] for n in range(3)]
-
-    def reader(ref, row, col):
-        def at(number, row_step=0, col_step=0):
-            return ref[
-                pl.ds((number * tall + row + row_step) * pitch + PAD + col + col_step, 8), :
-            ]
-
-        return at
-
-    def curl(at, first, factors, with_phi, with_theta):
-        tu, td, ph = factors
+    def curl(self, read, first, prepared):
+        (tu, td, ph), with_phi, with_theta = prepared
+        ru, rl = self.radial_ref[1], self.radial_ref[2]
         a, b, c = first, first + 1, first + 2
-        mid_b, mid_c = at(b), at(c)
-        radial = inverse_radius * (
-            (tu * at(c, 1) - td * at(c, -1)) - ph * (at(b, 0, 1) - at(b, 0, -1))
-        )
-        polar = with_phi * (at(a, 0, 1) - at(a, 0, -1)) - (ru * up(mid_c) - rl * down(mid_c))
-        azimuth = (ru * up(mid_b) - rl * down(mid_b)) - with_theta * (at(a, 1) - at(a, -1))
+        mid_b, mid_c = read(b), read(c)
+        radial = self.radial_ref[0] * (
+            (tu * read(c, 1) - td * read(c, -1)) - ph * (read(b, 0, 1) - read(b, 0, -1))
+        )
+        polar = with_phi * (read(a, 0, 1) - read(a, 0, -1)) - (
+            ru * self.up(mid_c) - rl * self.down(mid_c)
+        )
+        azimuth = (ru * self.up(mid_b) - rl * self.down(mid_b)) - with_theta * (
+            read(a, 1) - read(a, -1)
+        )
         return radial, polar, azimuth
 
-    def slope(at, number, with_phi, with_theta):
-        mid = at(number)
+    def slope(self, read, number, prepared):
+        _, with_phi, with_theta = prepared
+        mid = read(number)
         return (
-            du * up(mid) - dl * down(mid),
-            with_theta * (at(number, 1) - at(number, -1)),
-            with_phi * (at(number, 0, 1) - at(number, 0, -1)),
-        )
-
-    def outflow(at, first, factors):
-        tu, td, ph = factors
-        mid = at(first)
-        return (qu * up(mid) - ql * down(mid)) + inverse_radius * (
-            (tu * at(first + 1, 1) - td * at(first + 1, -1))
-            + ph * (at(first + 2, 0, 1) - at(first + 2, 0, -1))
-        )
-
-    def cross(x, y):
+            self.radial_ref[3] * self.up(mid) - self.radial_ref[4] * self.down(mid),
+            with_theta * (read(number, 1) - read(number, -1)),
+            with_phi * (read(number, 0, 1) - read(number, 0, -1)),
+        )
+
+    def outflow(self, read, first, prepared):
+        (tu, td, ph), _, _ = prepared
+        mid = read(first)
         return (
-            x[1] * y[2] - x[2] * y[1],
-            x[2] * y[0] - x[0] * y[2],
-            x[0] * y[1] - x[1] * y[0],
-        )
-
-    def dot(x, y):
-        return x[0] * y[0] + x[1] * y[1] + x[2] * y[2]
-
-    with_theta = inverse_radius * half_theta
-
-    def first_pass(row, carry):
-        factors = row_factors(row)
-        with_phi = inverse_radius * factors[2]
-        for chunk in range(0, wide, 8):
-            at = reader(plane_ref, row, chunk)
-
-            def put(number, value):
-                work_ref[pl.ds((number * tall + row) * pitch + PAD + chunk, 8), :] = value
-
-            flow = [at(n) for n in range(3)]
-            field = [at(n) for n in range(3, 6)]
-            current = curl(at, 3, factors, with_phi, with_theta)
-            spin = curl(at, 0, factors, with_phi, with_theta)
-            induced = cross(flow, field)
-            warm = slope(at, 6, with_phi, with_theta)
-            for n in range(3):
-                put(n, current[n])
-                put(3 + n, spin[n])
-                put(6 + n, induced[n] - ETA_COEF * current[n])
-                put(9 + n, warm[n])
-            put(12, at(7) + 0.5 * dot(flow, flow))
-        return carry
-
-    lax.fori_loop(first_row - 1, last_row + 1, first_pass, 0)
-
-    def second_pass(row, carry):
-        factors = row_factors(row)
-        with_phi = inverse_radius * factors[2]
-        for chunk in rate_chunks:
-            at = reader(plane_ref, row, chunk)
-            work = reader(work_ref, row, chunk)
-            flow = [at(n) for n in range(3)]
-            field = [at(n) for n in range(3, 6)]
-            current = [work(n) for n in range(3)]
-            spin = [work(3 + n) for n in range(3)]
-            warm = [work(9 + n) for n in range(3)]
-            field_rate = curl(work, 6, factors, with_phi, with_theta)
-            spin_curl = curl(work, 3, factors, with_phi, with_theta)
-            head = slope(work, 12, with_phi, with_theta)
-            lorentz = cross(current, field)
-            advect = cross(flow, spin)
-            speed = [
-                advect[n] + lorentz[n] - head[n] - NU_COEF * spin_curl[n] for n in range(3)
-            ]
-            speed[0] = speed[0] + ARCHIMEDES_LIFT * at(6)
-            heat = KAPPA_COEF * outflow(work, 9, factors) - dot(flow, warm)
-            squeeze = -SOUND_SQ * outflow(at, 0, factors)
-            emit(row, chunk, at, speed + list(field_rate) + [heat, squeeze])
-        return carry
-
-    lax.fori_loop(first_row, last_row, second_pass, 0)
-
-
-def first_section_kernel(loop, *refs):
-    rim, refs = refs[:5], refs[5:]
-    receive_ref, factor_ref, radial_ref, frame_in_ref = refs[:4]
-    got_refs, refs = refs[4 : 4 + loop.lat_count], refs[4 + loop.lat_count :]
-    frame_ref, rate_ref = refs[:2]
-    send_refs, (value_ref, plane_ref, work_ref) = refs[2:-3], refs[-3:]
-    tall, wide = loop.rows + 2 * HALO, loop.cols + 2 * HALO
+            self.radial_ref[5] * self.up(mid) - self.radial_ref[6] * self.down(mid)
+        ) + self.radial_ref[0] * (
+            (tu * read(first + 1, 1) - td * read(first + 1, -1))
+            + ph * (read(first + 2, 0, 1) - read(first + 2, 0, -1))
+        )
+
+    def first_pass(self, row, chunk):
+        prepared = self.prepare(row)
+        read = self.reader(self.plane_ref, row, chunk)
+
+        def put(number, value):
+            self.work_ref[self.at(number, row, chunk), :] = value
+
+        flow = [read(n) for n in range(3)]
+        field = [read(n) for n in range(3, 6)]
+        current = self.curl(read, 3, prepared)
+        spin = self.curl(read, 0, prepared)
+        induced = cross(flow, field)
+        warm = self.slope(read, 6, prepared)
+        for n in range(3):
+            put(n, current[n])
+            put(3 + n, spin[n])
+            put(6 + n, induced[n] - ETA_COEF * current[n])
+            put(9 + n, warm[n])
+        put(12, read(7) + 0.5 * dot(flow, flow))
+
+    def second_pass(self, row, chunk, emit):
+        prepared = self.prepare(row)
+        read = self.reader(self.plane_ref, row, chunk)
+        work = self.reader(self.work_ref, row, chunk)
+        flow = [read(n) for n in range(3)]
+        field = [read(n) for n in range(3, 6)]
+        current = [work(n) for n in range(3)]
+        spin = [work(3 + n) for n in range(3)]
+        warm = [work(9 + n) for n in range(3)]
+        field_rate = self.curl(work, 6, prepared)
+        spin_curl = self.curl(work, 3, prepared)
+        head = self.slope(work, 12, prepared)
+        lorentz = cross(current, field)
+        advect = cross(flow, spin)
+        speed = [advect[n] + lorentz[n] - head[n] - NU_COEF * spin_curl[n] for n in range(3)]
+        speed[0] = speed[0] + ARCHIMEDES_LIFT * read(6)
+        heat = KAPPA_COEF * self.outflow(work, 9, prepared) - dot(flow, warm)
+        squeeze = -SOUND_SQ * self.outflow(read, 0, prepared)
+        emit(row, chunk, read, speed + list(field_rate) + [heat, squeeze])
+
+    def over(self, rows, one_row, unroll):
+        def step(row, carry):
+            one_row(row)
+            return carry
+
+        lax.fori_loop(*rows, step, 0, unroll=unroll)
+
+    def everywhere(self, rows, chunks, emit):
+        def first(row):
+            for chunk in range(0, self.wide, 8):
+                self.first_pass(row, chunk)
+
+        def second(row):
+            for chunk in chunks:
+                self.second_pass(row, chunk, emit)
+
+        self.over((rows[0] - 1, rows[1] + 1), first, 2)
+        self.over(rows, second, 2)
+
+    def along_edges(self, rows, chunks, emit):
+        tall, wide = self.tall, self.wide
+        low_chunk, high_chunk = chunks[0], chunks[-1]
+
+        @pl.when(self.on_row_edge)
+        def _():
+            row = jnp.where(self.at_top, HALO - 1, tall - HALO - 1)
+            for step in range(2):
+                for chunk in range(0, wide, 8):
+                    self.first_pass(row + step, chunk)
+
+        @pl.when(self.on_col_edge)
+        def _():
+            chunk = pl.multiple_of(jnp.where(self.at_left, 0, wide - 8), 8)
+            self.over(
+                (rows[0] - 1, rows[1] + 1), lambda row: self.first_pass(row, chunk), 2
+            )
+
+        @pl.when(self.on_row_edge)
+        def _():
+            row = jnp.where(self.at_top, HALO, tall - HALO - 2)
+            for step in range(2):
+                for chunk in chunks:
+                    self.second_pass(row + step, chunk, emit)
+
+        @pl.when(self.on_col_edge)
+        def _():
+            chunk = jnp.where(self.at_left, low_chunk, high_chunk)
+            self.over(rows, lambda row: self.second_pass(row, chunk, emit), 2)
+
+
+def cross(x, y):
+    return (
+        x[1] * y[2] - x[2] * y[1],
+        x[2] * y[0] - x[0] * y[2],
+        x[0] * y[1] - x[1] * y[0],
+    )
+
+
+def dot(x, y):
+    return x[0] * y[0] + x[1] * y[1] + x[2] * y[2]
+
+
+def middle_state(loop, frame_ref, rate_ref):
+    wide = loop.cols + 2 * HALO
     first_row = lax.axis_index("lat") * loop.rows - HALO
     first_col = lax.axis_index("lon") * loop.cols - HALO
 
-    def emit(row, chunk, at, rate):
+    def emit(row, chunk, read, rate):
         in_row = (row + first_row >= 0) & (row + first_row < loop.nth)
         col = lax.broadcasted_iota(jnp.int32, (8, 128), 0) + (chunk + first_col)
         inside = (col >= jnp.where(in_row, 0, loop.nph)) & (col < loop.nph)
@@ -509,30 +555,73 @@
             rate_ref[f, row, pl.ds(chunk, 8), :] = rate[f]
             start = (row * wide + chunk) * TILE + f
             frame_ref[pl.ds(start, 8, stride=TILE), :] = jnp.where(
-                inside, at(f) + TIME_STEP * rate[f], 0.0
+                inside, read(f) + TIME_STEP * rate[f], 0.0
             )
 
-    section(
-        loop, receive_ref, factor_ref, radial_ref, frame_in_ref, got_refs, plane_ref, work_ref,
-        (2, tall - 2), range(0, wide, 8), emit,
-    )
-    mix_and_pack(loop, wide, rim, frame_ref, value_ref, send_refs)
-
-
-def second_section_kernel(loop, receive_ref, factor_ref, radial_ref, frame_ref, rate_ref, *refs):
-    got_refs, (change_ref, plane_ref, work_ref) = refs[: loop.lat_count], refs[loop.lat_count :]
-    rows, cols = loop.rows, loop.cols
-
-    def emit(row, chunk, at, rate):
+    return emit
+
+
+def total_change(loop, change_ref, rate_ref):
+    def emit(row, chunk, read, rate):
         for f in range(TILE):
-            start = ((row - HALO) * cols + chunk - HALO) * TILE + f
+            start = ((row - HALO) * loop.cols + chunk - HALO) * TILE + f
             change_ref[pl.ds(start, 8, stride=TILE), :] = (0.5 * TIME_STEP) * (
                 rate_ref[f, row, pl.ds(chunk, 8), :] + rate[f]
             )
 
-    section(
-        loop, receive_ref, factor_ref, radial_ref, frame_ref, got_refs, plane_ref, work_ref,
-        (HALO, HALO + rows), range(HALO, HALO + cols, 8), emit,
+    return emit
+
+
+def first_inner_kernel(
+    loop, factor_ref, radial_ref, frame_in_ref, after_ref, frame_ref, rate_ref, plane_ref, work_ref
+):
+    del after_ref
+    part = Section(loop, factor_ref, radial_ref, plane_ref, work_ref)
+    part.spread(frame_in_ref, (0, part.tall))
+    part.everywhere(
+        (2, part.tall - 2), range(0, part.wide, 8), middle_state(loop, frame_ref, rate_ref)
+    )
+
+
+def first_edge_kernel(loop, *refs):
+    rim, refs = refs[:5], refs[5:]
+    receive_ref, factor_ref, radial_ref = refs[:3]
+    got_refs, refs = refs[7 : 7 + loop.lat_count], refs[7 + loop.lat_count :]
+    frame_ref, rate_ref, plane_ref, work_ref = refs[:4]
+    send_refs, value_ref = refs[4:-1], refs[-1]
+    part = Section(loop, factor_ref, radial_ref, plane_ref, work_ref)
+    part.scatter(receive_ref, got_refs)
+    part.along_edges(
+        (2, part.tall - 2), range(0, part.wide, 8), middle_state(loop, frame_ref, rate_ref)
+    )
+    mix_and_pack(loop, part.wide, rim, frame_ref, value_ref, send_refs)
+
+
+def second_inner_kernel(
+    loop, factor_ref, radial_ref, frame_ref, rate_ref, after_ref, change_ref, plane_ref, work_ref
+):
+    del after_ref
+    part = Section(loop, factor_ref, radial_ref, plane_ref, work_ref)
+    part.spread(frame_ref, (2, part.tall - 2))
+    part.everywhere(
+        (HALO, HALO + loop.rows),
+        range(HALO, HALO + loop.cols, 8),
+        total_change(loop, change_ref, rate_ref),
+    )
+
+
+def second_edge_kernel(loop, receive_ref, factor_ref, radial_ref, rate_ref, inner_ref, *refs):
+    got_refs, refs = refs[2 : 2 + loop.lat_count], refs[2 + loop.lat_count :]
+    plane_ref, work_ref, change_ref = refs
+    part = Section(loop, factor_ref, radial_ref, plane_ref, work_ref)
+    for row in range(loop.rows):
+        here = tiles(row * loop.cols, loop.cols)
+        change_ref[here, :] = inner_ref[here, :]
+    part.scatter(receive_ref, got_refs)
+    part.along_edges(
+        (HALO, HALO + loop.rows),
+        range(HALO, HALO + loop.cols, 8),
+        total_change(loop, change_ref, rate_ref),
     )
 
 
@@ -642,12 +731,12 @@
         name="frame",
     )(*rim, block, lat_even, lat_odd, lon_even, lon_odd)
 
-    def exchange(packed):
+    def first_round(packed):
         got = [packed[0]] + [
             lax.ppermute(packed[step], "lon", lon_route(step, lon_count))
             for step in range(1, lon_count)
         ]
-        turned = pl.pallas_call(
+        return pl.pallas_call(
             lambda *refs: swap_kernel(loop, *refs),
             out_shape=[tile_array(lon_count * loop.slots)] * lat_count,
             in_specs=scalars(1) + whole(lon_count),
@@ -655,37 +744,59 @@
             compiler_params=grant(4),
             name="swap",
         )(swap_table, *got)
+
+    def second_round(turned):
         return [
             lax.ppermute(turned[step], ("panel", "lat"), lat_route(step, lat_count))
             for step in range(lat_count)
         ]
 
-    got = exchange(packed)
     planes = [
-        pltpu.VMEM((fields * tall * pitch, levels), f32),
-        pltpu.VMEM((13 * tall * pitch, levels), f32),
+        jax.ShapeDtypeStruct((fields * tall * pitch, levels), f32),
+        jax.ShapeDtypeStruct((13 * tall * pitch, levels), f32),
     ]
-    frame, rate, *packed = pl.pallas_call(
-        lambda *refs: first_section_kernel(loop, *refs),
-        out_shape=[tile_array(tall * wide), jax.ShapeDtypeStruct((fields, tall, wide, levels), f32)]
-        + packed_shapes,
-        in_specs=scalars(7) + whole(2 + lat_count),
-        out_specs=whole(2 + lon_count),
-        scratch_shapes=[pltpu.VMEM((entries * TILE, levels), f32)] + planes,
-        compiler_params=grant(24),
-        name="first_section",
-    )(*rim, receive_table, factors, radial, frame, *got)
-
-    got = exchange(packed)
-    change = pl.pallas_call(
-        lambda *refs: second_section_kernel(loop, *refs),
-        out_shape=tile_array(rows * cols),
-        in_specs=scalars(2) + whole(3 + lat_count),
-        out_specs=whole(1)[0],
-        scratch_shapes=planes,
-        compiler_params=grant(24),
-        name="second_section",
-    )(receive_table, factors, radial, frame, rate, *got)
+    rates = jax.ShapeDtypeStruct((fields, tall, wide, levels), f32)
+
+    turned = first_round(packed)
+    got = second_round(turned)
+    frame, rate, plane, work = pl.pallas_call(
+        lambda *refs: first_inner_kernel(loop, *refs),
+        out_shape=[tile_array(tall * wide), rates] + planes,
+        in_specs=scalars(1) + whole(3),
+        out_specs=whole(4),
+        compiler_params=grant(4),
+        name="first_inner",
+    )(factors, radial, frame, turned[-1])
+    frame, rate, _, _, *packed = pl.pallas_call(
+        lambda *refs: first_edge_kernel(loop, *refs),
+        out_shape=[tile_array(tall * wide), rates] + planes + packed_shapes,
+        in_specs=scalars(7) + whole(5 + lat_count),
+        out_specs=whole(4 + lon_count),
+        scratch_shapes=[pltpu.VMEM((entries * TILE, levels), f32)],
+        input_output_aliases={8: 0, 9: 1, 10: 2, 11: 3},
+        compiler_params=grant(4),
+        name="first_edge",
+    )(*rim, receive_table, factors, radial, frame, rate, plane, work, *got)
+
+    turned = first_round(packed)
+    got = second_round(turned)
+    inner, plane, work = pl.pallas_call(
+        lambda *refs: second_inner_kernel(loop, *refs),
+        out_shape=[tile_array(rows * cols)] + planes,
+        in_specs=scalars(1) + whole(4),
+        out_specs=whole(3),
+        compiler_params=grant(4),
+        name="second_inner",
+    )(factors, radial, frame, rate, turned[-1])
+    _, _, change = pl.pallas_call(
+        lambda *refs: second_edge_kernel(loop, *refs),
+        out_shape=planes + [tile_array(rows * cols)],
+        in_specs=scalars(2) + whole(5 + lat_count),
+        out_specs=whole(3),
+        input_output_aliases={5: 0, 6: 1},
+        compiler_params=grant(4),
+        name="second_edge",
+    )(receive_table, factors, radial, rate, inner, plane, work, *got)
     return change.reshape(1, rows, cols, fields, levels)
 
 

time: 76.3 us -> 71.6 us (0.938)
  waiting for transfers between devices: 25.9 us -> 16.3 us
  local copies, waits for them, and re-layouts: 1.03 us -> 4.44 us
  Pallas kernels: 16.7 us -> 19.6 us
  starting transfers between devices: 30.1 us -> 28.4 us
    ppermute x14, waiting for transfers between devices: 19.7 us -> 11.7 us  [the longest x6 6.52 us: first_round(): lax.ppermute(packed[step], 'lon', lon_route(step, lon_count))]
    pallas_call x4 -> x6, Pallas kernels: 14.2 us -> 17.1 us  [the longest x1 4.38 us: per_device(): pl.pallas_call(lambda *refs: first_edge_kernel(loop, *refs), out_shape=[t...]
    unnamed x17 -> x11, local copies, waits for them, and re-layouts: 0.11 us -> 2.19 us
    ppermute x1, waiting for transfers between devices: 1.7 us -> 0.01 us  [per_device(): other_cell = lax.ppermute(first_cell, 'panel', [(0, 1), (1, 0)])]
    ppermute x14, starting transfers between devices: 23.8 us -> 22.2 us  [the longest x8 16.2 us: second_round(): lax.ppermute(turned[step], ('panel', 'lat'), lat_route(step, lat_count))]
  transfers between devices with their start and end apart: 19 -> 19, of which waited for: 9 -> 7; matrix products, arithmetic and copies ran while one was open for 3% -> 6% of each run, Pallas kernels for 1% -> 11%
where the time goes in v5:
time: 71.6 us; the launch traced here: 71.2 us
  starting transfers between devices  28.4 us (40%)
  Pallas kernels  19.6 us (27%)
  waiting for transfers between devices  16.3 us (23%)
  local copies, waits for them, and re-layouts  4.44 us (6%)
  other arithmetic  2.23 us (3%)
    ppermute x8, starting transfers between devices, second_round(): lax.ppermute(turned[step], ('panel', 'lat'), lat_route(step, lat_count))  16.2 us
    ppermute x6, waiting for transfers between devices, first_round(): lax.ppermute(packed[step], 'lon', lon_route(step, lon_count))  6.52 us
    ppermute x6, starting transfers between devices, first_round(): lax.ppermute(packed[step], 'lon', lon_route(step, lon_count))  5.98 us
    ppermute x8, waiting for transfers between devices, second_round(): lax.ppermute(turned[step], ('panel', 'lat'), lat_route(step, lat_count))  5.2 us
    ppermute x1, waiting for transfers between devices, per_device(): lat_even = lax.ppermute(send_even, 'lat', even_pairs(lat_count))  4.54 us
    pallas_call x1, Pallas kernels, per_device(): pl.pallas_call(lambda *refs: first_edge_kernel(loop, *refs), out_shape=[t...  4.38 us
    pallas_call x1, Pallas kernels, per_device(): pl.pallas_call(lambda *refs: first_inner_kernel(loop, *refs), out_shape=[...  4.25 us
    pallas_call x1, Pallas kernels, per_device(): pl.pallas_call(lambda *refs: second_edge_kernel(loop, *refs), out_shape=p...  3.85 us
  transfers between devices with their start and end apart: 19, of which 7 were waited for; matrix products, arithmetic and copies ran while one was open for 6% of the time, Pallas kernels for 11%

profile of v5, /device:TPU:0, one launch (start us, length us, event | category | flops | bytes accessed | tf_op | source)
XLA Modules:
  0.0 71.2 jit_solution(2774745453017528252)
XLA Ops:
  0.0 1.2 %slice_select_fusion.2 = (f32[1,4,16,8,128]{4,3,2,1,0:T(8,128)S(1)}, f32[1,4,16,8,128]{4,3,2,1,0:T(8,128)S(1)}) fusion(f32[1,16,16,8,128]{4,3,2,1,0:T(8,128)} %param.9, pred[]{:T(512)S(6)} %eq.9), kind=kLoop, calls=%fused_computation.2 | loop fusion | flops 131072 | bytes 1048577 | tf_op jit(solution)/shard_map/jit(_where)/select_n | solution.py:687
  1.2 3.1 %collective-permute-start.1 = (f32[512,128]{1,0:T(8,128)S(1)}, f32[512,128]{1,0:T(8,128)S(1)}, u32[]{:S(2)}, u32[]{:S(2)}) collective-permute-start(f32[512,128]{1,0:T(8,128)S(1)} %bitcast.20), channel_id=1, source_target_pairs={{0,4},{4,0},{8,12},{12,8},{1,5},{5,1},{9,13},{13,9},{2,6},{6,2},{1... | collective-permute-start | bytes 786440 | tf_op jit(solution)/shard_map/ppermute | solution.py:688
  5.0 1.1 %slice_select_fusion = (f32[16,4,8,128]{3,2,1,0:T(8,128)S(1)}, f32[16,4,8,128]{3,2,1,0:T(8,128)S(1)}) fusion(f32[16,16,8,128]{3,2,1,0:T(8,128)} %bitcast.13, pred[]{:T(512)S(6)} %eq.10), kind=kLoop, calls=%fused_computation | loop fusion | flops 131072 | bytes 1048577 | tf_op jit(solution)/shard_map/jit(_where)/select_n | solution.py:711
  6.1 4.5 %collective-permute-done.1.refs_2_.refs_6_ = f32[512,128]{1,0:T(8,128)S(1)} collective-permute-done((f32[512,128]{1,0:T(8,128)S(1)}, f32[512,128]{1,0:T(8,128)S(1)}, u32[]{:S(2)}, u32[]{:S(2)}) %collective-permute-start.1) | collective-permute-done | bytes 262176 | tf_op jit(solution)/shard_map/ppermute | solution.py:688
  12.2 1.7 %collective-permute-start = (s32[2]{0:T(128)S(1)}, s32[2]{0:T(128)S(1)}, u32[]{:S(2)}, u32[]{:S(2)}) collective-permute-start(s32[2]{0:T(128)S(1)} %slice_reduce_fusion.refs_0_), channel_id=1, source_target_pairs={{0,16},{16,0},{1,17},{17,1},{2,18},{18,2},{3,19},{19,3},{4,20},{20... | collective-permute-start | bytes 32 | tf_op jit(solution)/shard_map/ppermute | solution.py:681
  18.2 1.9 %frame.1 = (f32[4608,128]{1,0:T(8,128)S(1)}, f32[104,128]{1,0:T(8,128)S(1)}, f32[104,128]{1,0:T(8,128)S(1)}, f32[104,128]{1,0:T(8,128)S(1)}, f32[104,128]{1,0:T(8,128)S(1)}) custom-call(s32[8,128]{1,0:T(8,128)S(1)} %get-tuple-element.38.refs_0_, s32[32,2]{1,0:T(8,128)S(1)} %copy.18.refs_1_, f32[32,16]{1,0:T(8,128)S(1)} %bitcast.17, ...), custom_call_target="tpu_custom_call" | custom-call | tf_op jit(solution)/shard_map/frame/pallas_call | solution.py:724
  20.1 2.6 %collective-permute-start.5 = (f32[104,128]{1,0:T(8,128)S(1)}, f32[104,128]{1,0:T(8,128)S(1)}, u32[]{:S(2)}, u32[]{:S(2)}) collective-permute-start(f32[104,128]{1,0:T(8,128)S(1)} %get-tuple-element.44), channel_id=1, source_target_pairs={{0,1},{1,0},{2,3},{3,2},{4,5},{5,4},{6,7},{7,6},{8,9},{9,8},{10,11... | collective-permute-start | bytes 159752 | tf_op jit(solution)/shard_map/ppermute | solution.py:736
  24.2 3.0 %collective-permute-done.6.refs_3_ = f32[104,128]{1,0:T(8,128)S(1)} collective-permute-done((f32[104,128]{1,0:T(8,128)S(1)}, f32[104,128]{1,0:T(8,128)S(1)}, u32[]{:S(2)}, u32[]{:S(2)}) %collective-permute-start.6) | collective-permute-done | bytes 53280 | tf_op jit(solution)/shard_map/ppermute | solution.py:736
  28.4 1.2 %collective-permute-start.8 = (f32[160,128]{1,0:T(8,128)S(1)}, f32[160,128]{1,0:T(8,128)S(1)}, u32[]{:S(2)}, u32[]{:S(2)}) collective-permute-start(f32[160,128]{1,0:T(8,128)S(1)} %get-tuple-element.52), channel_id=1, source_target_pairs={{0,16},{4,20},{8,24},{12,28},{16,0},{20,4},{24,8},{28,12},{1,17},{... | collective-permute-start | bytes 245768 | tf_op jit(solution)/shard_map/ppermute | solution.py:750
  29.6 4.9 %collective-permute-start.9 = (f32[160,128]{1,0:T(8,128)S(1)}, f32[160,128]{1,0:T(8,128)S(1)}, u32[]{:S(2)}, u32[]{:S(2)}) collective-permute-start(f32[160,128]{1,0:T(8,128)S(1)} %get-tuple-element.53), channel_id=1, source_target_pairs={{0,20},{4,16},{8,28},{12,24},{16,4},{20,0},{24,12},{28,8},{1,21},{... | collective-permute-start | bytes 245768 | tf_op jit(solution)/shard_map/ppermute | solution.py:750
  34.5 1.2 %collective-permute-start.10 = (f32[160,128]{1,0:T(8,128)S(1)}, f32[160,128]{1,0:T(8,128)S(1)}, u32[]{:S(2)}, u32[]{:S(2)}) collective-permute-start(f32[160,128]{1,0:T(8,128)S(1)} %get-tuple-element.54), channel_id=1, source_target_pairs={{0,24},{4,28},{8,16},{12,20},{16,8},{20,12},{24,0},{28,4},{1,25},{... | collective-permute-start | bytes 245768 | tf_op jit(solution)/shard_map/ppermute | solution.py:750
  35.7 2.1 %collective-permute-start.11 = (f32[160,128]{1,0:T(8,128)S(1)}, f32[160,128]{1,0:T(8,128)S(1)}, u32[]{:S(2)}, u32[]{:S(2)}) collective-permute-start(f32[160,128]{1,0:T(8,128)S(1)} %get-tuple-element.47.refs_3_), channel_id=1, source_target_pairs={{0,28},{4,24},{8,20},{12,16},{16,12},{20,8},{24,4},{28,0},{1,29},{... | collective-permute-start | bytes 245768 | tf_op jit(solution)/shard_map/ppermute | solution.py:750
  37.8 4.3 %first_inner.1 = (f32[4608,128]{1,0:T(8,128)S(1)}, f32[8,24,24,128]{3,2,1,0:T(8,128)S(1)}, f32[7680,128]{1,0:T(8,128)S(1)}, f32[12480,128]{1,0:T(8,128)S(1)}) custom-call(f32[288]{0:T(512)S(1)} %copy-done.3, f32[7,8,128]{2,1,0:T(8,128)S(1)} %copy-done.1, f32[4608,128]{1,0:T(8,128)S(1)} %get-tuple-element.41.refs_2_, f32[160,128]{1,0:T(8,128)S(1)} %get-tuple-element.47.refs_3_), custom_call_target="tpu_custom_call" | custom-call | tf_op jit(solution)/shard_map/first_inner/pallas_call | solution.py:762
  42.1 2.2 %collective-permute-done.10.refs_14_ = f32[160,128]{1,0:T(8,128)S(1)} collective-permute-done((f32[160,128]{1,0:T(8,128)S(1)}, f32[160,128]{1,0:T(8,128)S(1)}, u32[]{:S(2)}, u32[]{:S(2)}) %collective-permute-start.10) | collective-permute-done | bytes 81952 | tf_op jit(solution)/shard_map/ppermute | solution.py:750
  44.3 4.4 %first_edge.1 = (f32[4608,128]{1,0:T(8,128)S(1)}, f32[8,24,24,128]{3,2,1,0:T(8,128)S(1)}, f32[7680,128]{1,0:T(8,128)S(1)}, f32[12480,128]{1,0:T(8,128)S(1)}, f32...) custom-call(s32[8,128]{1,0:T(8,128)S(1)} %get-tuple-element.38.refs_, ...), custom_call_target="tpu_custom_call", output_to_operand_aliasing={{0}: (8, {}), {1}: (9, {}), {2}: (10, {}), {3}: (11, {})} | custom-call | tf_op jit(solution)/shard_map/first_edge/pallas_call | solution.py:770
  48.8 1.8 %collective-permute-start.14 = (f32[104,128]{1,0:T(8,128)S(1)}, f32[104,128]{1,0:T(8,128)S(1)}, u32[]{:S(2)}, u32[]{:S(2)}) collective-permute-start(f32[104,128]{1,0:T(8,128)S(1)} %get-tuple-element.60), channel_id=1, source_target_pairs={{0,3},{1,2},{2,1},{3,0},{4,7},{5,6},{6,5},{7,4},{8,11},{9,10},{10,... | collective-permute-start | bytes 159752 | tf_op jit(solution)/shard_map/ppermute | solution.py:736
  50.6 2.9 %collective-permute-done.13.refs_3_ = f32[104,128]{1,0:T(8,128)S(1)} collective-permute-done((f32[104,128]{1,0:T(8,128)S(1)}, f32[104,128]{1,0:T(8,128)S(1)}, u32[]{:S(2)}, u32[]{:S(2)}) %collective-permute-start.13) | collective-permute-done | bytes 53280 | tf_op jit(solution)/shard_map/ppermute | solution.py:736
  54.3 1.4 %collective-permute-start.15 = (f32[160,128]{1,0:T(8,128)S(1)}, f32[160,128]{1,0:T(8,128)S(1)}, u32[]{:S(2)}, u32[]{:S(2)}) collective-permute-start(f32[160,128]{1,0:T(8,128)S(1)} %get-tuple-element.65), channel_id=1, source_target_pairs={{0,16},{4,20},{8,24},{12,28},{16,0},{20,4},{24,8},{28,12},{1,17},{... | collective-permute-start | bytes 245768 | tf_op jit(solution)/shard_map/ppermute | solution.py:750
  55.7 1.7 %collective-permute-start.16 = (f32[160,128]{1,0:T(8,128)S(1)}, f32[160,128]{1,0:T(8,128)S(1)}, u32[]{:S(2)}, u32[]{:S(2)}) collective-permute-start(f32[160,128]{1,0:T(8,128)S(1)} %get-tuple-element.66), channel_id=1, source_target_pairs={{0,20},{4,16},{8,28},{12,24},{16,4},{20,0},{24,12},{28,8},{1,21},{... | collective-permute-start | bytes 245768 | tf_op jit(solution)/shard_map/ppermute | solution.py:750
  57.3 1.8 %collective-permute-start.17 = (f32[160,128]{1,0:T(8,128)S(1)}, f32[160,128]{1,0:T(8,128)S(1)}, u32[]{:S(2)}, u32[]{:S(2)}) collective-permute-start(f32[160,128]{1,0:T(8,128)S(1)} %get-tuple-element.67), channel_id=1, source_target_pairs={{0,24},{4,28},{8,16},{12,20},{16,8},{20,12},{24,0},{28,4},{1,25},{... | collective-permute-start | bytes 245768 | tf_op jit(solution)/shard_map/ppermute | solution.py:750
  59.1 2.0 %collective-permute-start.18 = (f32[160,128]{1,0:T(8,128)S(1)}, f32[160,128]{1,0:T(8,128)S(1)}, u32[]{:S(2)}, u32[]{:S(2)}) collective-permute-start(f32[160,128]{1,0:T(8,128)S(1)} %get-tuple-element.61.refs_4_), channel_id=1, source_target_pairs={{0,28},{4,24},{8,20},{12,16},{16,12},{20,8},{24,4},{28,0},{1,29},{... | collective-permute-start | bytes 245768 | tf_op jit(solution)/shard_map/ppermute | solution.py:750
  61.1 3.3 %second_inner.1 = (f32[2048,128]{1,0:T(8,128)S(1)}, f32[7680,128]{1,0:T(8,128)S(1)}, f32[12480,128]{1,0:T(8,128)S(1)}) custom-call(f32[288]{0:T(512)S(1)} %copy-done.3, f32[7,8,128]{2,1,0:T(8,128)S(1)} %copy-done.1, f32[4608,128]{1,0:T(8,128)S(1)} %get-tuple-element.56.refs_2_, f32[8,24,24,128]{3,2,1,0:T(8,128)S(1)} %get-tuple-element.55.refs_3_, ...), custom_call_target="tpu_custom_call" | custom-call | tf_op jit(solution)/shard_map/second_inner/pallas_call | solution.py:783
  64.4 2.9 %collective-permute-done.17.refs_9_ = f32[160,128]{1,0:T(8,128)S(1)} collective-permute-done((f32[160,128]{1,0:T(8,128)S(1)}, f32[160,128]{1,0:T(8,128)S(1)}, u32[]{:S(2)}, u32[]{:S(2)}) %collective-permute-start.17) | collective-permute-done | bytes 81952 | tf_op jit(solution)/shard_map/ppermute | solution.py:750
  67.4 3.8 %second_edge.1 = (f32[7680,128]{1,0:T(8,128)S(1)}, f32[12480,128]{1,0:T(8,128)S(1)}, f32[2048,128]{1,0:T(8,128)}) custom-call(s32[8,128]{1,0:T(8,128)S(1)} %get-tuple-element.37.refs_5_.refs_0_, f32[288]{0:T(512)S(1)} %copy-done.3, f32[7,8,128]{2,1,0:T(8,128)S(1)} %copy-done.1, ...), custom_call_target="tpu_custom_call", output_to_operand_aliasing={{0}: (5, {}), {1}: (6, {})} | custom-call | tf_op jit(solution)/shard_map/second_edge/pallas_call | solution.py:791
  (39 shorter events, 10.0 us)
Async XLA Ops:
  0.0 37.8 %copy-start.1 = (f32[7,8,128]{2,1,0:T(8,128)S(1)}, f32[7,8,128]{2,1,0:T(8,128)}, u32[]{:S(2)}) copy-start(f32[7,8,128]{2,1,0:T(8,128)} %constant.36.clone.refs_1_.refs_7_.refs_2_) | copy-start | bytes 86020
  0.0 37.8 %copy-start.3 = (f32[288]{0:T(512)S(1)}, f32[288]{0:T(512)}, u32[]{:S(2)}) copy-start(f32[288]{0:T(512)} %constant.35.clone.refs_0_.refs_6_.refs_1_) | copy-start | bytes 3460
  0.0 18.2 %copy-start = (f32[1,16,16,8,128]{4,3,2,1,0:T(8,128)S(1)}, f32[1,16,16,8,128]{4,3,2,1,0:T(8,128)}, u32[]{:S(2)}) copy-start(f32[1,16,16,8,128]{4,3,2,1,0:T(8,128)} %param.9) | copy-start | bytes 3145732
  1.2 9.4 %collective-permute-start.1 = (f32[512,128]{1,0:T(8,128)S(1)}, f32[512,128]{1,0:T(8,128)S(1)}, u32[]{:S(2)}, u32[]{:S(2)}) collective-permute-start(f32[512,128]{1,0:T(8,128)S(1)} %bitcast.20), channel_id=1, source_target_pairs={{0,4},{4,0},{8,12},{12,8},{1,5},{5,1},{9,13},{13,9},{2,6},{6,2},{1... | collective-permute-start | bytes 786440 | tf_op jit(solution)/shard_map/ppermute | solution.py:688
  4.3 6.3 %collective-permute-start.2 = (f32[512,128]{1,0:T(8,128)S(1)}, f32[512,128]{1,0:T(8,128)S(1)}, u32[]{:S(2)}, u32[]{:S(2)}) collective-permute-start(f32[512,128]{1,0:T(8,128)S(1)} %bitcast.19), channel_id=1, source_target_pairs={{4,8},{8,4},{5,9},{9,5},{6,10},{10,6},{7,11},{11,7},{20,24},{24,20... | collective-permute-start | bytes 786440 | tf_op jit(solution)/shard_map/ppermute | solution.py:689
  10.7 7.5 %collective-permute-start.3 = (f32[768,128]{1,0:T(8,128)S(1)}, f32[768,128]{1,0:T(8,128)S(1)}, u32[]{:S(2)}, u32[]{:S(2)}) collective-permute-start(f32[768,128]{1,0:T(8,128)S(1)} %get-tuple-element.39), channel_id=1, source_target_pairs={{0,1},{1,0},{2,3},{3,2},{4,5},{5,4},{6,7},{7,6},{8,9},{9,8},{10,11... | collective-permute-start | bytes 1179656 | tf_op jit(solution)/shard_map/ppermute | solution.py:720
  10.8 7.5 %collective-permute-start.4 = (f32[768,128]{1,0:T(8,128)S(1)}, f32[768,128]{1,0:T(8,128)S(1)}, u32[]{:S(2)}, u32[]{:S(2)}) collective-permute-start(f32[768,128]{1,0:T(8,128)S(1)} %get-tuple-element.40), channel_id=1, source_target_pairs={{1,2},{2,1},{5,6},{6,5},{9,10},{10,9},{13,14},{14,13},{17,18},{18,... | collective-permute-start | bytes 1179656 | tf_op jit(solution)/shard_map/ppermute | solution.py:721
  12.2 3.9 %collective-permute-start = (s32[2]{0:T(128)S(1)}, s32[2]{0:T(128)S(1)}, u32[]{:S(2)}, u32[]{:S(2)}) collective-permute-start(s32[2]{0:T(128)S(1)} %slice_reduce_fusion.refs_0_), channel_id=1, source_target_pairs={{0,16},{16,0},{1,17},{17,1},{2,18},{18,2},{3,19},{19,3},{4,20},{20... | collective-permute-start | bytes 32 | tf_op jit(solution)/shard_map/ppermute | solution.py:681
  16.2 0.7 copy-start.2
  16.9 0.7 copy-start.4
  20.1 4.1 %collective-permute-start.5 = (f32[104,128]{1,0:T(8,128)S(1)}, f32[104,128]{1,0:T(8,128)S(1)}, u32[]{:S(2)}, u32[]{:S(2)}) collective-permute-start(f32[104,128]{1,0:T(8,128)S(1)} %get-tuple-element.44), channel_id=1, source_target_pairs={{0,1},{1,0},{2,3},{3,2},{4,5},{5,4},{6,7},{7,6},{8,9},{9,8},{10,11... | collective-permute-start | bytes 159752 | tf_op jit(solution)/shard_map/ppermute | solution.py:736
  22.8 4.4 %collective-permute-start.6 = (f32[104,128]{1,0:T(8,128)S(1)}, f32[104,128]{1,0:T(8,128)S(1)}, u32[]{:S(2)}, u32[]{:S(2)}) collective-permute-start(f32[104,128]{1,0:T(8,128)S(1)} %get-tuple-element.45), channel_id=1, source_target_pairs={{0,2},{1,3},{2,0},{3,1},{4,6},{5,7},{6,4},{7,5},{8,10},{9,11},{10,... | collective-permute-start | bytes 159752 | tf_op jit(solution)/shard_map/ppermute | solution.py:736
  23.6 4.1 %collective-permute-start.7 = (f32[104,128]{1,0:T(8,128)S(1)}, f32[104,128]{1,0:T(8,128)S(1)}, u32[]{:S(2)}, u32[]{:S(2)}) collective-permute-start(f32[104,128]{1,0:T(8,128)S(1)} %get-tuple-element.46), channel_id=1, source_target_pairs={{0,3},{1,2},{2,1},{3,0},{4,7},{5,6},{6,5},{7,4},{8,11},{9,10},{10,... | collective-permute-start | bytes 159752 | tf_op jit(solution)/shard_map/ppermute | solution.py:736
  28.4 13.6 %collective-permute-start.8 = (f32[160,128]{1,0:T(8,128)S(1)}, f32[160,128]{1,0:T(8,128)S(1)}, u32[]{:S(2)}, u32[]{:S(2)}) collective-permute-start(f32[160,128]{1,0:T(8,128)S(1)} %get-tuple-element.52), channel_id=1, source_target_pairs={{0,16},{4,20},{8,24},{12,28},{16,0},{20,4},{24,8},{28,12},{1,17},{... | collective-permute-start | bytes 245768 | tf_op jit(solution)/shard_map/ppermute | solution.py:750
  29.6 12.4 %collective-permute-start.9 = (f32[160,128]{1,0:T(8,128)S(1)}, f32[160,128]{1,0:T(8,128)S(1)}, u32[]{:S(2)}, u32[]{:S(2)}) collective-permute-start(f32[160,128]{1,0:T(8,128)S(1)} %get-tuple-element.53), channel_id=1, source_target_pairs={{0,20},{4,16},{8,28},{12,24},{16,4},{20,0},{24,12},{28,8},{1,21},{... | collective-permute-start | bytes 245768 | tf_op jit(solution)/shard_map/ppermute | solution.py:750
  34.5 9.8 %collective-permute-start.10 = (f32[160,128]{1,0:T(8,128)S(1)}, f32[160,128]{1,0:T(8,128)S(1)}, u32[]{:S(2)}, u32[]{:S(2)}) collective-permute-start(f32[160,128]{1,0:T(8,128)S(1)} %get-tuple-element.54), channel_id=1, source_target_pairs={{0,24},{4,28},{8,16},{12,20},{16,8},{20,12},{24,0},{28,4},{1,25},{... | collective-permute-start | bytes 245768 | tf_op jit(solution)/shard_map/ppermute | solution.py:750
  35.7 8.6 %collective-permute-start.11 = (f32[160,128]{1,0:T(8,128)S(1)}, f32[160,128]{1,0:T(8,128)S(1)}, u32[]{:S(2)}, u32[]{:S(2)}) collective-permute-start(f32[160,128]{1,0:T(8,128)S(1)} %get-tuple-element.47.refs_3_), channel_id=1, source_target_pairs={{0,28},{4,24},{8,20},{12,16},{16,12},{20,8},{24,4},{28,0},{1,29},{... | collective-permute-start | bytes 245768 | tf_op jit(solution)/shard_map/ppermute | solution.py:750
  48.7 1.9 %collective-permute-start.12 = (f32[104,128]{1,0:T(8,128)S(1)}, f32[104,128]{1,0:T(8,128)S(1)}, u32[]{:S(2)}, u32[]{:S(2)}) collective-permute-start(f32[104,128]{1,0:T(8,128)S(1)} %get-tuple-element.58), channel_id=1, source_target_pairs={{0,1},{1,0},{2,3},{3,2},{4,5},{5,4},{6,7},{7,6},{8,9},{9,8},{10,11... | collective-permute-start | bytes 159752 | tf_op jit(solution)/shard_map/ppermute | solution.py:736
  48.8 4.8 %collective-permute-start.13 = (f32[104,128]{1,0:T(8,128)S(1)}, f32[104,128]{1,0:T(8,128)S(1)}, u32[]{:S(2)}, u32[]{:S(2)}) collective-permute-start(f32[104,128]{1,0:T(8,128)S(1)} %get-tuple-element.59), channel_id=1, source_target_pairs={{0,2},{1,3},{2,0},{3,1},{4,6},{5,7},{6,4},{7,5},{8,10},{9,11},{10,... | collective-permute-start | bytes 159752 | tf_op jit(solution)/shard_map/ppermute | solution.py:736
  48.8 4.8 %collective-permute-start.14 = (f32[104,128]{1,0:T(8,128)S(1)}, f32[104,128]{1,0:T(8,128)S(1)}, u32[]{:S(2)}, u32[]{:S(2)}) collective-permute-start(f32[104,128]{1,0:T(8,128)S(1)} %get-tuple-element.60), channel_id=1, source_target_pairs={{0,3},{1,2},{2,1},{3,0},{4,7},{5,6},{6,5},{7,4},{8,11},{9,10},{10,... | collective-permute-start | bytes 159752 | tf_op jit(solution)/shard_map/ppermute | solution.py:736
  54.3 10.1 %collective-permute-start.15 = (f32[160,128]{1,0:T(8,128)S(1)}, f32[160,128]{1,0:T(8,128)S(1)}, u32[]{:S(2)}, u32[]{:S(2)}) collective-permute-start(f32[160,128]{1,0:T(8,128)S(1)} %get-tuple-element.65), channel_id=1, source_target_pairs={{0,16},{4,20},{8,24},{12,28},{16,0},{20,4},{24,8},{28,12},{1,17},{... | collective-permute-start | bytes 245768 | tf_op jit(solution)/shard_map/ppermute | solution.py:750
  55.7 8.8 %collective-permute-start.16 = (f32[160,128]{1,0:T(8,128)S(1)}, f32[160,128]{1,0:T(8,128)S(1)}, u32[]{:S(2)}, u32[]{:S(2)}) collective-permute-start(f32[160,128]{1,0:T(8,128)S(1)} %get-tuple-element.66), channel_id=1, source_target_pairs={{0,20},{4,16},{8,28},{12,24},{16,4},{20,0},{24,12},{28,8},{1,21},{... | collective-permute-start | bytes 245768 | tf_op jit(solution)/shard_map/ppermute | solution.py:750
  57.3 10.1 %collective-permute-start.17 = (f32[160,128]{1,0:T(8,128)S(1)}, f32[160,128]{1,0:T(8,128)S(1)}, u32[]{:S(2)}, u32[]{:S(2)}) collective-permute-start(f32[160,128]{1,0:T(8,128)S(1)} %get-tuple-element.67), channel_id=1, source_target_pairs={{0,24},{4,28},{8,16},{12,20},{16,8},{20,12},{24,0},{28,4},{1,25},{... | collective-permute-start | bytes 245768 | tf_op jit(solution)/shard_map/ppermute | solution.py:750
  59.1 8.3 %collective-permute-start.18 = (f32[160,128]{1,0:T(8,128)S(1)}, f32[160,128]{1,0:T(8,128)S(1)}, u32[]{:S(2)}, u32[]{:S(2)}) collective-permute-start(f32[160,128]{1,0:T(8,128)S(1)} %get-tuple-element.61.refs_4_), channel_id=1, source_target_pairs={{0,28},{4,24},{8,20},{12,16},{16,12},{20,8},{24,4},{28,0},{1,29},{... | collective-permute-start | bytes 245768 | tf_op jit(solution)/shard_map/ppermute | solution.py:750

commit v6 on v5

--- a/solution.py
+++ b/solution.py
@@ -32,15 +32,15 @@
     return index ^ step if is_power_of_two(count) else (index + count - step) % count
 
 
-def even_pairs(count):
-    return [(i, i ^ 1) for i in range(count) if i ^ 1 < count]
-
-
-def odd_pairs(count):
-    route = []
-    for low in range(1, count - 1, 2):
-        route += [(low, low + 1), (low + 1, low)]
-    return route
+def swap_route(parity, count):
+    mate = list(range(count))
+    for low in range(parity, count - 1, 2):
+        mate[low], mate[low + 1] = low + 1, low
+    return [
+        (side * count + i, (side if mate[i] != i else 1 - side) * count + mate[i])
+        for side in range(2)
+        for i in range(count)
+    ]
 
 
 def lon_route(step, count):
@@ -278,11 +278,11 @@
     first_col = lax.axis_index("lon") * loop.cols - HALO + 1
 
     def one_entry(entry, carry):
-        base = (base_ref[entry, 0] - first_row) * wide + (base_ref[entry, 1] - first_col)
+        base = (base_ref[0, entry] - first_row) * wide + (base_ref[1, entry] - first_col)
         total = None
         for a in range(4):
             for b in range(4):
-                weight = weight_ref[entry, 4 * a + b]
+                weight = weight_ref[4 * a + b, entry]
                 part = weight * frame_ref[tiles(base + a * wide + b, 1), :]
                 total = part if total is None else total + part
         cosine, sine = cosine_ref[entry], sine_ref[entry]
@@ -336,6 +336,16 @@
     def _():
         copy_rows(0, rows + 2 * HALO, lon_even_ref, 0, HALO)
         copy_rows(0, rows + 2 * HALO, lon_odd_ref, HALO + cols, HALO)
+
+    lat, lon = lax.axis_index("lat"), lax.axis_index("lon")
+    zeros = jnp.zeros((HALO * TILE, frame_ref.shape[1]), jnp.float32)
+    for at_row, top in ((lat == 0, 0), (lat == loop.lat_count - 1, HALO + rows)):
+        for at_col, left in ((lon == 0, 0), (lon == loop.lon_count - 1, HALO + cols)):
+
+            @pl.when(at_row & at_col)
+            def _():
+                for row in range(HALO):
+                    frame_ref[tiles((top + row) * wide + left, HALO), :] = zeros
 
     mix_and_pack(loop, wide, rim, frame_ref, value_ref, send_refs)
 
@@ -513,8 +523,9 @@
         @pl.when(self.on_col_edge)
         def _():
             chunk = pl.multiple_of(jnp.where(self.at_left, 0, wide - 8), 8)
+            count = rows[1] - rows[0]
             self.over(
-                (rows[0] - 1, rows[1] + 1), lambda row: self.first_pass(row, chunk), 2
+                (rows[0] - 1, rows[1] + 1), lambda row: self.first_pass(row, chunk), count // 2 + 1
             )
 
         @pl.when(self.on_row_edge)
@@ -527,7 +538,8 @@
         @pl.when(self.on_col_edge)
         def _():
             chunk = jnp.where(self.at_left, low_chunk, high_chunk)
-            self.over(rows, lambda row: self.second_pass(row, chunk, emit), 2)
+            count = rows[1] - rows[0]
+            self.over(rows, lambda row: self.second_pass(row, chunk, emit), count // 2)
 
 
 def cross(x, y):
@@ -685,8 +697,8 @@
     head, tail = cells[:HALO], cells[rows - HALO :]
     send_even = jnp.where(last_first, tail, head).reshape(HALO * cols * fields, levels)
     send_odd = jnp.where(last_first, head, tail).reshape(HALO * cols * fields, levels)
-    lat_even = lax.ppermute(send_even, "lat", even_pairs(lat_count))
-    lat_odd = lax.ppermute(send_odd, "lat", odd_pairs(lat_count))
+    lat_even = lax.ppermute(send_even, ("panel", "lat"), swap_route(0, lat_count))
+    lat_odd = lax.ppermute(send_odd, ("panel", "lat"), swap_route(1, lat_count))
 
     send_ids = table_ids(1, lon_count, loop.column_slots)[[1, 0, 2]]
     got_ids = table_ids(lat_count, lon_count, loop.slots)
@@ -701,7 +713,7 @@
         name="tables",
     )(first_cell, other_cell, jnp.asarray(send_ids), jnp.asarray(got_ids), jnp.asarray(got_ids))
     angle = rim_angle[0]
-    rim = (send_table, rim_base[0], rim_weight[0], jnp.cos(angle), jnp.sin(angle))
+    rim = (send_table, rim_base[0].T, rim_weight[0].T, jnp.cos(angle), jnp.sin(angle))
     factors = jnp.asarray(row_factors(rows, lat_count, loop.nth, loop.nph))
     radial = jnp.asarray(radial_factors(levels, loop.nth))
 
@@ -717,8 +729,8 @@
         compiler_params=grant(4),
         name="strips",
     )(own_even, own_odd, lat_even, lat_odd)
-    lon_even = lax.ppermute(strip_even, "lon", even_pairs(lon_count))
-    lon_odd = lax.ppermute(strip_odd, "lon", odd_pairs(lon_count))
+    lon_even = lax.ppermute(strip_even, ("panel", "lon"), swap_route(0, lon_count))
+    lon_odd = lax.ppermute(strip_odd, ("panel", "lon"), swap_route(1, lon_count))
 
     packed_shapes = [tile_array(loop.column_slots)] * lon_count
     frame, *packed = pl.pallas_call(

time: 71.6 us -> 68.7 us (0.959)
  starting transfers between devices: 28.4 us -> 24.3 us
  waiting for transfers between devices: 16.3 us -> 20.2 us
  Pallas kernels: 19.6 us -> 17.1 us
    ppermute x1, waiting for transfers between devices: 0.01 us -> 4.3 us  [per_device(): other_cell = lax.ppermute(first_cell, 'panel', [(0, 1), (1, 0)])]
    ppermute x8, starting transfers between devices: 16.2 us -> 13.6 us  [second_round(): lax.ppermute(turned[step], ('panel', 'lat'), lat_route(step, lat_count))]
    ppermute x6, starting transfers between devices: 5.98 us -> 3.83 us  [first_round(): lax.ppermute(packed[step], 'lon', lon_route(step, lon_count))]
    ppermute x4, starting transfers between devices: 4.55 us -> 6.26 us  [the longest x1 3.14 us: per_device(): lax.ppermute(send_even, ('panel', 'lat'), swap_route(0, lat_count))]
    pallas_call x1, Pallas kernels: 4.38 us -> 2.95 us  [per_device(): pl.pallas_call(lambda *refs: first_edge_kernel(loop, *refs), out_shape=[t...]
    ppermute x1, starting transfers between devices: 1.71 us -> 0.59 us  [per_device(): other_cell = lax.ppermute(first_cell, 'panel', [(0, 1), (1, 0)])]
    pallas_call x1, Pallas kernels: 3.85 us -> 2.95 us  [per_device(): pl.pallas_call(lambda *refs: second_edge_kernel(loop, *refs), out_shape=p...]
    squeeze x1 -> x0, local copies, waits for them, and re-layouts: 0.76 us -> none  [per_device(): rim_base[0]]
  transfers between devices with their start and end apart: 19 -> 19, of which waited for: 7 -> 9; matrix products, arithmetic and copies ran while one was open for 6% -> 4% of each run, Pallas kernels for 11% -> 12%
where the time goes in v6:
time: 68.7 us; the launch traced here: 68.3 us
  starting transfers between devices  24.3 us (35%)
  waiting for transfers between devices  20.2 us (29%)
  Pallas kernels  17.1 us (25%)
  local copies, waits for them, and re-layouts  4.29 us (6%)
  other arithmetic  2.23 us (3%)
    ppermute x8, starting transfers between devices, second_round(): lax.ppermute(turned[step], ('panel', 'lat'), lat_route(step, lat_count))  13.6 us
    ppermute x6, waiting for transfers between devices, first_round(): lax.ppermute(packed[step], 'lon', lon_route(step, lon_count))  6.21 us
    ppermute x8, waiting for transfers between devices, second_round(): lax.ppermute(turned[step], ('panel', 'lat'), lat_route(step, lat_count))  4.51 us
    ppermute x1, waiting for transfers between devices, per_device(): other_cell = lax.ppermute(first_cell, 'panel', [(0, 1), (1, 0)])  4.3 us
    pallas_call x1, Pallas kernels, per_device(): pl.pallas_call(lambda *refs: first_inner_kernel(loop, *refs), out_shape=[...  4.25 us
    ppermute x6, starting transfers between devices, first_round(): lax.ppermute(packed[step], 'lon', lon_route(step, lon_count))  3.83 us
    ppermute x1, waiting for transfers between devices, per_device(): lax.ppermute(send_even, ('panel', 'lat'), swap_route(0, lat_count))  3.74 us
    pallas_call x1, Pallas kernels, per_device(): pl.pallas_call(lambda *refs: second_inner_kernel(loop, *refs), out_shape=...  3.32 us
  transfers between devices with their start and end apart: 19, of which 9 were waited for; matrix products, arithmetic and copies ran while one was open for 4% of the time, Pallas kernels for 12%

profile of v6, /device:TPU:0, one launch (start us, length us, event | category | flops | bytes accessed | tf_op | source)
XLA Modules:
  0.0 68.3 jit_solution(11690177248815366085)
XLA Ops:
  1.2 3.1 %collective-permute-start.1 = (f32[512,128]{1,0:T(8,128)S(1)}, f32[512,128]{1,0:T(8,128)S(1)}, u32[]{:S(2)}, u32[]{:S(2)}) collective-permute-start(f32[512,128]{1,0:T(8,128)S(1)} %bitcast.26), channel_id=1, source_target_pairs={{0,4},{4,0},{8,12},{12,8},{16,20},{20,16},{24,28},{28,24},{1,5},{5... | collective-permute-start | bytes 786440 | tf_op jit(solution)/shard_map/ppermute | solution.py:700
  4.3 1.5 %collective-permute-start.2 = (f32[512,128]{1,0:T(8,128)S(1)}, f32[512,128]{1,0:T(8,128)S(1)}, u32[]{:S(2)}, u32[]{:S(2)}) collective-permute-start(f32[512,128]{1,0:T(8,128)S(1)} %bitcast.25), channel_id=1, source_target_pairs={{0,16},{4,8},{8,4},{12,28},{16,0},{20,24},{24,20},{28,12},{1,17},{... | collective-permute-start | bytes 786440 | tf_op jit(solution)/shard_map/ppermute | solution.py:701
  6.9 3.7 %collective-permute-done.1.refs_2_.refs_6_ = f32[512,128]{1,0:T(8,128)S(1)} collective-permute-done((f32[512,128]{1,0:T(8,128)S(1)}, f32[512,128]{1,0:T(8,128)S(1)}, u32[]{:S(2)}, u32[]{:S(2)}) %collective-permute-start.1) | collective-permute-done | bytes 262176 | tf_op jit(solution)/shard_map/ppermute | solution.py:700
  10.6 1.5 %collective-permute-done.2.refs_3_.refs_7_ = f32[512,128]{1,0:T(8,128)S(1)} collective-permute-done((f32[512,128]{1,0:T(8,128)S(1)}, f32[512,128]{1,0:T(8,128)S(1)}, u32[]{:S(2)}, u32[]{:S(2)}) %collective-permute-start.2) | collective-permute-done | bytes 262176 | tf_op jit(solution)/shard_map/ppermute | solution.py:701
  12.2 1.6 %collective-permute-start.4 = (f32[768,128]{1,0:T(8,128)S(1)}, f32[768,128]{1,0:T(8,128)S(1)}, u32[]{:S(2)}, u32[]{:S(2)}) collective-permute-start(f32[768,128]{1,0:T(8,128)S(1)} %get-tuple-element.40), channel_id=1, source_target_pairs={{0,16},{1,2},{2,1},{3,19},{16,0},{17,18},{18,17},{19,3},{4,20},{5,... | collective-permute-start | bytes 1179656 | tf_op jit(solution)/shard_map/ppermute | solution.py:733
  15.9 4.3 %collective-permute-done.refs_1_ = s32[2]{0:T(128)S(1)} collective-permute-done((s32[2]{0:T(128)S(1)}, s32[2]{0:T(128)S(1)}, u32[]{:S(2)}, u32[]{:S(2)}) %collective-permute-start) | collective-permute-done | bytes 40 | tf_op jit(solution)/shard_map/ppermute | solution.py:693
  23.6 1.6 %frame.1 = (f32[4608,128]{1,0:T(8,128)S(1)}, f32[104,128]{1,0:T(8,128)S(1)}, f32[104,128]{1,0:T(8,128)S(1)}, f32[104,128]{1,0:T(8,128)S(1)}, f32[104,128]{1,0:T(8,128)S(1)}) custom-call(s32[8,128]{1,0:T(8,128)S(1)} %get-tuple-element.38.refs_0_, s32[2,32]{1,0:T(2,128)S(1)} %bitcast.23, f32[16,32]{1,0:T(8,128)S(1)} %bitcast.21, ...), custom_call_target="tpu_custom_call" | custom-call | tf_op jit(solution)/shard_map/frame/pallas_call | solution.py:736
  27.1 2.7 %collective-permute-done.6.refs_3_ = f32[104,128]{1,0:T(8,128)S(1)} collective-permute-done((f32[104,128]{1,0:T(8,128)S(1)}, f32[104,128]{1,0:T(8,128)S(1)}, u32[]{:S(2)}, u32[]{:S(2)}) %collective-permute-start.6) | collective-permute-done | bytes 53280 | tf_op jit(solution)/shard_map/ppermute | solution.py:748
  31.0 1.6 %collective-permute-start.8 = (f32[160,128]{1,0:T(8,128)S(1)}, f32[160,128]{1,0:T(8,128)S(1)}, u32[]{:S(2)}, u32[]{:S(2)}) collective-permute-start(f32[160,128]{1,0:T(8,128)S(1)} %get-tuple-element.52), channel_id=1, source_target_pairs={{0,16},{4,20},{8,24},{12,28},{16,0},{20,4},{24,8},{28,12},{1,17},{... | collective-permute-start | bytes 245768 | tf_op jit(solution)/shard_map/ppermute | solution.py:762
  32.6 1.4 %collective-permute-start.9 = (f32[160,128]{1,0:T(8,128)S(1)}, f32[160,128]{1,0:T(8,128)S(1)}, u32[]{:S(2)}, u32[]{:S(2)}) collective-permute-start(f32[160,128]{1,0:T(8,128)S(1)} %get-tuple-element.53), channel_id=1, source_target_pairs={{0,20},{4,16},{8,28},{12,24},{16,4},{20,0},{24,12},{28,8},{1,21},{... | collective-permute-start | bytes 245768 | tf_op jit(solution)/shard_map/ppermute | solution.py:762
  34.0 2.6 %collective-permute-start.10 = (f32[160,128]{1,0:T(8,128)S(1)}, f32[160,128]{1,0:T(8,128)S(1)}, u32[]{:S(2)}, u32[]{:S(2)}) collective-permute-start(f32[160,128]{1,0:T(8,128)S(1)} %get-tuple-element.54), channel_id=1, source_target_pairs={{0,24},{4,28},{8,16},{12,20},{16,8},{20,12},{24,0},{28,4},{1,25},{... | collective-permute-start | bytes 245768 | tf_op jit(solution)/shard_map/ppermute | solution.py:762
  36.5 1.3 %collective-permute-start.11 = (f32[160,128]{1,0:T(8,128)S(1)}, f32[160,128]{1,0:T(8,128)S(1)}, u32[]{:S(2)}, u32[]{:S(2)}) collective-permute-start(f32[160,128]{1,0:T(8,128)S(1)} %get-tuple-element.47.refs_3_), channel_id=1, source_target_pairs={{0,28},{4,24},{8,20},{12,16},{16,12},{20,8},{24,4},{28,0},{1,29},{... | collective-permute-start | bytes 245768 | tf_op jit(solution)/shard_map/ppermute | solution.py:762
  37.9 4.3 %first_inner.1 = (f32[4608,128]{1,0:T(8,128)S(1)}, f32[8,24,24,128]{3,2,1,0:T(8,128)S(1)}, f32[7680,128]{1,0:T(8,128)S(1)}, f32[12480,128]{1,0:T(8,128)S(1)}) custom-call(f32[288]{0:T(512)S(1)} %copy-done.5, f32[7,8,128]{2,1,0:T(8,128)S(1)} %copy-done.1, f32[4608,128]{1,0:T(8,128)S(1)} %get-tuple-element.41.refs_2_, f32[160,128]{1,0:T(8,128)S(1)} %get-tuple-element.47.refs_3_), custom_call_target="tpu_custom_call" | custom-call | tf_op jit(solution)/shard_map/first_inner/pallas_call | solution.py:774
  42.1 1.6 %collective-permute-done.10.refs_14_ = f32[160,128]{1,0:T(8,128)S(1)} collective-permute-done((f32[160,128]{1,0:T(8,128)S(1)}, f32[160,128]{1,0:T(8,128)S(1)}, u32[]{:S(2)}, u32[]{:S(2)}) %collective-permute-start.10) | collective-permute-done | bytes 81952 | tf_op jit(solution)/shard_map/ppermute | solution.py:762
  43.7 2.9 %first_edge.1 = (f32[4608,128]{1,0:T(8,128)S(1)}, f32[8,24,24,128]{3,2,1,0:T(8,128)S(1)}, f32[7680,128]{1,0:T(8,128)S(1)}, f32[12480,128]{1,0:T(8,128)S(1)}, f32...) custom-call(s32[8,128]{1,0:T(8,128)S(1)} %get-tuple-element.38.refs_, ...), custom_call_target="tpu_custom_call", output_to_operand_aliasing={{0}: (8, {}), {1}: (9, {}), {2}: (10, {}), {3}: (11, {})} | custom-call | tf_op jit(solution)/shard_map/first_edge/pallas_call | solution.py:782
  46.9 1.8 %collective-permute-start.14 = (f32[104,128]{1,0:T(8,128)S(1)}, f32[104,128]{1,0:T(8,128)S(1)}, u32[]{:S(2)}, u32[]{:S(2)}) collective-permute-start(f32[104,128]{1,0:T(8,128)S(1)} %get-tuple-element.60), channel_id=1, source_target_pairs={{0,3},{1,2},{2,1},{3,0},{4,7},{5,6},{6,5},{7,4},{8,11},{9,10},{10,... | collective-permute-start | bytes 159752 | tf_op jit(solution)/shard_map/ppermute | solution.py:748
  48.6 2.9 %collective-permute-done.13.refs_3_ = f32[104,128]{1,0:T(8,128)S(1)} collective-permute-done((f32[104,128]{1,0:T(8,128)S(1)}, f32[104,128]{1,0:T(8,128)S(1)}, u32[]{:S(2)}, u32[]{:S(2)}) %collective-permute-start.13) | collective-permute-done | bytes 53280 | tf_op jit(solution)/shard_map/ppermute | solution.py:748
  52.3 1.7 %collective-permute-start.15 = (f32[160,128]{1,0:T(8,128)S(1)}, f32[160,128]{1,0:T(8,128)S(1)}, u32[]{:S(2)}, u32[]{:S(2)}) collective-permute-start(f32[160,128]{1,0:T(8,128)S(1)} %get-tuple-element.65), channel_id=1, source_target_pairs={{0,16},{4,20},{8,24},{12,28},{16,0},{20,4},{24,8},{28,12},{1,17},{... | collective-permute-start | bytes 245768 | tf_op jit(solution)/shard_map/ppermute | solution.py:762
  54.0 1.5 %collective-permute-start.16 = (f32[160,128]{1,0:T(8,128)S(1)}, f32[160,128]{1,0:T(8,128)S(1)}, u32[]{:S(2)}, u32[]{:S(2)}) collective-permute-start(f32[160,128]{1,0:T(8,128)S(1)} %get-tuple-element.66), channel_id=1, source_target_pairs={{0,20},{4,16},{8,28},{12,24},{16,4},{20,0},{24,12},{28,8},{1,21},{... | collective-permute-start | bytes 245768 | tf_op jit(solution)/shard_map/ppermute | solution.py:762
  55.5 2.0 %collective-permute-start.17 = (f32[160,128]{1,0:T(8,128)S(1)}, f32[160,128]{1,0:T(8,128)S(1)}, u32[]{:S(2)}, u32[]{:S(2)}) collective-permute-start(f32[160,128]{1,0:T(8,128)S(1)} %get-tuple-element.67), channel_id=1, source_target_pairs={{0,24},{4,28},{8,16},{12,20},{16,8},{20,12},{24,0},{28,4},{1,25},{... | collective-permute-start | bytes 245768 | tf_op jit(solution)/shard_map/ppermute | solution.py:762
  57.5 1.6 %collective-permute-start.18 = (f32[160,128]{1,0:T(8,128)S(1)}, f32[160,128]{1,0:T(8,128)S(1)}, u32[]{:S(2)}, u32[]{:S(2)}) collective-permute-start(f32[160,128]{1,0:T(8,128)S(1)} %get-tuple-element.61.refs_4_), channel_id=1, source_target_pairs={{0,28},{4,24},{8,20},{12,16},{16,12},{20,8},{24,4},{28,0},{1,29},{... | collective-permute-start | bytes 245768 | tf_op jit(solution)/shard_map/ppermute | solution.py:762
  59.1 3.3 %second_inner.1 = (f32[2048,128]{1,0:T(8,128)S(1)}, f32[7680,128]{1,0:T(8,128)S(1)}, f32[12480,128]{1,0:T(8,128)S(1)}) custom-call(f32[288]{0:T(512)S(1)} %copy-done.5, f32[7,8,128]{2,1,0:T(8,128)S(1)} %copy-done.1, f32[4608,128]{1,0:T(8,128)S(1)} %get-tuple-element.56.refs_2_, f32[8,24,24,128]{3,2,1,0:T(8,128)S(1)} %get-tuple-element.55.refs_3_, ...), custom_call_target="tpu_custom_call" | custom-call | tf_op jit(solution)/shard_map/second_inner/pallas_call | solution.py:795
  62.4 2.9 %collective-permute-done.17.refs_9_ = f32[160,128]{1,0:T(8,128)S(1)} collective-permute-done((f32[160,128]{1,0:T(8,128)S(1)}, f32[160,128]{1,0:T(8,128)S(1)}, u32[]{:S(2)}, u32[]{:S(2)}) %collective-permute-start.17) | collective-permute-done | bytes 81952 | tf_op jit(solution)/shard_map/ppermute | solution.py:762
  65.4 3.0 %second_edge.1 = (f32[7680,128]{1,0:T(8,128)S(1)}, f32[12480,128]{1,0:T(8,128)S(1)}, f32[2048,128]{1,0:T(8,128)}) custom-call(s32[8,128]{1,0:T(8,128)S(1)} %get-tuple-element.37.refs_5_.refs_0_, f32[288]{0:T(512)S(1)} %copy-done.5, f32[7,8,128]{2,1,0:T(8,128)S(1)} %copy-done.1, ...), custom_call_target="tpu_custom_call", output_to_operand_aliasing={{0}: (5, {}), {1}: (6, {})} | custom-call | tf_op jit(solution)/shard_map/second_edge/pallas_call | solution.py:803
  (45 shorter events, 11.9 us)
Async XLA Ops:
  0.0 37.9 %copy-start.1 = (f32[7,8,128]{2,1,0:T(8,128)S(1)}, f32[7,8,128]{2,1,0:T(8,128)}, u32[]{:S(2)}) copy-start(f32[7,8,128]{2,1,0:T(8,128)} %constant.36.clone.refs_1_.refs_7_.refs_2_) | copy-start | bytes 86020
  0.0 37.9 %copy-start.5 = (f32[288]{0:T(512)S(1)}, f32[288]{0:T(512)}, u32[]{:S(2)}) copy-start(f32[288]{0:T(512)} %constant.35.clone.refs_0_.refs_6_.refs_1_) | copy-start | bytes 3460
  0.0 22.2 %copy-start = (f32[1,16,16,8,128]{4,3,2,1,0:T(8,128)S(1)}, f32[1,16,16,8,128]{4,3,2,1,0:T(8,128)}, u32[]{:S(2)}) copy-start(f32[1,16,16,8,128]{4,3,2,1,0:T(8,128)} %param.9) | copy-start | bytes 3145732
  0.0 43.7 %copy-start.4 = (f32[1,32,16]{1,2,0:T(8,128)S(1)}, f32[1,32,16]{1,2,0:T(8,128)}, u32[]{:S(2)}) copy-start(f32[1,32,16]{1,2,0:T(8,128)} %param.11) | copy-start | bytes 6148
  0.0 43.7 %copy-start.8 = (s32[1,32,2]{1,2,0:T(2,128)S(1)}, s32[1,32,2]{1,2,0:T(2,128)}, u32[]{:S(2)}) copy-start(s32[1,32,2]{1,2,0:T(2,128)} %param.10) | copy-start | bytes 772
  1.2 9.4 %collective-permute-start.1 = (f32[512,128]{1,0:T(8,128)S(1)}, f32[512,128]{1,0:T(8,128)S(1)}, u32[]{:S(2)}, u32[]{:S(2)}) collective-permute-start(f32[512,128]{1,0:T(8,128)S(1)} %bitcast.26), channel_id=1, source_target_pairs={{0,4},{4,0},{8,12},{12,8},{16,20},{20,16},{24,28},{28,24},{1,5},{5... | collective-permute-start | bytes 786440 | tf_op jit(solution)/shard_map/ppermute | solution.py:700
  4.3 7.8 %collective-permute-start.2 = (f32[512,128]{1,0:T(8,128)S(1)}, f32[512,128]{1,0:T(8,128)S(1)}, u32[]{:S(2)}, u32[]{:S(2)}) collective-permute-start(f32[512,128]{1,0:T(8,128)S(1)} %bitcast.25), channel_id=1, source_target_pairs={{0,16},{4,8},{8,4},{12,28},{16,0},{20,24},{24,20},{28,12},{1,17},{... | collective-permute-start | bytes 786440 | tf_op jit(solution)/shard_map/ppermute | solution.py:701
  12.2 10.0 %collective-permute-start.3 = (f32[768,128]{1,0:T(8,128)S(1)}, f32[768,128]{1,0:T(8,128)S(1)}, u32[]{:S(2)}, u32[]{:S(2)}) collective-permute-start(f32[768,128]{1,0:T(8,128)S(1)} %get-tuple-element.39), channel_id=1, source_target_pairs={{0,1},{1,0},{2,3},{3,2},{16,17},{17,16},{18,19},{19,18},{4,5},{5,4... | collective-permute-start | bytes 1179656 | tf_op jit(solution)/shard_map/ppermute | solution.py:732
  12.2 10.0 %collective-permute-start.4 = (f32[768,128]{1,0:T(8,128)S(1)}, f32[768,128]{1,0:T(8,128)S(1)}, u32[]{:S(2)}, u32[]{:S(2)}) collective-permute-start(f32[768,128]{1,0:T(8,128)S(1)} %get-tuple-element.40), channel_id=1, source_target_pairs={{0,16},{1,2},{2,1},{3,19},{16,0},{17,18},{18,17},{19,3},{4,20},{5,... | collective-permute-start | bytes 1179656 | tf_op jit(solution)/shard_map/ppermute | solution.py:733
  14.6 5.6 %collective-permute-start = (s32[2]{0:T(128)S(1)}, s32[2]{0:T(128)S(1)}, u32[]{:S(2)}, u32[]{:S(2)}) collective-permute-start(s32[2]{0:T(128)S(1)} %slice_reduce_fusion.refs_0_), channel_id=1, source_target_pairs={{0,16},{16,0},{1,17},{17,1},{2,18},{18,2},{3,19},{19,3},{4,20},{20... | collective-permute-start | bytes 32 | tf_op jit(solution)/shard_map/ppermute | solution.py:693
  25.2 1.9 %collective-permute-start.5 = (f32[104,128]{1,0:T(8,128)S(1)}, f32[104,128]{1,0:T(8,128)S(1)}, u32[]{:S(2)}, u32[]{:S(2)}) collective-permute-start(f32[104,128]{1,0:T(8,128)S(1)} %get-tuple-element.44), channel_id=1, source_target_pairs={{0,1},{1,0},{2,3},{3,2},{4,5},{5,4},{6,7},{7,6},{8,9},{9,8},{10,11... | collective-permute-start | bytes 159752 | tf_op jit(solution)/shard_map/ppermute | solution.py:748
  25.3 4.5 %collective-permute-start.6 = (f32[104,128]{1,0:T(8,128)S(1)}, f32[104,128]{1,0:T(8,128)S(1)}, u32[]{:S(2)}, u32[]{:S(2)}) collective-permute-start(f32[104,128]{1,0:T(8,128)S(1)} %get-tuple-element.45), channel_id=1, source_target_pairs={{0,2},{1,3},{2,0},{3,1},{4,6},{5,7},{6,4},{7,5},{8,10},{9,11},{10,... | collective-permute-start | bytes 159752 | tf_op jit(solution)/shard_map/ppermute | solution.py:748
  26.2 4.1 %collective-permute-start.7 = (f32[104,128]{1,0:T(8,128)S(1)}, f32[104,128]{1,0:T(8,128)S(1)}, u32[]{:S(2)}, u32[]{:S(2)}) collective-permute-start(f32[104,128]{1,0:T(8,128)S(1)} %get-tuple-element.46), channel_id=1, source_target_pairs={{0,3},{1,2},{2,1},{3,0},{4,7},{5,6},{6,5},{7,4},{8,11},{9,10},{10,... | collective-permute-start | bytes 159752 | tf_op jit(solution)/shard_map/ppermute | solution.py:748
  31.0 11.1 %collective-permute-start.8 = (f32[160,128]{1,0:T(8,128)S(1)}, f32[160,128]{1,0:T(8,128)S(1)}, u32[]{:S(2)}, u32[]{:S(2)}) collective-permute-start(f32[160,128]{1,0:T(8,128)S(1)} %get-tuple-element.52), channel_id=1, source_target_pairs={{0,16},{4,20},{8,24},{12,28},{16,0},{20,4},{24,8},{28,12},{1,17},{... | collective-permute-start | bytes 245768 | tf_op jit(solution)/shard_map/ppermute | solution.py:762
  32.6 9.5 %collective-permute-start.9 = (f32[160,128]{1,0:T(8,128)S(1)}, f32[160,128]{1,0:T(8,128)S(1)}, u32[]{:S(2)}, u32[]{:S(2)}) collective-permute-start(f32[160,128]{1,0:T(8,128)S(1)} %get-tuple-element.53), channel_id=1, source_target_pairs={{0,20},{4,16},{8,28},{12,24},{16,4},{20,0},{24,12},{28,8},{1,21},{... | collective-permute-start | bytes 245768 | tf_op jit(solution)/shard_map/ppermute | solution.py:762
  34.0 9.8 %collective-permute-start.10 = (f32[160,128]{1,0:T(8,128)S(1)}, f32[160,128]{1,0:T(8,128)S(1)}, u32[]{:S(2)}, u32[]{:S(2)}) collective-permute-start(f32[160,128]{1,0:T(8,128)S(1)} %get-tuple-element.54), channel_id=1, source_target_pairs={{0,24},{4,28},{8,16},{12,20},{16,8},{20,12},{24,0},{28,4},{1,25},{... | collective-permute-start | bytes 245768 | tf_op jit(solution)/shard_map/ppermute | solution.py:762
  36.5 7.2 %collective-permute-start.11 = (f32[160,128]{1,0:T(8,128)S(1)}, f32[160,128]{1,0:T(8,128)S(1)}, u32[]{:S(2)}, u32[]{:S(2)}) collective-permute-start(f32[160,128]{1,0:T(8,128)S(1)} %get-tuple-element.47.refs_3_), channel_id=1, source_target_pairs={{0,28},{4,24},{8,20},{12,16},{16,12},{20,8},{24,4},{28,0},{1,29},{... | collective-permute-start | bytes 245768 | tf_op jit(solution)/shard_map/ppermute | solution.py:762
  46.7 1.9 %collective-permute-start.12 = (f32[104,128]{1,0:T(8,128)S(1)}, f32[104,128]{1,0:T(8,128)S(1)}, u32[]{:S(2)}, u32[]{:S(2)}) collective-permute-start(f32[104,128]{1,0:T(8,128)S(1)} %get-tuple-element.58), channel_id=1, source_target_pairs={{0,1},{1,0},{2,3},{3,2},{4,5},{5,4},{6,7},{7,6},{8,9},{9,8},{10,11... | collective-permute-start | bytes 159752 | tf_op jit(solution)/shard_map/ppermute | solution.py:748
  46.8 4.8 %collective-permute-start.13 = (f32[104,128]{1,0:T(8,128)S(1)}, f32[104,128]{1,0:T(8,128)S(1)}, u32[]{:S(2)}, u32[]{:S(2)}) collective-permute-start(f32[104,128]{1,0:T(8,128)S(1)} %get-tuple-element.59), channel_id=1, source_target_pairs={{0,2},{1,3},{2,0},{3,1},{4,6},{5,7},{6,4},{7,5},{8,10},{9,11},{10,... | collective-permute-start | bytes 159752 | tf_op jit(solution)/shard_map/ppermute | solution.py:748
  46.9 4.8 %collective-permute-start.14 = (f32[104,128]{1,0:T(8,128)S(1)}, f32[104,128]{1,0:T(8,128)S(1)}, u32[]{:S(2)}, u32[]{:S(2)}) collective-permute-start(f32[104,128]{1,0:T(8,128)S(1)} %get-tuple-element.60), channel_id=1, source_target_pairs={{0,3},{1,2},{2,1},{3,0},{4,7},{5,6},{6,5},{7,4},{8,11},{9,10},{10,... | collective-permute-start | bytes 159752 | tf_op jit(solution)/shard_map/ppermute | solution.py:748
  52.3 10.1 %collective-permute-start.15 = (f32[160,128]{1,0:T(8,128)S(1)}, f32[160,128]{1,0:T(8,128)S(1)}, u32[]{:S(2)}, u32[]{:S(2)}) collective-permute-start(f32[160,128]{1,0:T(8,128)S(1)} %get-tuple-element.65), channel_id=1, source_target_pairs={{0,16},{4,20},{8,24},{12,28},{16,0},{20,4},{24,8},{28,12},{1,17},{... | collective-permute-start | bytes 245768 | tf_op jit(solution)/shard_map/ppermute | solution.py:762
  54.0 8.5 %collective-permute-start.16 = (f32[160,128]{1,0:T(8,128)S(1)}, f32[160,128]{1,0:T(8,128)S(1)}, u32[]{:S(2)}, u32[]{:S(2)}) collective-permute-start(f32[160,128]{1,0:T(8,128)S(1)} %get-tuple-element.66), channel_id=1, source_target_pairs={{0,20},{4,16},{8,28},{12,24},{16,4},{20,0},{24,12},{28,8},{1,21},{... | collective-permute-start | bytes 245768 | tf_op jit(solution)/shard_map/ppermute | solution.py:762
  55.5 9.9 %collective-permute-start.17 = (f32[160,128]{1,0:T(8,128)S(1)}, f32[160,128]{1,0:T(8,128)S(1)}, u32[]{:S(2)}, u32[]{:S(2)}) collective-permute-start(f32[160,128]{1,0:T(8,128)S(1)} %get-tuple-element.67), channel_id=1, source_target_pairs={{0,24},{4,28},{8,16},{12,20},{16,8},{20,12},{24,0},{28,4},{1,25},{... | collective-permute-start | bytes 245768 | tf_op jit(solution)/shard_map/ppermute | solution.py:762
  57.5 7.9 %collective-permute-start.18 = (f32[160,128]{1,0:T(8,128)S(1)}, f32[160,128]{1,0:T(8,128)S(1)}, u32[]{:S(2)}, u32[]{:S(2)}) collective-permute-start(f32[160,128]{1,0:T(8,128)S(1)} %get-tuple-element.61.refs_4_), channel_id=1, source_target_pairs={{0,28},{4,24},{8,20},{12,16},{16,12},{20,8},{24,4},{28,0},{1,29},{... | collective-permute-start | bytes 245768 | tf_op jit(solution)/shard_map/ppermute | solution.py:762
  (4 other events, 2.8 us)

commit v7 on v6

--- a/solution.py
+++ b/solution.py
@@ -32,15 +32,27 @@
     return index ^ step if is_power_of_two(count) else (index + count - step) % count
 
 
-def swap_route(parity, count):
+def swap_route(parity, lat_count, lon_count, along_lat):
+    count, across = (lat_count, lon_count) if along_lat else (lon_count, lat_count)
     mate = list(range(count))
     for low in range(parity, count - 1, 2):
         mate[low], mate[low + 1] = low + 1, low
-    return [
-        (side * count + i, (side if mate[i] != i else 1 - side) * count + mate[i])
-        for side in range(2)
-        for i in range(count)
-    ]
+    route = []
+    for side in range(2):
+        for lat in range(lat_count):
+            for lon in range(lon_count):
+                here, other = (lat, lon) if along_lat else (lon, lat)
+                there = mate[here]
+                if there == here:
+                    other = other ^ 1 if other ^ 1 < across else other
+                target = (there, other) if along_lat else (other, there)
+                route.append(
+                    (
+                        (side * lat_count + lat) * lon_count + lon,
+                        (side * lat_count + target[0]) * lon_count + target[1],
+                    )
+                )
+    return route
 
 
 def lon_route(step, count):
@@ -210,10 +222,28 @@
 
 def table_kernel(
     loop, pitch, cell_ref, other_ref, send_id_ref, swap_id_ref, got_id_ref,
-    send_ref, swap_ref, receive_ref,
+    base_ref, weight_ref, turn_ref, send_ref, swap_ref, receive_ref, corner_ref, spread_ref,
 ):
+    entries = loop.entries
+    diagonal = lax.broadcasted_iota(jnp.int32, (entries, entries), 0) == (
+        lax.broadcasted_iota(jnp.int32, (entries, entries), 1)
+    )
+    for number in range(18):
+        ref, row = (weight_ref, number) if number < 16 else (turn_ref, number - 16)
+        column = jnp.sum(
+            jnp.where(diagonal, ref[row : row + 1, :], 0.0), axis=1, keepdims=True
+        )
+        spread_ref[pl.ds(number * entries, entries), :] = jnp.broadcast_to(
+            column, (entries, spread_ref.shape[1])
+        )
+
     lat, lon = lax.axis_index("lat"), lax.axis_index("lon")
     lat_count, lon_count = loop.lat_count, loop.lon_count
+    wide = loop.cols + 2 * HALO
+    base = (base_ref[0:1, :] - lat * loop.rows + HALO - 1) * wide + (
+        base_ref[1:2, :] - lon * loop.cols + HALO - 1
+    )
+    corner_ref[0:1, 0:entries] = base
     mine = loop.position(cell_ref[0], cell_ref[1])
     other = loop.position(other_ref[0], other_ref[1])
 
@@ -270,22 +300,24 @@
 
 
 def mix_and_pack(loop, wide, rim, frame_ref, value_ref, send_refs):
-    send_table_ref, base_ref, weight_ref, cosine_ref, sine_ref = rim
+    send_table_ref, corner_ref, spread_ref = rim
+    entries = loop.entries
     field = lax.broadcasted_iota(jnp.int32, (TILE, 128), 0)
     takes_next = (field == 1) | (field == 4)
     turned = takes_next | (field == 2) | (field == 5)
-    first_row = lax.axis_index("lat") * loop.rows - HALO + 1
-    first_col = lax.axis_index("lon") * loop.cols - HALO + 1
 
     def one_entry(entry, carry):
-        base = (base_ref[0, entry] - first_row) * wide + (base_ref[1, entry] - first_col)
+        base = corner_ref[0, entry]
+
+        def over_tile(number):
+            return spread_ref[pl.ds(number * entries + entry, TILE, stride=0), :]
+
         total = None
         for a in range(4):
             for b in range(4):
-                weight = weight_ref[4 * a + b, entry]
-                part = weight * frame_ref[tiles(base + a * wide + b, 1), :]
+                part = over_tile(4 * a + b) * frame_ref[tiles(base + a * wide + b, 1), :]
                 total = part if total is None else total + part
-        cosine, sine = cosine_ref[entry], sine_ref[entry]
+        cosine, sine = over_tile(16), over_tile(17)
         other = jnp.where(
             takes_next, pltpu.roll(total, TILE - 1, 0), pltpu.roll(total, 1, 0)
         )
@@ -301,7 +333,7 @@
 
 
 def frame_kernel(loop, *refs):
-    rim, refs = refs[:5], refs[5:]
+    rim, refs = refs[:3], refs[3:]
     state_ref, lat_even_ref, lat_odd_ref, lon_even_ref, lon_odd_ref, frame_ref = refs[:6]
     send_refs, value_ref = refs[6:-1], refs[-1]
     rows, cols = loop.rows, loop.cols
@@ -596,7 +628,7 @@
 
 
 def first_edge_kernel(loop, *refs):
-    rim, refs = refs[:5], refs[5:]
+    rim, refs = refs[:3], refs[3:]
     receive_ref, factor_ref, radial_ref = refs[:3]
     got_refs, refs = refs[7 : 7 + loop.lat_count], refs[7 + loop.lat_count :]
     frame_ref, rate_ref, plane_ref, work_ref = refs[:4]
@@ -692,28 +724,43 @@
     first_cell = rim_target[0, 0]
     other_cell = lax.ppermute(first_cell, "panel", [(0, 1), (1, 0)])
 
+    everyone = ("panel", "lat", "lon")
     cells = state[0]
     last_first = lax.axis_index("lat") % 2 == 0
     head, tail = cells[:HALO], cells[rows - HALO :]
     send_even = jnp.where(last_first, tail, head).reshape(HALO * cols * fields, levels)
     send_odd = jnp.where(last_first, head, tail).reshape(HALO * cols * fields, levels)
-    lat_even = lax.ppermute(send_even, ("panel", "lat"), swap_route(0, lat_count))
-    lat_odd = lax.ppermute(send_odd, ("panel", "lat"), swap_route(1, lat_count))
+    lat_even = lax.ppermute(send_even, everyone, swap_route(0, lat_count, lon_count, True))
+    lat_odd = lax.ppermute(send_odd, everyone, swap_route(1, lat_count, lon_count, True))
 
     send_ids = table_ids(1, lon_count, loop.column_slots)[[1, 0, 2]]
     got_ids = table_ids(lat_count, lon_count, loop.slots)
-    send_table, swap_table, receive_table = pl.pallas_call(
+    angle = rim_angle[0]
+    turn = jnp.stack([jnp.cos(angle), jnp.sin(angle)])
+    send_table, swap_table, receive_table, corner_table, spread_weights = pl.pallas_call(
         lambda *refs: table_kernel(loop, pitch, *refs),
         out_shape=[
             jax.ShapeDtypeStruct(ids.shape[1:], jnp.int32) for ids in (send_ids, got_ids, got_ids)
+        ]
+        + [
+            jax.ShapeDtypeStruct((8, -(-entries // 128) * 128), jnp.int32),
+            jax.ShapeDtypeStruct((18 * entries + TILE, levels), f32),
         ],
-        in_specs=scalars(2) + whole(3),
-        out_specs=whole(3),
+        in_specs=scalars(2) + whole(6),
+        out_specs=whole(5),
         compiler_params=grant(4),
         name="tables",
-    )(first_cell, other_cell, jnp.asarray(send_ids), jnp.asarray(got_ids), jnp.asarray(got_ids))
-    angle = rim_angle[0]
-    rim = (send_table, rim_base[0].T, rim_weight[0].T, jnp.cos(angle), jnp.sin(angle))
+    )(
+        first_cell,
+        other_cell,
+        jnp.asarray(send_ids),
+        jnp.asarray(got_ids),
+        jnp.asarray(got_ids),
+        rim_base[0].T,
+        rim_weight[0].T,
+        turn,
+    )
+    rim = (send_table, corner_table, spread_weights)
     factors = jnp.asarray(row_factors(rows, lat_count, loop.nth, loop.nph))
     radial = jnp.asarray(radial_factors(levels, loop.nth))
 
@@ -729,14 +776,14 @@
         compiler_params=grant(4),
         name="strips",
     )(own_even, own_odd, lat_even, lat_odd)
-    lon_even = lax.ppermute(strip_even, ("panel", "lon"), swap_route(0, lon_count))
-    lon_odd = lax.ppermute(strip_odd, ("panel", "lon"), swap_route(1, lon_count))
+    lon_even = lax.ppermute(strip_even, everyone, swap_route(0, lat_count, lon_count, False))
+    lon_odd = lax.ppermute(strip_odd, everyone, swap_route(1, lat_count, lon_count, False))
 
     packed_shapes = [tile_array(loop.column_slots)] * lon_count
     frame, *packed = pl.pallas_call(
         lambda *refs: frame_kernel(loop, *refs),
         out_shape=[tile_array(tall * wide)] + packed_shapes,
-        in_specs=scalars(5) + whole(5),
+        in_specs=scalars(2) + whole(6),
         out_specs=whole(1 + lon_count),
         scratch_shapes=[pltpu.VMEM((entries * TILE, levels), f32)],
         compiler_params=grant(8),
@@ -782,10 +829,10 @@
     frame, rate, _, _, *packed = pl.pallas_call(
         lambda *refs: first_edge_kernel(loop, *refs),
         out_shape=[tile_array(tall * wide), rates] + planes + packed_shapes,
-        in_specs=scalars(7) + whole(5 + lat_count),
+        in_specs=scalars(2) + whole(1) + scalars(2) + whole(5 + lat_count),
         out_specs=whole(4 + lon_count),
         scratch_shapes=[pltpu.VMEM((entries * TILE, levels), f32)],
-        input_output_aliases={8: 0, 9: 1, 10: 2, 11: 3},
+        input_output_aliases={6: 0, 7: 1, 8: 2, 9: 3},
         compiler_params=grant(4),
         name="first_edge",
     )(*rim, receive_table, factors, radial, frame, rate, plane, work, *got)

time: 68.7 us -> 65.7 us (0.956)
  waiting for transfers between devices: 20.2 us -> 17 us
  starting transfers between devices: 24.3 us -> 25.1 us
  Pallas kernels: 17.1 us -> 16.4 us
    ppermute x1, waiting for transfers between devices: 4.3 us -> 1.37 us  [per_device(): other_cell = lax.ppermute(first_cell, 'panel', [(0, 1), (1, 0)])]
    ppermute x1, starting transfers between devices: 0.59 us -> 1.55 us  [per_device(): other_cell = lax.ppermute(first_cell, 'panel', [(0, 1), (1, 0)])]
    cos x0 -> x1, local copies, waits for them, and re-layouts: none -> 0.69 us  [per_device(): turn = jnp.stack([jnp.cos(angle), jnp.sin(angle)])]
    sin x1 -> x0, local copies, waits for them, and re-layouts: 0.69 us -> none  [per_device(): jnp.sin(angle)]
    unnamed x18 -> x14, local copies, waits for them, and re-layouts: 2.8 us -> 2.8 us
  transfers between devices with their start and end apart: 19 -> 19, of which waited for: 9 -> 9; matrix products, arithmetic and copies ran while one was open for 4% -> 4% of each run, Pallas kernels for 12% -> 13%
where the time goes in v7:
time: 65.7 us; the launch traced here: 65.2 us
  starting transfers between devices  25.1 us (38%)
  waiting for transfers between devices  17 us (26%)
  Pallas kernels  16.4 us (25%)
  local copies, waits for them, and re-layouts  4.29 us (7%)
  other arithmetic  2.24 us (3%)
    ppermute x8, starting transfers between devices, second_round(): lax.ppermute(turned[step], ('panel', 'lat'), lat_route(step, lat_count))  13.6 us
    ppermute x6, waiting for transfers between devices, first_round(): lax.ppermute(packed[step], 'lon', lon_route(step, lon_count))  6.06 us
    ppermute x1, waiting for transfers between devices, per_device(): lax.ppermute(send_even, everyone, swap_route(0, lat_count, lon_count, True))  5.22 us
    ppermute x8, waiting for transfers between devices, second_round(): lax.ppermute(turned[step], ('panel', 'lat'), lat_route(step, lat_count))  4.32 us
    pallas_call x1, Pallas kernels, per_device(): pl.pallas_call(lambda *refs: first_inner_kernel(loop, *refs), out_shape=[...  4.25 us
    ppermute x6, starting transfers between devices, first_round(): lax.ppermute(packed[step], 'lon', lon_route(step, lon_count))  3.84 us
    pallas_call x1, Pallas kernels, per_device(): pl.pallas_call(lambda *refs: second_inner_kernel(loop, *refs), out_shape=...  3.32 us
    ppermute x1, starting transfers between devices, per_device(): lax.ppermute(send_even, everyone, swap_route(0, lat_count, lon_count, True))  3.13 us
  transfers between devices with their start and end apart: 19, of which 9 were waited for; matrix products, arithmetic and copies ran while one was open for 4% of the time, Pallas kernels for 13%

profile of v7, /device:TPU:0, one launch (start us, length us, event | category | flops | bytes accessed | tf_op | source)
XLA Modules:
  0.0 65.2 jit_solution(11482045359585909934)
XLA Ops:
  0.0 1.2 %slice_select_fusion.2 = (f32[1,4,16,8,128]{4,3,2,1,0:T(8,128)S(1)}, f32[1,4,16,8,128]{4,3,2,1,0:T(8,128)S(1)}) fusion(f32[1,16,16,8,128]{4,3,2,1,0:T(8,128)} %param.9, pred[]{:T(512)S(6)} %eq.9), kind=kLoop, calls=%fused_computation.2 | loop fusion | flops 131072 | bytes 1048577 | tf_op jit(solution)/shard_map/jit(_where)/select_n | solution.py:732
  1.2 3.1 %collective-permute-start.1 = (f32[512,128]{1,0:T(8,128)S(1)}, f32[512,128]{1,0:T(8,128)S(1)}, u32[]{:S(2)}, u32[]{:S(2)}) collective-permute-start(f32[512,128]{1,0:T(8,128)S(1)} %bitcast.20), channel_id=1, source_target_pairs={{0,4},{1,5},{2,6},{3,7},{4,0},{5,1},{6,2},{7,3},{8,12},{9,13},{10,... | collective-permute-start | bytes 786440 | tf_op jit(solution)/shard_map/ppermute | solution.py:733
  4.3 1.1 %slice_select_fusion = (f32[16,4,8,128]{3,2,1,0:T(8,128)S(1)}, f32[16,4,8,128]{3,2,1,0:T(8,128)S(1)}) fusion(f32[16,16,8,128]{3,2,1,0:T(8,128)} %bitcast.13, pred[]{:T(512)S(6)} %eq.10), kind=kLoop, calls=%fused_computation | loop fusion | flops 131072 | bytes 1048577 | tf_op jit(solution)/shard_map/jit(_where)/select_n | solution.py:770
  5.4 5.2 %collective-permute-done.1.refs_2_.refs_4_ = f32[512,128]{1,0:T(8,128)S(1)} collective-permute-done((f32[512,128]{1,0:T(8,128)S(1)}, f32[512,128]{1,0:T(8,128)S(1)}, u32[]{:S(2)}, u32[]{:S(2)}) %collective-permute-start.1) | collective-permute-done | bytes 262176 | tf_op jit(solution)/shard_map/ppermute | solution.py:733
  10.8 2.9 %collective-permute-start.4 = (f32[768,128]{1,0:T(8,128)S(1)}, f32[768,128]{1,0:T(8,128)S(1)}, u32[]{:S(2)}, u32[]{:S(2)}) collective-permute-start(f32[768,128]{1,0:T(8,128)S(1)} %get-tuple-element.44), channel_id=1, source_target_pairs={{0,4},{1,2},{2,1},{3,7},{4,0},{5,6},{6,5},{7,3},{8,12},{9,10},{10,... | collective-permute-start | bytes 1179656 | tf_op jit(solution)/shard_map/ppermute | solution.py:780
  14.5 1.5 %collective-permute-start = (s32[2]{0:T(128)S(1)}, s32[2]{0:T(128)S(1)}, u32[]{:S(2)}, u32[]{:S(2)}) collective-permute-start(s32[2]{0:T(128)S(1)} %slice_reduce_fusion.refs_0_), channel_id=1, source_target_pairs={{0,16},{16,0},{1,17},{17,1},{2,18},{18,2},{3,19},{19,3},{4,20},{20... | collective-permute-start | bytes 32 | tf_op jit(solution)/shard_map/ppermute | solution.py:725
  16.7 1.4 %collective-permute-done.refs_1_ = s32[2]{0:T(128)S(1)} collective-permute-done((s32[2]{0:T(128)S(1)}, s32[2]{0:T(128)S(1)}, u32[]{:S(2)}, u32[]{:S(2)}) %collective-permute-start) | collective-permute-done | bytes 40 | tf_op jit(solution)/shard_map/ppermute | solution.py:725
  21.6 1.2 %frame.1 = (f32[4608,128]{1,0:T(8,128)S(1)}, f32[104,128]{1,0:T(8,128)S(1)}, f32[104,128]{1,0:T(8,128)S(1)}, f32[104,128]{1,0:T(8,128)S(1)}, f32[104,128]{1,0:T(8,128)S(1)}) custom-call(s32[8,128]{1,0:T(8,128)S(1)} %get-tuple-element.40.refs_0_, s32[8,128]{1,0:T(8,128)S(1)} %get-tuple-element.41.refs_1_, f32[584,128]{1,0:T(8,128)S(1)} %get-tuple-element.42.refs_2_, ...), custom_call_target="tpu_custom_call" | custom-call | tf_op jit(solution)/shard_map/frame/pallas_call | solution.py:783
  24.8 2.8 %collective-permute-done.6.refs_3_ = f32[104,128]{1,0:T(8,128)S(1)} collective-permute-done((f32[104,128]{1,0:T(8,128)S(1)}, f32[104,128]{1,0:T(8,128)S(1)}, u32[]{:S(2)}, u32[]{:S(2)}) %collective-permute-start.6) | collective-permute-done | bytes 53280 | tf_op jit(solution)/shard_map/ppermute | solution.py:795
  28.6 1.6 %collective-permute-start.8 = (f32[160,128]{1,0:T(8,128)S(1)}, f32[160,128]{1,0:T(8,128)S(1)}, u32[]{:S(2)}, u32[]{:S(2)}) collective-permute-start(f32[160,128]{1,0:T(8,128)S(1)} %get-tuple-element.56), channel_id=1, source_target_pairs={{0,16},{4,20},{8,24},{12,28},{16,0},{20,4},{24,8},{28,12},{1,17},{... | collective-permute-start | bytes 245768 | tf_op jit(solution)/shard_map/ppermute | solution.py:809
  31.1 3.1 %collective-permute-start.10 = (f32[160,128]{1,0:T(8,128)S(1)}, f32[160,128]{1,0:T(8,128)S(1)}, u32[]{:S(2)}, u32[]{:S(2)}) collective-permute-start(f32[160,128]{1,0:T(8,128)S(1)} %get-tuple-element.58), channel_id=1, source_target_pairs={{0,24},{4,28},{8,16},{12,20},{16,8},{20,12},{24,0},{28,4},{1,25},{... | collective-permute-start | bytes 245768 | tf_op jit(solution)/shard_map/ppermute | solution.py:809
  34.2 1.2 %collective-permute-start.11 = (f32[160,128]{1,0:T(8,128)S(1)}, f32[160,128]{1,0:T(8,128)S(1)}, u32[]{:S(2)}, u32[]{:S(2)}) collective-permute-start(f32[160,128]{1,0:T(8,128)S(1)} %get-tuple-element.51.refs_3_), channel_id=1, source_target_pairs={{0,28},{4,24},{8,20},{12,16},{16,12},{20,8},{24,4},{28,0},{1,29},{... | collective-permute-start | bytes 245768 | tf_op jit(solution)/shard_map/ppermute | solution.py:809
  35.4 4.3 %first_inner.1 = (f32[4608,128]{1,0:T(8,128)S(1)}, f32[8,24,24,128]{3,2,1,0:T(8,128)S(1)}, f32[7680,128]{1,0:T(8,128)S(1)}, f32[12480,128]{1,0:T(8,128)S(1)}) custom-call(f32[288]{0:T(512)S(1)} %copy-done.3, f32[7,8,128]{2,1,0:T(8,128)S(1)} %copy-done.1, f32[4608,128]{1,0:T(8,128)S(1)} %get-tuple-element.45.refs_2_, f32[160,128]{1,0:T(8,128)S(1)} %get-tuple-element.51.refs_3_), custom_call_target="tpu_custom_call" | custom-call | tf_op jit(solution)/shard_map/first_inner/pallas_call | solution.py:821
  40.0 1.5 %collective-permute-done.11.refs_13_ = f32[160,128]{1,0:T(8,128)S(1)} collective-permute-done((f32[160,128]{1,0:T(8,128)S(1)}, f32[160,128]{1,0:T(8,128)S(1)}, u32[]{:S(2)}, u32[]{:S(2)}) %collective-permute-start.11) | collective-permute-done | bytes 81952 | tf_op jit(solution)/shard_map/ppermute | solution.py:809
  41.5 2.6 %first_edge.1 = (f32[4608,128]{1,0:T(8,128)S(1)}, f32[8,24,24,128]{3,2,1,0:T(8,128)S(1)}, f32[7680,128]{1,0:T(8,128)S(1)}, f32[12480,128]{1,0:T(8,128)S(1)}, f32...) custom-call(s32[8,128]{1,0:T(8,128)S(1)} %get-tuple-element.40.refs_, ...), custom_call_target="tpu_custom_call", output_to_operand_aliasing={{0}: (6, {}), {1}: (7, {}), {2}: (8, {}), {3}: (9, {})} | custom-call | tf_op jit(solution)/shard_map/first_edge/pallas_call | solution.py:829
  44.2 1.7 %collective-permute-start.14 = (f32[104,128]{1,0:T(8,128)S(1)}, f32[104,128]{1,0:T(8,128)S(1)}, u32[]{:S(2)}, u32[]{:S(2)}) collective-permute-start(f32[104,128]{1,0:T(8,128)S(1)} %get-tuple-element.64), channel_id=1, source_target_pairs={{0,3},{1,2},{2,1},{3,0},{4,7},{5,6},{6,5},{7,4},{8,11},{9,10},{10,... | collective-permute-start | bytes 159752 | tf_op jit(solution)/shard_map/ppermute | solution.py:795
  46.0 2.9 %collective-permute-done.13.refs_3_ = f32[104,128]{1,0:T(8,128)S(1)} collective-permute-done((f32[104,128]{1,0:T(8,128)S(1)}, f32[104,128]{1,0:T(8,128)S(1)}, u32[]{:S(2)}, u32[]{:S(2)}) %collective-permute-start.13) | collective-permute-done | bytes 53280 | tf_op jit(solution)/shard_map/ppermute | solution.py:795
  49.6 1.4 %collective-permute-start.15 = (f32[160,128]{1,0:T(8,128)S(1)}, f32[160,128]{1,0:T(8,128)S(1)}, u32[]{:S(2)}, u32[]{:S(2)}) collective-permute-start(f32[160,128]{1,0:T(8,128)S(1)} %get-tuple-element.69), channel_id=1, source_target_pairs={{0,16},{4,20},{8,24},{12,28},{16,0},{20,4},{24,8},{28,12},{1,17},{... | collective-permute-start | bytes 245768 | tf_op jit(solution)/shard_map/ppermute | solution.py:809
  51.0 1.5 %collective-permute-start.16 = (f32[160,128]{1,0:T(8,128)S(1)}, f32[160,128]{1,0:T(8,128)S(1)}, u32[]{:S(2)}, u32[]{:S(2)}) collective-permute-start(f32[160,128]{1,0:T(8,128)S(1)} %get-tuple-element.70), channel_id=1, source_target_pairs={{0,20},{4,16},{8,28},{12,24},{16,4},{20,0},{24,12},{28,8},{1,21},{... | collective-permute-start | bytes 245768 | tf_op jit(solution)/shard_map/ppermute | solution.py:809
  52.5 2.3 %collective-permute-start.17 = (f32[160,128]{1,0:T(8,128)S(1)}, f32[160,128]{1,0:T(8,128)S(1)}, u32[]{:S(2)}, u32[]{:S(2)}) collective-permute-start(f32[160,128]{1,0:T(8,128)S(1)} %get-tuple-element.71), channel_id=1, source_target_pairs={{0,24},{4,28},{8,16},{12,20},{16,8},{20,12},{24,0},{28,4},{1,25},{... | collective-permute-start | bytes 245768 | tf_op jit(solution)/shard_map/ppermute | solution.py:809
  54.8 1.6 %collective-permute-start.18 = (f32[160,128]{1,0:T(8,128)S(1)}, f32[160,128]{1,0:T(8,128)S(1)}, u32[]{:S(2)}, u32[]{:S(2)}) collective-permute-start(f32[160,128]{1,0:T(8,128)S(1)} %get-tuple-element.65.refs_4_), channel_id=1, source_target_pairs={{0,28},{4,24},{8,20},{12,16},{16,12},{20,8},{24,4},{28,0},{1,29},{... | collective-permute-start | bytes 245768 | tf_op jit(solution)/shard_map/ppermute | solution.py:809
  56.4 3.3 %second_inner.1 = (f32[2048,128]{1,0:T(8,128)S(1)}, f32[7680,128]{1,0:T(8,128)S(1)}, f32[12480,128]{1,0:T(8,128)S(1)}) custom-call(f32[288]{0:T(512)S(1)} %copy-done.3, f32[7,8,128]{2,1,0:T(8,128)S(1)} %copy-done.1, f32[4608,128]{1,0:T(8,128)S(1)} %get-tuple-element.60.refs_2_, f32[8,24,24,128]{3,2,1,0:T(8,128)S(1)} %get-tuple-element.59.refs_3_, ...), custom_call_target="tpu_custom_call" | custom-call | tf_op jit(solution)/shard_map/second_inner/pallas_call | solution.py:842
  59.8 2.5 %collective-permute-done.17.refs_9_ = f32[160,128]{1,0:T(8,128)S(1)} collective-permute-done((f32[160,128]{1,0:T(8,128)S(1)}, f32[160,128]{1,0:T(8,128)S(1)}, u32[]{:S(2)}, u32[]{:S(2)}) %collective-permute-start.17) | collective-permute-done | bytes 81952 | tf_op jit(solution)/shard_map/ppermute | solution.py:809
  62.3 3.0 %second_edge.1 = (f32[7680,128]{1,0:T(8,128)S(1)}, f32[12480,128]{1,0:T(8,128)S(1)}, f32[2048,128]{1,0:T(8,128)}) custom-call(s32[8,128]{1,0:T(8,128)S(1)} %get-tuple-element.39.refs_3_.refs_0_, f32[288]{0:T(512)S(1)} %copy-done.3, f32[7,8,128]{2,1,0:T(8,128)S(1)} %copy-done.1, ...), custom_call_target="tpu_custom_call", output_to_operand_aliasing={{0}: (5, {}), {1}: (6, {})} | custom-call | tf_op jit(solution)/shard_map/second_edge/pallas_call | solution.py:850
  (42 shorter events, 10.2 us)
Async XLA Ops:
  0.0 35.4 %copy-start.1 = (f32[7,8,128]{2,1,0:T(8,128)S(1)}, f32[7,8,128]{2,1,0:T(8,128)}, u32[]{:S(2)}) copy-start(f32[7,8,128]{2,1,0:T(8,128)} %constant.36.clone.refs_1_.refs_5_.refs_2_) | copy-start | bytes 86020
  0.0 35.4 %copy-start.3 = (f32[288]{0:T(512)S(1)}, f32[288]{0:T(512)}, u32[]{:S(2)}) copy-start(f32[288]{0:T(512)} %constant.35.clone.refs_0_.refs_4_.refs_1_) | copy-start | bytes 3460
  0.0 21.6 %copy-start = (f32[1,16,16,8,128]{4,3,2,1,0:T(8,128)S(1)}, f32[1,16,16,8,128]{4,3,2,1,0:T(8,128)}, u32[]{:S(2)}) copy-start(f32[1,16,16,8,128]{4,3,2,1,0:T(8,128)} %param.9) | copy-start | bytes 3145732
  1.2 9.4 %collective-permute-start.1 = (f32[512,128]{1,0:T(8,128)S(1)}, f32[512,128]{1,0:T(8,128)S(1)}, u32[]{:S(2)}, u32[]{:S(2)}) collective-permute-start(f32[512,128]{1,0:T(8,128)S(1)} %bitcast.20), channel_id=1, source_target_pairs={{0,4},{1,5},{2,6},{3,7},{4,0},{5,1},{6,2},{7,3},{8,12},{9,13},{10,... | collective-permute-start | bytes 786440 | tf_op jit(solution)/shard_map/ppermute | solution.py:733
  4.3 6.3 %collective-permute-start.2 = (f32[512,128]{1,0:T(8,128)S(1)}, f32[512,128]{1,0:T(8,128)S(1)}, u32[]{:S(2)}, u32[]{:S(2)}) collective-permute-start(f32[512,128]{1,0:T(8,128)S(1)} %bitcast.19), channel_id=1, source_target_pairs={{0,1},{1,0},{2,3},{3,2},{4,8},{5,9},{6,10},{7,11},{8,4},{9,5},{10,... | collective-permute-start | bytes 786440 | tf_op jit(solution)/shard_map/ppermute | solution.py:734
  10.7 10.9 %collective-permute-start.3 = (f32[768,128]{1,0:T(8,128)S(1)}, f32[768,128]{1,0:T(8,128)S(1)}, u32[]{:S(2)}, u32[]{:S(2)}) collective-permute-start(f32[768,128]{1,0:T(8,128)S(1)} %get-tuple-element.43), channel_id=1, source_target_pairs={{0,1},{1,0},{2,3},{3,2},{4,5},{5,4},{6,7},{7,6},{8,9},{9,8},{10,11... | collective-permute-start | bytes 1179656 | tf_op jit(solution)/shard_map/ppermute | solution.py:779
  10.8 10.9 %collective-permute-start.4 = (f32[768,128]{1,0:T(8,128)S(1)}, f32[768,128]{1,0:T(8,128)S(1)}, u32[]{:S(2)}, u32[]{:S(2)}) collective-permute-start(f32[768,128]{1,0:T(8,128)S(1)} %get-tuple-element.44), channel_id=1, source_target_pairs={{0,4},{1,2},{2,1},{3,7},{4,0},{5,6},{6,5},{7,3},{8,12},{9,10},{10,... | collective-permute-start | bytes 1179656 | tf_op jit(solution)/shard_map/ppermute | solution.py:780
  14.5 3.6 %collective-permute-start = (s32[2]{0:T(128)S(1)}, s32[2]{0:T(128)S(1)}, u32[]{:S(2)}, u32[]{:S(2)}) collective-permute-start(s32[2]{0:T(128)S(1)} %slice_reduce_fusion.refs_0_), channel_id=1, source_target_pairs={{0,16},{16,0},{1,17},{17,1},{2,18},{18,2},{3,19},{19,3},{4,20},{20... | collective-permute-start | bytes 32 | tf_op jit(solution)/shard_map/ppermute | solution.py:725
  18.1 0.7 %copy-start.2 = (s32[3,8,128]{2,1,0:T(8,128)S(1)}, s32[3,8,128]{2,1,0:T(8,128)}, u32[]{:S(2)}) copy-start(s32[3,8,128]{2,1,0:T(8,128)} %constant.34.clone.refs_3_.refs_4_) | copy-start | bytes 36868
  18.8 0.7 %copy-start.4 = (s32[3,8,128]{2,1,0:T(8,128)S(1)}, s32[3,8,128]{2,1,0:T(8,128)}, u32[]{:S(2)}) copy-start(s32[3,8,128]{2,1,0:T(8,128)} %constant.33.clone.refs_2_) | copy-start | bytes 36868
  22.9 1.9 %collective-permute-start.5 = (f32[104,128]{1,0:T(8,128)S(1)}, f32[104,128]{1,0:T(8,128)S(1)}, u32[]{:S(2)}, u32[]{:S(2)}) collective-permute-start(f32[104,128]{1,0:T(8,128)S(1)} %get-tuple-element.48), channel_id=1, source_target_pairs={{0,1},{1,0},{2,3},{3,2},{4,5},{5,4},{6,7},{7,6},{8,9},{9,8},{10,11... | collective-permute-start | bytes 159752 | tf_op jit(solution)/shard_map/ppermute | solution.py:795
  23.0 4.7 %collective-permute-start.6 = (f32[104,128]{1,0:T(8,128)S(1)}, f32[104,128]{1,0:T(8,128)S(1)}, u32[]{:S(2)}, u32[]{:S(2)}) collective-permute-start(f32[104,128]{1,0:T(8,128)S(1)} %get-tuple-element.49), channel_id=1, source_target_pairs={{0,2},{1,3},{2,0},{3,1},{4,6},{5,7},{6,4},{7,5},{8,10},{9,11},{10,... | collective-permute-start | bytes 159752 | tf_op jit(solution)/shard_map/ppermute | solution.py:795
  23.8 4.1 %collective-permute-start.7 = (f32[104,128]{1,0:T(8,128)S(1)}, f32[104,128]{1,0:T(8,128)S(1)}, u32[]{:S(2)}, u32[]{:S(2)}) collective-permute-start(f32[104,128]{1,0:T(8,128)S(1)} %get-tuple-element.50), channel_id=1, source_target_pairs={{0,3},{1,2},{2,1},{3,0},{4,7},{5,6},{6,5},{7,4},{8,11},{9,10},{10,... | collective-permute-start | bytes 159752 | tf_op jit(solution)/shard_map/ppermute | solution.py:795
  28.6 11.1 %collective-permute-start.8 = (f32[160,128]{1,0:T(8,128)S(1)}, f32[160,128]{1,0:T(8,128)S(1)}, u32[]{:S(2)}, u32[]{:S(2)}) collective-permute-start(f32[160,128]{1,0:T(8,128)S(1)} %get-tuple-element.56), channel_id=1, source_target_pairs={{0,16},{4,20},{8,24},{12,28},{16,0},{20,4},{24,8},{28,12},{1,17},{... | collective-permute-start | bytes 245768 | tf_op jit(solution)/shard_map/ppermute | solution.py:809
  30.1 9.5 %collective-permute-start.9 = (f32[160,128]{1,0:T(8,128)S(1)}, f32[160,128]{1,0:T(8,128)S(1)}, u32[]{:S(2)}, u32[]{:S(2)}) collective-permute-start(f32[160,128]{1,0:T(8,128)S(1)} %get-tuple-element.57), channel_id=1, source_target_pairs={{0,20},{4,16},{8,28},{12,24},{16,4},{20,0},{24,12},{28,8},{1,21},{... | collective-permute-start | bytes 245768 | tf_op jit(solution)/shard_map/ppermute | solution.py:809
  31.1 8.9 %collective-permute-start.10 = (f32[160,128]{1,0:T(8,128)S(1)}, f32[160,128]{1,0:T(8,128)S(1)}, u32[]{:S(2)}, u32[]{:S(2)}) collective-permute-start(f32[160,128]{1,0:T(8,128)S(1)} %get-tuple-element.58), channel_id=1, source_target_pairs={{0,24},{4,28},{8,16},{12,20},{16,8},{20,12},{24,0},{28,4},{1,25},{... | collective-permute-start | bytes 245768 | tf_op jit(solution)/shard_map/ppermute | solution.py:809
  34.2 7.2 %collective-permute-start.11 = (f32[160,128]{1,0:T(8,128)S(1)}, f32[160,128]{1,0:T(8,128)S(1)}, u32[]{:S(2)}, u32[]{:S(2)}) collective-permute-start(f32[160,128]{1,0:T(8,128)S(1)} %get-tuple-element.51.refs_3_), channel_id=1, source_target_pairs={{0,28},{4,24},{8,20},{12,16},{16,12},{20,8},{24,4},{28,0},{1,29},{... | collective-permute-start | bytes 245768 | tf_op jit(solution)/shard_map/ppermute | solution.py:809
  44.0 1.9 %collective-permute-start.12 = (f32[104,128]{1,0:T(8,128)S(1)}, f32[104,128]{1,0:T(8,128)S(1)}, u32[]{:S(2)}, u32[]{:S(2)}) collective-permute-start(f32[104,128]{1,0:T(8,128)S(1)} %get-tuple-element.62), channel_id=1, source_target_pairs={{0,1},{1,0},{2,3},{3,2},{4,5},{5,4},{6,7},{7,6},{8,9},{9,8},{10,11... | collective-permute-start | bytes 159752 | tf_op jit(solution)/shard_map/ppermute | solution.py:795
  44.1 4.8 %collective-permute-start.13 = (f32[104,128]{1,0:T(8,128)S(1)}, f32[104,128]{1,0:T(8,128)S(1)}, u32[]{:S(2)}, u32[]{:S(2)}) collective-permute-start(f32[104,128]{1,0:T(8,128)S(1)} %get-tuple-element.63), channel_id=1, source_target_pairs={{0,2},{1,3},{2,0},{3,1},{4,6},{5,7},{6,4},{7,5},{8,10},{9,11},{10,... | collective-permute-start | bytes 159752 | tf_op jit(solution)/shard_map/ppermute | solution.py:795
  44.2 4.7 %collective-permute-start.14 = (f32[104,128]{1,0:T(8,128)S(1)}, f32[104,128]{1,0:T(8,128)S(1)}, u32[]{:S(2)}, u32[]{:S(2)}) collective-permute-start(f32[104,128]{1,0:T(8,128)S(1)} %get-tuple-element.64), channel_id=1, source_target_pairs={{0,3},{1,2},{2,1},{3,0},{4,7},{5,6},{6,5},{7,4},{8,11},{9,10},{10,... | collective-permute-start | bytes 159752 | tf_op jit(solution)/shard_map/ppermute | solution.py:795
  49.6 10.1 %collective-permute-start.15 = (f32[160,128]{1,0:T(8,128)S(1)}, f32[160,128]{1,0:T(8,128)S(1)}, u32[]{:S(2)}, u32[]{:S(2)}) collective-permute-start(f32[160,128]{1,0:T(8,128)S(1)} %get-tuple-element.69), channel_id=1, source_target_pairs={{0,16},{4,20},{8,24},{12,28},{16,0},{20,4},{24,8},{28,12},{1,17},{... | collective-permute-start | bytes 245768 | tf_op jit(solution)/shard_map/ppermute | solution.py:809
  51.0 8.8 %collective-permute-start.16 = (f32[160,128]{1,0:T(8,128)S(1)}, f32[160,128]{1,0:T(8,128)S(1)}, u32[]{:S(2)}, u32[]{:S(2)}) collective-permute-start(f32[160,128]{1,0:T(8,128)S(1)} %get-tuple-element.70), channel_id=1, source_target_pairs={{0,20},{4,16},{8,28},{12,24},{16,4},{20,0},{24,12},{28,8},{1,21},{... | collective-permute-start | bytes 245768 | tf_op jit(solution)/shard_map/ppermute | solution.py:809
  52.5 9.8 %collective-permute-start.17 = (f32[160,128]{1,0:T(8,128)S(1)}, f32[160,128]{1,0:T(8,128)S(1)}, u32[]{:S(2)}, u32[]{:S(2)}) collective-permute-start(f32[160,128]{1,0:T(8,128)S(1)} %get-tuple-element.71), channel_id=1, source_target_pairs={{0,24},{4,28},{8,16},{12,20},{16,8},{20,12},{24,0},{28,4},{1,25},{... | collective-permute-start | bytes 245768 | tf_op jit(solution)/shard_map/ppermute | solution.py:809
  54.8 7.5 %collective-permute-start.18 = (f32[160,128]{1,0:T(8,128)S(1)}, f32[160,128]{1,0:T(8,128)S(1)}, u32[]{:S(2)}, u32[]{:S(2)}) collective-permute-start(f32[160,128]{1,0:T(8,128)S(1)} %get-tuple-element.65.refs_4_), channel_id=1, source_target_pairs={{0,28},{4,24},{8,20},{12,16},{16,12},{20,8},{24,4},{28,0},{1,29},{... | collective-permute-start | bytes 245768 | tf_op jit(solution)/shard_map/ppermute | solution.py:809
  (2 other events, 1.4 us)

commit v8 on v7

--- a/solution.py
+++ b/solution.py
@@ -18,6 +18,19 @@
 HALO = 4
 PAD = 8
 TILE = 8
+
+
+def hardest_first(step):
+    return -step.bit_length(), step
+
+
+def start_order(first, count):
+    return sorted(range(first, count), key=hardest_first)
+
+
+def by_step(first, refs):
+    order = start_order(first, first + len(refs))
+    return [refs[order.index(step)] for step in range(first, first + len(refs))]
 
 
 def is_power_of_two(count):
@@ -190,14 +203,6 @@
     return -(-count // 1024) * 8
 
 
-def table_ids(outer, inner, slots):
-    rows = padded_rows(outer * inner * slots)
-    flat = np.minimum(np.arange(rows * 128), outer * inner * slots - 1)
-    return np.stack(
-        [flat // (inner * slots), flat // slots % inner, flat % slots]
-    ).reshape(3, rows, 128).astype(np.int32)
-
-
 def whole(count):
     return [pl.BlockSpec(memory_space=pltpu.VMEM)] * count
 
@@ -220,10 +225,7 @@
     return pl.ds(pl.multiple_of(index * TILE, TILE), count * TILE)
 
 
-def table_kernel(
-    loop, pitch, cell_ref, other_ref, send_id_ref, swap_id_ref, got_id_ref,
-    base_ref, weight_ref, turn_ref, send_ref, swap_ref, receive_ref, corner_ref, spread_ref,
-):
+def weight_kernel(loop, base_ref, weight_ref, turn_ref, corner_ref, spread_ref):
     entries = loop.entries
     diagonal = lax.broadcasted_iota(jnp.int32, (entries, entries), 0) == (
         lax.broadcasted_iota(jnp.int32, (entries, entries), 1)
@@ -236,30 +238,44 @@
         spread_ref[pl.ds(number * entries, entries), :] = jnp.broadcast_to(
             column, (entries, spread_ref.shape[1])
         )
-
+    wide = loop.cols + 2 * HALO
+    corner_ref[0:1, 0:entries] = (
+        base_ref[0:1, :] - lax.axis_index("lat") * loop.rows + HALO - 1
+    ) * wide + (base_ref[1:2, :] - lax.axis_index("lon") * loop.cols + HALO - 1)
+
+
+def digits(shape, outer, inner, slots):
+    flat = lax.broadcasted_iota(jnp.int32, shape, 0) * shape[1] + lax.broadcasted_iota(
+        jnp.int32, shape, 1
+    )
+    high = jnp.zeros(shape, jnp.int32)
+    for n in range(1, outer):
+        high = high + jnp.where(flat >= n * inner * slots, 1, 0)
+    rest = flat - high * (inner * slots)
+    middle = jnp.zeros(shape, jnp.int32)
+    for n in range(1, inner):
+        middle = middle + jnp.where(rest >= n * slots, 1, 0)
+    return high, middle, jnp.minimum(rest - middle * slots, slots - 1)
+
+
+def table_kernel(loop, pitch, cell_ref, other_ref, send_ref, swap_ref, receive_ref):
     lat, lon = lax.axis_index("lat"), lax.axis_index("lon")
     lat_count, lon_count = loop.lat_count, loop.lon_count
-    wide = loop.cols + 2 * HALO
-    base = (base_ref[0:1, :] - lat * loop.rows + HALO - 1) * wide + (
-        base_ref[1:2, :] - lon * loop.cols + HALO - 1
-    )
-    corner_ref[0:1, 0:entries] = base
     mine = loop.position(cell_ref[0], cell_ref[1])
     other = loop.position(other_ref[0], other_ref[1])
 
-    step, _, slot = [send_id_ref[n] for n in range(3)]
+    _, step, slot = digits(send_ref.shape, 1, lon_count, loop.column_slots)
     entry = loop.column_entry(
         to_device(lon, step, lon_count), lat * lon_count + lon, other, slot
     )
     send_ref[...] = loop.wrap(entry)
 
-    lat_step, lon_step, slot = [swap_id_ref[n] for n in range(3)]
+    lat_step, lon_step, slot = digits(swap_ref.shape, lat_count, lon_count, loop.slots)
     donor = lat * lon_count + from_device(lon, lon_step, lon_count)
     here = jnp.full_like(slot, lon)
     ahead = loop.column_slot(to_device(lat, lat_step, lat_count), here, donor, other)
     swap_ref[...] = jnp.minimum(ahead + slot, loop.column_slots - 1)
 
-    lat_step, lon_step, slot = [got_id_ref[n] for n in range(3)]
     donor = from_device(lat, lat_step, lat_count) * lon_count + from_device(
         lon, lon_step, lon_count
     )
@@ -272,7 +288,10 @@
     receive_ref[...] = jnp.where(place < start + span, spot, 0)
 
 
-def strip_kernel(rows, cols, own_even_ref, own_odd_ref, even_ref, odd_ref, *send_refs):
+def strip_kernel(
+    rows, cols, after_ref, own_even_ref, own_odd_ref, even_ref, odd_ref, *send_refs
+):
+    del after_ref
     lat_even = lax.rem(lax.axis_index("lat"), 2) == 0
     lon_even = lax.rem(lax.axis_index("lon"), 2) == 0
     high = cols - HALO
@@ -334,7 +353,7 @@
 
 def frame_kernel(loop, *refs):
     rim, refs = refs[:3], refs[3:]
-    state_ref, lat_even_ref, lat_odd_ref, lon_even_ref, lon_odd_ref, frame_ref = refs[:6]
+    state_ref, lat_even_ref, lat_odd_ref, lon_odd_ref, lon_even_ref, frame_ref = refs[:6]
     send_refs, value_ref = refs[6:-1], refs[-1]
     rows, cols = loop.rows, loop.cols
     wide = cols + 2 * HALO
@@ -383,7 +402,8 @@
 
 
 def swap_kernel(loop, table_ref, *refs):
-    got_refs, out_refs = refs[: loop.lon_count], refs[loop.lon_count :]
+    got_refs = [refs[0]] + by_step(1, refs[1 : loop.lon_count])
+    out_refs = refs[loop.lon_count :]
     for lat_step in range(loop.lat_count):
         for lon_step in range(loop.lon_count):
             for slot in range(loop.slots):
@@ -419,6 +439,7 @@
 
     def scatter(self, receive_ref, got_refs):
         arrivals = self.loop.lon_count * self.loop.slots
+        got_refs = by_step(0, got_refs)
         for lat_step in range(self.loop.lat_count):
             for place in range(arrivals):
                 spot = lookup(receive_ref, lat_step * arrivals + place)
@@ -733,33 +754,31 @@
     lat_even = lax.ppermute(send_even, everyone, swap_route(0, lat_count, lon_count, True))
     lat_odd = lax.ppermute(send_odd, everyone, swap_route(1, lat_count, lon_count, True))
 
-    send_ids = table_ids(1, lon_count, loop.column_slots)[[1, 0, 2]]
-    got_ids = table_ids(lat_count, lon_count, loop.slots)
     angle = rim_angle[0]
-    turn = jnp.stack([jnp.cos(angle), jnp.sin(angle)])
-    send_table, swap_table, receive_table, corner_table, spread_weights = pl.pallas_call(
-        lambda *refs: table_kernel(loop, pitch, *refs),
+    corner_table, spread_weights = pl.pallas_call(
+        lambda *refs: weight_kernel(loop, *refs),
         out_shape=[
-            jax.ShapeDtypeStruct(ids.shape[1:], jnp.int32) for ids in (send_ids, got_ids, got_ids)
-        ]
-        + [
             jax.ShapeDtypeStruct((8, -(-entries // 128) * 128), jnp.int32),
             jax.ShapeDtypeStruct((18 * entries + TILE, levels), f32),
         ],
-        in_specs=scalars(2) + whole(6),
-        out_specs=whole(5),
+        in_specs=whole(3),
+        out_specs=whole(2),
+        compiler_params=grant(4),
+        name="weights",
+    )(rim_base[0].T, rim_weight[0].T, jnp.stack([jnp.cos(angle), jnp.sin(angle)]))
+    send_count = lon_count * loop.column_slots
+    got_count = lat_count * lon_count * loop.slots
+    send_table, swap_table, receive_table = pl.pallas_call(
+        lambda *refs: table_kernel(loop, pitch, *refs),
+        out_shape=[
+            jax.ShapeDtypeStruct((padded_rows(count), 128), jnp.int32)
+            for count in (send_count, got_count, got_count)
+        ],
+        in_specs=scalars(2),
+        out_specs=whole(3),
         compiler_params=grant(4),
         name="tables",
-    )(
-        first_cell,
-        other_cell,
-        jnp.asarray(send_ids),
-        jnp.asarray(got_ids),
-        jnp.asarray(got_ids),
-        rim_base[0].T,
-        rim_weight[0].T,
-        turn,
-    )
+    )(first_cell, other_cell)
     rim = (send_table, corner_table, spread_weights)
     factors = jnp.asarray(row_factors(rows, lat_count, loop.nth, loop.nph))
     radial = jnp.asarray(radial_factors(levels, loop.nth))
@@ -771,13 +790,13 @@
     strip_even, strip_odd = pl.pallas_call(
         lambda *refs: strip_kernel(rows, cols, *refs),
         out_shape=[tile_array(tall * HALO)] * 2,
-        in_specs=whole(4),
+        in_specs=whole(5),
         out_specs=whole(2),
         compiler_params=grant(4),
         name="strips",
-    )(own_even, own_odd, lat_even, lat_odd)
+    )(corner_table, own_even, own_odd, lat_even, lat_odd)
+    lon_odd = lax.ppermute(strip_odd, everyone, swap_route(1, lat_count, lon_count, False))
     lon_even = lax.ppermute(strip_even, everyone, swap_route(0, lat_count, lon_count, False))
-    lon_odd = lax.ppermute(strip_odd, everyone, swap_route(1, lat_count, lon_count, False))
 
     packed_shapes = [tile_array(loop.column_slots)] * lon_count
     frame, *packed = pl.pallas_call(
@@ -788,12 +807,12 @@
         scratch_shapes=[pltpu.VMEM((entries * TILE, levels), f32)],
         compiler_params=grant(8),
         name="frame",
-    )(*rim, block, lat_even, lat_odd, lon_even, lon_odd)
+    )(*rim, block, lat_even, lat_odd, lon_odd, lon_even)
 
     def first_round(packed):
         got = [packed[0]] + [
             lax.ppermute(packed[step], "lon", lon_route(step, lon_count))
-            for step in range(1, lon_count)
+            for step in start_order(1, lon_count)
         ]
         return pl.pallas_call(
             lambda *refs: swap_kernel(loop, *refs),
@@ -807,7 +826,7 @@
     def second_round(turned):
         return [
             lax.ppermute(turned[step], ("panel", "lat"), lat_route(step, lat_count))
-            for step in range(lat_count)
+            for step in start_order(0, lat_count)
         ]
 
     planes = [
@@ -825,7 +844,7 @@
         out_specs=whole(4),
         compiler_params=grant(4),
         name="first_inner",
-    )(factors, radial, frame, turned[-1])
+    )(factors, radial, frame, turned[0])
     frame, rate, _, _, *packed = pl.pallas_call(
         lambda *refs: first_edge_kernel(loop, *refs),
         out_shape=[tile_array(tall * wide), rates] + planes + packed_shapes,
@@ -846,7 +865,7 @@
         out_specs=whole(3),
         compiler_params=grant(4),
         name="second_inner",
-    )(factors, radial, frame, rate, turned[-1])
+    )(factors, radial, frame, rate, turned[0])
     _, _, change = pl.pallas_call(
         lambda *refs: second_edge_kernel(loop, *refs),
         out_shape=planes + [tile_array(rows * cols)],

time: 65.7 us -> 64.4 us (0.980)
  local copies, waits for them, and re-layouts: 4.29 us -> 2.87 us
    ppermute x8, waiting for transfers between devices: 4.32 us -> 6.77 us  [second_round(): lax.ppermute(turned[step], ('panel', 'lat'), lat_route(step, lat_count))]
    ppermute x1, waiting for transfers between devices: 5.22 us -> 2.96 us  [per_device(): lax.ppermute(send_even, everyone, swap_route(0, lat_count, lon_count, True))]
    ppermute x6, waiting for transfers between devices: 6.06 us -> 4.43 us  [first_round(): lax.ppermute(packed[step], 'lon', lon_route(step, lon_count))]
    unnamed x14 -> x10, local copies, waits for them, and re-layouts: 2.8 us -> 1.38 us
    ppermute x1, waiting for transfers between devices: 0.01 us -> 0.73 us  [per_device(): lax.ppermute(strip_odd, everyone, swap_route(1, lat_count, lon_count, Fal...]
    ppermute x1, waiting for transfers between devices: 1.37 us -> 2.08 us  [per_device(): other_cell = lax.ppermute(first_cell, 'panel', [(0, 1), (1, 0)])]
  transfers between devices with their start and end apart: 19 -> 19, of which waited for: 9 -> 12; matrix products, arithmetic and copies ran while one was open for 4% -> 4% of each run, Pallas kernels for 13% -> 13%
where the time goes in v8:
time: 64.4 us; the launch traced here: 64.1 us
  starting transfers between devices  25.4 us (39%)
  waiting for transfers between devices  17 us (26%)
  Pallas kernels  16.5 us (26%)
  local copies, waits for them, and re-layouts  2.87 us (4%)
  other arithmetic  2.25 us (3%)
    ppermute x8, starting transfers between devices, second_round(): lax.ppermute(turned[step], ('panel', 'lat'), lat_route(step, lat_count))  13.4 us
    ppermute x8, waiting for transfers between devices, second_round(): lax.ppermute(turned[step], ('panel', 'lat'), lat_route(step, lat_count))  6.77 us
    ppermute x6, waiting for transfers between devices, first_round(): lax.ppermute(packed[step], 'lon', lon_route(step, lon_count))  4.43 us
    ppermute x6, starting transfers between devices, first_round(): lax.ppermute(packed[step], 'lon', lon_route(step, lon_count))  4.41 us
    pallas_call x1, Pallas kernels, per_device(): pl.pallas_call(lambda *refs: first_inner_kernel(loop, *refs), out_shape=[...  4.25 us
    pallas_call x1, Pallas kernels, per_device(): pl.pallas_call(lambda *refs: second_inner_kernel(loop, *refs), out_shape=...  3.32 us
    ppermute x1, starting transfers between devices, per_device(): lax.ppermute(send_even, everyone, swap_route(0, lat_count, lon_count, True))  3.13 us
    ppermute x1, waiting for transfers between devices, per_device(): lax.ppermute(send_even, everyone, swap_route(0, lat_count, lon_count, True))  2.96 us
  transfers between devices with their start and end apart: 19, of which 12 were waited for; matrix products, arithmetic and copies ran while one was open for 4% of the time, Pallas kernels for 13%

profile of v8, /device:TPU:0, one launch (start us, length us, event | category | flops | bytes accessed | tf_op | source)
XLA Modules:
  0.0 64.1 jit_solution(1927573770699201499)
XLA Ops:
  0.0 1.2 %slice_select_fusion.2 = (f32[1,4,16,8,128]{4,3,2,1,0:T(8,128)S(1)}, f32[1,4,16,8,128]{4,3,2,1,0:T(8,128)S(1)}) fusion(f32[1,16,16,8,128]{4,3,2,1,0:T(8,128)} %param.7, pred[]{:T(512)S(6)} %eq.9), kind=kLoop, calls=%fused_computation.2 | loop fusion | flops 131072 | bytes 1048577 | tf_op jit(solution)/shard_map/jit(_where)/select_n | solution.py:753
  1.2 3.1 %collective-permute-start.1 = (f32[512,128]{1,0:T(8,128)S(1)}, f32[512,128]{1,0:T(8,128)S(1)}, u32[]{:S(2)}, u32[]{:S(2)}) collective-permute-start(f32[512,128]{1,0:T(8,128)S(1)} %bitcast.20), channel_id=1, source_target_pairs={{0,4},{1,5},{2,6},{3,7},{4,0},{5,1},{6,2},{7,3},{8,12},{9,13},{10,... | collective-permute-start | bytes 786440 | tf_op jit(solution)/shard_map/ppermute | solution.py:754
  7.7 3.0 %collective-permute-done.1.refs_3_.refs_4_ = f32[512,128]{1,0:T(8,128)S(1)} collective-permute-done((f32[512,128]{1,0:T(8,128)S(1)}, f32[512,128]{1,0:T(8,128)S(1)}, u32[]{:S(2)}, u32[]{:S(2)}) %collective-permute-start.1) | collective-permute-done | bytes 262176 | tf_op jit(solution)/shard_map/ppermute | solution.py:754
  10.7 2.9 %collective-permute-start.3 = (f32[768,128]{1,0:T(8,128)S(1)}, f32[768,128]{1,0:T(8,128)S(1)}, u32[]{:S(2)}, u32[]{:S(2)}) collective-permute-start(f32[768,128]{1,0:T(8,128)S(1)} %get-tuple-element.43), channel_id=1, source_target_pairs={{0,4},{1,2},{2,1},{3,7},{4,0},{5,6},{6,5},{7,3},{8,12},{9,10},{10,... | collective-permute-start | bytes 1179656 | tf_op jit(solution)/shard_map/ppermute | solution.py:798
  14.4 1.5 %collective-permute-start = (s32[2]{0:T(128)S(1)}, s32[2]{0:T(128)S(1)}, u32[]{:S(2)}, u32[]{:S(2)}) collective-permute-start(s32[2]{0:T(128)S(1)} %slice_reduce_fusion.refs_0_), channel_id=1, source_target_pairs={{0,16},{16,0},{1,17},{17,1},{2,18},{18,2},{3,19},{19,3},{4,20},{20... | collective-permute-start | bytes 32 | tf_op jit(solution)/shard_map/ppermute | solution.py:746
  15.9 2.1 %collective-permute-done.refs_1_ = s32[2]{0:T(128)S(1)} collective-permute-done((s32[2]{0:T(128)S(1)}, s32[2]{0:T(128)S(1)}, u32[]{:S(2)}, u32[]{:S(2)}) %collective-permute-start) | collective-permute-done | bytes 40 | tf_op jit(solution)/shard_map/ppermute | solution.py:746
  19.4 1.2 %frame.1 = (f32[4608,128]{1,0:T(8,128)S(1)}, f32[104,128]{1,0:T(8,128)S(1)}, f32[104,128]{1,0:T(8,128)S(1)}, f32[104,128]{1,0:T(8,128)S(1)}, f32[104,128]{1,0:T(8,128)S(1)}) custom-call(s32[8,128]{1,0:T(8,128)S(1)} %get-tuple-element.40.refs_0_, s32[8,128]{1,0:T(8,128)S(1)} %get-tuple-element.41.refs_0_.refs_1_, f32[584,128]{1,0:T(8,128)S(1)} %get-tuple-element.42.refs_2_, ...), custom_call_target="tpu_custom_call" | custom-call | tf_op jit(solution)/shard_map/frame/pallas_call | solution.py:802
  21.0 1.8 %collective-permute-start.7 = (f32[104,128]{1,0:T(8,128)S(1)}, f32[104,128]{1,0:T(8,128)S(1)}, u32[]{:S(2)}, u32[]{:S(2)}) collective-permute-start(f32[104,128]{1,0:T(8,128)S(1)} %get-tuple-element.50), channel_id=1, source_target_pairs={{0,1},{1,0},{2,3},{3,2},{4,5},{5,4},{6,7},{7,6},{8,9},{9,8},{10,11... | collective-permute-start | bytes 159752 | tf_op jit(solution)/shard_map/ppermute | solution.py:814
  22.8 2.3 %collective-permute-done.5.refs_2_ = f32[104,128]{1,0:T(8,128)S(1)} collective-permute-done((f32[104,128]{1,0:T(8,128)S(1)}, f32[104,128]{1,0:T(8,128)S(1)}, u32[]{:S(2)}, u32[]{:S(2)}) %collective-permute-start.5) | collective-permute-done | bytes 53280 | tf_op jit(solution)/shard_map/ppermute | solution.py:814
  25.8 4.9 %collective-permute-start.8 = (f32[160,128]{1,0:T(8,128)S(1)}, f32[160,128]{1,0:T(8,128)S(1)}, u32[]{:S(2)}, u32[]{:S(2)}) collective-permute-start(f32[160,128]{1,0:T(8,128)S(1)} %get-tuple-element.56), channel_id=1, source_target_pairs={{0,24},{4,28},{8,16},{12,20},{16,8},{20,12},{24,0},{28,4},{1,25},{... | collective-permute-start | bytes 245768 | tf_op jit(solution)/shard_map/ppermute | solution.py:828
  30.6 1.1 %collective-permute-start.9 = (f32[160,128]{1,0:T(8,128)S(1)}, f32[160,128]{1,0:T(8,128)S(1)}, u32[]{:S(2)}, u32[]{:S(2)}) collective-permute-start(f32[160,128]{1,0:T(8,128)S(1)} %get-tuple-element.57), channel_id=1, source_target_pairs={{0,28},{4,24},{8,20},{12,16},{16,12},{20,8},{24,4},{28,0},{1,29},{... | collective-permute-start | bytes 245768 | tf_op jit(solution)/shard_map/ppermute | solution.py:828
  31.8 1.5 %collective-permute-start.11 = (f32[160,128]{1,0:T(8,128)S(1)}, f32[160,128]{1,0:T(8,128)S(1)}, u32[]{:S(2)}, u32[]{:S(2)}) collective-permute-start(f32[160,128]{1,0:T(8,128)S(1)} %get-tuple-element.51.refs_3_), channel_id=1, source_target_pairs={{0,16},{4,20},{8,24},{12,28},{16,0},{20,4},{24,8},{28,12},{1,17},{... | collective-permute-start | bytes 245768 | tf_op jit(solution)/shard_map/ppermute | solution.py:828
  33.3 4.3 %first_inner.1 = (f32[4608,128]{1,0:T(8,128)S(1)}, f32[8,24,24,128]{3,2,1,0:T(8,128)S(1)}, f32[7680,128]{1,0:T(8,128)S(1)}, f32[12480,128]{1,0:T(8,128)S(1)}) custom-call(f32[288]{0:T(512)S(1)} %copy-done.2, f32[7,8,128]{2,1,0:T(8,128)S(1)} %copy-done.1, f32[4608,128]{1,0:T(8,128)S(1)} %get-tuple-element.45.refs_2_, f32[160,128]{1,0:T(8,128)S(1)} %get-tuple-element.51.refs_3_), custom_call_target="tpu_custom_call" | custom-call | tf_op jit(solution)/shard_map/first_inner/pallas_call | solution.py:840
  38.8 1.2 %collective-permute-done.11.refs_13_ = f32[160,128]{1,0:T(8,128)S(1)} collective-permute-done((f32[160,128]{1,0:T(8,128)S(1)}, f32[160,128]{1,0:T(8,128)S(1)}, u32[]{:S(2)}, u32[]{:S(2)}) %collective-permute-start.11) | collective-permute-done | bytes 81952 | tf_op jit(solution)/shard_map/ppermute | solution.py:828
  40.0 2.6 %first_edge.1 = (f32[4608,128]{1,0:T(8,128)S(1)}, f32[8,24,24,128]{3,2,1,0:T(8,128)S(1)}, f32[7680,128]{1,0:T(8,128)S(1)}, f32[12480,128]{1,0:T(8,128)S(1)}, f32...) custom-call(s32[8,128]{1,0:T(8,128)S(1)} %get-tuple-element.40.refs_, ...), custom_call_target="tpu_custom_call", output_to_operand_aliasing={{0}: (6, {}), {1}: (7, {}), {2}: (8, {}), {3}: (9, {})} | custom-call | tf_op jit(solution)/shard_map/first_edge/pallas_call | solution.py:848
  43.0 1.8 %collective-permute-start.14 = (f32[104,128]{1,0:T(8,128)S(1)}, f32[104,128]{1,0:T(8,128)S(1)}, u32[]{:S(2)}, u32[]{:S(2)}) collective-permute-start(f32[104,128]{1,0:T(8,128)S(1)} %get-tuple-element.64), channel_id=1, source_target_pairs={{0,1},{1,0},{2,3},{3,2},{4,5},{5,4},{6,7},{7,6},{8,9},{9,8},{10,11... | collective-permute-start | bytes 159752 | tf_op jit(solution)/shard_map/ppermute | solution.py:814
  44.8 2.2 %collective-permute-done.12.refs_2_ = f32[104,128]{1,0:T(8,128)S(1)} collective-permute-done((f32[104,128]{1,0:T(8,128)S(1)}, f32[104,128]{1,0:T(8,128)S(1)}, u32[]{:S(2)}, u32[]{:S(2)}) %collective-permute-start.12) | collective-permute-done | bytes 53280 | tf_op jit(solution)/shard_map/ppermute | solution.py:814
  47.6 2.5 %collective-permute-start.15 = (f32[160,128]{1,0:T(8,128)S(1)}, f32[160,128]{1,0:T(8,128)S(1)}, u32[]{:S(2)}, u32[]{:S(2)}) collective-permute-start(f32[160,128]{1,0:T(8,128)S(1)} %get-tuple-element.69), channel_id=1, source_target_pairs={{0,24},{4,28},{8,16},{12,20},{16,8},{20,12},{24,0},{28,4},{1,25},{... | collective-permute-start | bytes 245768 | tf_op jit(solution)/shard_map/ppermute | solution.py:828
  50.1 1.5 %collective-permute-start.16 = (f32[160,128]{1,0:T(8,128)S(1)}, f32[160,128]{1,0:T(8,128)S(1)}, u32[]{:S(2)}, u32[]{:S(2)}) collective-permute-start(f32[160,128]{1,0:T(8,128)S(1)} %get-tuple-element.70), channel_id=1, source_target_pairs={{0,28},{4,24},{8,20},{12,16},{16,12},{20,8},{24,4},{28,0},{1,29},{... | collective-permute-start | bytes 245768 | tf_op jit(solution)/shard_map/ppermute | solution.py:828
  52.2 1.3 %collective-permute-start.18 = (f32[160,128]{1,0:T(8,128)S(1)}, f32[160,128]{1,0:T(8,128)S(1)}, u32[]{:S(2)}, u32[]{:S(2)}) collective-permute-start(f32[160,128]{1,0:T(8,128)S(1)} %get-tuple-element.65.refs_4_), channel_id=1, source_target_pairs={{0,16},{4,20},{8,24},{12,28},{16,0},{20,4},{24,8},{28,12},{1,17},{... | collective-permute-start | bytes 245768 | tf_op jit(solution)/shard_map/ppermute | solution.py:828
  53.5 3.3 %second_inner.1 = (f32[2048,128]{1,0:T(8,128)S(1)}, f32[7680,128]{1,0:T(8,128)S(1)}, f32[12480,128]{1,0:T(8,128)S(1)}) custom-call(f32[288]{0:T(512)S(1)} %copy-done.2, f32[7,8,128]{2,1,0:T(8,128)S(1)} %copy-done.1, f32[4608,128]{1,0:T(8,128)S(1)} %get-tuple-element.60.refs_2_, f32[8,24,24,128]{3,2,1,0:T(8,128)S(1)} %get-tuple-element.59.refs_3_, ...), custom_call_target="tpu_custom_call" | custom-call | tf_op jit(solution)/shard_map/second_inner/pallas_call | solution.py:861
  58.2 1.4 %collective-permute-done.17.refs_9_ = f32[160,128]{1,0:T(8,128)S(1)} collective-permute-done((f32[160,128]{1,0:T(8,128)S(1)}, f32[160,128]{1,0:T(8,128)S(1)}, u32[]{:S(2)}, u32[]{:S(2)}) %collective-permute-start.17) | collective-permute-done | bytes 81952 | tf_op jit(solution)/shard_map/ppermute | solution.py:828
  59.6 1.6 %collective-permute-done.18.refs_10_ = f32[160,128]{1,0:T(8,128)S(1)} collective-permute-done((f32[160,128]{1,0:T(8,128)S(1)}, f32[160,128]{1,0:T(8,128)S(1)}, u32[]{:S(2)}, u32[]{:S(2)}) %collective-permute-start.18) | collective-permute-done | bytes 81952 | tf_op jit(solution)/shard_map/ppermute | solution.py:828
  61.2 3.0 %second_edge.1 = (f32[7680,128]{1,0:T(8,128)S(1)}, f32[12480,128]{1,0:T(8,128)S(1)}, f32[2048,128]{1,0:T(8,128)}) custom-call(s32[8,128]{1,0:T(8,128)S(1)} %get-tuple-element.39.refs_3_.refs_0_, f32[288]{0:T(512)S(1)} %copy-done.2, f32[7,8,128]{2,1,0:T(8,128)S(1)} %copy-done.1, ...), custom_call_target="tpu_custom_call", output_to_operand_aliasing={{0}: (5, {}), {1}: (6, {})} | custom-call | tf_op jit(solution)/shard_map/second_edge/pallas_call | solution.py:869
  (39 shorter events, 10.8 us)
Async XLA Ops:
  0.0 33.3 %copy-start.1 = (f32[7,8,128]{2,1,0:T(8,128)S(1)}, f32[7,8,128]{2,1,0:T(8,128)}, u32[]{:S(2)}) copy-start(f32[7,8,128]{2,1,0:T(8,128)} %constant.30.clone.refs_1_.refs_5_.refs_2_) | copy-start | bytes 86020
  0.0 33.3 %copy-start.2 = (f32[288]{0:T(512)S(1)}, f32[288]{0:T(512)}, u32[]{:S(2)}) copy-start(f32[288]{0:T(512)} %constant.29.clone.refs_0_.refs_4_.refs_1_) | copy-start | bytes 3460
  0.0 19.4 %copy-start = (f32[1,16,16,8,128]{4,3,2,1,0:T(8,128)S(1)}, f32[1,16,16,8,128]{4,3,2,1,0:T(8,128)}, u32[]{:S(2)}) copy-start(f32[1,16,16,8,128]{4,3,2,1,0:T(8,128)} %param.7) | copy-start | bytes 3145732
  1.2 9.4 %collective-permute-start.1 = (f32[512,128]{1,0:T(8,128)S(1)}, f32[512,128]{1,0:T(8,128)S(1)}, u32[]{:S(2)}, u32[]{:S(2)}) collective-permute-start(f32[512,128]{1,0:T(8,128)S(1)} %bitcast.20), channel_id=1, source_target_pairs={{0,4},{1,5},{2,6},{3,7},{4,0},{5,1},{6,2},{7,3},{8,12},{9,13},{10,... | collective-permute-start | bytes 786440 | tf_op jit(solution)/shard_map/ppermute | solution.py:754
  4.3 6.3 %collective-permute-start.2 = (f32[512,128]{1,0:T(8,128)S(1)}, f32[512,128]{1,0:T(8,128)S(1)}, u32[]{:S(2)}, u32[]{:S(2)}) collective-permute-start(f32[512,128]{1,0:T(8,128)S(1)} %bitcast.19), channel_id=1, source_target_pairs={{0,1},{1,0},{2,3},{3,2},{4,8},{5,9},{6,10},{7,11},{8,4},{9,5},{10,... | collective-permute-start | bytes 786440 | tf_op jit(solution)/shard_map/ppermute | solution.py:755
  5.0 0.7 %copy-start.3 = (f32[1,32,16]{1,2,0:T(8,128)S(1)}, f32[1,32,16]{1,2,0:T(8,128)}, u32[]{:S(2)}) copy-start(f32[1,32,16]{1,2,0:T(8,128)} %param.9) | copy-start | bytes 6148
  5.7 0.7 %copy-start.4 = (s32[1,32,2]{1,2,0:T(2,128)S(1)}, s32[1,32,2]{1,2,0:T(2,128)}, u32[]{:S(2)}) copy-start(s32[1,32,2]{1,2,0:T(2,128)} %param.8) | copy-start | bytes 772
  10.7 8.7 %collective-permute-start.3 = (f32[768,128]{1,0:T(8,128)S(1)}, f32[768,128]{1,0:T(8,128)S(1)}, u32[]{:S(2)}, u32[]{:S(2)}) collective-permute-start(f32[768,128]{1,0:T(8,128)S(1)} %get-tuple-element.43), channel_id=1, source_target_pairs={{0,4},{1,2},{2,1},{3,7},{4,0},{5,6},{6,5},{7,3},{8,12},{9,10},{10,... | collective-permute-start | bytes 1179656 | tf_op jit(solution)/shard_map/ppermute | solution.py:798
  13.6 5.8 %collective-permute-start.4 = (f32[768,128]{1,0:T(8,128)S(1)}, f32[768,128]{1,0:T(8,128)S(1)}, u32[]{:S(2)}, u32[]{:S(2)}) collective-permute-start(f32[768,128]{1,0:T(8,128)S(1)} %get-tuple-element.44), channel_id=1, source_target_pairs={{0,1},{1,0},{2,3},{3,2},{4,5},{5,4},{6,7},{7,6},{8,9},{9,8},{10,11... | collective-permute-start | bytes 1179656 | tf_op jit(solution)/shard_map/ppermute | solution.py:799
  14.4 3.6 %collective-permute-start = (s32[2]{0:T(128)S(1)}, s32[2]{0:T(128)S(1)}, u32[]{:S(2)}, u32[]{:S(2)}) collective-permute-start(s32[2]{0:T(128)S(1)} %slice_reduce_fusion.refs_0_), channel_id=1, source_target_pairs={{0,16},{16,0},{1,17},{17,1},{2,18},{18,2},{3,19},{19,3},{4,20},{20... | collective-permute-start | bytes 32 | tf_op jit(solution)/shard_map/ppermute | solution.py:746
  20.6 4.5 %collective-permute-start.5 = (f32[104,128]{1,0:T(8,128)S(1)}, f32[104,128]{1,0:T(8,128)S(1)}, u32[]{:S(2)}, u32[]{:S(2)}) collective-permute-start(f32[104,128]{1,0:T(8,128)S(1)} %get-tuple-element.48), channel_id=1, source_target_pairs={{0,2},{1,3},{2,0},{3,1},{4,6},{5,7},{6,4},{7,5},{8,10},{9,11},{10,... | collective-permute-start | bytes 159752 | tf_op jit(solution)/shard_map/ppermute | solution.py:814
  20.9 4.1 %collective-permute-start.6 = (f32[104,128]{1,0:T(8,128)S(1)}, f32[104,128]{1,0:T(8,128)S(1)}, u32[]{:S(2)}, u32[]{:S(2)}) collective-permute-start(f32[104,128]{1,0:T(8,128)S(1)} %get-tuple-element.49), channel_id=1, source_target_pairs={{0,3},{1,2},{2,1},{3,0},{4,7},{5,6},{6,5},{7,4},{8,11},{9,10},{10,... | collective-permute-start | bytes 159752 | tf_op jit(solution)/shard_map/ppermute | solution.py:814
  21.0 4.1 %collective-permute-start.7 = (f32[104,128]{1,0:T(8,128)S(1)}, f32[104,128]{1,0:T(8,128)S(1)}, u32[]{:S(2)}, u32[]{:S(2)}) collective-permute-start(f32[104,128]{1,0:T(8,128)S(1)} %get-tuple-element.50), channel_id=1, source_target_pairs={{0,1},{1,0},{2,3},{3,2},{4,5},{5,4},{6,7},{7,6},{8,9},{9,8},{10,11... | collective-permute-start | bytes 159752 | tf_op jit(solution)/shard_map/ppermute | solution.py:814
  25.8 11.8 %collective-permute-start.8 = (f32[160,128]{1,0:T(8,128)S(1)}, f32[160,128]{1,0:T(8,128)S(1)}, u32[]{:S(2)}, u32[]{:S(2)}) collective-permute-start(f32[160,128]{1,0:T(8,128)S(1)} %get-tuple-element.56), channel_id=1, source_target_pairs={{0,24},{4,28},{8,16},{12,20},{16,8},{20,12},{24,0},{28,4},{1,25},{... | collective-permute-start | bytes 245768 | tf_op jit(solution)/shard_map/ppermute | solution.py:828
  30.6 7.8 %collective-permute-start.9 = (f32[160,128]{1,0:T(8,128)S(1)}, f32[160,128]{1,0:T(8,128)S(1)}, u32[]{:S(2)}, u32[]{:S(2)}) collective-permute-start(f32[160,128]{1,0:T(8,128)S(1)} %get-tuple-element.57), channel_id=1, source_target_pairs={{0,28},{4,24},{8,20},{12,16},{16,12},{20,8},{24,4},{28,0},{1,29},{... | collective-permute-start | bytes 245768 | tf_op jit(solution)/shard_map/ppermute | solution.py:828
  31.8 7.0 %collective-permute-start.10 = (f32[160,128]{1,0:T(8,128)S(1)}, f32[160,128]{1,0:T(8,128)S(1)}, u32[]{:S(2)}, u32[]{:S(2)}) collective-permute-start(f32[160,128]{1,0:T(8,128)S(1)} %get-tuple-element.58), channel_id=1, source_target_pairs={{0,20},{4,16},{8,28},{12,24},{16,4},{20,0},{24,12},{28,8},{1,21},{... | collective-permute-start | bytes 245768 | tf_op jit(solution)/shard_map/ppermute | solution.py:828
  31.8 8.2 %collective-permute-start.11 = (f32[160,128]{1,0:T(8,128)S(1)}, f32[160,128]{1,0:T(8,128)S(1)}, u32[]{:S(2)}, u32[]{:S(2)}) collective-permute-start(f32[160,128]{1,0:T(8,128)S(1)} %get-tuple-element.51.refs_3_), channel_id=1, source_target_pairs={{0,16},{4,20},{8,24},{12,28},{16,0},{20,4},{24,8},{28,12},{1,17},{... | collective-permute-start | bytes 245768 | tf_op jit(solution)/shard_map/ppermute | solution.py:828
  42.6 4.4 %collective-permute-start.12 = (f32[104,128]{1,0:T(8,128)S(1)}, f32[104,128]{1,0:T(8,128)S(1)}, u32[]{:S(2)}, u32[]{:S(2)}) collective-permute-start(f32[104,128]{1,0:T(8,128)S(1)} %get-tuple-element.62), channel_id=1, source_target_pairs={{0,2},{1,3},{2,0},{3,1},{4,6},{5,7},{6,4},{7,5},{8,10},{9,11},{10,... | collective-permute-start | bytes 159752 | tf_op jit(solution)/shard_map/ppermute | solution.py:814
  42.8 4.1 %collective-permute-start.13 = (f32[104,128]{1,0:T(8,128)S(1)}, f32[104,128]{1,0:T(8,128)S(1)}, u32[]{:S(2)}, u32[]{:S(2)}) collective-permute-start(f32[104,128]{1,0:T(8,128)S(1)} %get-tuple-element.63), channel_id=1, source_target_pairs={{0,3},{1,2},{2,1},{3,0},{4,7},{5,6},{6,5},{7,4},{8,11},{9,10},{10,... | collective-permute-start | bytes 159752 | tf_op jit(solution)/shard_map/ppermute | solution.py:814
  43.0 4.0 %collective-permute-start.14 = (f32[104,128]{1,0:T(8,128)S(1)}, f32[104,128]{1,0:T(8,128)S(1)}, u32[]{:S(2)}, u32[]{:S(2)}) collective-permute-start(f32[104,128]{1,0:T(8,128)S(1)} %get-tuple-element.64), channel_id=1, source_target_pairs={{0,1},{1,0},{2,3},{3,2},{4,5},{5,4},{6,7},{7,6},{8,9},{9,8},{10,11... | collective-permute-start | bytes 159752 | tf_op jit(solution)/shard_map/ppermute | solution.py:814
  47.6 10.3 %collective-permute-start.15 = (f32[160,128]{1,0:T(8,128)S(1)}, f32[160,128]{1,0:T(8,128)S(1)}, u32[]{:S(2)}, u32[]{:S(2)}) collective-permute-start(f32[160,128]{1,0:T(8,128)S(1)} %get-tuple-element.69), channel_id=1, source_target_pairs={{0,24},{4,28},{8,16},{12,20},{16,8},{20,12},{24,0},{28,4},{1,25},{... | collective-permute-start | bytes 245768 | tf_op jit(solution)/shard_map/ppermute | solution.py:828
  50.1 8.1 %collective-permute-start.16 = (f32[160,128]{1,0:T(8,128)S(1)}, f32[160,128]{1,0:T(8,128)S(1)}, u32[]{:S(2)}, u32[]{:S(2)}) collective-permute-start(f32[160,128]{1,0:T(8,128)S(1)} %get-tuple-element.70), channel_id=1, source_target_pairs={{0,28},{4,24},{8,20},{12,16},{16,12},{20,8},{24,4},{28,0},{1,29},{... | collective-permute-start | bytes 245768 | tf_op jit(solution)/shard_map/ppermute | solution.py:828
  51.6 8.0 %collective-permute-start.17 = (f32[160,128]{1,0:T(8,128)S(1)}, f32[160,128]{1,0:T(8,128)S(1)}, u32[]{:S(2)}, u32[]{:S(2)}) collective-permute-start(f32[160,128]{1,0:T(8,128)S(1)} %get-tuple-element.71), channel_id=1, source_target_pairs={{0,20},{4,16},{8,28},{12,24},{16,4},{20,0},{24,12},{28,8},{1,21},{... | collective-permute-start | bytes 245768 | tf_op jit(solution)/shard_map/ppermute | solution.py:828
  52.2 9.0 %collective-permute-start.18 = (f32[160,128]{1,0:T(8,128)S(1)}, f32[160,128]{1,0:T(8,128)S(1)}, u32[]{:S(2)}, u32[]{:S(2)}) collective-permute-start(f32[160,128]{1,0:T(8,128)S(1)} %get-tuple-element.65.refs_4_), channel_id=1, source_target_pairs={{0,16},{4,20},{8,24},{12,28},{16,0},{20,4},{24,8},{28,12},{1,17},{... | collective-permute-start | bytes 245768 | tf_op jit(solution)/shard_map/ppermute | solution.py:828

commit v9 on v8

--- a/solution.py
+++ b/solution.py
@@ -94,6 +94,8 @@
         self.slots = -(-max(corner, one_row, one_col) // self.blocks)
         self.half = -(-one_row // self.blocks)
         side = 4 * (cols + HALO) + 2 * self.nth
+        leads = [2 * (cols + HALO) + 2 * (n * rows - HALO) for n in range(1, lat_count)]
+        self.even_leads = all(lead % self.blocks == 0 for lead in leads)
         self.column_slots = max(-(-side // self.blocks), 2 * self.half)
 
     def position(self, row, col):
@@ -189,12 +191,16 @@
         skipped = jnp.where(jnp.logical_not(side) & (slot >= self.half), self.half, 0)
         return jnp.where(lower, bottom, top) + slot - skipped
 
-    def column_slot(self, lat, lon, donor, offset):
+    def column_slot(self, lat, lon, donor=None, offset=None):
         side = (lon == 0) | (lon == self.lon_count - 1)
         start, _ = self.stretch(lat, lon)
-        ahead = self.first_entry(start, donor, offset) - self.first_entry(
-            jnp.where(lon == 0, self.bottom_start(lon), self.top_start(lon)), donor, offset
-        )
+        column = jnp.where(lon == 0, self.bottom_start(lon), self.top_start(lon))
+        if donor is None:
+            ahead = lax.div(start - column, jnp.int32(self.blocks))
+        else:
+            ahead = self.first_entry(start, donor, offset) - self.first_entry(
+                column, donor, offset
+            )
         middle = jnp.where(lat == self.lat_count - 1, self.half, 0)
         return jnp.where(side, jnp.maximum(ahead, 0), middle)
 
@@ -351,44 +357,52 @@
             send_ref[tiles(slot, 1), :] = value_ref[tiles(entry, 1), :]
 
 
+def middle_kernel(rows, cols, state_ref, lat_even_ref, lat_odd_ref, frame_ref):
+    wide = cols + 2 * HALO
+    lat_even = lax.rem(lax.axis_index("lat"), 2) == 0
+
+    def copy_rows(first, count, source):
+        for row in range(count):
+            frame_ref[tiles((first + row) * wide + HALO, cols), :] = source[
+                tiles(row * cols, cols), :
+            ]
+
+    copy_rows(HALO, rows, state_ref)
+
+    @pl.when(lat_even)
+    def _():
+        copy_rows(0, HALO, lat_odd_ref)
+        copy_rows(HALO + rows, HALO, lat_even_ref)
+
+    @pl.when(jnp.logical_not(lat_even))
+    def _():
+        copy_rows(0, HALO, lat_even_ref)
+        copy_rows(HALO + rows, HALO, lat_odd_ref)
+
+
 def frame_kernel(loop, *refs):
     rim, refs = refs[:3], refs[3:]
-    state_ref, lat_even_ref, lat_odd_ref, lon_odd_ref, lon_even_ref, frame_ref = refs[:6]
-    send_refs, value_ref = refs[6:-1], refs[-1]
+    lon_odd_ref, lon_even_ref, _, frame_ref = refs[:4]
+    send_refs, value_ref = refs[4:-1], refs[-1]
     rows, cols = loop.rows, loop.cols
     wide = cols + 2 * HALO
-    lat_even = lax.rem(lax.axis_index("lat"), 2) == 0
-    lon_even = lax.rem(lax.axis_index("lon"), 2) == 0
-
-    def copy_rows(first, count, source, left, width):
-        for row in range(count):
-            frame_ref[tiles((first + row) * wide + left, width), :] = source[
-                tiles(row * width, width), :
-            ]
-
-    copy_rows(HALO, rows, state_ref, HALO, cols)
-
-    @pl.when(lat_even)
-    def _():
-        copy_rows(0, HALO, lat_odd_ref, HALO, cols)
-        copy_rows(HALO + rows, HALO, lat_even_ref, HALO, cols)
-
-    @pl.when(jnp.logical_not(lat_even))
-    def _():
-        copy_rows(0, HALO, lat_even_ref, HALO, cols)
-        copy_rows(HALO + rows, HALO, lat_odd_ref, HALO, cols)
+    lat, lon = lax.axis_index("lat"), lax.axis_index("lon")
+    lon_even = lax.rem(lon, 2) == 0
+
+    def copy_columns(source, left):
+        for row in range(rows + 2 * HALO):
+            frame_ref[tiles(row * wide + left, HALO), :] = source[tiles(row * HALO, HALO), :]
 
     @pl.when(lon_even)
     def _():
-        copy_rows(0, rows + 2 * HALO, lon_odd_ref, 0, HALO)
-        copy_rows(0, rows + 2 * HALO, lon_even_ref, HALO + cols, HALO)
+        copy_columns(lon_odd_ref, 0)
+        copy_columns(lon_even_ref, HALO + cols)
 
     @pl.when(jnp.logical_not(lon_even))
     def _():
-        copy_rows(0, rows + 2 * HALO, lon_even_ref, 0, HALO)
-        copy_rows(0, rows + 2 * HALO, lon_odd_ref, HALO + cols, HALO)
-
-    lat, lon = lax.axis_index("lat"), lax.axis_index("lon")
+        copy_columns(lon_even_ref, 0)
+        copy_columns(lon_odd_ref, HALO + cols)
+
     zeros = jnp.zeros((HALO * TILE, frame_ref.shape[1]), jnp.float32)
     for at_row, top in ((lat == 0, 0), (lat == loop.lat_count - 1, HALO + rows)):
         for at_col, left in ((lon == 0, 0), (lon == loop.lon_count - 1, HALO + cols)):
@@ -401,14 +415,24 @@
     mix_and_pack(loop, wide, rim, frame_ref, value_ref, send_refs)
 
 
-def swap_kernel(loop, table_ref, *refs):
+def swap_kernel(loop, *refs):
+    table_ref = None
+    if not loop.even_leads:
+        table_ref, refs = refs[0], refs[1:]
     got_refs = [refs[0]] + by_step(1, refs[1 : loop.lon_count])
     out_refs = refs[loop.lon_count :]
+    lat, lon = lax.axis_index("lat"), lax.axis_index("lon")
     for lat_step in range(loop.lat_count):
+        if loop.even_leads:
+            lead = loop.column_slot(to_device(lat, lat_step, loop.lat_count), lon)
+            lead = jnp.minimum(lead, loop.column_slots - loop.slots)
         for lon_step in range(loop.lon_count):
             for slot in range(loop.slots):
                 place = lon_step * loop.slots + slot
-                source = lookup(table_ref, lat_step * loop.lon_count * loop.slots + place)
+                if loop.even_leads:
+                    source = lead + slot
+                else:
+                    source = lookup(table_ref, lat_step * loop.lon_count * loop.slots + place)
                 out_refs[lat_step][tiles(place, 1), :] = got_refs[lon_step][tiles(source, 1), :]
 
 
@@ -780,6 +804,7 @@
         name="tables",
     )(first_cell, other_cell)
     rim = (send_table, corner_table, spread_weights)
+    swap_tables = () if loop.even_leads else (swap_table,)
     factors = jnp.asarray(row_factors(rows, lat_count, loop.nth, loop.nph))
     radial = jnp.asarray(radial_factors(levels, loop.nth))
 
@@ -798,16 +823,25 @@
     lon_odd = lax.ppermute(strip_odd, everyone, swap_route(1, lat_count, lon_count, False))
     lon_even = lax.ppermute(strip_even, everyone, swap_route(0, lat_count, lon_count, False))
 
+    frame = pl.pallas_call(
+        lambda *refs: middle_kernel(rows, cols, *refs[1:]),
+        out_shape=tile_array(tall * wide),
+        in_specs=whole(4),
+        out_specs=whole(1)[0],
+        compiler_params=grant(4),
+        name="middle",
+    )(strip_even, block, lat_even, lat_odd)
     packed_shapes = [tile_array(loop.column_slots)] * lon_count
     frame, *packed = pl.pallas_call(
         lambda *refs: frame_kernel(loop, *refs),
         out_shape=[tile_array(tall * wide)] + packed_shapes,
-        in_specs=scalars(2) + whole(6),
+        in_specs=scalars(2) + whole(4),
         out_specs=whole(1 + lon_count),
         scratch_shapes=[pltpu.VMEM((entries * TILE, levels), f32)],
-        compiler_params=grant(8),
+        input_output_aliases={5: 0},
+        compiler_params=grant(4),
         name="frame",
-    )(*rim, block, lat_even, lat_odd, lon_odd, lon_even)
+    )(*rim, lon_odd, lon_even, frame)
 
     def first_round(packed):
         got = [packed[0]] + [
@@ -817,11 +851,11 @@
         return pl.pallas_call(
             lambda *refs: swap_kernel(loop, *refs),
             out_shape=[tile_array(lon_count * loop.slots)] * lat_count,
-            in_specs=scalars(1) + whole(lon_count),
+            in_specs=scalars(len(swap_tables)) + whole(lon_count),
             out_specs=whole(lat_count),
             compiler_params=grant(4),
             name="swap",
-        )(swap_table, *got)
+        )(*swap_tables, *got)
 
     def second_round(turned):
         return [

time: 64.4 us -> 63 us (0.978)
  waiting for transfers between devices: 17 us -> 16.2 us
  Pallas kernels: 16.5 us -> 15.8 us
    pallas_call x2, Pallas kernels: 1.33 us -> 0.07 us  [first_round(): pl.pallas_call(lambda *refs: swap_kernel(loop, *refs), out_shape=[tile_ar...]
    ppermute x1, waiting for transfers between devices: 0.73 us -> 0.04 us  [per_device(): lax.ppermute(strip_odd, everyone, swap_route(1, lat_count, lon_count, Fal...]
  transfers between devices with their start and end apart: 19 -> 19, of which waited for: 12 -> 11; matrix products, arithmetic and copies ran while one was open for 4% -> 4% of each run, Pallas kernels for 13% -> 14%
where the time goes in v9:
time: 63 us; the launch traced here: 62.8 us
  starting transfers between devices  25.4 us (40%)
  waiting for transfers between devices  16.2 us (26%)
  Pallas kernels  15.8 us (25%)
  local copies, waits for them, and re-layouts  2.87 us (5%)
  other arithmetic  2.24 us (4%)
    ppermute x8, starting transfers between devices, second_round(): lax.ppermute(turned[step], ('panel', 'lat'), lat_route(step, lat_count))  13.4 us
    ppermute x8, waiting for transfers between devices, second_round(): lax.ppermute(turned[step], ('panel', 'lat'), lat_route(step, lat_count))  6.71 us
    ppermute x6, waiting for transfers between devices, first_round(): lax.ppermute(packed[step], 'lon', lon_route(step, lon_count))  4.42 us
    ppermute x6, starting transfers between devices, first_round(): lax.ppermute(packed[step], 'lon', lon_route(step, lon_count))  4.41 us
    pallas_call x1, Pallas kernels, per_device(): pl.pallas_call(lambda *refs: first_inner_kernel(loop, *refs), out_shape=[...  4.26 us
    pallas_call x1, Pallas kernels, per_device(): pl.pallas_call(lambda *refs: second_inner_kernel(loop, *refs), out_shape=...  3.36 us
    ppermute x1, starting transfers between devices, per_device(): lax.ppermute(send_even, everyone, swap_route(0, lat_count, lon_count, True))  3.12 us
    pallas_call x1, Pallas kernels, per_device(): pl.pallas_call(lambda *refs: second_edge_kernel(loop, *refs), out_shape=p...  2.97 us
  transfers between devices with their start and end apart: 19, of which 11 were waited for; matrix products, arithmetic and copies ran while one was open for 4% of the time, Pallas kernels for 14%

profile of v9, /device:TPU:0, one launch (start us, length us, event | category | flops | bytes accessed | tf_op | source)
XLA Modules:
  0.0 62.8 jit_solution(14744723327829198473)
XLA Ops:
  0.0 1.2 %slice_select_fusion.2 = (f32[1,4,16,8,128]{4,3,2,1,0:T(8,128)S(1)}, f32[1,4,16,8,128]{4,3,2,1,0:T(8,128)S(1)}) fusion(f32[1,16,16,8,128]{4,3,2,1,0:T(8,128)} %param.7, pred[]{:T(512)S(6)} %eq.10), kind=kLoop, calls=%fused_computation.2 | loop fusion | flops 131072 | bytes 1048577 | tf_op jit(solution)/shard_map/jit(_where)/select_n | solution.py:777
  1.2 3.1 %collective-permute-start.1 = (f32[512,128]{1,0:T(8,128)S(1)}, f32[512,128]{1,0:T(8,128)S(1)}, u32[]{:S(2)}, u32[]{:S(2)}) collective-permute-start(f32[512,128]{1,0:T(8,128)S(1)} %bitcast.20), channel_id=1, source_target_pairs={{0,4},{1,5},{2,6},{3,7},{4,0},{5,1},{6,2},{7,3},{8,12},{9,13},{10,... | collective-permute-start | bytes 786440 | tf_op jit(solution)/shard_map/ppermute | solution.py:778
  7.6 3.0 %collective-permute-done.1.refs_3_.refs_2_ = f32[512,128]{1,0:T(8,128)S(1)} collective-permute-done((f32[512,128]{1,0:T(8,128)S(1)}, f32[512,128]{1,0:T(8,128)S(1)}, u32[]{:S(2)}, u32[]{:S(2)}) %collective-permute-start.1) | collective-permute-done | bytes 262176 | tf_op jit(solution)/shard_map/ppermute | solution.py:778
  10.7 2.9 %collective-permute-start.3 = (f32[768,128]{1,0:T(8,128)S(1)}, f32[768,128]{1,0:T(8,128)S(1)}, u32[]{:S(2)}, u32[]{:S(2)}) collective-permute-start(f32[768,128]{1,0:T(8,128)S(1)} %get-tuple-element.42), channel_id=1, source_target_pairs={{0,4},{1,2},{2,1},{3,7},{4,0},{5,6},{6,5},{7,3},{8,12},{9,10},{10,... | collective-permute-start | bytes 1179656 | tf_op jit(solution)/shard_map/ppermute | solution.py:823
  14.4 1.5 %collective-permute-start = (s32[2]{0:T(128)S(1)}, s32[2]{0:T(128)S(1)}, u32[]{:S(2)}, u32[]{:S(2)}) collective-permute-start(s32[2]{0:T(128)S(1)} %slice_reduce_fusion.refs_0_), channel_id=1, source_target_pairs={{0,16},{16,0},{1,17},{17,1},{2,18},{18,2},{3,19},{19,3},{4,20},{20... | collective-permute-start | bytes 32 | tf_op jit(solution)/shard_map/ppermute | solution.py:770
  15.9 2.1 %collective-permute-done.refs_1_ = s32[2]{0:T(128)S(1)} collective-permute-done((s32[2]{0:T(128)S(1)}, s32[2]{0:T(128)S(1)}, u32[]{:S(2)}, u32[]{:S(2)}) %collective-permute-start) | collective-permute-done | bytes 40 | tf_op jit(solution)/shard_map/ppermute | solution.py:770
  18.0 1.2 %tables.1 = (s32[8,128]{1,0:T(8,128)S(1)}, s32[8,128]{1,0:T(8,128)}, s32[8,128]{1,0:T(8,128)S(1)}) custom-call(s32[2]{0:T(128)S(1)} %slice_reduce_fusion.refs_0_, s32[2]{0:T(128)S(1)} %collective-permute-done.refs_1_), custom_call_target="tpu_custom_call" | custom-call | tf_op jit(solution)/shard_map/tables/pallas_call | solution.py:795
  21.5 1.2 %collective-permute-start.7 = (f32[104,128]{1,0:T(8,128)S(1)}, f32[104,128]{1,0:T(8,128)S(1)}, u32[]{:S(2)}, u32[]{:S(2)}) collective-permute-start(f32[104,128]{1,0:T(8,128)S(1)} %get-tuple-element.48), channel_id=1, source_target_pairs={{0,1},{1,0},{2,3},{3,2},{4,5},{5,4},{6,7},{7,6},{8,9},{9,8},{10,11... | collective-permute-start | bytes 159752 | tf_op jit(solution)/shard_map/ppermute | solution.py:848
  22.7 2.2 %collective-permute-done.5.refs_1_ = f32[104,128]{1,0:T(8,128)S(1)} collective-permute-done((f32[104,128]{1,0:T(8,128)S(1)}, f32[104,128]{1,0:T(8,128)S(1)}, u32[]{:S(2)}, u32[]{:S(2)}) %collective-permute-start.5) | collective-permute-done | bytes 53280 | tf_op jit(solution)/shard_map/ppermute | solution.py:848
  25.0 4.9 %collective-permute-start.8 = (f32[160,128]{1,0:T(8,128)S(1)}, f32[160,128]{1,0:T(8,128)S(1)}, u32[]{:S(2)}, u32[]{:S(2)}) collective-permute-start(f32[160,128]{1,0:T(8,128)S(1)} %get-tuple-element.54), channel_id=1, source_target_pairs={{0,24},{4,28},{8,16},{12,20},{16,8},{20,12},{24,0},{28,4},{1,25},{... | collective-permute-start | bytes 245768 | tf_op jit(solution)/shard_map/ppermute | solution.py:862
  29.9 1.1 %collective-permute-start.9 = (f32[160,128]{1,0:T(8,128)S(1)}, f32[160,128]{1,0:T(8,128)S(1)}, u32[]{:S(2)}, u32[]{:S(2)}) collective-permute-start(f32[160,128]{1,0:T(8,128)S(1)} %get-tuple-element.55), channel_id=1, source_target_pairs={{0,28},{4,24},{8,20},{12,16},{16,12},{20,8},{24,4},{28,0},{1,29},{... | collective-permute-start | bytes 245768 | tf_op jit(solution)/shard_map/ppermute | solution.py:862
  31.0 1.5 %collective-permute-start.11 = (f32[160,128]{1,0:T(8,128)S(1)}, f32[160,128]{1,0:T(8,128)S(1)}, u32[]{:S(2)}, u32[]{:S(2)}) collective-permute-start(f32[160,128]{1,0:T(8,128)S(1)} %get-tuple-element.49.refs_3_), channel_id=1, source_target_pairs={{0,16},{4,20},{8,24},{12,28},{16,0},{20,4},{24,8},{28,12},{1,17},{... | collective-permute-start | bytes 245768 | tf_op jit(solution)/shard_map/ppermute | solution.py:862
  32.5 4.3 %first_inner.1 = (f32[4608,128]{1,0:T(8,128)S(1)}, f32[8,24,24,128]{3,2,1,0:T(8,128)S(1)}, f32[7680,128]{1,0:T(8,128)S(1)}, f32[12480,128]{1,0:T(8,128)S(1)}) custom-call(f32[288]{0:T(512)S(1)} %copy-done.2, f32[7,8,128]{2,1,0:T(8,128)S(1)} %copy-done.1, f32[4608,128]{1,0:T(8,128)S(1)} %get-tuple-element.44.refs_2_, f32[160,128]{1,0:T(8,128)S(1)} %get-tuple-element.49.refs_3_), custom_call_target="tpu_custom_call" | custom-call | tf_op jit(solution)/shard_map/first_inner/pallas_call | solution.py:874
  38.0 1.2 %collective-permute-done.11.refs_13_ = f32[160,128]{1,0:T(8,128)S(1)} collective-permute-done((f32[160,128]{1,0:T(8,128)S(1)}, f32[160,128]{1,0:T(8,128)S(1)}, u32[]{:S(2)}, u32[]{:S(2)}) %collective-permute-start.11) | collective-permute-done | bytes 81952 | tf_op jit(solution)/shard_map/ppermute | solution.py:862
  39.2 2.6 %first_edge.1 = (f32[4608,128]{1,0:T(8,128)S(1)}, f32[8,24,24,128]{3,2,1,0:T(8,128)S(1)}, f32[7680,128]{1,0:T(8,128)S(1)}, f32[12480,128]{1,0:T(8,128)S(1)}, f32...) custom-call(s32[8,128]{1,0:T(8,128)S(1)} %get-tuple-element.39.refs_, ...), custom_call_target="tpu_custom_call", output_to_operand_aliasing={{0}: (6, {}), {1}: (7, {}), {2}: (8, {}), {3}: (9, {})} | custom-call | tf_op jit(solution)/shard_map/first_edge/pallas_call | solution.py:882
  42.2 1.8 %collective-permute-start.14 = (f32[104,128]{1,0:T(8,128)S(1)}, f32[104,128]{1,0:T(8,128)S(1)}, u32[]{:S(2)}, u32[]{:S(2)}) collective-permute-start(f32[104,128]{1,0:T(8,128)S(1)} %get-tuple-element.62), channel_id=1, source_target_pairs={{0,1},{1,0},{2,3},{3,2},{4,5},{5,4},{6,7},{7,6},{8,9},{9,8},{10,11... | collective-permute-start | bytes 159752 | tf_op jit(solution)/shard_map/ppermute | solution.py:848
  44.0 2.2 %collective-permute-done.12.refs_1_ = f32[104,128]{1,0:T(8,128)S(1)} collective-permute-done((f32[104,128]{1,0:T(8,128)S(1)}, f32[104,128]{1,0:T(8,128)S(1)}, u32[]{:S(2)}, u32[]{:S(2)}) %collective-permute-start.12) | collective-permute-done | bytes 53280 | tf_op jit(solution)/shard_map/ppermute | solution.py:848
  46.2 2.5 %collective-permute-start.15 = (f32[160,128]{1,0:T(8,128)S(1)}, f32[160,128]{1,0:T(8,128)S(1)}, u32[]{:S(2)}, u32[]{:S(2)}) collective-permute-start(f32[160,128]{1,0:T(8,128)S(1)} %get-tuple-element.67), channel_id=1, source_target_pairs={{0,24},{4,28},{8,16},{12,20},{16,8},{20,12},{24,0},{28,4},{1,25},{... | collective-permute-start | bytes 245768 | tf_op jit(solution)/shard_map/ppermute | solution.py:862
  48.7 1.5 %collective-permute-start.16 = (f32[160,128]{1,0:T(8,128)S(1)}, f32[160,128]{1,0:T(8,128)S(1)}, u32[]{:S(2)}, u32[]{:S(2)}) collective-permute-start(f32[160,128]{1,0:T(8,128)S(1)} %get-tuple-element.68), channel_id=1, source_target_pairs={{0,28},{4,24},{8,20},{12,16},{16,12},{20,8},{24,4},{28,0},{1,29},{... | collective-permute-start | bytes 245768 | tf_op jit(solution)/shard_map/ppermute | solution.py:862
  50.8 1.3 %collective-permute-start.18 = (f32[160,128]{1,0:T(8,128)S(1)}, f32[160,128]{1,0:T(8,128)S(1)}, u32[]{:S(2)}, u32[]{:S(2)}) collective-permute-start(f32[160,128]{1,0:T(8,128)S(1)} %get-tuple-element.63.refs_4_), channel_id=1, source_target_pairs={{0,16},{4,20},{8,24},{12,28},{16,0},{20,4},{24,8},{28,12},{1,17},{... | collective-permute-start | bytes 245768 | tf_op jit(solution)/shard_map/ppermute | solution.py:862
  52.1 3.4 %second_inner.1 = (f32[2048,128]{1,0:T(8,128)S(1)}, f32[7680,128]{1,0:T(8,128)S(1)}, f32[12480,128]{1,0:T(8,128)S(1)}) custom-call(f32[288]{0:T(512)S(1)} %copy-done.2, f32[7,8,128]{2,1,0:T(8,128)S(1)} %copy-done.1, f32[4608,128]{1,0:T(8,128)S(1)} %get-tuple-element.58.refs_2_, f32[8,24,24,128]{3,2,1,0:T(8,128)S(1)} %get-tuple-element.57.refs_3_, ...), custom_call_target="tpu_custom_call" | custom-call | tf_op jit(solution)/shard_map/second_inner/pallas_call | solution.py:895
  56.8 1.4 %collective-permute-done.17.refs_9_ = f32[160,128]{1,0:T(8,128)S(1)} collective-permute-done((f32[160,128]{1,0:T(8,128)S(1)}, f32[160,128]{1,0:T(8,128)S(1)}, u32[]{:S(2)}, u32[]{:S(2)}) %collective-permute-start.17) | collective-permute-done | bytes 81952 | tf_op jit(solution)/shard_map/ppermute | solution.py:862
  58.2 1.6 %collective-permute-done.18.refs_10_ = f32[160,128]{1,0:T(8,128)S(1)} collective-permute-done((f32[160,128]{1,0:T(8,128)S(1)}, f32[160,128]{1,0:T(8,128)S(1)}, u32[]{:S(2)}, u32[]{:S(2)}) %collective-permute-start.18) | collective-permute-done | bytes 81952 | tf_op jit(solution)/shard_map/ppermute | solution.py:862
  59.8 3.0 %second_edge.1 = (f32[7680,128]{1,0:T(8,128)S(1)}, f32[12480,128]{1,0:T(8,128)S(1)}, f32[2048,128]{1,0:T(8,128)}) custom-call(s32[8,128]{1,0:T(8,128)S(1)} %get-tuple-element.38.refs_3_.refs_0_, f32[288]{0:T(512)S(1)} %copy-done.2, f32[7,8,128]{2,1,0:T(8,128)S(1)} %copy-done.1, ...), custom_call_target="tpu_custom_call", output_to_operand_aliasing={{0}: (5, {}), {1}: (6, {})} | custom-call | tf_op jit(solution)/shard_map/second_edge/pallas_call | solution.py:903
  (40 shorter events, 10.1 us)
Async XLA Ops:
  0.0 19.2 %copy-start = (f32[1,16,16,8,128]{4,3,2,1,0:T(8,128)S(1)}, f32[1,16,16,8,128]{4,3,2,1,0:T(8,128)}, u32[]{:S(2)}) copy-start(f32[1,16,16,8,128]{4,3,2,1,0:T(8,128)} %param.7) | copy-start | bytes 3145732
  1.2 9.4 %collective-permute-start.1 = (f32[512,128]{1,0:T(8,128)S(1)}, f32[512,128]{1,0:T(8,128)S(1)}, u32[]{:S(2)}, u32[]{:S(2)}) collective-permute-start(f32[512,128]{1,0:T(8,128)S(1)} %bitcast.20), channel_id=1, source_target_pairs={{0,4},{1,5},{2,6},{3,7},{4,0},{5,1},{6,2},{7,3},{8,12},{9,13},{10,... | collective-permute-start | bytes 786440 | tf_op jit(solution)/shard_map/ppermute | solution.py:778
  4.3 6.3 %collective-permute-start.2 = (f32[512,128]{1,0:T(8,128)S(1)}, f32[512,128]{1,0:T(8,128)S(1)}, u32[]{:S(2)}, u32[]{:S(2)}) collective-permute-start(f32[512,128]{1,0:T(8,128)S(1)} %bitcast.19), channel_id=1, source_target_pairs={{0,1},{1,0},{2,3},{3,2},{4,8},{5,9},{6,10},{7,11},{8,4},{9,5},{10,... | collective-permute-start | bytes 786440 | tf_op jit(solution)/shard_map/ppermute | solution.py:779
  5.0 0.7 %copy-start.3 = (f32[1,32,16]{1,2,0:T(8,128)S(1)}, f32[1,32,16]{1,2,0:T(8,128)}, u32[]{:S(2)}) copy-start(f32[1,32,16]{1,2,0:T(8,128)} %param.9) | copy-start | bytes 6148
  5.7 0.7 %copy-start.4 = (s32[1,32,2]{1,2,0:T(2,128)S(1)}, s32[1,32,2]{1,2,0:T(2,128)}, u32[]{:S(2)}) copy-start(s32[1,32,2]{1,2,0:T(2,128)} %param.8) | copy-start | bytes 772
  10.7 8.7 %collective-permute-start.3 = (f32[768,128]{1,0:T(8,128)S(1)}, f32[768,128]{1,0:T(8,128)S(1)}, u32[]{:S(2)}, u32[]{:S(2)}) collective-permute-start(f32[768,128]{1,0:T(8,128)S(1)} %get-tuple-element.42), channel_id=1, source_target_pairs={{0,4},{1,2},{2,1},{3,7},{4,0},{5,6},{6,5},{7,3},{8,12},{9,10},{10,... | collective-permute-start | bytes 1179656 | tf_op jit(solution)/shard_map/ppermute | solution.py:823
  13.6 5.8 %collective-permute-start.4 = (f32[768,128]{1,0:T(8,128)S(1)}, f32[768,128]{1,0:T(8,128)S(1)}, u32[]{:S(2)}, u32[]{:S(2)}) collective-permute-start(f32[768,128]{1,0:T(8,128)S(1)} %get-tuple-element.43.refs_0_), channel_id=1, source_target_pairs={{0,1},{1,0},{2,3},{3,2},{4,5},{5,4},{6,7},{7,6},{8,9},{9,8},{10,11... | collective-permute-start | bytes 1179656 | tf_op jit(solution)/shard_map/ppermute | solution.py:824
  14.4 3.6 %collective-permute-start = (s32[2]{0:T(128)S(1)}, s32[2]{0:T(128)S(1)}, u32[]{:S(2)}, u32[]{:S(2)}) collective-permute-start(s32[2]{0:T(128)S(1)} %slice_reduce_fusion.refs_0_), channel_id=1, source_target_pairs={{0,16},{16,0},{1,17},{17,1},{2,18},{18,2},{3,19},{19,3},{4,20},{20... | collective-permute-start | bytes 32 | tf_op jit(solution)/shard_map/ppermute | solution.py:770
  19.2 13.3 %copy-start.1 = (f32[7,8,128]{2,1,0:T(8,128)S(1)}, f32[7,8,128]{2,1,0:T(8,128)}, u32[]{:S(2)}) copy-start(f32[7,8,128]{2,1,0:T(8,128)} %constant.30.clone.refs_1_.refs_5_.refs_2_) | copy-start | bytes 86020
  19.2 13.3 %copy-start.2 = (f32[288]{0:T(512)S(1)}, f32[288]{0:T(512)}, u32[]{:S(2)}) copy-start(f32[288]{0:T(512)} %constant.29.clone.refs_0_.refs_4_.refs_1_) | copy-start | bytes 3460
  20.5 4.5 %collective-permute-start.5 = (f32[104,128]{1,0:T(8,128)S(1)}, f32[104,128]{1,0:T(8,128)S(1)}, u32[]{:S(2)}, u32[]{:S(2)}) collective-permute-start(f32[104,128]{1,0:T(8,128)S(1)} %get-tuple-element.46), channel_id=1, source_target_pairs={{0,2},{1,3},{2,0},{3,1},{4,6},{5,7},{6,4},{7,5},{8,10},{9,11},{10,... | collective-permute-start | bytes 159752 | tf_op jit(solution)/shard_map/ppermute | solution.py:848
  20.8 4.1 %collective-permute-start.6 = (f32[104,128]{1,0:T(8,128)S(1)}, f32[104,128]{1,0:T(8,128)S(1)}, u32[]{:S(2)}, u32[]{:S(2)}) collective-permute-start(f32[104,128]{1,0:T(8,128)S(1)} %get-tuple-element.47), channel_id=1, source_target_pairs={{0,3},{1,2},{2,1},{3,0},{4,7},{5,6},{6,5},{7,4},{8,11},{9,10},{10,... | collective-permute-start | bytes 159752 | tf_op jit(solution)/shard_map/ppermute | solution.py:848
  21.5 3.4 %collective-permute-start.7 = (f32[104,128]{1,0:T(8,128)S(1)}, f32[104,128]{1,0:T(8,128)S(1)}, u32[]{:S(2)}, u32[]{:S(2)}) collective-permute-start(f32[104,128]{1,0:T(8,128)S(1)} %get-tuple-element.48), channel_id=1, source_target_pairs={{0,1},{1,0},{2,3},{3,2},{4,5},{5,4},{6,7},{7,6},{8,9},{9,8},{10,11... | collective-permute-start | bytes 159752 | tf_op jit(solution)/shard_map/ppermute | solution.py:848
  25.0 11.8 %collective-permute-start.8 = (f32[160,128]{1,0:T(8,128)S(1)}, f32[160,128]{1,0:T(8,128)S(1)}, u32[]{:S(2)}, u32[]{:S(2)}) collective-permute-start(f32[160,128]{1,0:T(8,128)S(1)} %get-tuple-element.54), channel_id=1, source_target_pairs={{0,24},{4,28},{8,16},{12,20},{16,8},{20,12},{24,0},{28,4},{1,25},{... | collective-permute-start | bytes 245768 | tf_op jit(solution)/shard_map/ppermute | solution.py:862
  29.9 7.8 %collective-permute-start.9 = (f32[160,128]{1,0:T(8,128)S(1)}, f32[160,128]{1,0:T(8,128)S(1)}, u32[]{:S(2)}, u32[]{:S(2)}) collective-permute-start(f32[160,128]{1,0:T(8,128)S(1)} %get-tuple-element.55), channel_id=1, source_target_pairs={{0,28},{4,24},{8,20},{12,16},{16,12},{20,8},{24,4},{28,0},{1,29},{... | collective-permute-start | bytes 245768 | tf_op jit(solution)/shard_map/ppermute | solution.py:862
  31.0 7.0 %collective-permute-start.10 = (f32[160,128]{1,0:T(8,128)S(1)}, f32[160,128]{1,0:T(8,128)S(1)}, u32[]{:S(2)}, u32[]{:S(2)}) collective-permute-start(f32[160,128]{1,0:T(8,128)S(1)} %get-tuple-element.56), channel_id=1, source_target_pairs={{0,20},{4,16},{8,28},{12,24},{16,4},{20,0},{24,12},{28,8},{1,21},{... | collective-permute-start | bytes 245768 | tf_op jit(solution)/shard_map/ppermute | solution.py:862
  31.0 8.2 %collective-permute-start.11 = (f32[160,128]{1,0:T(8,128)S(1)}, f32[160,128]{1,0:T(8,128)S(1)}, u32[]{:S(2)}, u32[]{:S(2)}) collective-permute-start(f32[160,128]{1,0:T(8,128)S(1)} %get-tuple-element.49.refs_3_), channel_id=1, source_target_pairs={{0,16},{4,20},{8,24},{12,28},{16,0},{20,4},{24,8},{28,12},{1,17},{... | collective-permute-start | bytes 245768 | tf_op jit(solution)/shard_map/ppermute | solution.py:862
  41.8 4.4 %collective-permute-start.12 = (f32[104,128]{1,0:T(8,128)S(1)}, f32[104,128]{1,0:T(8,128)S(1)}, u32[]{:S(2)}, u32[]{:S(2)}) collective-permute-start(f32[104,128]{1,0:T(8,128)S(1)} %get-tuple-element.60), channel_id=1, source_target_pairs={{0,2},{1,3},{2,0},{3,1},{4,6},{5,7},{6,4},{7,5},{8,10},{9,11},{10,... | collective-permute-start | bytes 159752 | tf_op jit(solution)/shard_map/ppermute | solution.py:848
  42.1 4.1 %collective-permute-start.13 = (f32[104,128]{1,0:T(8,128)S(1)}, f32[104,128]{1,0:T(8,128)S(1)}, u32[]{:S(2)}, u32[]{:S(2)}) collective-permute-start(f32[104,128]{1,0:T(8,128)S(1)} %get-tuple-element.61), channel_id=1, source_target_pairs={{0,3},{1,2},{2,1},{3,0},{4,7},{5,6},{6,5},{7,4},{8,11},{9,10},{10,... | collective-permute-start | bytes 159752 | tf_op jit(solution)/shard_map/ppermute | solution.py:848
  42.2 4.0 %collective-permute-start.14 = (f32[104,128]{1,0:T(8,128)S(1)}, f32[104,128]{1,0:T(8,128)S(1)}, u32[]{:S(2)}, u32[]{:S(2)}) collective-permute-start(f32[104,128]{1,0:T(8,128)S(1)} %get-tuple-element.62), channel_id=1, source_target_pairs={{0,1},{1,0},{2,3},{3,2},{4,5},{5,4},{6,7},{7,6},{8,9},{9,8},{10,11... | collective-permute-start | bytes 159752 | tf_op jit(solution)/shard_map/ppermute | solution.py:848
  46.2 10.3 %collective-permute-start.15 = (f32[160,128]{1,0:T(8,128)S(1)}, f32[160,128]{1,0:T(8,128)S(1)}, u32[]{:S(2)}, u32[]{:S(2)}) collective-permute-start(f32[160,128]{1,0:T(8,128)S(1)} %get-tuple-element.67), channel_id=1, source_target_pairs={{0,24},{4,28},{8,16},{12,20},{16,8},{20,12},{24,0},{28,4},{1,25},{... | collective-permute-start | bytes 245768 | tf_op jit(solution)/shard_map/ppermute | solution.py:862
  48.7 8.1 %collective-permute-start.16 = (f32[160,128]{1,0:T(8,128)S(1)}, f32[160,128]{1,0:T(8,128)S(1)}, u32[]{:S(2)}, u32[]{:S(2)}) collective-permute-start(f32[160,128]{1,0:T(8,128)S(1)} %get-tuple-element.68), channel_id=1, source_target_pairs={{0,28},{4,24},{8,20},{12,16},{16,12},{20,8},{24,4},{28,0},{1,29},{... | collective-permute-start | bytes 245768 | tf_op jit(solution)/shard_map/ppermute | solution.py:862
  50.2 8.0 %collective-permute-start.17 = (f32[160,128]{1,0:T(8,128)S(1)}, f32[160,128]{1,0:T(8,128)S(1)}, u32[]{:S(2)}, u32[]{:S(2)}) collective-permute-start(f32[160,128]{1,0:T(8,128)S(1)} %get-tuple-element.69), channel_id=1, source_target_pairs={{0,20},{4,16},{8,28},{12,24},{16,4},{20,0},{24,12},{28,8},{1,21},{... | collective-permute-start | bytes 245768 | tf_op jit(solution)/shard_map/ppermute | solution.py:862
  50.8 9.0 %collective-permute-start.18 = (f32[160,128]{1,0:T(8,128)S(1)}, f32[160,128]{1,0:T(8,128)S(1)}, u32[]{:S(2)}, u32[]{:S(2)}) collective-permute-start(f32[160,128]{1,0:T(8,128)S(1)} %get-tuple-element.63.refs_4_), channel_id=1, source_target_pairs={{0,16},{4,20},{8,24},{12,28},{16,0},{20,4},{24,8},{28,12},{1,17},{... | collective-permute-start | bytes 245768 | tf_op jit(solution)/shard_map/ppermute | solution.py:862

commit v10 on v9

--- a/solution.py
+++ b/solution.py
@@ -206,7 +206,7 @@
 
 
 def padded_rows(count):
-    return -(-count // 1024) * 8
+    return -(-count // 8) * 8
 
 
 def whole(count):
@@ -218,7 +218,7 @@
 
 
 def lookup(table_ref, index):
-    return table_ref[index // 128, index % 128]
+    return table_ref[index, 0]
 
 
 def grant(mebibytes):
@@ -245,15 +245,19 @@
             column, (entries, spread_ref.shape[1])
         )
     wide = loop.cols + 2 * HALO
-    corner_ref[0:1, 0:entries] = (
-        base_ref[0:1, :] - lax.axis_index("lat") * loop.rows + HALO - 1
-    ) * wide + (base_ref[1:2, :] - lax.axis_index("lon") * loop.cols + HALO - 1)
+    base = (base_ref[0:1, :] - lax.axis_index("lat") * loop.rows + HALO - 1) * wide + (
+        base_ref[1:2, :] - lax.axis_index("lon") * loop.cols + HALO - 1
+    )
+    column = jnp.sum(
+        jnp.where(diagonal, base.astype(jnp.float32), 0.0), axis=1, keepdims=True
+    )
+    corner_ref[pl.ds(0, entries), :] = jnp.broadcast_to(
+        column, (entries, corner_ref.shape[1])
+    ).astype(jnp.int32)
 
 
 def digits(shape, outer, inner, slots):
-    flat = lax.broadcasted_iota(jnp.int32, shape, 0) * shape[1] + lax.broadcasted_iota(
-        jnp.int32, shape, 1
-    )
+    flat = lax.broadcasted_iota(jnp.int32, shape, 0)
     high = jnp.zeros(shape, jnp.int32)
     for n in range(1, outer):
         high = high + jnp.where(flat >= n * inner * slots, 1, 0)
@@ -264,7 +268,7 @@
     return high, middle, jnp.minimum(rest - middle * slots, slots - 1)
 
 
-def table_kernel(loop, pitch, cell_ref, other_ref, send_ref, swap_ref, receive_ref):
+def table_kernel(loop, pitch, cell_ref, other_ref, send_ref, receive_ref, swap_ref=None):
     lat, lon = lax.axis_index("lat"), lax.axis_index("lon")
     lat_count, lon_count = loop.lat_count, loop.lon_count
     mine = loop.position(cell_ref[0], cell_ref[1])
@@ -276,11 +280,12 @@
     )
     send_ref[...] = loop.wrap(entry)
 
-    lat_step, lon_step, slot = digits(swap_ref.shape, lat_count, lon_count, loop.slots)
-    donor = lat * lon_count + from_device(lon, lon_step, lon_count)
-    here = jnp.full_like(slot, lon)
-    ahead = loop.column_slot(to_device(lat, lat_step, lat_count), here, donor, other)
-    swap_ref[...] = jnp.minimum(ahead + slot, loop.column_slots - 1)
+    lat_step, lon_step, slot = digits(receive_ref.shape, lat_count, lon_count, loop.slots)
+    if swap_ref is not None:
+        donor = lat * lon_count + from_device(lon, lon_step, lon_count)
+        here = jnp.full_like(slot, lon)
+        ahead = loop.column_slot(to_device(lat, lat_step, lat_count), here, donor, other)
+        swap_ref[...] = jnp.minimum(ahead + slot, loop.column_slots - 1)
 
     donor = from_device(lat, lat_step, lat_count) * lon_count + from_device(
         lon, lon_step, lon_count
@@ -332,7 +337,7 @@
     turned = takes_next | (field == 2) | (field == 5)
 
     def one_entry(entry, carry):
-        base = corner_ref[0, entry]
+        base = lookup(corner_ref, entry)
 
         def over_tile(number):
             return spread_ref[pl.ds(number * entries + entry, TILE, stride=0), :]
@@ -481,7 +486,10 @@
         return read
 
     def prepare(self, row):
-        factors = [self.factor_ref[(self.lat * 3 + n) * self.tall + row] for n in range(3)]
+        factors = [
+            self.factor_ref[pl.ds((self.lat * 3 + n) * self.tall + row, 8, stride=0), :]
+            for n in range(3)
+        ]
         inverse_radius = self.radial_ref[0]
         with_theta = inverse_radius * (self.loop.nth / math.pi)
         return factors, inverse_radius * factors[2], with_theta
@@ -737,7 +745,7 @@
     return np.repeat(rows[:, None, :], 8, axis=1).astype(np.float32)
 
 
-def row_factors(rows, lat_count, nth, nph):
+def row_factors(rows, lat_count, nth, nph, levels):
     polar_step, azimuth_step = math.pi / (2 * nth), 1.5 * math.pi / nph
     tall = rows + 2 * HALO
     parts = []
@@ -750,7 +758,8 @@
             sines[:-2] / middle * (0.5 / polar_step),
             (0.5 / azimuth_step) / middle,
         ]
-    return np.concatenate(parts).astype(np.float32)
+    flat = np.concatenate(parts + [np.zeros(8)]).astype(np.float32)
+    return np.repeat(flat[:, None], levels, axis=1)
 
 
 def per_device(state, rim_base, rim_weight, rim_angle, rim_target):
@@ -782,7 +791,7 @@
     corner_table, spread_weights = pl.pallas_call(
         lambda *refs: weight_kernel(loop, *refs),
         out_shape=[
-            jax.ShapeDtypeStruct((8, -(-entries // 128) * 128), jnp.int32),
+            jax.ShapeDtypeStruct((padded_rows(entries), 128), jnp.int32),
             jax.ShapeDtypeStruct((18 * entries + TILE, levels), f32),
         ],
         in_specs=whole(3),
@@ -792,20 +801,19 @@
     )(rim_base[0].T, rim_weight[0].T, jnp.stack([jnp.cos(angle), jnp.sin(angle)]))
     send_count = lon_count * loop.column_slots
     got_count = lat_count * lon_count * loop.slots
-    send_table, swap_table, receive_table = pl.pallas_call(
+    counts = [send_count, got_count] + [got_count] * (not loop.even_leads)
+    send_table, receive_table, *swap_tables = pl.pallas_call(
         lambda *refs: table_kernel(loop, pitch, *refs),
         out_shape=[
-            jax.ShapeDtypeStruct((padded_rows(count), 128), jnp.int32)
-            for count in (send_count, got_count, got_count)
+            jax.ShapeDtypeStruct((padded_rows(count), 128), jnp.int32) for count in counts
         ],
         in_specs=scalars(2),
-        out_specs=whole(3),
+        out_specs=whole(len(counts)),
         compiler_params=grant(4),
         name="tables",
     )(first_cell, other_cell)
     rim = (send_table, corner_table, spread_weights)
-    swap_tables = () if loop.even_leads else (swap_table,)
-    factors = jnp.asarray(row_factors(rows, lat_count, loop.nth, loop.nph))
+    factors = jnp.asarray(row_factors(rows, lat_count, loop.nth, loop.nph, levels))
     radial = jnp.asarray(radial_factors(levels, loop.nth))
 
     east_first = lax.axis_index("lon") % 2 == 0
@@ -835,7 +843,7 @@
     frame, *packed = pl.pallas_call(
         lambda *refs: frame_kernel(loop, *refs),
         out_shape=[tile_array(tall * wide)] + packed_shapes,
-        in_specs=scalars(2) + whole(4),
+        in_specs=whole(6),
         out_specs=whole(1 + lon_count),
         scratch_shapes=[pltpu.VMEM((entries * TILE, levels), f32)],
         input_output_aliases={5: 0},
@@ -851,7 +859,7 @@
         return pl.pallas_call(
             lambda *refs: swap_kernel(loop, *refs),
             out_shape=[tile_array(lon_count * loop.slots)] * lat_count,
-            in_specs=scalars(len(swap_tables)) + whole(lon_count),
+            in_specs=whole(len(swap_tables) + lon_count),
             out_specs=whole(lat_count),
             compiler_params=grant(4),
             name="swap",
@@ -874,7 +882,7 @@
     frame, rate, plane, work = pl.pallas_call(
         lambda *refs: first_inner_kernel(loop, *refs),
         out_shape=[tile_array(tall * wide), rates] + planes,
-        in_specs=scalars(1) + whole(3),
+        in_specs=whole(4),
         out_specs=whole(4),
         compiler_params=grant(4),
         name="first_inner",
@@ -882,7 +890,7 @@
     frame, rate, _, _, *packed = pl.pallas_call(
         lambda *refs: first_edge_kernel(loop, *refs),
         out_shape=[tile_array(tall * wide), rates] + planes + packed_shapes,
-        in_specs=scalars(2) + whole(1) + scalars(2) + whole(5 + lat_count),
+        in_specs=whole(10 + lat_count),
         out_specs=whole(4 + lon_count),
         scratch_shapes=[pltpu.VMEM((entries * TILE, levels), f32)],
         input_output_aliases={6: 0, 7: 1, 8: 2, 9: 3},
@@ -895,7 +903,7 @@
     inner, plane, work = pl.pallas_call(
         lambda *refs: second_inner_kernel(loop, *refs),
         out_shape=[tile_array(rows * cols)] + planes,
-        in_specs=scalars(1) + whole(4),
+        in_specs=whole(5),
         out_specs=whole(3),
         compiler_params=grant(4),
         name="second_inner",
@@ -903,7 +911,7 @@
     _, _, change = pl.pallas_call(
         lambda *refs: second_edge_kernel(loop, *refs),
         out_shape=planes + [tile_array(rows * cols)],
-        in_specs=scalars(2) + whole(5 + lat_count),
+        in_specs=whole(7 + lat_count),
         out_specs=whole(3),
         input_output_aliases={5: 0, 6: 1},
         compiler_params=grant(4),

time: 63 us -> 61.5 us (0.976)
  Pallas kernels: 15.8 us -> 12.8 us
  waiting for transfers between devices: 16.2 us -> 17.8 us
    ppermute x8, waiting for transfers between devices: 6.71 us -> 7.81 us  [second_round(): lax.ppermute(turned[step], ('panel', 'lat'), lat_route(step, lat_count))]
  transfers between devices with their start and end apart: 19 -> 19, of which waited for: 11 -> 12; matrix products, arithmetic and copies ran while one was open for 4% -> 4% of each run, Pallas kernels for 14% -> 12%
where the time goes in v10:
time: 61.5 us; the launch traced here: 61.3 us
  starting transfers between devices  25.5 us (41%)
  waiting for transfers between devices  17.8 us (29%)
  Pallas kernels  12.8 us (21%)
  local copies, waits for them, and re-layouts  2.88 us (5%)
  other arithmetic  2.24 us (4%)
    ppermute x8, starting transfers between devices, second_round(): lax.ppermute(turned[step], ('panel', 'lat'), lat_route(step, lat_count))  13.4 us
    ppermute x8, waiting for transfers between devices, second_round(): lax.ppermute(turned[step], ('panel', 'lat'), lat_route(step, lat_count))  7.81 us
    ppermute x6, waiting for transfers between devices, first_round(): lax.ppermute(packed[step], 'lon', lon_route(step, lon_count))  4.43 us
    ppermute x6, starting transfers between devices, first_round(): lax.ppermute(packed[step], 'lon', lon_route(step, lon_count))  4.41 us
    pallas_call x1, Pallas kernels, per_device(): pl.pallas_call(lambda *refs: first_inner_kernel(loop, *refs), out_shape=[...  3.74 us
    ppermute x1, starting transfers between devices, per_device(): lax.ppermute(send_even, everyone, swap_route(0, lat_count, lon_count, True))  3.12 us
    ppermute x1, waiting for transfers between devices, per_device(): lax.ppermute(send_even, everyone, swap_route(0, lat_count, lon_count, True))  2.95 us
    ppermute x1, starting transfers between devices, per_device(): lax.ppermute(strip_odd, everyone, swap_route(1, lat_count, lon_count, Fal...  2.93 us
  transfers between devices with their start and end apart: 19, of which 12 were waited for; matrix products, arithmetic and copies ran while one was open for 4% of the time, Pallas kernels for 12%

profile of v10, /device:TPU:0, one launch (start us, length us, event | category | flops | bytes accessed | tf_op | source)
XLA Modules:
  0.0 61.3 jit_solution(3572679047076380986)
XLA Ops:
  1.2 3.1 %collective-permute-start.1 = (f32[512,128]{1,0:T(8,128)S(1)}, f32[512,128]{1,0:T(8,128)S(1)}, u32[]{:S(2)}, u32[]{:S(2)}) collective-permute-start(f32[512,128]{1,0:T(8,128)S(1)} %bitcast.20), channel_id=1, source_target_pairs={{0,4},{1,5},{2,6},{3,7},{4,0},{5,1},{6,2},{7,3},{8,12},{9,13},{10,... | collective-permute-start | bytes 786440 | tf_op jit(solution)/shard_map/ppermute | solution.py:787
  7.6 3.0 %collective-permute-done.1.refs_3_.refs_2_ = f32[512,128]{1,0:T(8,128)S(1)} collective-permute-done((f32[512,128]{1,0:T(8,128)S(1)}, f32[512,128]{1,0:T(8,128)S(1)}, u32[]{:S(2)}, u32[]{:S(2)}) %collective-permute-start.1) | collective-permute-done | bytes 262176 | tf_op jit(solution)/shard_map/ppermute | solution.py:787
  10.7 2.9 %collective-permute-start.3 = (f32[768,128]{1,0:T(8,128)S(1)}, f32[768,128]{1,0:T(8,128)S(1)}, u32[]{:S(2)}, u32[]{:S(2)}) collective-permute-start(f32[768,128]{1,0:T(8,128)S(1)} %get-tuple-element.42), channel_id=1, source_target_pairs={{0,4},{1,2},{2,1},{3,7},{4,0},{5,6},{6,5},{7,3},{8,12},{9,10},{10,... | collective-permute-start | bytes 1179656 | tf_op jit(solution)/shard_map/ppermute | solution.py:831
  14.4 1.5 %collective-permute-start = (s32[2]{0:T(128)S(1)}, s32[2]{0:T(128)S(1)}, u32[]{:S(2)}, u32[]{:S(2)}) collective-permute-start(s32[2]{0:T(128)S(1)} %slice_reduce_fusion.refs_0_), channel_id=1, source_target_pairs={{0,16},{16,0},{1,17},{17,1},{2,18},{18,2},{3,19},{19,3},{4,20},{20... | collective-permute-start | bytes 32 | tf_op jit(solution)/shard_map/ppermute | solution.py:779
  15.9 2.1 %collective-permute-done.refs_1_ = s32[2]{0:T(128)S(1)} collective-permute-done((s32[2]{0:T(128)S(1)}, s32[2]{0:T(128)S(1)}, u32[]{:S(2)}, u32[]{:S(2)}) %collective-permute-start) | collective-permute-done | bytes 40 | tf_op jit(solution)/shard_map/ppermute | solution.py:779
  20.7 1.6 %collective-permute-start.7 = (f32[104,128]{1,0:T(8,128)S(1)}, f32[104,128]{1,0:T(8,128)S(1)}, u32[]{:S(2)}, u32[]{:S(2)}) collective-permute-start(f32[104,128]{1,0:T(8,128)S(1)} %get-tuple-element.48), channel_id=1, source_target_pairs={{0,1},{1,0},{2,3},{3,2},{4,5},{5,4},{6,7},{7,6},{8,9},{9,8},{10,11... | collective-permute-start | bytes 159752 | tf_op jit(solution)/shard_map/ppermute | solution.py:856
  22.3 2.3 %collective-permute-done.5.refs_1_ = f32[104,128]{1,0:T(8,128)S(1)} collective-permute-done((f32[104,128]{1,0:T(8,128)S(1)}, f32[104,128]{1,0:T(8,128)S(1)}, u32[]{:S(2)}, u32[]{:S(2)}) %collective-permute-start.5) | collective-permute-done | bytes 53280 | tf_op jit(solution)/shard_map/ppermute | solution.py:856
  24.6 4.9 %collective-permute-start.8 = (f32[160,128]{1,0:T(8,128)S(1)}, f32[160,128]{1,0:T(8,128)S(1)}, u32[]{:S(2)}, u32[]{:S(2)}) collective-permute-start(f32[160,128]{1,0:T(8,128)S(1)} %get-tuple-element.54), channel_id=1, source_target_pairs={{0,24},{4,28},{8,16},{12,20},{16,8},{20,12},{24,0},{28,4},{1,25},{... | collective-permute-start | bytes 245768 | tf_op jit(solution)/shard_map/ppermute | solution.py:870
  29.4 1.2 %collective-permute-start.9 = (f32[160,128]{1,0:T(8,128)S(1)}, f32[160,128]{1,0:T(8,128)S(1)}, u32[]{:S(2)}, u32[]{:S(2)}) collective-permute-start(f32[160,128]{1,0:T(8,128)S(1)} %get-tuple-element.55), channel_id=1, source_target_pairs={{0,28},{4,24},{8,20},{12,16},{16,12},{20,8},{24,4},{28,0},{1,29},{... | collective-permute-start | bytes 245768 | tf_op jit(solution)/shard_map/ppermute | solution.py:870
  30.6 1.5 %collective-permute-start.11 = (f32[160,128]{1,0:T(8,128)S(1)}, f32[160,128]{1,0:T(8,128)S(1)}, u32[]{:S(2)}, u32[]{:S(2)}) collective-permute-start(f32[160,128]{1,0:T(8,128)S(1)} %get-tuple-element.49.refs_3_), channel_id=1, source_target_pairs={{0,16},{4,20},{8,24},{12,28},{16,0},{20,4},{24,8},{28,12},{1,17},{... | collective-permute-start | bytes 245768 | tf_op jit(solution)/shard_map/ppermute | solution.py:870
  32.1 3.7 %first_inner.1 = (f32[4608,128]{1,0:T(8,128)S(1)}, f32[8,24,24,128]{3,2,1,0:T(8,128)S(1)}, f32[7680,128]{1,0:T(8,128)S(1)}, f32[12480,128]{1,0:T(8,128)S(1)}) custom-call(f32[296,128]{1,0:T(8,128)S(1)} %copy-done.1, f32[7,8,128]{2,1,0:T(8,128)S(1)} %copy-done.2, f32[4608,128]{1,0:T(8,128)S(1)} %get-tuple-element.44.refs_2_, ...), custom_call_target="tpu_custom_call" | custom-call | tf_op jit(solution)/shard_map/first_inner/pallas_call | solution.py:882
  35.9 1.3 %collective-permute-done.9.refs_11_ = f32[160,128]{1,0:T(8,128)S(1)} collective-permute-done((f32[160,128]{1,0:T(8,128)S(1)}, f32[160,128]{1,0:T(8,128)S(1)}, u32[]{:S(2)}, u32[]{:S(2)}) %collective-permute-start.9) | collective-permute-done | bytes 81952 | tf_op jit(solution)/shard_map/ppermute | solution.py:870
  37.6 1.2 %collective-permute-done.11.refs_13_ = f32[160,128]{1,0:T(8,128)S(1)} collective-permute-done((f32[160,128]{1,0:T(8,128)S(1)}, f32[160,128]{1,0:T(8,128)S(1)}, u32[]{:S(2)}, u32[]{:S(2)}) %collective-permute-start.11) | collective-permute-done | bytes 81952 | tf_op jit(solution)/shard_map/ppermute | solution.py:870
  38.8 2.1 %first_edge.1 = (f32[4608,128]{1,0:T(8,128)S(1)}, f32[8,24,24,128]{3,2,1,0:T(8,128)S(1)}, f32[7680,128]{1,0:T(8,128)S(1)}, f32[12480,128]{1,0:T(8,128)S(1)}, f32...) custom-call(s32[56,128]{1,0:T(8,128)S(1)} %get-tuple-element.39.refs, ...), custom_call_target="tpu_custom_call", output_to_operand_aliasing={{0}: (6, {}), {1}: (7, {}), {2}: (8, {}), {3}: (9, {})} | custom-call | tf_op jit(solution)/shard_map/first_edge/pallas_call | solution.py:890
  41.3 1.8 %collective-permute-start.14 = (f32[104,128]{1,0:T(8,128)S(1)}, f32[104,128]{1,0:T(8,128)S(1)}, u32[]{:S(2)}, u32[]{:S(2)}) collective-permute-start(f32[104,128]{1,0:T(8,128)S(1)} %get-tuple-element.62), channel_id=1, source_target_pairs={{0,1},{1,0},{2,3},{3,2},{4,5},{5,4},{6,7},{7,6},{8,9},{9,8},{10,11... | collective-permute-start | bytes 159752 | tf_op jit(solution)/shard_map/ppermute | solution.py:856
  43.1 2.2 %collective-permute-done.12.refs_1_ = f32[104,128]{1,0:T(8,128)S(1)} collective-permute-done((f32[104,128]{1,0:T(8,128)S(1)}, f32[104,128]{1,0:T(8,128)S(1)}, u32[]{:S(2)}, u32[]{:S(2)}) %collective-permute-start.12) | collective-permute-done | bytes 53280 | tf_op jit(solution)/shard_map/ppermute | solution.py:856
  45.3 2.5 %collective-permute-start.15 = (f32[160,128]{1,0:T(8,128)S(1)}, f32[160,128]{1,0:T(8,128)S(1)}, u32[]{:S(2)}, u32[]{:S(2)}) collective-permute-start(f32[160,128]{1,0:T(8,128)S(1)} %get-tuple-element.67), channel_id=1, source_target_pairs={{0,24},{4,28},{8,16},{12,20},{16,8},{20,12},{24,0},{28,4},{1,25},{... | collective-permute-start | bytes 245768 | tf_op jit(solution)/shard_map/ppermute | solution.py:870
  47.8 1.5 %collective-permute-start.16 = (f32[160,128]{1,0:T(8,128)S(1)}, f32[160,128]{1,0:T(8,128)S(1)}, u32[]{:S(2)}, u32[]{:S(2)}) collective-permute-start(f32[160,128]{1,0:T(8,128)S(1)} %get-tuple-element.68), channel_id=1, source_target_pairs={{0,28},{4,24},{8,20},{12,16},{16,12},{20,8},{24,4},{28,0},{1,29},{... | collective-permute-start | bytes 245768 | tf_op jit(solution)/shard_map/ppermute | solution.py:870
  49.9 1.3 %collective-permute-start.18 = (f32[160,128]{1,0:T(8,128)S(1)}, f32[160,128]{1,0:T(8,128)S(1)}, u32[]{:S(2)}, u32[]{:S(2)}) collective-permute-start(f32[160,128]{1,0:T(8,128)S(1)} %get-tuple-element.63.refs_4_), channel_id=1, source_target_pairs={{0,16},{4,20},{8,24},{12,28},{16,0},{20,4},{24,8},{28,12},{1,17},{... | collective-permute-start | bytes 245768 | tf_op jit(solution)/shard_map/ppermute | solution.py:870
  51.3 2.8 %second_inner.1 = (f32[2048,128]{1,0:T(8,128)S(1)}, f32[7680,128]{1,0:T(8,128)S(1)}, f32[12480,128]{1,0:T(8,128)S(1)}) custom-call(f32[296,128]{1,0:T(8,128)S(1)} %copy-done.1, f32[7,8,128]{2,1,0:T(8,128)S(1)} %copy-done.2, f32[4608,128]{1,0:T(8,128)S(1)} %get-tuple-element.58.refs_2_, f32[8,24,24,128]{3,2,1,0:T(8,128)S(1)} %get-tuple-element.57.refs_3_, ...), custom_call_target="tpu_custom_call" | custom-call | tf_op jit(solution)/shard_map/second_inner/pallas_call | solution.py:903
  54.0 1.6 %collective-permute-done.15.refs_7_ = f32[160,128]{1,0:T(8,128)S(1)} collective-permute-done((f32[160,128]{1,0:T(8,128)S(1)}, f32[160,128]{1,0:T(8,128)S(1)}, u32[]{:S(2)}, u32[]{:S(2)}) %collective-permute-start.15) | collective-permute-done | bytes 81952 | tf_op jit(solution)/shard_map/ppermute | solution.py:870
  55.9 1.4 %collective-permute-done.17.refs_9_ = f32[160,128]{1,0:T(8,128)S(1)} collective-permute-done((f32[160,128]{1,0:T(8,128)S(1)}, f32[160,128]{1,0:T(8,128)S(1)}, u32[]{:S(2)}, u32[]{:S(2)}) %collective-permute-start.17) | collective-permute-done | bytes 81952 | tf_op jit(solution)/shard_map/ppermute | solution.py:870
  57.3 1.6 %collective-permute-done.18.refs_10_ = f32[160,128]{1,0:T(8,128)S(1)} collective-permute-done((f32[160,128]{1,0:T(8,128)S(1)}, f32[160,128]{1,0:T(8,128)S(1)}, u32[]{:S(2)}, u32[]{:S(2)}) %collective-permute-start.18) | collective-permute-done | bytes 81952 | tf_op jit(solution)/shard_map/ppermute | solution.py:870
  58.9 2.4 %second_edge.1 = (f32[7680,128]{1,0:T(8,128)S(1)}, f32[12480,128]{1,0:T(8,128)S(1)}, f32[2048,128]{1,0:T(8,128)}) custom-call(s32[80,128]{1,0:T(8,128)S(1)} %get-tuple-element.38.refs_3_.refs_0_, f32[296,128]{1,0:T(8,128)S(1)} %copy-done.1, f32[7,8,128]{2,1,0:T(8,128)S(1)} %copy-done.2, ...), custom_call_target="tpu_custom_call", output_to_operand_aliasing={{0}: (5, {}), {1}: (6, {})} | custom-call | tf_op jit(solution)/shard_map/second_edge/pallas_call | solution.py:911
  (40 shorter events, 9.7 us)
Async XLA Ops:
  0.0 18.7 %copy-start = (f32[1,16,16,8,128]{4,3,2,1,0:T(8,128)S(1)}, f32[1,16,16,8,128]{4,3,2,1,0:T(8,128)}, u32[]{:S(2)}) copy-start(f32[1,16,16,8,128]{4,3,2,1,0:T(8,128)} %param.7) | copy-start | bytes 3145732
  1.2 9.4 %collective-permute-start.1 = (f32[512,128]{1,0:T(8,128)S(1)}, f32[512,128]{1,0:T(8,128)S(1)}, u32[]{:S(2)}, u32[]{:S(2)}) collective-permute-start(f32[512,128]{1,0:T(8,128)S(1)} %bitcast.20), channel_id=1, source_target_pairs={{0,4},{1,5},{2,6},{3,7},{4,0},{5,1},{6,2},{7,3},{8,12},{9,13},{10,... | collective-permute-start | bytes 786440 | tf_op jit(solution)/shard_map/ppermute | solution.py:787
  4.3 6.3 %collective-permute-start.2 = (f32[512,128]{1,0:T(8,128)S(1)}, f32[512,128]{1,0:T(8,128)S(1)}, u32[]{:S(2)}, u32[]{:S(2)}) collective-permute-start(f32[512,128]{1,0:T(8,128)S(1)} %bitcast.19), channel_id=1, source_target_pairs={{0,1},{1,0},{2,3},{3,2},{4,8},{5,9},{6,10},{7,11},{8,4},{9,5},{10,... | collective-permute-start | bytes 786440 | tf_op jit(solution)/shard_map/ppermute | solution.py:788
  5.0 0.7 %copy-start.3 = (f32[1,32,16]{1,2,0:T(8,128)S(1)}, f32[1,32,16]{1,2,0:T(8,128)}, u32[]{:S(2)}) copy-start(f32[1,32,16]{1,2,0:T(8,128)} %param.9) | copy-start | bytes 6148
  5.7 0.7 %copy-start.4 = (s32[1,32,2]{1,2,0:T(2,128)S(1)}, s32[1,32,2]{1,2,0:T(2,128)}, u32[]{:S(2)}) copy-start(s32[1,32,2]{1,2,0:T(2,128)} %param.8) | copy-start | bytes 772
  10.7 8.7 %collective-permute-start.3 = (f32[768,128]{1,0:T(8,128)S(1)}, f32[768,128]{1,0:T(8,128)S(1)}, u32[]{:S(2)}, u32[]{:S(2)}) collective-permute-start(f32[768,128]{1,0:T(8,128)S(1)} %get-tuple-element.42), channel_id=1, source_target_pairs={{0,4},{1,2},{2,1},{3,7},{4,0},{5,6},{6,5},{7,3},{8,12},{9,10},{10,... | collective-permute-start | bytes 1179656 | tf_op jit(solution)/shard_map/ppermute | solution.py:831
  13.6 5.8 %collective-permute-start.4 = (f32[768,128]{1,0:T(8,128)S(1)}, f32[768,128]{1,0:T(8,128)S(1)}, u32[]{:S(2)}, u32[]{:S(2)}) collective-permute-start(f32[768,128]{1,0:T(8,128)S(1)} %get-tuple-element.43.refs_0_), channel_id=1, source_target_pairs={{0,1},{1,0},{2,3},{3,2},{4,5},{5,4},{6,7},{7,6},{8,9},{9,8},{10,11... | collective-permute-start | bytes 1179656 | tf_op jit(solution)/shard_map/ppermute | solution.py:832
  14.4 3.6 %collective-permute-start = (s32[2]{0:T(128)S(1)}, s32[2]{0:T(128)S(1)}, u32[]{:S(2)}, u32[]{:S(2)}) collective-permute-start(s32[2]{0:T(128)S(1)} %slice_reduce_fusion.refs_0_), channel_id=1, source_target_pairs={{0,16},{16,0},{1,17},{17,1},{2,18},{18,2},{3,19},{19,3},{4,20},{20... | collective-permute-start | bytes 32 | tf_op jit(solution)/shard_map/ppermute | solution.py:779
  18.7 13.4 %copy-start.1 = (f32[296,128]{1,0:T(8,128)S(1)}, f32[296,128]{1,0:T(8,128)}, u32[]{:S(2)}) copy-start(f32[296,128]{1,0:T(8,128)} %constant.29.clone.refs_0_.refs_4_.refs_1_) | copy-start | bytes 454660
  18.7 13.4 %copy-start.2 = (f32[7,8,128]{2,1,0:T(8,128)S(1)}, f32[7,8,128]{2,1,0:T(8,128)}, u32[]{:S(2)}) copy-start(f32[7,8,128]{2,1,0:T(8,128)} %constant.30.clone.refs_1_.refs_5_.refs_2_) | copy-start | bytes 86020
  20.1 4.5 %collective-permute-start.5 = (f32[104,128]{1,0:T(8,128)S(1)}, f32[104,128]{1,0:T(8,128)S(1)}, u32[]{:S(2)}, u32[]{:S(2)}) collective-permute-start(f32[104,128]{1,0:T(8,128)S(1)} %get-tuple-element.46), channel_id=1, source_target_pairs={{0,2},{1,3},{2,0},{3,1},{4,6},{5,7},{6,4},{7,5},{8,10},{9,11},{10,... | collective-permute-start | bytes 159752 | tf_op jit(solution)/shard_map/ppermute | solution.py:856
  20.4 4.1 %collective-permute-start.6 = (f32[104,128]{1,0:T(8,128)S(1)}, f32[104,128]{1,0:T(8,128)S(1)}, u32[]{:S(2)}, u32[]{:S(2)}) collective-permute-start(f32[104,128]{1,0:T(8,128)S(1)} %get-tuple-element.47), channel_id=1, source_target_pairs={{0,3},{1,2},{2,1},{3,0},{4,7},{5,6},{6,5},{7,4},{8,11},{9,10},{10,... | collective-permute-start | bytes 159752 | tf_op jit(solution)/shard_map/ppermute | solution.py:856
  20.7 3.8 %collective-permute-start.7 = (f32[104,128]{1,0:T(8,128)S(1)}, f32[104,128]{1,0:T(8,128)S(1)}, u32[]{:S(2)}, u32[]{:S(2)}) collective-permute-start(f32[104,128]{1,0:T(8,128)S(1)} %get-tuple-element.48), channel_id=1, source_target_pairs={{0,1},{1,0},{2,3},{3,2},{4,5},{5,4},{6,7},{7,6},{8,9},{9,8},{10,11... | collective-permute-start | bytes 159752 | tf_op jit(solution)/shard_map/ppermute | solution.py:856
  24.6 11.3 %collective-permute-start.8 = (f32[160,128]{1,0:T(8,128)S(1)}, f32[160,128]{1,0:T(8,128)S(1)}, u32[]{:S(2)}, u32[]{:S(2)}) collective-permute-start(f32[160,128]{1,0:T(8,128)S(1)} %get-tuple-element.54), channel_id=1, source_target_pairs={{0,24},{4,28},{8,16},{12,20},{16,8},{20,12},{24,0},{28,4},{1,25},{... | collective-permute-start | bytes 245768 | tf_op jit(solution)/shard_map/ppermute | solution.py:870
  29.4 7.8 %collective-permute-start.9 = (f32[160,128]{1,0:T(8,128)S(1)}, f32[160,128]{1,0:T(8,128)S(1)}, u32[]{:S(2)}, u32[]{:S(2)}) collective-permute-start(f32[160,128]{1,0:T(8,128)S(1)} %get-tuple-element.55), channel_id=1, source_target_pairs={{0,28},{4,24},{8,20},{12,16},{16,12},{20,8},{24,4},{28,0},{1,29},{... | collective-permute-start | bytes 245768 | tf_op jit(solution)/shard_map/ppermute | solution.py:870
  30.6 7.0 %collective-permute-start.10 = (f32[160,128]{1,0:T(8,128)S(1)}, f32[160,128]{1,0:T(8,128)S(1)}, u32[]{:S(2)}, u32[]{:S(2)}) collective-permute-start(f32[160,128]{1,0:T(8,128)S(1)} %get-tuple-element.56), channel_id=1, source_target_pairs={{0,20},{4,16},{8,28},{12,24},{16,4},{20,0},{24,12},{28,8},{1,21},{... | collective-permute-start | bytes 245768 | tf_op jit(solution)/shard_map/ppermute | solution.py:870
  30.6 8.2 %collective-permute-start.11 = (f32[160,128]{1,0:T(8,128)S(1)}, f32[160,128]{1,0:T(8,128)S(1)}, u32[]{:S(2)}, u32[]{:S(2)}) collective-permute-start(f32[160,128]{1,0:T(8,128)S(1)} %get-tuple-element.49.refs_3_), channel_id=1, source_target_pairs={{0,16},{4,20},{8,24},{12,28},{16,0},{20,4},{24,8},{28,12},{1,17},{... | collective-permute-start | bytes 245768 | tf_op jit(solution)/shard_map/ppermute | solution.py:870
  40.9 4.4 %collective-permute-start.12 = (f32[104,128]{1,0:T(8,128)S(1)}, f32[104,128]{1,0:T(8,128)S(1)}, u32[]{:S(2)}, u32[]{:S(2)}) collective-permute-start(f32[104,128]{1,0:T(8,128)S(1)} %get-tuple-element.60), channel_id=1, source_target_pairs={{0,2},{1,3},{2,0},{3,1},{4,6},{5,7},{6,4},{7,5},{8,10},{9,11},{10,... | collective-permute-start | bytes 159752 | tf_op jit(solution)/shard_map/ppermute | solution.py:856
  41.2 4.1 %collective-permute-start.13 = (f32[104,128]{1,0:T(8,128)S(1)}, f32[104,128]{1,0:T(8,128)S(1)}, u32[]{:S(2)}, u32[]{:S(2)}) collective-permute-start(f32[104,128]{1,0:T(8,128)S(1)} %get-tuple-element.61), channel_id=1, source_target_pairs={{0,3},{1,2},{2,1},{3,0},{4,7},{5,6},{6,5},{7,4},{8,11},{9,10},{10,... | collective-permute-start | bytes 159752 | tf_op jit(solution)/shard_map/ppermute | solution.py:856
  41.3 4.0 %collective-permute-start.14 = (f32[104,128]{1,0:T(8,128)S(1)}, f32[104,128]{1,0:T(8,128)S(1)}, u32[]{:S(2)}, u32[]{:S(2)}) collective-permute-start(f32[104,128]{1,0:T(8,128)S(1)} %get-tuple-element.62), channel_id=1, source_target_pairs={{0,1},{1,0},{2,3},{3,2},{4,5},{5,4},{6,7},{7,6},{8,9},{9,8},{10,11... | collective-permute-start | bytes 159752 | tf_op jit(solution)/shard_map/ppermute | solution.py:856
  45.3 10.3 %collective-permute-start.15 = (f32[160,128]{1,0:T(8,128)S(1)}, f32[160,128]{1,0:T(8,128)S(1)}, u32[]{:S(2)}, u32[]{:S(2)}) collective-permute-start(f32[160,128]{1,0:T(8,128)S(1)} %get-tuple-element.67), channel_id=1, source_target_pairs={{0,24},{4,28},{8,16},{12,20},{16,8},{20,12},{24,0},{28,4},{1,25},{... | collective-permute-start | bytes 245768 | tf_op jit(solution)/shard_map/ppermute | solution.py:870
  47.8 8.1 %collective-permute-start.16 = (f32[160,128]{1,0:T(8,128)S(1)}, f32[160,128]{1,0:T(8,128)S(1)}, u32[]{:S(2)}, u32[]{:S(2)}) collective-permute-start(f32[160,128]{1,0:T(8,128)S(1)} %get-tuple-element.68), channel_id=1, source_target_pairs={{0,28},{4,24},{8,20},{12,16},{16,12},{20,8},{24,4},{28,0},{1,29},{... | collective-permute-start | bytes 245768 | tf_op jit(solution)/shard_map/ppermute | solution.py:870
  49.3 8.0 %collective-permute-start.17 = (f32[160,128]{1,0:T(8,128)S(1)}, f32[160,128]{1,0:T(8,128)S(1)}, u32[]{:S(2)}, u32[]{:S(2)}) collective-permute-start(f32[160,128]{1,0:T(8,128)S(1)} %get-tuple-element.69), channel_id=1, source_target_pairs={{0,20},{4,16},{8,28},{12,24},{16,4},{20,0},{24,12},{28,8},{1,21},{... | collective-permute-start | bytes 245768 | tf_op jit(solution)/shard_map/ppermute | solution.py:870
  49.9 9.0 %collective-permute-start.18 = (f32[160,128]{1,0:T(8,128)S(1)}, f32[160,128]{1,0:T(8,128)S(1)}, u32[]{:S(2)}, u32[]{:S(2)}) collective-permute-start(f32[160,128]{1,0:T(8,128)S(1)} %get-tuple-element.63.refs_4_), channel_id=1, source_target_pairs={{0,16},{4,20},{8,24},{12,28},{16,0},{20,4},{24,8},{28,12},{1,17},{... | collective-permute-start | bytes 245768 | tf_op jit(solution)/shard_map/ppermute | solution.py:870

commit v11 on v10

--- a/solution.py
+++ b/solution.py
@@ -72,12 +72,28 @@
     return [(i, to_device(i, step, count)) for i in range(count)]
 
 
-def lat_route(step, count):
-    return [
-        (side * count + i, (1 - side) * count + to_device(i, step, count))
-        for side in range(2)
-        for i in range(count)
-    ]
+def lat_route(step, lat_count, lon_count):
+    route = []
+    inner = set(range(1, lat_count - 1))
+    for side in range(2):
+        for lon in range(lon_count):
+            target = {lat: (1 - side, to_device(lat, step, lat_count), lon) for lat in range(lat_count)}
+            if 0 < lon < lon_count - 1 and lon_count % 2 == 0:
+                idle = {lat for lat in target if target[lat][1] in inner}
+                mate = (lon - 1 ^ 1) + 1
+                for lat in idle & inner:
+                    target[lat] = (side, lat, mate)
+                for lat, free in zip(sorted(idle - inner), sorted(inner - idle)):
+                    target[lat] = (side, free, lon)
+            for lat, (there, row, col) in target.items():
+                route.append(
+                    (
+                        (side * lat_count + lat) * lon_count + lon,
+                        (there * lat_count + row) * lon_count + col,
+                    )
+                )
+    assert len({there for _, there in route}) == len(route)
+    return route
 
 
 class Loop:
@@ -867,7 +883,7 @@
 
     def second_round(turned):
         return [
-            lax.ppermute(turned[step], ("panel", "lat"), lat_route(step, lat_count))
+            lax.ppermute(turned[step], everyone, lat_route(step, lat_count, lon_count))
             for step in start_order(0, lat_count)
         ]
 

time: 61.5 us -> 60.1 us (0.977)
  waiting for transfers between devices: 17.8 us -> 16.3 us
    ppermute x8, waiting for transfers between devices: 7.81 us -> 6.25 us  [second_round(): lax.ppermute(turned[step], everyone, lat_route(step, lat_count, lon_count))]
  transfers between devices with their start and end apart: 19 -> 19, of which waited for: 12 -> 11; matrix products, arithmetic and copies ran while one was open for 4% -> 4% of each run, Pallas kernels for 12% -> 12%
where the time goes in v11:
time: 60.1 us; the launch traced here: 59.8 us
  starting transfers between devices  25.4 us (42%)
  waiting for transfers between devices  16.3 us (27%)
  Pallas kernels  12.8 us (21%)
  local copies, waits for them, and re-layouts  2.88 us (5%)
  other arithmetic  2.24 us (4%)
    ppermute x8, starting transfers between devices, second_round(): lax.ppermute(turned[step], everyone, lat_route(step, lat_count, lon_count))  13.4 us
    ppermute x8, waiting for transfers between devices, second_round(): lax.ppermute(turned[step], everyone, lat_route(step, lat_count, lon_count))  6.25 us
    ppermute x6, waiting for transfers between devices, first_round(): lax.ppermute(packed[step], 'lon', lon_route(step, lon_count))  4.57 us
    ppermute x6, starting transfers between devices, first_round(): lax.ppermute(packed[step], 'lon', lon_route(step, lon_count))  4.41 us
    pallas_call x1, Pallas kernels, per_device(): pl.pallas_call(lambda *refs: first_inner_kernel(loop, *refs), out_shape=[...  3.74 us
    ppermute x1, starting transfers between devices, per_device(): lax.ppermute(send_even, everyone, swap_route(0, lat_count, lon_count, True))  3.12 us
    ppermute x1, waiting for transfers between devices, per_device(): lax.ppermute(send_even, everyone, swap_route(0, lat_count, lon_count, True))  2.95 us
    ppermute x1, starting transfers between devices, per_device(): lax.ppermute(strip_odd, everyone, swap_route(1, lat_count, lon_count, Fal...  2.93 us
  transfers between devices with their start and end apart: 19, of which 11 were waited for; matrix products, arithmetic and copies ran while one was open for 4% of the time, Pallas kernels for 12%

profile of v11, /device:TPU:0, one launch (start us, length us, event | category | flops | bytes accessed | tf_op | source)
XLA Modules:
  0.0 59.8 jit_solution(15878018882700360167)
XLA Ops:
  0.0 1.2 %slice_select_fusion.2 = (f32[1,4,16,8,128]{4,3,2,1,0:T(8,128)S(1)}, f32[1,4,16,8,128]{4,3,2,1,0:T(8,128)S(1)}) fusion(f32[1,16,16,8,128]{4,3,2,1,0:T(8,128)} %param.7, pred[]{:T(512)S(6)} %eq.10), kind=kLoop, calls=%fused_computation.2 | loop fusion | flops 131072 | bytes 1048577 | tf_op jit(solution)/shard_map/jit(_where)/select_n | solution.py:802
  1.2 3.1 %collective-permute-start.1 = (f32[512,128]{1,0:T(8,128)S(1)}, f32[512,128]{1,0:T(8,128)S(1)}, u32[]{:S(2)}, u32[]{:S(2)}) collective-permute-start(f32[512,128]{1,0:T(8,128)S(1)} %bitcast.20), channel_id=1, source_target_pairs={{0,4},{1,5},{2,6},{3,7},{4,0},{5,1},{6,2},{7,3},{8,12},{9,13},{10,... | collective-permute-start | bytes 786440 | tf_op jit(solution)/shard_map/ppermute | solution.py:803
  6.6 1.1 %slice_select_fusion = (f32[16,4,8,128]{3,2,1,0:T(8,128)S(1)}, f32[16,4,8,128]{3,2,1,0:T(8,128)S(1)}) fusion(f32[16,16,8,128]{3,2,1,0:T(8,128)} %bitcast.13, pred[]{:T(512)S(6)} %eq.9), kind=kLoop, calls=%fused_computation | loop fusion | flops 131072 | bytes 1048577 | tf_op jit(solution)/shard_map/jit(_where)/select_n | solution.py:838
  7.6 3.0 %collective-permute-done.1.refs_3_.refs_2_ = f32[512,128]{1,0:T(8,128)S(1)} collective-permute-done((f32[512,128]{1,0:T(8,128)S(1)}, f32[512,128]{1,0:T(8,128)S(1)}, u32[]{:S(2)}, u32[]{:S(2)}) %collective-permute-start.1) | collective-permute-done | bytes 262176 | tf_op jit(solution)/shard_map/ppermute | solution.py:803
  10.7 2.9 %collective-permute-start.3 = (f32[768,128]{1,0:T(8,128)S(1)}, f32[768,128]{1,0:T(8,128)S(1)}, u32[]{:S(2)}, u32[]{:S(2)}) collective-permute-start(f32[768,128]{1,0:T(8,128)S(1)} %get-tuple-element.42), channel_id=1, source_target_pairs={{0,4},{1,2},{2,1},{3,7},{4,0},{5,6},{6,5},{7,3},{8,12},{9,10},{10,... | collective-permute-start | bytes 1179656 | tf_op jit(solution)/shard_map/ppermute | solution.py:847
  14.4 1.5 %collective-permute-start = (s32[2]{0:T(128)S(1)}, s32[2]{0:T(128)S(1)}, u32[]{:S(2)}, u32[]{:S(2)}) collective-permute-start(s32[2]{0:T(128)S(1)} %slice_reduce_fusion.refs_0_), channel_id=1, source_target_pairs={{0,16},{16,0},{1,17},{17,1},{2,18},{18,2},{3,19},{19,3},{4,20},{20... | collective-permute-start | bytes 32 | tf_op jit(solution)/shard_map/ppermute | solution.py:795
  15.9 2.1 %collective-permute-done.refs_1_ = s32[2]{0:T(128)S(1)} collective-permute-done((s32[2]{0:T(128)S(1)}, s32[2]{0:T(128)S(1)}, u32[]{:S(2)}, u32[]{:S(2)}) %collective-permute-start) | collective-permute-done | bytes 40 | tf_op jit(solution)/shard_map/ppermute | solution.py:795
  20.7 1.6 %collective-permute-start.7 = (f32[104,128]{1,0:T(8,128)S(1)}, f32[104,128]{1,0:T(8,128)S(1)}, u32[]{:S(2)}, u32[]{:S(2)}) collective-permute-start(f32[104,128]{1,0:T(8,128)S(1)} %get-tuple-element.48), channel_id=1, source_target_pairs={{0,1},{1,0},{2,3},{3,2},{4,5},{5,4},{6,7},{7,6},{8,9},{9,8},{10,11... | collective-permute-start | bytes 159752 | tf_op jit(solution)/shard_map/ppermute | solution.py:872
  22.3 2.3 %collective-permute-done.5.refs_1_ = f32[104,128]{1,0:T(8,128)S(1)} collective-permute-done((f32[104,128]{1,0:T(8,128)S(1)}, f32[104,128]{1,0:T(8,128)S(1)}, u32[]{:S(2)}, u32[]{:S(2)}) %collective-permute-start.5) | collective-permute-done | bytes 53280 | tf_op jit(solution)/shard_map/ppermute | solution.py:872
  24.6 4.8 %collective-permute-start.8 = (f32[160,128]{1,0:T(8,128)S(1)}, f32[160,128]{1,0:T(8,128)S(1)}, u32[]{:S(2)}, u32[]{:S(2)}) collective-permute-start(f32[160,128]{1,0:T(8,128)S(1)} %get-tuple-element.54), channel_id=1, source_target_pairs={{0,24},{4,28},{8,16},{12,20},{1,5},{5,29},{9,17},{13,9},{2,6},{6,3... | collective-permute-start | bytes 245768 | tf_op jit(solution)/shard_map/ppermute | solution.py:886
  29.4 1.2 %collective-permute-start.9 = (f32[160,128]{1,0:T(8,128)S(1)}, f32[160,128]{1,0:T(8,128)S(1)}, u32[]{:S(2)}, u32[]{:S(2)}) collective-permute-start(f32[160,128]{1,0:T(8,128)S(1)} %get-tuple-element.55), channel_id=1, source_target_pairs={{0,28},{4,24},{8,20},{12,16},{1,29},{5,6},{9,10},{13,17},{2,30},{6... | collective-permute-start | bytes 245768 | tf_op jit(solution)/shard_map/ppermute | solution.py:886
  30.6 1.5 %collective-permute-start.11 = (f32[160,128]{1,0:T(8,128)S(1)}, f32[160,128]{1,0:T(8,128)S(1)}, u32[]{:S(2)}, u32[]{:S(2)}) collective-permute-start(f32[160,128]{1,0:T(8,128)S(1)} %get-tuple-element.49.refs_3_), channel_id=1, source_target_pairs={{0,16},{4,20},{8,24},{12,28},{1,17},{5,6},{9,10},{13,29},{2,18},{6... | collective-permute-start | bytes 245768 | tf_op jit(solution)/shard_map/ppermute | solution.py:886
  32.1 3.7 %first_inner.1 = (f32[4608,128]{1,0:T(8,128)S(1)}, f32[8,24,24,128]{3,2,1,0:T(8,128)S(1)}, f32[7680,128]{1,0:T(8,128)S(1)}, f32[12480,128]{1,0:T(8,128)S(1)}) custom-call(f32[296,128]{1,0:T(8,128)S(1)} %copy-done.1, f32[7,8,128]{2,1,0:T(8,128)S(1)} %copy-done.2, f32[4608,128]{1,0:T(8,128)S(1)} %get-tuple-element.44.refs_2_, ...), custom_call_target="tpu_custom_call" | custom-call | tf_op jit(solution)/shard_map/first_inner/pallas_call | solution.py:898
  37.0 1.3 %collective-permute-done.11.refs_13_ = f32[160,128]{1,0:T(8,128)S(1)} collective-permute-done((f32[160,128]{1,0:T(8,128)S(1)}, f32[160,128]{1,0:T(8,128)S(1)}, u32[]{:S(2)}, u32[]{:S(2)}) %collective-permute-start.11) | collective-permute-done | bytes 81952 | tf_op jit(solution)/shard_map/ppermute | solution.py:886
  38.3 2.1 %first_edge.1 = (f32[4608,128]{1,0:T(8,128)S(1)}, f32[8,24,24,128]{3,2,1,0:T(8,128)S(1)}, f32[7680,128]{1,0:T(8,128)S(1)}, f32[12480,128]{1,0:T(8,128)S(1)}, f32...) custom-call(s32[56,128]{1,0:T(8,128)S(1)} %get-tuple-element.39.refs, ...), custom_call_target="tpu_custom_call", output_to_operand_aliasing={{0}: (6, {}), {1}: (7, {}), {2}: (8, {}), {3}: (9, {})} | custom-call | tf_op jit(solution)/shard_map/first_edge/pallas_call | solution.py:906
  41.0 1.7 %collective-permute-start.14 = (f32[104,128]{1,0:T(8,128)S(1)}, f32[104,128]{1,0:T(8,128)S(1)}, u32[]{:S(2)}, u32[]{:S(2)}) collective-permute-start(f32[104,128]{1,0:T(8,128)S(1)} %get-tuple-element.62), channel_id=1, source_target_pairs={{0,1},{1,0},{2,3},{3,2},{4,5},{5,4},{6,7},{7,6},{8,9},{9,8},{10,11... | collective-permute-start | bytes 159752 | tf_op jit(solution)/shard_map/ppermute | solution.py:872
  42.6 2.3 %collective-permute-done.12.refs_1_ = f32[104,128]{1,0:T(8,128)S(1)} collective-permute-done((f32[104,128]{1,0:T(8,128)S(1)}, f32[104,128]{1,0:T(8,128)S(1)}, u32[]{:S(2)}, u32[]{:S(2)}) %collective-permute-start.12) | collective-permute-done | bytes 53280 | tf_op jit(solution)/shard_map/ppermute | solution.py:872
  45.0 1.2 %collective-permute-start.15 = (f32[160,128]{1,0:T(8,128)S(1)}, f32[160,128]{1,0:T(8,128)S(1)}, u32[]{:S(2)}, u32[]{:S(2)}) collective-permute-start(f32[160,128]{1,0:T(8,128)S(1)} %get-tuple-element.67), channel_id=1, source_target_pairs={{0,24},{4,28},{8,16},{12,20},{1,5},{5,29},{9,17},{13,9},{2,6},{6,3... | collective-permute-start | bytes 245768 | tf_op jit(solution)/shard_map/ppermute | solution.py:886
  46.2 1.6 %collective-permute-start.16 = (f32[160,128]{1,0:T(8,128)S(1)}, f32[160,128]{1,0:T(8,128)S(1)}, u32[]{:S(2)}, u32[]{:S(2)}) collective-permute-start(f32[160,128]{1,0:T(8,128)S(1)} %get-tuple-element.68), channel_id=1, source_target_pairs={{0,28},{4,24},{8,20},{12,16},{1,29},{5,6},{9,10},{13,17},{2,30},{6... | collective-permute-start | bytes 245768 | tf_op jit(solution)/shard_map/ppermute | solution.py:886
  47.8 2.1 %collective-permute-start.17 = (f32[160,128]{1,0:T(8,128)S(1)}, f32[160,128]{1,0:T(8,128)S(1)}, u32[]{:S(2)}, u32[]{:S(2)}) collective-permute-start(f32[160,128]{1,0:T(8,128)S(1)} %get-tuple-element.69), channel_id=1, source_target_pairs={{0,20},{4,16},{8,28},{12,24},{1,5},{5,17},{9,29},{13,9},{2,6},{6,1... | collective-permute-start | bytes 245768 | tf_op jit(solution)/shard_map/ppermute | solution.py:886
  50.9 2.8 %second_inner.1 = (f32[2048,128]{1,0:T(8,128)S(1)}, f32[7680,128]{1,0:T(8,128)S(1)}, f32[12480,128]{1,0:T(8,128)S(1)}) custom-call(f32[296,128]{1,0:T(8,128)S(1)} %copy-done.1, f32[7,8,128]{2,1,0:T(8,128)S(1)} %copy-done.2, f32[4608,128]{1,0:T(8,128)S(1)} %get-tuple-element.58.refs_2_, f32[8,24,24,128]{3,2,1,0:T(8,128)S(1)} %get-tuple-element.57.refs_3_, ...), custom_call_target="tpu_custom_call" | custom-call | tf_op jit(solution)/shard_map/second_inner/pallas_call | solution.py:919
  54.2 1.7 %collective-permute-done.17.refs_9_ = f32[160,128]{1,0:T(8,128)S(1)} collective-permute-done((f32[160,128]{1,0:T(8,128)S(1)}, f32[160,128]{1,0:T(8,128)S(1)}, u32[]{:S(2)}, u32[]{:S(2)}) %collective-permute-start.17) | collective-permute-done | bytes 81952 | tf_op jit(solution)/shard_map/ppermute | solution.py:886
  55.8 1.7 %collective-permute-done.18.refs_10_ = f32[160,128]{1,0:T(8,128)S(1)} collective-permute-done((f32[160,128]{1,0:T(8,128)S(1)}, f32[160,128]{1,0:T(8,128)S(1)}, u32[]{:S(2)}, u32[]{:S(2)}) %collective-permute-start.18) | collective-permute-done | bytes 81952 | tf_op jit(solution)/shard_map/ppermute | solution.py:886
  57.5 2.4 %second_edge.1 = (f32[7680,128]{1,0:T(8,128)S(1)}, f32[12480,128]{1,0:T(8,128)S(1)}, f32[2048,128]{1,0:T(8,128)}) custom-call(s32[80,128]{1,0:T(8,128)S(1)} %get-tuple-element.38.refs_3_.refs_0_, f32[296,128]{1,0:T(8,128)S(1)} %copy-done.1, f32[7,8,128]{2,1,0:T(8,128)S(1)} %copy-done.2, ...), custom_call_target="tpu_custom_call", output_to_operand_aliasing={{0}: (5, {}), {1}: (6, {})} | custom-call | tf_op jit(solution)/shard_map/second_edge/pallas_call | solution.py:927
  (40 shorter events, 9.0 us)
Async XLA Ops:
  0.0 18.7 %copy-start = (f32[1,16,16,8,128]{4,3,2,1,0:T(8,128)S(1)}, f32[1,16,16,8,128]{4,3,2,1,0:T(8,128)}, u32[]{:S(2)}) copy-start(f32[1,16,16,8,128]{4,3,2,1,0:T(8,128)} %param.7) | copy-start | bytes 3145732
  1.2 9.4 %collective-permute-start.1 = (f32[512,128]{1,0:T(8,128)S(1)}, f32[512,128]{1,0:T(8,128)S(1)}, u32[]{:S(2)}, u32[]{:S(2)}) collective-permute-start(f32[512,128]{1,0:T(8,128)S(1)} %bitcast.20), channel_id=1, source_target_pairs={{0,4},{1,5},{2,6},{3,7},{4,0},{5,1},{6,2},{7,3},{8,12},{9,13},{10,... | collective-permute-start | bytes 786440 | tf_op jit(solution)/shard_map/ppermute | solution.py:803
  4.3 6.3 %collective-permute-start.2 = (f32[512,128]{1,0:T(8,128)S(1)}, f32[512,128]{1,0:T(8,128)S(1)}, u32[]{:S(2)}, u32[]{:S(2)}) collective-permute-start(f32[512,128]{1,0:T(8,128)S(1)} %bitcast.19), channel_id=1, source_target_pairs={{0,1},{1,0},{2,3},{3,2},{4,8},{5,9},{6,10},{7,11},{8,4},{9,5},{10,... | collective-permute-start | bytes 786440 | tf_op jit(solution)/shard_map/ppermute | solution.py:804
  5.0 0.7 %copy-start.3 = (f32[1,32,16]{1,2,0:T(8,128)S(1)}, f32[1,32,16]{1,2,0:T(8,128)}, u32[]{:S(2)}) copy-start(f32[1,32,16]{1,2,0:T(8,128)} %param.9) | copy-start | bytes 6148
  5.7 0.7 %copy-start.4 = (s32[1,32,2]{1,2,0:T(2,128)S(1)}, s32[1,32,2]{1,2,0:T(2,128)}, u32[]{:S(2)}) copy-start(s32[1,32,2]{1,2,0:T(2,128)} %param.8) | copy-start | bytes 772
  10.7 8.7 %collective-permute-start.3 = (f32[768,128]{1,0:T(8,128)S(1)}, f32[768,128]{1,0:T(8,128)S(1)}, u32[]{:S(2)}, u32[]{:S(2)}) collective-permute-start(f32[768,128]{1,0:T(8,128)S(1)} %get-tuple-element.42), channel_id=1, source_target_pairs={{0,4},{1,2},{2,1},{3,7},{4,0},{5,6},{6,5},{7,3},{8,12},{9,10},{10,... | collective-permute-start | bytes 1179656 | tf_op jit(solution)/shard_map/ppermute | solution.py:847
  13.6 5.8 %collective-permute-start.4 = (f32[768,128]{1,0:T(8,128)S(1)}, f32[768,128]{1,0:T(8,128)S(1)}, u32[]{:S(2)}, u32[]{:S(2)}) collective-permute-start(f32[768,128]{1,0:T(8,128)S(1)} %get-tuple-element.43.refs_0_), channel_id=1, source_target_pairs={{0,1},{1,0},{2,3},{3,2},{4,5},{5,4},{6,7},{7,6},{8,9},{9,8},{10,11... | collective-permute-start | bytes 1179656 | tf_op jit(solution)/shard_map/ppermute | solution.py:848
  14.4 3.6 %collective-permute-start = (s32[2]{0:T(128)S(1)}, s32[2]{0:T(128)S(1)}, u32[]{:S(2)}, u32[]{:S(2)}) collective-permute-start(s32[2]{0:T(128)S(1)} %slice_reduce_fusion.refs_0_), channel_id=1, source_target_pairs={{0,16},{16,0},{1,17},{17,1},{2,18},{18,2},{3,19},{19,3},{4,20},{20... | collective-permute-start | bytes 32 | tf_op jit(solution)/shard_map/ppermute | solution.py:795
  18.7 13.4 %copy-start.1 = (f32[296,128]{1,0:T(8,128)S(1)}, f32[296,128]{1,0:T(8,128)}, u32[]{:S(2)}) copy-start(f32[296,128]{1,0:T(8,128)} %constant.29.clone.refs_0_.refs_4_.refs_1_) | copy-start | bytes 454660
  18.7 13.4 %copy-start.2 = (f32[7,8,128]{2,1,0:T(8,128)S(1)}, f32[7,8,128]{2,1,0:T(8,128)}, u32[]{:S(2)}) copy-start(f32[7,8,128]{2,1,0:T(8,128)} %constant.30.clone.refs_1_.refs_5_.refs_2_) | copy-start | bytes 86020
  20.1 4.5 %collective-permute-start.5 = (f32[104,128]{1,0:T(8,128)S(1)}, f32[104,128]{1,0:T(8,128)S(1)}, u32[]{:S(2)}, u32[]{:S(2)}) collective-permute-start(f32[104,128]{1,0:T(8,128)S(1)} %get-tuple-element.46), channel_id=1, source_target_pairs={{0,2},{1,3},{2,0},{3,1},{4,6},{5,7},{6,4},{7,5},{8,10},{9,11},{10,... | collective-permute-start | bytes 159752 | tf_op jit(solution)/shard_map/ppermute | solution.py:872
  20.4 4.1 %collective-permute-start.6 = (f32[104,128]{1,0:T(8,128)S(1)}, f32[104,128]{1,0:T(8,128)S(1)}, u32[]{:S(2)}, u32[]{:S(2)}) collective-permute-start(f32[104,128]{1,0:T(8,128)S(1)} %get-tuple-element.47), channel_id=1, source_target_pairs={{0,3},{1,2},{2,1},{3,0},{4,7},{5,6},{6,5},{7,4},{8,11},{9,10},{10,... | collective-permute-start | bytes 159752 | tf_op jit(solution)/shard_map/ppermute | solution.py:872
  20.7 3.8 %collective-permute-start.7 = (f32[104,128]{1,0:T(8,128)S(1)}, f32[104,128]{1,0:T(8,128)S(1)}, u32[]{:S(2)}, u32[]{:S(2)}) collective-permute-start(f32[104,128]{1,0:T(8,128)S(1)} %get-tuple-element.48), channel_id=1, source_target_pairs={{0,1},{1,0},{2,3},{3,2},{4,5},{5,4},{6,7},{7,6},{8,9},{9,8},{10,11... | collective-permute-start | bytes 159752 | tf_op jit(solution)/shard_map/ppermute | solution.py:872
  24.6 11.3 %collective-permute-start.8 = (f32[160,128]{1,0:T(8,128)S(1)}, f32[160,128]{1,0:T(8,128)S(1)}, u32[]{:S(2)}, u32[]{:S(2)}) collective-permute-start(f32[160,128]{1,0:T(8,128)S(1)} %get-tuple-element.54), channel_id=1, source_target_pairs={{0,24},{4,28},{8,16},{12,20},{1,5},{5,29},{9,17},{13,9},{2,6},{6,3... | collective-permute-start | bytes 245768 | tf_op jit(solution)/shard_map/ppermute | solution.py:886
  29.4 7.3 %collective-permute-start.9 = (f32[160,128]{1,0:T(8,128)S(1)}, f32[160,128]{1,0:T(8,128)S(1)}, u32[]{:S(2)}, u32[]{:S(2)}) collective-permute-start(f32[160,128]{1,0:T(8,128)S(1)} %get-tuple-element.55), channel_id=1, source_target_pairs={{0,28},{4,24},{8,20},{12,16},{1,29},{5,6},{9,10},{13,17},{2,30},{6... | collective-permute-start | bytes 245768 | tf_op jit(solution)/shard_map/ppermute | solution.py:886
  30.6 6.4 %collective-permute-start.10 = (f32[160,128]{1,0:T(8,128)S(1)}, f32[160,128]{1,0:T(8,128)S(1)}, u32[]{:S(2)}, u32[]{:S(2)}) collective-permute-start(f32[160,128]{1,0:T(8,128)S(1)} %get-tuple-element.56), channel_id=1, source_target_pairs={{0,20},{4,16},{8,28},{12,24},{1,5},{5,17},{9,29},{13,9},{2,6},{6,1... | collective-permute-start | bytes 245768 | tf_op jit(solution)/shard_map/ppermute | solution.py:886
  30.6 7.7 %collective-permute-start.11 = (f32[160,128]{1,0:T(8,128)S(1)}, f32[160,128]{1,0:T(8,128)S(1)}, u32[]{:S(2)}, u32[]{:S(2)}) collective-permute-start(f32[160,128]{1,0:T(8,128)S(1)} %get-tuple-element.49.refs_3_), channel_id=1, source_target_pairs={{0,16},{4,20},{8,24},{12,28},{1,17},{5,6},{9,10},{13,29},{2,18},{6... | collective-permute-start | bytes 245768 | tf_op jit(solution)/shard_map/ppermute | solution.py:886
  40.4 4.5 %collective-permute-start.12 = (f32[104,128]{1,0:T(8,128)S(1)}, f32[104,128]{1,0:T(8,128)S(1)}, u32[]{:S(2)}, u32[]{:S(2)}) collective-permute-start(f32[104,128]{1,0:T(8,128)S(1)} %get-tuple-element.60), channel_id=1, source_target_pairs={{0,2},{1,3},{2,0},{3,1},{4,6},{5,7},{6,4},{7,5},{8,10},{9,11},{10,... | collective-permute-start | bytes 159752 | tf_op jit(solution)/shard_map/ppermute | solution.py:872
  40.8 4.1 %collective-permute-start.13 = (f32[104,128]{1,0:T(8,128)S(1)}, f32[104,128]{1,0:T(8,128)S(1)}, u32[]{:S(2)}, u32[]{:S(2)}) collective-permute-start(f32[104,128]{1,0:T(8,128)S(1)} %get-tuple-element.61), channel_id=1, source_target_pairs={{0,3},{1,2},{2,1},{3,0},{4,7},{5,6},{6,5},{7,4},{8,11},{9,10},{10,... | collective-permute-start | bytes 159752 | tf_op jit(solution)/shard_map/ppermute | solution.py:872
  41.0 4.0 %collective-permute-start.14 = (f32[104,128]{1,0:T(8,128)S(1)}, f32[104,128]{1,0:T(8,128)S(1)}, u32[]{:S(2)}, u32[]{:S(2)}) collective-permute-start(f32[104,128]{1,0:T(8,128)S(1)} %get-tuple-element.62), channel_id=1, source_target_pairs={{0,1},{1,0},{2,3},{3,2},{4,5},{5,4},{6,7},{7,6},{8,9},{9,8},{10,11... | collective-permute-start | bytes 159752 | tf_op jit(solution)/shard_map/ppermute | solution.py:872
  45.0 9.2 %collective-permute-start.15 = (f32[160,128]{1,0:T(8,128)S(1)}, f32[160,128]{1,0:T(8,128)S(1)}, u32[]{:S(2)}, u32[]{:S(2)}) collective-permute-start(f32[160,128]{1,0:T(8,128)S(1)} %get-tuple-element.67), channel_id=1, source_target_pairs={{0,24},{4,28},{8,16},{12,20},{1,5},{5,29},{9,17},{13,9},{2,6},{6,3... | collective-permute-start | bytes 245768 | tf_op jit(solution)/shard_map/ppermute | solution.py:886
  46.2 7.9 %collective-permute-start.16 = (f32[160,128]{1,0:T(8,128)S(1)}, f32[160,128]{1,0:T(8,128)S(1)}, u32[]{:S(2)}, u32[]{:S(2)}) collective-permute-start(f32[160,128]{1,0:T(8,128)S(1)} %get-tuple-element.68), channel_id=1, source_target_pairs={{0,28},{4,24},{8,20},{12,16},{1,29},{5,6},{9,10},{13,17},{2,30},{6... | collective-permute-start | bytes 245768 | tf_op jit(solution)/shard_map/ppermute | solution.py:886
  47.8 8.0 %collective-permute-start.17 = (f32[160,128]{1,0:T(8,128)S(1)}, f32[160,128]{1,0:T(8,128)S(1)}, u32[]{:S(2)}, u32[]{:S(2)}) collective-permute-start(f32[160,128]{1,0:T(8,128)S(1)} %get-tuple-element.69), channel_id=1, source_target_pairs={{0,20},{4,16},{8,28},{12,24},{1,5},{5,17},{9,29},{13,9},{2,6},{6,1... | collective-permute-start | bytes 245768 | tf_op jit(solution)/shard_map/ppermute | solution.py:886
  49.9 7.6 %collective-permute-start.18 = (f32[160,128]{1,0:T(8,128)S(1)}, f32[160,128]{1,0:T(8,128)S(1)}, u32[]{:S(2)}, u32[]{:S(2)}) collective-permute-start(f32[160,128]{1,0:T(8,128)S(1)} %get-tuple-element.63.refs_4_), channel_id=1, source_target_pairs={{0,16},{4,20},{8,24},{12,28},{1,17},{5,6},{9,10},{13,29},{2,18},{6... | collective-permute-start | bytes 245768 | tf_op jit(solution)/shard_map/ppermute | solution.py:886

commit v12 on v11

--- a/solution.py
+++ b/solution.py
@@ -20,12 +20,11 @@
 TILE = 8
 
 
-def hardest_first(step):
-    return -step.bit_length(), step
-
-
 def start_order(first, count):
-    return sorted(range(first, count), key=hardest_first)
+    down = first == 1
+    odd = sorted((n for n in range(first, count) if n % 2), reverse=down)
+    even = sorted((n for n in range(first, count) if n % 2 == 0), reverse=not down)
+    return odd + even
 
 
 def by_step(first, refs):

time: 60.1 us -> 58.3 us (0.970)
  waiting for transfers between devices: 16.3 us -> 14.4 us
    ppermute x8, waiting for transfers between devices: 6.25 us -> 3.81 us  [second_round(): lax.ppermute(turned[step], everyone, lat_route(step, lat_count, lon_count))]
  transfers between devices with their start and end apart: 19 -> 19, of which waited for: 11 -> 10; matrix products, arithmetic and copies ran while one was open for 4% -> 4% of each run, Pallas kernels for 12% -> 13%
where the time goes in v12:
time: 58.3 us; the launch traced here: 58 us
  starting transfers between devices  25.5 us (44%)
  waiting for transfers between devices  14.4 us (25%)
  Pallas kernels  12.8 us (22%)
  local copies, waits for them, and re-layouts  2.88 us (5%)
  other arithmetic  2.24 us (4%)
    ppermute x8, starting transfers between devices, second_round(): lax.ppermute(turned[step], everyone, lat_route(step, lat_count, lon_count))  13.5 us
    ppermute x6, waiting for transfers between devices, first_round(): lax.ppermute(packed[step], 'lon', lon_route(step, lon_count))  5.11 us
    ppermute x6, starting transfers between devices, first_round(): lax.ppermute(packed[step], 'lon', lon_route(step, lon_count))  4.4 us
    ppermute x8, waiting for transfers between devices, second_round(): lax.ppermute(turned[step], everyone, lat_route(step, lat_count, lon_count))  3.81 us
    pallas_call x1, Pallas kernels, per_device(): pl.pallas_call(lambda *refs: first_inner_kernel(loop, *refs), out_shape=[...  3.74 us
    ppermute x1, starting transfers between devices, per_device(): lax.ppermute(send_even, everyone, swap_route(0, lat_count, lon_count, True))  3.12 us
    ppermute x1, waiting for transfers between devices, per_device(): lax.ppermute(send_even, everyone, swap_route(0, lat_count, lon_count, True))  2.95 us
    ppermute x1, starting transfers between devices, per_device(): lax.ppermute(strip_odd, everyone, swap_route(1, lat_count, lon_count, Fal...  2.93 us
  transfers between devices with their start and end apart: 19, of which 10 were waited for; matrix products, arithmetic and copies ran while one was open for 4% of the time, Pallas kernels for 13%

profile of v12, /device:TPU:0, one launch (start us, length us, event | category | flops | bytes accessed | tf_op | source)
XLA Modules:
  0.0 58.0 jit_solution(684114247734189813)
XLA Ops:
  0.0 1.2 %slice_select_fusion.2 = (f32[1,4,16,8,128]{4,3,2,1,0:T(8,128)S(1)}, f32[1,4,16,8,128]{4,3,2,1,0:T(8,128)S(1)}) fusion(f32[1,16,16,8,128]{4,3,2,1,0:T(8,128)} %param.7, pred[]{:T(512)S(6)} %eq.10), kind=kLoop, calls=%fused_computation.2 | loop fusion | flops 131072 | bytes 1048577 | tf_op jit(solution)/shard_map/jit(_where)/select_n | solution.py:801
  1.2 3.1 %collective-permute-start.1 = (f32[512,128]{1,0:T(8,128)S(1)}, f32[512,128]{1,0:T(8,128)S(1)}, u32[]{:S(2)}, u32[]{:S(2)}) collective-permute-start(f32[512,128]{1,0:T(8,128)S(1)} %bitcast.20), channel_id=1, source_target_pairs={{0,4},{1,5},{2,6},{3,7},{4,0},{5,1},{6,2},{7,3},{8,12},{9,13},{10,... | collective-permute-start | bytes 786440 | tf_op jit(solution)/shard_map/ppermute | solution.py:802
  7.6 3.0 %collective-permute-done.1.refs_3_.refs_2_ = f32[512,128]{1,0:T(8,128)S(1)} collective-permute-done((f32[512,128]{1,0:T(8,128)S(1)}, f32[512,128]{1,0:T(8,128)S(1)}, u32[]{:S(2)}, u32[]{:S(2)}) %collective-permute-start.1) | collective-permute-done | bytes 262176 | tf_op jit(solution)/shard_map/ppermute | solution.py:802
  10.7 2.9 %collective-permute-start.3 = (f32[768,128]{1,0:T(8,128)S(1)}, f32[768,128]{1,0:T(8,128)S(1)}, u32[]{:S(2)}, u32[]{:S(2)}) collective-permute-start(f32[768,128]{1,0:T(8,128)S(1)} %get-tuple-element.42), channel_id=1, source_target_pairs={{0,4},{1,2},{2,1},{3,7},{4,0},{5,6},{6,5},{7,3},{8,12},{9,10},{10,... | collective-permute-start | bytes 1179656 | tf_op jit(solution)/shard_map/ppermute | solution.py:846
  14.4 1.5 %collective-permute-start = (s32[2]{0:T(128)S(1)}, s32[2]{0:T(128)S(1)}, u32[]{:S(2)}, u32[]{:S(2)}) collective-permute-start(s32[2]{0:T(128)S(1)} %slice_reduce_fusion.refs_0_), channel_id=1, source_target_pairs={{0,16},{16,0},{1,17},{17,1},{2,18},{18,2},{3,19},{19,3},{4,20},{20... | collective-permute-start | bytes 32 | tf_op jit(solution)/shard_map/ppermute | solution.py:794
  15.9 2.1 %collective-permute-done.refs_1_ = s32[2]{0:T(128)S(1)} collective-permute-done((s32[2]{0:T(128)S(1)}, s32[2]{0:T(128)S(1)}, u32[]{:S(2)}, u32[]{:S(2)}) %collective-permute-start) | collective-permute-done | bytes 40 | tf_op jit(solution)/shard_map/ppermute | solution.py:794
  20.5 1.8 %collective-permute-start.7 = (f32[104,128]{1,0:T(8,128)S(1)}, f32[104,128]{1,0:T(8,128)S(1)}, u32[]{:S(2)}, u32[]{:S(2)}) collective-permute-start(f32[104,128]{1,0:T(8,128)S(1)} %get-tuple-element.48), channel_id=1, source_target_pairs={{0,2},{1,3},{2,0},{3,1},{4,6},{5,7},{6,4},{7,5},{8,10},{9,11},{10,... | collective-permute-start | bytes 159752 | tf_op jit(solution)/shard_map/ppermute | solution.py:871
  22.3 1.4 %collective-permute-done.5.refs_1_ = f32[104,128]{1,0:T(8,128)S(1)} collective-permute-done((f32[104,128]{1,0:T(8,128)S(1)}, f32[104,128]{1,0:T(8,128)S(1)}, u32[]{:S(2)}, u32[]{:S(2)}) %collective-permute-start.5) | collective-permute-done | bytes 53280 | tf_op jit(solution)/shard_map/ppermute | solution.py:871
  23.7 1.1 %collective-permute-done.7.refs_3_ = f32[104,128]{1,0:T(8,128)S(1)} collective-permute-done((f32[104,128]{1,0:T(8,128)S(1)}, f32[104,128]{1,0:T(8,128)S(1)}, u32[]{:S(2)}, u32[]{:S(2)}) %collective-permute-start.7) | collective-permute-done | bytes 53280 | tf_op jit(solution)/shard_map/ppermute | solution.py:871
  24.9 3.5 %collective-permute-start.8 = (f32[160,128]{1,0:T(8,128)S(1)}, f32[160,128]{1,0:T(8,128)S(1)}, u32[]{:S(2)}, u32[]{:S(2)}) collective-permute-start(f32[160,128]{1,0:T(8,128)S(1)} %get-tuple-element.54), channel_id=1, source_target_pairs={{0,20},{4,16},{8,28},{12,24},{1,5},{5,17},{9,29},{13,9},{2,6},{6,1... | collective-permute-start | bytes 245768 | tf_op jit(solution)/shard_map/ppermute | solution.py:885
  28.4 2.6 %collective-permute-start.9 = (f32[160,128]{1,0:T(8,128)S(1)}, f32[160,128]{1,0:T(8,128)S(1)}, u32[]{:S(2)}, u32[]{:S(2)}) collective-permute-start(f32[160,128]{1,0:T(8,128)S(1)} %get-tuple-element.55), channel_id=1, source_target_pairs={{0,28},{4,24},{8,20},{12,16},{1,29},{5,6},{9,10},{13,17},{2,30},{6... | collective-permute-start | bytes 245768 | tf_op jit(solution)/shard_map/ppermute | solution.py:885
  31.0 1.5 %collective-permute-start.11 = (f32[160,128]{1,0:T(8,128)S(1)}, f32[160,128]{1,0:T(8,128)S(1)}, u32[]{:S(2)}, u32[]{:S(2)}) collective-permute-start(f32[160,128]{1,0:T(8,128)S(1)} %get-tuple-element.49.refs_3_), channel_id=1, source_target_pairs={{0,16},{4,20},{8,24},{12,28},{1,17},{5,6},{9,10},{13,29},{2,18},{6... | collective-permute-start | bytes 245768 | tf_op jit(solution)/shard_map/ppermute | solution.py:885
  32.5 3.7 %first_inner.1 = (f32[4608,128]{1,0:T(8,128)S(1)}, f32[8,24,24,128]{3,2,1,0:T(8,128)S(1)}, f32[7680,128]{1,0:T(8,128)S(1)}, f32[12480,128]{1,0:T(8,128)S(1)}) custom-call(f32[296,128]{1,0:T(8,128)S(1)} %copy-done.1, f32[7,8,128]{2,1,0:T(8,128)S(1)} %copy-done.2, f32[4608,128]{1,0:T(8,128)S(1)} %get-tuple-element.44.refs_2_, ...), custom_call_target="tpu_custom_call" | custom-call | tf_op jit(solution)/shard_map/first_inner/pallas_call | solution.py:897
  36.3 1.2 %collective-permute-done.10.refs_12_ = f32[160,128]{1,0:T(8,128)S(1)} collective-permute-done((f32[160,128]{1,0:T(8,128)S(1)}, f32[160,128]{1,0:T(8,128)S(1)}, u32[]{:S(2)}, u32[]{:S(2)}) %collective-permute-start.10) | collective-permute-done | bytes 81952 | tf_op jit(solution)/shard_map/ppermute | solution.py:885
  37.5 2.1 %first_edge.1 = (f32[4608,128]{1,0:T(8,128)S(1)}, f32[8,24,24,128]{3,2,1,0:T(8,128)S(1)}, f32[7680,128]{1,0:T(8,128)S(1)}, f32[12480,128]{1,0:T(8,128)S(1)}, f32...) custom-call(s32[56,128]{1,0:T(8,128)S(1)} %get-tuple-element.39.refs, ...), custom_call_target="tpu_custom_call", output_to_operand_aliasing={{0}: (6, {}), {1}: (7, {}), {2}: (8, {}), {3}: (9, {})} | custom-call | tf_op jit(solution)/shard_map/first_edge/pallas_call | solution.py:905
  40.1 1.7 %collective-permute-start.14 = (f32[104,128]{1,0:T(8,128)S(1)}, f32[104,128]{1,0:T(8,128)S(1)}, u32[]{:S(2)}, u32[]{:S(2)}) collective-permute-start(f32[104,128]{1,0:T(8,128)S(1)} %get-tuple-element.62), channel_id=1, source_target_pairs={{0,2},{1,3},{2,0},{3,1},{4,6},{5,7},{6,4},{7,5},{8,10},{9,11},{10,... | collective-permute-start | bytes 159752 | tf_op jit(solution)/shard_map/ppermute | solution.py:871
  41.8 1.4 %collective-permute-done.12.refs_1_ = f32[104,128]{1,0:T(8,128)S(1)} collective-permute-done((f32[104,128]{1,0:T(8,128)S(1)}, f32[104,128]{1,0:T(8,128)S(1)}, u32[]{:S(2)}, u32[]{:S(2)}) %collective-permute-start.12) | collective-permute-done | bytes 53280 | tf_op jit(solution)/shard_map/ppermute | solution.py:871
  43.2 1.1 %collective-permute-done.14.refs_3_ = f32[104,128]{1,0:T(8,128)S(1)} collective-permute-done((f32[104,128]{1,0:T(8,128)S(1)}, f32[104,128]{1,0:T(8,128)S(1)}, u32[]{:S(2)}, u32[]{:S(2)}) %collective-permute-start.14) | collective-permute-done | bytes 53280 | tf_op jit(solution)/shard_map/ppermute | solution.py:871
  44.4 1.2 %collective-permute-start.15 = (f32[160,128]{1,0:T(8,128)S(1)}, f32[160,128]{1,0:T(8,128)S(1)}, u32[]{:S(2)}, u32[]{:S(2)}) collective-permute-start(f32[160,128]{1,0:T(8,128)S(1)} %get-tuple-element.67), channel_id=1, source_target_pairs={{0,20},{4,16},{8,28},{12,24},{1,5},{5,17},{9,29},{13,9},{2,6},{6,1... | collective-permute-start | bytes 245768 | tf_op jit(solution)/shard_map/ppermute | solution.py:885
  45.6 2.7 %collective-permute-start.16 = (f32[160,128]{1,0:T(8,128)S(1)}, f32[160,128]{1,0:T(8,128)S(1)}, u32[]{:S(2)}, u32[]{:S(2)}) collective-permute-start(f32[160,128]{1,0:T(8,128)S(1)} %get-tuple-element.68), channel_id=1, source_target_pairs={{0,28},{4,24},{8,20},{12,16},{1,29},{5,6},{9,10},{13,17},{2,30},{6... | collective-permute-start | bytes 245768 | tf_op jit(solution)/shard_map/ppermute | solution.py:885
  48.4 1.2 %collective-permute-start.17 = (f32[160,128]{1,0:T(8,128)S(1)}, f32[160,128]{1,0:T(8,128)S(1)}, u32[]{:S(2)}, u32[]{:S(2)}) collective-permute-start(f32[160,128]{1,0:T(8,128)S(1)} %get-tuple-element.69), channel_id=1, source_target_pairs={{0,24},{4,28},{8,16},{12,20},{1,5},{5,29},{9,17},{13,9},{2,6},{6,3... | collective-permute-start | bytes 245768 | tf_op jit(solution)/shard_map/ppermute | solution.py:885
  50.3 2.8 %second_inner.1 = (f32[2048,128]{1,0:T(8,128)S(1)}, f32[7680,128]{1,0:T(8,128)S(1)}, f32[12480,128]{1,0:T(8,128)S(1)}) custom-call(f32[296,128]{1,0:T(8,128)S(1)} %copy-done.1, f32[7,8,128]{2,1,0:T(8,128)S(1)} %copy-done.2, f32[4608,128]{1,0:T(8,128)S(1)} %get-tuple-element.58.refs_2_, f32[8,24,24,128]{3,2,1,0:T(8,128)S(1)} %get-tuple-element.57.refs_3_, ...), custom_call_target="tpu_custom_call" | custom-call | tf_op jit(solution)/shard_map/second_inner/pallas_call | solution.py:918
  53.5 2.2 %collective-permute-done.17.refs_9_ = f32[160,128]{1,0:T(8,128)S(1)} collective-permute-done((f32[160,128]{1,0:T(8,128)S(1)}, f32[160,128]{1,0:T(8,128)S(1)}, u32[]{:S(2)}, u32[]{:S(2)}) %collective-permute-start.17) | collective-permute-done | bytes 81952 | tf_op jit(solution)/shard_map/ppermute | solution.py:885
  55.7 2.4 %second_edge.1 = (f32[7680,128]{1,0:T(8,128)S(1)}, f32[12480,128]{1,0:T(8,128)S(1)}, f32[2048,128]{1,0:T(8,128)}) custom-call(s32[80,128]{1,0:T(8,128)S(1)} %get-tuple-element.38.refs_3_.refs_0_, f32[296,128]{1,0:T(8,128)S(1)} %copy-done.1, f32[7,8,128]{2,1,0:T(8,128)S(1)} %copy-done.2, ...), custom_call_target="tpu_custom_call", output_to_operand_aliasing={{0}: (5, {}), {1}: (6, {})} | custom-call | tf_op jit(solution)/shard_map/second_edge/pallas_call | solution.py:926
  (40 shorter events, 8.3 us)
Async XLA Ops:
  0.0 18.7 %copy-start = (f32[1,16,16,8,128]{4,3,2,1,0:T(8,128)S(1)}, f32[1,16,16,8,128]{4,3,2,1,0:T(8,128)}, u32[]{:S(2)}) copy-start(f32[1,16,16,8,128]{4,3,2,1,0:T(8,128)} %param.7) | copy-start | bytes 3145732
  1.2 9.4 %collective-permute-start.1 = (f32[512,128]{1,0:T(8,128)S(1)}, f32[512,128]{1,0:T(8,128)S(1)}, u32[]{:S(2)}, u32[]{:S(2)}) collective-permute-start(f32[512,128]{1,0:T(8,128)S(1)} %bitcast.20), channel_id=1, source_target_pairs={{0,4},{1,5},{2,6},{3,7},{4,0},{5,1},{6,2},{7,3},{8,12},{9,13},{10,... | collective-permute-start | bytes 786440 | tf_op jit(solution)/shard_map/ppermute | solution.py:802
  4.3 6.3 %collective-permute-start.2 = (f32[512,128]{1,0:T(8,128)S(1)}, f32[512,128]{1,0:T(8,128)S(1)}, u32[]{:S(2)}, u32[]{:S(2)}) collective-permute-start(f32[512,128]{1,0:T(8,128)S(1)} %bitcast.19), channel_id=1, source_target_pairs={{0,1},{1,0},{2,3},{3,2},{4,8},{5,9},{6,10},{7,11},{8,4},{9,5},{10,... | collective-permute-start | bytes 786440 | tf_op jit(solution)/shard_map/ppermute | solution.py:803
  5.0 0.7 %copy-start.3 = (f32[1,32,16]{1,2,0:T(8,128)S(1)}, f32[1,32,16]{1,2,0:T(8,128)}, u32[]{:S(2)}) copy-start(f32[1,32,16]{1,2,0:T(8,128)} %param.9) | copy-start | bytes 6148
  5.7 0.7 %copy-start.4 = (s32[1,32,2]{1,2,0:T(2,128)S(1)}, s32[1,32,2]{1,2,0:T(2,128)}, u32[]{:S(2)}) copy-start(s32[1,32,2]{1,2,0:T(2,128)} %param.8) | copy-start | bytes 772
  10.7 8.7 %collective-permute-start.3 = (f32[768,128]{1,0:T(8,128)S(1)}, f32[768,128]{1,0:T(8,128)S(1)}, u32[]{:S(2)}, u32[]{:S(2)}) collective-permute-start(f32[768,128]{1,0:T(8,128)S(1)} %get-tuple-element.42), channel_id=1, source_target_pairs={{0,4},{1,2},{2,1},{3,7},{4,0},{5,6},{6,5},{7,3},{8,12},{9,10},{10,... | collective-permute-start | bytes 1179656 | tf_op jit(solution)/shard_map/ppermute | solution.py:846
  13.6 5.8 %collective-permute-start.4 = (f32[768,128]{1,0:T(8,128)S(1)}, f32[768,128]{1,0:T(8,128)S(1)}, u32[]{:S(2)}, u32[]{:S(2)}) collective-permute-start(f32[768,128]{1,0:T(8,128)S(1)} %get-tuple-element.43.refs_0_), channel_id=1, source_target_pairs={{0,1},{1,0},{2,3},{3,2},{4,5},{5,4},{6,7},{7,6},{8,9},{9,8},{10,11... | collective-permute-start | bytes 1179656 | tf_op jit(solution)/shard_map/ppermute | solution.py:847
  14.4 3.6 %collective-permute-start = (s32[2]{0:T(128)S(1)}, s32[2]{0:T(128)S(1)}, u32[]{:S(2)}, u32[]{:S(2)}) collective-permute-start(s32[2]{0:T(128)S(1)} %slice_reduce_fusion.refs_0_), channel_id=1, source_target_pairs={{0,16},{16,0},{1,17},{17,1},{2,18},{18,2},{3,19},{19,3},{4,20},{20... | collective-permute-start | bytes 32 | tf_op jit(solution)/shard_map/ppermute | solution.py:794
  18.7 13.8 %copy-start.1 = (f32[296,128]{1,0:T(8,128)S(1)}, f32[296,128]{1,0:T(8,128)}, u32[]{:S(2)}) copy-start(f32[296,128]{1,0:T(8,128)} %constant.29.clone.refs_0_.refs_4_.refs_1_) | copy-start | bytes 454660
  18.7 13.7 %copy-start.2 = (f32[7,8,128]{2,1,0:T(8,128)S(1)}, f32[7,8,128]{2,1,0:T(8,128)}, u32[]{:S(2)}) copy-start(f32[7,8,128]{2,1,0:T(8,128)} %constant.30.clone.refs_1_.refs_5_.refs_2_) | copy-start | bytes 86020
  20.1 3.6 %collective-permute-start.5 = (f32[104,128]{1,0:T(8,128)S(1)}, f32[104,128]{1,0:T(8,128)S(1)}, u32[]{:S(2)}, u32[]{:S(2)}) collective-permute-start(f32[104,128]{1,0:T(8,128)S(1)} %get-tuple-element.46), channel_id=1, source_target_pairs={{0,3},{1,2},{2,1},{3,0},{4,7},{5,6},{6,5},{7,4},{8,11},{9,10},{10,... | collective-permute-start | bytes 159752 | tf_op jit(solution)/shard_map/ppermute | solution.py:871
  20.1 3.5 %collective-permute-start.6 = (f32[104,128]{1,0:T(8,128)S(1)}, f32[104,128]{1,0:T(8,128)S(1)}, u32[]{:S(2)}, u32[]{:S(2)}) collective-permute-start(f32[104,128]{1,0:T(8,128)S(1)} %get-tuple-element.47), channel_id=1, source_target_pairs={{0,1},{1,0},{2,3},{3,2},{4,5},{5,4},{6,7},{7,6},{8,9},{9,8},{10,11... | collective-permute-start | bytes 159752 | tf_op jit(solution)/shard_map/ppermute | solution.py:871
  20.5 4.3 %collective-permute-start.7 = (f32[104,128]{1,0:T(8,128)S(1)}, f32[104,128]{1,0:T(8,128)S(1)}, u32[]{:S(2)}, u32[]{:S(2)}) collective-permute-start(f32[104,128]{1,0:T(8,128)S(1)} %get-tuple-element.48), channel_id=1, source_target_pairs={{0,2},{1,3},{2,0},{3,1},{4,6},{5,7},{6,4},{7,5},{8,10},{9,11},{10,... | collective-permute-start | bytes 159752 | tf_op jit(solution)/shard_map/ppermute | solution.py:871
  24.9 11.4 %collective-permute-start.8 = (f32[160,128]{1,0:T(8,128)S(1)}, f32[160,128]{1,0:T(8,128)S(1)}, u32[]{:S(2)}, u32[]{:S(2)}) collective-permute-start(f32[160,128]{1,0:T(8,128)S(1)} %get-tuple-element.54), channel_id=1, source_target_pairs={{0,20},{4,16},{8,28},{12,24},{1,5},{5,17},{9,29},{13,9},{2,6},{6,1... | collective-permute-start | bytes 245768 | tf_op jit(solution)/shard_map/ppermute | solution.py:885
  28.4 7.9 %collective-permute-start.9 = (f32[160,128]{1,0:T(8,128)S(1)}, f32[160,128]{1,0:T(8,128)S(1)}, u32[]{:S(2)}, u32[]{:S(2)}) collective-permute-start(f32[160,128]{1,0:T(8,128)S(1)} %get-tuple-element.55), channel_id=1, source_target_pairs={{0,28},{4,24},{8,20},{12,16},{1,29},{5,6},{9,10},{13,17},{2,30},{6... | collective-permute-start | bytes 245768 | tf_op jit(solution)/shard_map/ppermute | solution.py:885
  31.0 6.5 %collective-permute-start.10 = (f32[160,128]{1,0:T(8,128)S(1)}, f32[160,128]{1,0:T(8,128)S(1)}, u32[]{:S(2)}, u32[]{:S(2)}) collective-permute-start(f32[160,128]{1,0:T(8,128)S(1)} %get-tuple-element.56), channel_id=1, source_target_pairs={{0,24},{4,28},{8,16},{12,20},{1,5},{5,29},{9,17},{13,9},{2,6},{6,3... | collective-permute-start | bytes 245768 | tf_op jit(solution)/shard_map/ppermute | solution.py:885
  31.0 6.5 %collective-permute-start.11 = (f32[160,128]{1,0:T(8,128)S(1)}, f32[160,128]{1,0:T(8,128)S(1)}, u32[]{:S(2)}, u32[]{:S(2)}) collective-permute-start(f32[160,128]{1,0:T(8,128)S(1)} %get-tuple-element.49.refs_3_), channel_id=1, source_target_pairs={{0,16},{4,20},{8,24},{12,28},{1,17},{5,6},{9,10},{13,29},{2,18},{6... | collective-permute-start | bytes 245768 | tf_op jit(solution)/shard_map/ppermute | solution.py:885
  39.6 3.6 %collective-permute-start.12 = (f32[104,128]{1,0:T(8,128)S(1)}, f32[104,128]{1,0:T(8,128)S(1)}, u32[]{:S(2)}, u32[]{:S(2)}) collective-permute-start(f32[104,128]{1,0:T(8,128)S(1)} %get-tuple-element.60), channel_id=1, source_target_pairs={{0,3},{1,2},{2,1},{3,0},{4,7},{5,6},{6,5},{7,4},{8,11},{9,10},{10,... | collective-permute-start | bytes 159752 | tf_op jit(solution)/shard_map/ppermute | solution.py:871
  39.7 3.5 %collective-permute-start.13 = (f32[104,128]{1,0:T(8,128)S(1)}, f32[104,128]{1,0:T(8,128)S(1)}, u32[]{:S(2)}, u32[]{:S(2)}) collective-permute-start(f32[104,128]{1,0:T(8,128)S(1)} %get-tuple-element.61), channel_id=1, source_target_pairs={{0,1},{1,0},{2,3},{3,2},{4,5},{5,4},{6,7},{7,6},{8,9},{9,8},{10,11... | collective-permute-start | bytes 159752 | tf_op jit(solution)/shard_map/ppermute | solution.py:871
  40.1 4.3 %collective-permute-start.14 = (f32[104,128]{1,0:T(8,128)S(1)}, f32[104,128]{1,0:T(8,128)S(1)}, u32[]{:S(2)}, u32[]{:S(2)}) collective-permute-start(f32[104,128]{1,0:T(8,128)S(1)} %get-tuple-element.62), channel_id=1, source_target_pairs={{0,2},{1,3},{2,0},{3,1},{4,6},{5,7},{6,4},{7,5},{8,10},{9,11},{10,... | collective-permute-start | bytes 159752 | tf_op jit(solution)/shard_map/ppermute | solution.py:871
  44.4 8.7 %collective-permute-start.15 = (f32[160,128]{1,0:T(8,128)S(1)}, f32[160,128]{1,0:T(8,128)S(1)}, u32[]{:S(2)}, u32[]{:S(2)}) collective-permute-start(f32[160,128]{1,0:T(8,128)S(1)} %get-tuple-element.67), channel_id=1, source_target_pairs={{0,20},{4,16},{8,28},{12,24},{1,5},{5,17},{9,29},{13,9},{2,6},{6,1... | collective-permute-start | bytes 245768 | tf_op jit(solution)/shard_map/ppermute | solution.py:885
  45.6 7.8 %collective-permute-start.16 = (f32[160,128]{1,0:T(8,128)S(1)}, f32[160,128]{1,0:T(8,128)S(1)}, u32[]{:S(2)}, u32[]{:S(2)}) collective-permute-start(f32[160,128]{1,0:T(8,128)S(1)} %get-tuple-element.68), channel_id=1, source_target_pairs={{0,28},{4,24},{8,20},{12,16},{1,29},{5,6},{9,10},{13,17},{2,30},{6... | collective-permute-start | bytes 245768 | tf_op jit(solution)/shard_map/ppermute | solution.py:885
  48.4 7.3 %collective-permute-start.17 = (f32[160,128]{1,0:T(8,128)S(1)}, f32[160,128]{1,0:T(8,128)S(1)}, u32[]{:S(2)}, u32[]{:S(2)}) collective-permute-start(f32[160,128]{1,0:T(8,128)S(1)} %get-tuple-element.69), channel_id=1, source_target_pairs={{0,24},{4,28},{8,16},{12,20},{1,5},{5,29},{9,17},{13,9},{2,6},{6,3... | collective-permute-start | bytes 245768 | tf_op jit(solution)/shard_map/ppermute | solution.py:885
  49.5 6.1 %collective-permute-start.18 = (f32[160,128]{1,0:T(8,128)S(1)}, f32[160,128]{1,0:T(8,128)S(1)}, u32[]{:S(2)}, u32[]{:S(2)}) collective-permute-start(f32[160,128]{1,0:T(8,128)S(1)} %get-tuple-element.63.refs_4_), channel_id=1, source_target_pairs={{0,16},{4,20},{8,24},{12,28},{1,17},{5,6},{9,10},{13,29},{2,18},{6... | collective-permute-start | bytes 245768 | tf_op jit(solution)/shard_map/ppermute | solution.py:885

commit v13 on v12

--- a/solution.py
+++ b/solution.py
@@ -370,7 +370,7 @@
         value_ref[tiles(entry, 1), :] = jnp.where(turned, mixed, total)
         return carry
 
-    lax.fori_loop(0, loop.entries, one_entry, 0, unroll=4)
+    lax.fori_loop(0, loop.entries, one_entry, 0, unroll=8 if loop.entries % 8 == 0 else 4)
     for step, send_ref in enumerate(send_refs):
         for slot in range(loop.column_slots):
             entry = lookup(send_table_ref, step * loop.column_slots + slot)

time: 58.3 us -> 58 us (level)
  no operation moved by 1% of the time
where the time goes in v13:
time: 58 us; the launch traced here: 57.7 us
  starting transfers between devices  25.5 us (44%)
  waiting for transfers between devices  14.4 us (25%)
  Pallas kernels  12.5 us (22%)
  local copies, waits for them, and re-layouts  2.88 us (5%)
  other arithmetic  2.24 us (4%)
    ppermute x8, starting transfers between devices, second_round(): lax.ppermute(turned[step], everyone, lat_route(step, lat_count, lon_count))  13.5 us
    ppermute x6, waiting for transfers between devices, first_round(): lax.ppermute(packed[step], 'lon', lon_route(step, lon_count))  5.11 us
    ppermute x6, starting transfers between devices, first_round(): lax.ppermute(packed[step], 'lon', lon_route(step, lon_count))  4.4 us
    ppermute x8, waiting for transfers between devices, second_round(): lax.ppermute(turned[step], everyone, lat_route(step, lat_count, lon_count))  3.82 us
    pallas_call x1, Pallas kernels, per_device(): pl.pallas_call(lambda *refs: first_inner_kernel(loop, *refs), out_shape=[...  3.74 us
    ppermute x1, starting transfers between devices, per_device(): lax.ppermute(send_even, everyone, swap_route(0, lat_count, lon_count, True))  3.12 us
    ppermute x1, waiting for transfers between devices, per_device(): lax.ppermute(send_even, everyone, swap_route(0, lat_count, lon_count, True))  2.95 us
    ppermute x1, starting transfers between devices, per_device(): lax.ppermute(strip_odd, everyone, swap_route(1, lat_count, lon_count, Fal...  2.93 us
  transfers between devices with their start and end apart: 19, of which 10 were waited for; matrix products, arithmetic and copies ran while one was open for 4% of the time, Pallas kernels for 13%

profile of v13, /device:TPU:0, one launch (start us, length us, event | category | flops | bytes accessed | tf_op | source)
XLA Modules:
  0.0 57.7 jit_solution(10149276736231398603)
XLA Ops:
  0.0 1.2 %slice_select_fusion.2 = (f32[1,4,16,8,128]{4,3,2,1,0:T(8,128)S(1)}, f32[1,4,16,8,128]{4,3,2,1,0:T(8,128)S(1)}) fusion(f32[1,16,16,8,128]{4,3,2,1,0:T(8,128)} %param.7, pred[]{:T(512)S(6)} %eq.10), kind=kLoop, calls=%fused_computation.2 | loop fusion | flops 131072 | bytes 1048577 | tf_op jit(solution)/shard_map/jit(_where)/select_n | solution.py:801
  1.2 3.1 %collective-permute-start.1 = (f32[512,128]{1,0:T(8,128)S(1)}, f32[512,128]{1,0:T(8,128)S(1)}, u32[]{:S(2)}, u32[]{:S(2)}) collective-permute-start(f32[512,128]{1,0:T(8,128)S(1)} %bitcast.20), channel_id=1, source_target_pairs={{0,4},{1,5},{2,6},{3,7},{4,0},{5,1},{6,2},{7,3},{8,12},{9,13},{10,... | collective-permute-start | bytes 786440 | tf_op jit(solution)/shard_map/ppermute | solution.py:802
  7.6 3.0 %collective-permute-done.1.refs_3_.refs_2_ = f32[512,128]{1,0:T(8,128)S(1)} collective-permute-done((f32[512,128]{1,0:T(8,128)S(1)}, f32[512,128]{1,0:T(8,128)S(1)}, u32[]{:S(2)}, u32[]{:S(2)}) %collective-permute-start.1) | collective-permute-done | bytes 262176 | tf_op jit(solution)/shard_map/ppermute | solution.py:802
  10.7 2.9 %collective-permute-start.3 = (f32[768,128]{1,0:T(8,128)S(1)}, f32[768,128]{1,0:T(8,128)S(1)}, u32[]{:S(2)}, u32[]{:S(2)}) collective-permute-start(f32[768,128]{1,0:T(8,128)S(1)} %get-tuple-element.42), channel_id=1, source_target_pairs={{0,4},{1,2},{2,1},{3,7},{4,0},{5,6},{6,5},{7,3},{8,12},{9,10},{10,... | collective-permute-start | bytes 1179656 | tf_op jit(solution)/shard_map/ppermute | solution.py:846
  14.4 1.5 %collective-permute-start = (s32[2]{0:T(128)S(1)}, s32[2]{0:T(128)S(1)}, u32[]{:S(2)}, u32[]{:S(2)}) collective-permute-start(s32[2]{0:T(128)S(1)} %slice_reduce_fusion.refs_0_), channel_id=1, source_target_pairs={{0,16},{16,0},{1,17},{17,1},{2,18},{18,2},{3,19},{19,3},{4,20},{20... | collective-permute-start | bytes 32 | tf_op jit(solution)/shard_map/ppermute | solution.py:794
  15.9 2.1 %collective-permute-done.refs_1_ = s32[2]{0:T(128)S(1)} collective-permute-done((s32[2]{0:T(128)S(1)}, s32[2]{0:T(128)S(1)}, u32[]{:S(2)}, u32[]{:S(2)}) %collective-permute-start) | collective-permute-done | bytes 40 | tf_op jit(solution)/shard_map/ppermute | solution.py:794
  20.4 1.8 %collective-permute-start.7 = (f32[104,128]{1,0:T(8,128)S(1)}, f32[104,128]{1,0:T(8,128)S(1)}, u32[]{:S(2)}, u32[]{:S(2)}) collective-permute-start(f32[104,128]{1,0:T(8,128)S(1)} %get-tuple-element.48), channel_id=1, source_target_pairs={{0,2},{1,3},{2,0},{3,1},{4,6},{5,7},{6,4},{7,5},{8,10},{9,11},{10,... | collective-permute-start | bytes 159752 | tf_op jit(solution)/shard_map/ppermute | solution.py:871
  22.1 1.4 %collective-permute-done.5.refs_1_ = f32[104,128]{1,0:T(8,128)S(1)} collective-permute-done((f32[104,128]{1,0:T(8,128)S(1)}, f32[104,128]{1,0:T(8,128)S(1)}, u32[]{:S(2)}, u32[]{:S(2)}) %collective-permute-start.5) | collective-permute-done | bytes 53280 | tf_op jit(solution)/shard_map/ppermute | solution.py:871
  23.5 1.1 %collective-permute-done.7.refs_3_ = f32[104,128]{1,0:T(8,128)S(1)} collective-permute-done((f32[104,128]{1,0:T(8,128)S(1)}, f32[104,128]{1,0:T(8,128)S(1)}, u32[]{:S(2)}, u32[]{:S(2)}) %collective-permute-start.7) | collective-permute-done | bytes 53280 | tf_op jit(solution)/shard_map/ppermute | solution.py:871
  24.7 3.5 %collective-permute-start.8 = (f32[160,128]{1,0:T(8,128)S(1)}, f32[160,128]{1,0:T(8,128)S(1)}, u32[]{:S(2)}, u32[]{:S(2)}) collective-permute-start(f32[160,128]{1,0:T(8,128)S(1)} %get-tuple-element.54), channel_id=1, source_target_pairs={{0,20},{4,16},{8,28},{12,24},{1,5},{5,17},{9,29},{13,9},{2,6},{6,1... | collective-permute-start | bytes 245768 | tf_op jit(solution)/shard_map/ppermute | solution.py:885
  28.2 2.6 %collective-permute-start.9 = (f32[160,128]{1,0:T(8,128)S(1)}, f32[160,128]{1,0:T(8,128)S(1)}, u32[]{:S(2)}, u32[]{:S(2)}) collective-permute-start(f32[160,128]{1,0:T(8,128)S(1)} %get-tuple-element.55), channel_id=1, source_target_pairs={{0,28},{4,24},{8,20},{12,16},{1,29},{5,6},{9,10},{13,17},{2,30},{6... | collective-permute-start | bytes 245768 | tf_op jit(solution)/shard_map/ppermute | solution.py:885
  30.8 1.5 %collective-permute-start.11 = (f32[160,128]{1,0:T(8,128)S(1)}, f32[160,128]{1,0:T(8,128)S(1)}, u32[]{:S(2)}, u32[]{:S(2)}) collective-permute-start(f32[160,128]{1,0:T(8,128)S(1)} %get-tuple-element.49.refs_3_), channel_id=1, source_target_pairs={{0,16},{4,20},{8,24},{12,28},{1,17},{5,6},{9,10},{13,29},{2,18},{6... | collective-permute-start | bytes 245768 | tf_op jit(solution)/shard_map/ppermute | solution.py:885
  32.3 3.7 %first_inner.1 = (f32[4608,128]{1,0:T(8,128)S(1)}, f32[8,24,24,128]{3,2,1,0:T(8,128)S(1)}, f32[7680,128]{1,0:T(8,128)S(1)}, f32[12480,128]{1,0:T(8,128)S(1)}) custom-call(f32[296,128]{1,0:T(8,128)S(1)} %copy-done.1, f32[7,8,128]{2,1,0:T(8,128)S(1)} %copy-done.2, f32[4608,128]{1,0:T(8,128)S(1)} %get-tuple-element.44.refs_2_, ...), custom_call_target="tpu_custom_call" | custom-call | tf_op jit(solution)/shard_map/first_inner/pallas_call | solution.py:897
  36.1 1.2 %collective-permute-done.10.refs_12_ = f32[160,128]{1,0:T(8,128)S(1)} collective-permute-done((f32[160,128]{1,0:T(8,128)S(1)}, f32[160,128]{1,0:T(8,128)S(1)}, u32[]{:S(2)}, u32[]{:S(2)}) %collective-permute-start.10) | collective-permute-done | bytes 81952 | tf_op jit(solution)/shard_map/ppermute | solution.py:885
  37.3 2.0 %first_edge.1 = (f32[4608,128]{1,0:T(8,128)S(1)}, f32[8,24,24,128]{3,2,1,0:T(8,128)S(1)}, f32[7680,128]{1,0:T(8,128)S(1)}, f32[12480,128]{1,0:T(8,128)S(1)}, f32...) custom-call(s32[56,128]{1,0:T(8,128)S(1)} %get-tuple-element.39.refs, ...), custom_call_target="tpu_custom_call", output_to_operand_aliasing={{0}: (6, {}), {1}: (7, {}), {2}: (8, {}), {3}: (9, {})} | custom-call | tf_op jit(solution)/shard_map/first_edge/pallas_call | solution.py:905
  39.7 1.8 %collective-permute-start.14 = (f32[104,128]{1,0:T(8,128)S(1)}, f32[104,128]{1,0:T(8,128)S(1)}, u32[]{:S(2)}, u32[]{:S(2)}) collective-permute-start(f32[104,128]{1,0:T(8,128)S(1)} %get-tuple-element.62), channel_id=1, source_target_pairs={{0,2},{1,3},{2,0},{3,1},{4,6},{5,7},{6,4},{7,5},{8,10},{9,11},{10,... | collective-permute-start | bytes 159752 | tf_op jit(solution)/shard_map/ppermute | solution.py:871
  41.5 1.4 %collective-permute-done.12.refs_1_ = f32[104,128]{1,0:T(8,128)S(1)} collective-permute-done((f32[104,128]{1,0:T(8,128)S(1)}, f32[104,128]{1,0:T(8,128)S(1)}, u32[]{:S(2)}, u32[]{:S(2)}) %collective-permute-start.12) | collective-permute-done | bytes 53280 | tf_op jit(solution)/shard_map/ppermute | solution.py:871
  42.9 1.1 %collective-permute-done.14.refs_3_ = f32[104,128]{1,0:T(8,128)S(1)} collective-permute-done((f32[104,128]{1,0:T(8,128)S(1)}, f32[104,128]{1,0:T(8,128)S(1)}, u32[]{:S(2)}, u32[]{:S(2)}) %collective-permute-start.14) | collective-permute-done | bytes 53280 | tf_op jit(solution)/shard_map/ppermute | solution.py:871
  44.1 1.2 %collective-permute-start.15 = (f32[160,128]{1,0:T(8,128)S(1)}, f32[160,128]{1,0:T(8,128)S(1)}, u32[]{:S(2)}, u32[]{:S(2)}) collective-permute-start(f32[160,128]{1,0:T(8,128)S(1)} %get-tuple-element.67), channel_id=1, source_target_pairs={{0,20},{4,16},{8,28},{12,24},{1,5},{5,17},{9,29},{13,9},{2,6},{6,1... | collective-permute-start | bytes 245768 | tf_op jit(solution)/shard_map/ppermute | solution.py:885
  45.3 2.7 %collective-permute-start.16 = (f32[160,128]{1,0:T(8,128)S(1)}, f32[160,128]{1,0:T(8,128)S(1)}, u32[]{:S(2)}, u32[]{:S(2)}) collective-permute-start(f32[160,128]{1,0:T(8,128)S(1)} %get-tuple-element.68), channel_id=1, source_target_pairs={{0,28},{4,24},{8,20},{12,16},{1,29},{5,6},{9,10},{13,17},{2,30},{6... | collective-permute-start | bytes 245768 | tf_op jit(solution)/shard_map/ppermute | solution.py:885
  48.0 1.2 %collective-permute-start.17 = (f32[160,128]{1,0:T(8,128)S(1)}, f32[160,128]{1,0:T(8,128)S(1)}, u32[]{:S(2)}, u32[]{:S(2)}) collective-permute-start(f32[160,128]{1,0:T(8,128)S(1)} %get-tuple-element.69), channel_id=1, source_target_pairs={{0,24},{4,28},{8,16},{12,20},{1,5},{5,29},{9,17},{13,9},{2,6},{6,3... | collective-permute-start | bytes 245768 | tf_op jit(solution)/shard_map/ppermute | solution.py:885
  50.0 2.8 %second_inner.1 = (f32[2048,128]{1,0:T(8,128)S(1)}, f32[7680,128]{1,0:T(8,128)S(1)}, f32[12480,128]{1,0:T(8,128)S(1)}) custom-call(f32[296,128]{1,0:T(8,128)S(1)} %copy-done.1, f32[7,8,128]{2,1,0:T(8,128)S(1)} %copy-done.2, f32[4608,128]{1,0:T(8,128)S(1)} %get-tuple-element.58.refs_2_, f32[8,24,24,128]{3,2,1,0:T(8,128)S(1)} %get-tuple-element.57.refs_3_, ...), custom_call_target="tpu_custom_call" | custom-call | tf_op jit(solution)/shard_map/second_inner/pallas_call | solution.py:918
  53.2 2.2 %collective-permute-done.17.refs_9_ = f32[160,128]{1,0:T(8,128)S(1)} collective-permute-done((f32[160,128]{1,0:T(8,128)S(1)}, f32[160,128]{1,0:T(8,128)S(1)}, u32[]{:S(2)}, u32[]{:S(2)}) %collective-permute-start.17) | collective-permute-done | bytes 81952 | tf_op jit(solution)/shard_map/ppermute | solution.py:885
  55.4 2.4 %second_edge.1 = (f32[7680,128]{1,0:T(8,128)S(1)}, f32[12480,128]{1,0:T(8,128)S(1)}, f32[2048,128]{1,0:T(8,128)}) custom-call(s32[80,128]{1,0:T(8,128)S(1)} %get-tuple-element.38.refs_3_.refs_0_, f32[296,128]{1,0:T(8,128)S(1)} %copy-done.1, f32[7,8,128]{2,1,0:T(8,128)S(1)} %copy-done.2, ...), custom_call_target="tpu_custom_call", output_to_operand_aliasing={{0}: (5, {}), {1}: (6, {})} | custom-call | tf_op jit(solution)/shard_map/second_edge/pallas_call | solution.py:926
  (40 shorter events, 8.2 us)
Async XLA Ops:
  0.0 18.7 %copy-start = (f32[1,16,16,8,128]{4,3,2,1,0:T(8,128)S(1)}, f32[1,16,16,8,128]{4,3,2,1,0:T(8,128)}, u32[]{:S(2)}) copy-start(f32[1,16,16,8,128]{4,3,2,1,0:T(8,128)} %param.7) | copy-start | bytes 3145732
  1.2 9.4 %collective-permute-start.1 = (f32[512,128]{1,0:T(8,128)S(1)}, f32[512,128]{1,0:T(8,128)S(1)}, u32[]{:S(2)}, u32[]{:S(2)}) collective-permute-start(f32[512,128]{1,0:T(8,128)S(1)} %bitcast.20), channel_id=1, source_target_pairs={{0,4},{1,5},{2,6},{3,7},{4,0},{5,1},{6,2},{7,3},{8,12},{9,13},{10,... | collective-permute-start | bytes 786440 | tf_op jit(solution)/shard_map/ppermute | solution.py:802
  4.3 6.3 %collective-permute-start.2 = (f32[512,128]{1,0:T(8,128)S(1)}, f32[512,128]{1,0:T(8,128)S(1)}, u32[]{:S(2)}, u32[]{:S(2)}) collective-permute-start(f32[512,128]{1,0:T(8,128)S(1)} %bitcast.19), channel_id=1, source_target_pairs={{0,1},{1,0},{2,3},{3,2},{4,8},{5,9},{6,10},{7,11},{8,4},{9,5},{10,... | collective-permute-start | bytes 786440 | tf_op jit(solution)/shard_map/ppermute | solution.py:803
  5.0 0.7 %copy-start.3 = (f32[1,32,16]{1,2,0:T(8,128)S(1)}, f32[1,32,16]{1,2,0:T(8,128)}, u32[]{:S(2)}) copy-start(f32[1,32,16]{1,2,0:T(8,128)} %param.9) | copy-start | bytes 6148
  5.7 0.7 %copy-start.4 = (s32[1,32,2]{1,2,0:T(2,128)S(1)}, s32[1,32,2]{1,2,0:T(2,128)}, u32[]{:S(2)}) copy-start(s32[1,32,2]{1,2,0:T(2,128)} %param.8) | copy-start | bytes 772
  10.7 8.7 %collective-permute-start.3 = (f32[768,128]{1,0:T(8,128)S(1)}, f32[768,128]{1,0:T(8,128)S(1)}, u32[]{:S(2)}, u32[]{:S(2)}) collective-permute-start(f32[768,128]{1,0:T(8,128)S(1)} %get-tuple-element.42), channel_id=1, source_target_pairs={{0,4},{1,2},{2,1},{3,7},{4,0},{5,6},{6,5},{7,3},{8,12},{9,10},{10,... | collective-permute-start | bytes 1179656 | tf_op jit(solution)/shard_map/ppermute | solution.py:846
  13.6 5.8 %collective-permute-start.4 = (f32[768,128]{1,0:T(8,128)S(1)}, f32[768,128]{1,0:T(8,128)S(1)}, u32[]{:S(2)}, u32[]{:S(2)}) collective-permute-start(f32[768,128]{1,0:T(8,128)S(1)} %get-tuple-element.43.refs_0_), channel_id=1, source_target_pairs={{0,1},{1,0},{2,3},{3,2},{4,5},{5,4},{6,7},{7,6},{8,9},{9,8},{10,11... | collective-permute-start | bytes 1179656 | tf_op jit(solution)/shard_map/ppermute | solution.py:847
  14.4 3.6 %collective-permute-start = (s32[2]{0:T(128)S(1)}, s32[2]{0:T(128)S(1)}, u32[]{:S(2)}, u32[]{:S(2)}) collective-permute-start(s32[2]{0:T(128)S(1)} %slice_reduce_fusion.refs_0_), channel_id=1, source_target_pairs={{0,16},{16,0},{1,17},{17,1},{2,18},{18,2},{3,19},{19,3},{4,20},{20... | collective-permute-start | bytes 32 | tf_op jit(solution)/shard_map/ppermute | solution.py:794
  18.7 13.6 %copy-start.1 = (f32[296,128]{1,0:T(8,128)S(1)}, f32[296,128]{1,0:T(8,128)}, u32[]{:S(2)}) copy-start(f32[296,128]{1,0:T(8,128)} %constant.29.clone.refs_0_.refs_4_.refs_1_) | copy-start | bytes 454660
  18.7 13.6 %copy-start.2 = (f32[7,8,128]{2,1,0:T(8,128)S(1)}, f32[7,8,128]{2,1,0:T(8,128)}, u32[]{:S(2)}) copy-start(f32[7,8,128]{2,1,0:T(8,128)} %constant.30.clone.refs_1_.refs_5_.refs_2_) | copy-start | bytes 86020
  19.9 3.6 %collective-permute-start.5 = (f32[104,128]{1,0:T(8,128)S(1)}, f32[104,128]{1,0:T(8,128)S(1)}, u32[]{:S(2)}, u32[]{:S(2)}) collective-permute-start(f32[104,128]{1,0:T(8,128)S(1)} %get-tuple-element.46), channel_id=1, source_target_pairs={{0,3},{1,2},{2,1},{3,0},{4,7},{5,6},{6,5},{7,4},{8,11},{9,10},{10,... | collective-permute-start | bytes 159752 | tf_op jit(solution)/shard_map/ppermute | solution.py:871
  20.0 3.5 %collective-permute-start.6 = (f32[104,128]{1,0:T(8,128)S(1)}, f32[104,128]{1,0:T(8,128)S(1)}, u32[]{:S(2)}, u32[]{:S(2)}) collective-permute-start(f32[104,128]{1,0:T(8,128)S(1)} %get-tuple-element.47), channel_id=1, source_target_pairs={{0,1},{1,0},{2,3},{3,2},{4,5},{5,4},{6,7},{7,6},{8,9},{9,8},{10,11... | collective-permute-start | bytes 159752 | tf_op jit(solution)/shard_map/ppermute | solution.py:871
  20.4 4.3 %collective-permute-start.7 = (f32[104,128]{1,0:T(8,128)S(1)}, f32[104,128]{1,0:T(8,128)S(1)}, u32[]{:S(2)}, u32[]{:S(2)}) collective-permute-start(f32[104,128]{1,0:T(8,128)S(1)} %get-tuple-element.48), channel_id=1, source_target_pairs={{0,2},{1,3},{2,0},{3,1},{4,6},{5,7},{6,4},{7,5},{8,10},{9,11},{10,... | collective-permute-start | bytes 159752 | tf_op jit(solution)/shard_map/ppermute | solution.py:871
  24.7 11.4 %collective-permute-start.8 = (f32[160,128]{1,0:T(8,128)S(1)}, f32[160,128]{1,0:T(8,128)S(1)}, u32[]{:S(2)}, u32[]{:S(2)}) collective-permute-start(f32[160,128]{1,0:T(8,128)S(1)} %get-tuple-element.54), channel_id=1, source_target_pairs={{0,20},{4,16},{8,28},{12,24},{1,5},{5,17},{9,29},{13,9},{2,6},{6,1... | collective-permute-start | bytes 245768 | tf_op jit(solution)/shard_map/ppermute | solution.py:885
  28.2 7.9 %collective-permute-start.9 = (f32[160,128]{1,0:T(8,128)S(1)}, f32[160,128]{1,0:T(8,128)S(1)}, u32[]{:S(2)}, u32[]{:S(2)}) collective-permute-start(f32[160,128]{1,0:T(8,128)S(1)} %get-tuple-element.55), channel_id=1, source_target_pairs={{0,28},{4,24},{8,20},{12,16},{1,29},{5,6},{9,10},{13,17},{2,30},{6... | collective-permute-start | bytes 245768 | tf_op jit(solution)/shard_map/ppermute | solution.py:885
  30.8 6.5 %collective-permute-start.10 = (f32[160,128]{1,0:T(8,128)S(1)}, f32[160,128]{1,0:T(8,128)S(1)}, u32[]{:S(2)}, u32[]{:S(2)}) collective-permute-start(f32[160,128]{1,0:T(8,128)S(1)} %get-tuple-element.56), channel_id=1, source_target_pairs={{0,24},{4,28},{8,16},{12,20},{1,5},{5,29},{9,17},{13,9},{2,6},{6,3... | collective-permute-start | bytes 245768 | tf_op jit(solution)/shard_map/ppermute | solution.py:885
  30.8 6.5 %collective-permute-start.11 = (f32[160,128]{1,0:T(8,128)S(1)}, f32[160,128]{1,0:T(8,128)S(1)}, u32[]{:S(2)}, u32[]{:S(2)}) collective-permute-start(f32[160,128]{1,0:T(8,128)S(1)} %get-tuple-element.49.refs_3_), channel_id=1, source_target_pairs={{0,16},{4,20},{8,24},{12,28},{1,17},{5,6},{9,10},{13,29},{2,18},{6... | collective-permute-start | bytes 245768 | tf_op jit(solution)/shard_map/ppermute | solution.py:885
  39.3 3.6 %collective-permute-start.12 = (f32[104,128]{1,0:T(8,128)S(1)}, f32[104,128]{1,0:T(8,128)S(1)}, u32[]{:S(2)}, u32[]{:S(2)}) collective-permute-start(f32[104,128]{1,0:T(8,128)S(1)} %get-tuple-element.60), channel_id=1, source_target_pairs={{0,3},{1,2},{2,1},{3,0},{4,7},{5,6},{6,5},{7,4},{8,11},{9,10},{10,... | collective-permute-start | bytes 159752 | tf_op jit(solution)/shard_map/ppermute | solution.py:871
  39.4 3.5 %collective-permute-start.13 = (f32[104,128]{1,0:T(8,128)S(1)}, f32[104,128]{1,0:T(8,128)S(1)}, u32[]{:S(2)}, u32[]{:S(2)}) collective-permute-start(f32[104,128]{1,0:T(8,128)S(1)} %get-tuple-element.61), channel_id=1, source_target_pairs={{0,1},{1,0},{2,3},{3,2},{4,5},{5,4},{6,7},{7,6},{8,9},{9,8},{10,11... | collective-permute-start | bytes 159752 | tf_op jit(solution)/shard_map/ppermute | solution.py:871
  39.7 4.3 %collective-permute-start.14 = (f32[104,128]{1,0:T(8,128)S(1)}, f32[104,128]{1,0:T(8,128)S(1)}, u32[]{:S(2)}, u32[]{:S(2)}) collective-permute-start(f32[104,128]{1,0:T(8,128)S(1)} %get-tuple-element.62), channel_id=1, source_target_pairs={{0,2},{1,3},{2,0},{3,1},{4,6},{5,7},{6,4},{7,5},{8,10},{9,11},{10,... | collective-permute-start | bytes 159752 | tf_op jit(solution)/shard_map/ppermute | solution.py:871
  44.1 8.7 %collective-permute-start.15 = (f32[160,128]{1,0:T(8,128)S(1)}, f32[160,128]{1,0:T(8,128)S(1)}, u32[]{:S(2)}, u32[]{:S(2)}) collective-permute-start(f32[160,128]{1,0:T(8,128)S(1)} %get-tuple-element.67), channel_id=1, source_target_pairs={{0,20},{4,16},{8,28},{12,24},{1,5},{5,17},{9,29},{13,9},{2,6},{6,1... | collective-permute-start | bytes 245768 | tf_op jit(solution)/shard_map/ppermute | solution.py:885
  45.3 7.8 %collective-permute-start.16 = (f32[160,128]{1,0:T(8,128)S(1)}, f32[160,128]{1,0:T(8,128)S(1)}, u32[]{:S(2)}, u32[]{:S(2)}) collective-permute-start(f32[160,128]{1,0:T(8,128)S(1)} %get-tuple-element.68), channel_id=1, source_target_pairs={{0,28},{4,24},{8,20},{12,16},{1,29},{5,6},{9,10},{13,17},{2,30},{6... | collective-permute-start | bytes 245768 | tf_op jit(solution)/shard_map/ppermute | solution.py:885
  48.0 7.3 %collective-permute-start.17 = (f32[160,128]{1,0:T(8,128)S(1)}, f32[160,128]{1,0:T(8,128)S(1)}, u32[]{:S(2)}, u32[]{:S(2)}) collective-permute-start(f32[160,128]{1,0:T(8,128)S(1)} %get-tuple-element.69), channel_id=1, source_target_pairs={{0,24},{4,28},{8,16},{12,20},{1,5},{5,29},{9,17},{13,9},{2,6},{6,3... | collective-permute-start | bytes 245768 | tf_op jit(solution)/shard_map/ppermute | solution.py:885
  49.2 6.2 %collective-permute-start.18 = (f32[160,128]{1,0:T(8,128)S(1)}, f32[160,128]{1,0:T(8,128)S(1)}, u32[]{:S(2)}, u32[]{:S(2)}) collective-permute-start(f32[160,128]{1,0:T(8,128)S(1)} %get-tuple-element.63.refs_4_), channel_id=1, source_target_pairs={{0,16},{4,20},{8,24},{12,28},{1,17},{5,6},{9,10},{13,29},{2,18},{6... | collective-permute-start | bytes 245768 | tf_op jit(solution)/shard_map/ppermute | solution.py:885
